TPU v7x, 32 devices: a whole 2x2x4 slice. The times are simulated.
32 devices in a mesh: gx: 16 (over z, x, core), gz: 2 (over y).
Axes of the slice: x: 2, y: 2, z: 4, core: 2. Of those that a mesh axis runs over, the one named last changes fastest.
Arguments:
- saved_flow_speed_vector: bfloat16 [2, 3, 64, 32, 256], P(None, None, 'gx', None, 'gz'), may hold values from -11 to 11
- saved_mass_concentration: bfloat16 [2, 64, 32, 256], P(None, 'gx', None, 'gz'), may hold values from 0.5 to 2
- saved_thermal_excess: bfloat16 [2, 64, 32, 256], P(None, 'gx', None, 'gz'), may hold values from -5 to 5
- costate_vector_subsequent: float32 [5, 64, 32, 256], P(None, 'gx', None, 'gz'), may hold values from -6 to 6
Outputs:
- adjoint_out: float32 [5, 64, 32, 256], P(None, 'gx', None, 'gz')
- coef_grad: float32 [2, 64, 32], P(None, 'gx')
All inputs are finite; a program needn't handle non-finite values.
Results may differ from a plain program's by a relative error of at most 0.00065.
Values may be sent and summed in bfloat16 or wider, within the bound.
No kernel may reach another device: no remote copies, remote signals or barrier semaphores. Data moves between devices by JAX's collectives and lax.ppermute only.
A program may use at most 64 MiB of HBM per device.

v0:
```python
import jax
import jax.numpy as jnp
from jax import lax
from jax.sharding import PartitionSpec as P

REVERSE_MARCHES = 2


PAIRS = ((0, 0), (1, 1), (2, 2), (0, 1), (0, 2), (1, 2))
WEIGHTS = (1.0, 1.0, 1.0, 2.0, 2.0, 2.0)
EPSILON = 1e-06
NU_MOL = 0.05
PRANDTL = 0.72
PRANDTL_TURB = 0.9
TIME_STEP = 0.04


def padded_2(block, sides, width):
    for axis, dim in sides:
        count = lax.axis_size(axis)
        forward = [(i, i + 1) for i in range(count - 1)]
        forward.append((count - 1, 0))
        backward = [(target, source) for source, target in forward]
        low = lax.ppermute(
            lax.slice_in_dim(block, block.shape[dim] - width, None, axis=dim), axis, forward
        )
        high = lax.ppermute(lax.slice_in_dim(block, 0, width, axis=dim), axis, backward)
        block = jnp.concatenate([low, block, high], axis=dim)
    return block


def trimmed(values, offset_x, offset_z, margin):
    size_x = values.shape[-3]
    size_z = values.shape[-1]
    return values[
        ...,
        margin + offset_x : size_x - margin + offset_x,
        :,
        margin + offset_z : size_z - margin + offset_z,
    ]


def deriv_x(values, margin):
    return (
        8.0 * (trimmed(values, 1, 0, margin) - trimmed(values, -1, 0, margin))
        - (trimmed(values, 2, 0, margin) - trimmed(values, -2, 0, margin))
    ) / 12.0


def deriv_z(values, margin):
    return (
        8.0 * (trimmed(values, 0, 1, margin) - trimmed(values, 0, -1, margin))
        - (trimmed(values, 0, 2, margin) - trimmed(values, 0, -2, margin))
    ) / 12.0


def wall_shifts(center):
    zeros_row = jnp.zeros(center.shape[:-2] + (1,) + center.shape[-1:], jnp.float32)
    shifted_up = jnp.concatenate([center[..., 1:, :], zeros_row], axis=-2)
    shifted_down = jnp.concatenate([zeros_row, center[..., :-1, :]], axis=-2)
    return (shifted_up, shifted_down)


def deriv_y(center):
    shifted_up, shifted_down = wall_shifts(center)
    return 0.5 * (shifted_up - shifted_down)


def laplace(values, margin):
    center = trimmed(values, 0, 0, margin)
    shifted_up, shifted_down = wall_shifts(center)
    neighbours = (
        trimmed(values, 1, 0, margin)
        + trimmed(values, -1, 0, margin)
        + trimmed(values, 0, 1, margin)
        + trimmed(values, 0, -1, margin)
    )
    return neighbours + shifted_up + shifted_down - 6.0 * center


def gradients(saved_primal_fields, margin):
    return jnp.stack(
        [
            deriv_x(saved_primal_fields, margin),
            deriv_y(trimmed(saved_primal_fields, 0, 0, margin)),
            deriv_z(saved_primal_fields, margin),
        ]
    )


def strain_parts(gradient):
    return [
        0.5 * (gradient[index_a, index_b] + gradient[index_b, index_a])
        for index_a, index_b in PAIRS
    ]


def norm_of(components):
    running = 0.0
    for weight, component in zip(WEIGHTS, components):
        running = running + weight * component * component
    return jnp.sqrt(2.0 * running + EPSILON)


def filter_inputs(center, gradient):
    components = strain_parts(gradient)
    strain_size = norm_of(components)
    velocity = [center[0], center[1], center[2]]
    products = [velocity[index_a] * velocity[index_b] for index_a, index_b in PAIRS]
    scaled = [strain_size * component for component in components]
    return (jnp.stack(velocity + products + components + scaled), strain_size)


def smooth(values):
    size_x = values.shape[-3]
    along_x = (
        0.25 * values[..., : size_x - 2, :, :]
        + 0.5 * values[..., 1 : size_x - 1, :, :]
        + 0.25 * values[..., 2:, :, :]
    )
    size_z = along_x.shape[-1]
    return (
        0.25 * along_x[..., : size_z - 2]
        + 0.5 * along_x[..., 1 : size_z - 1]
        + 0.25 * along_x[..., 2:]
    )


def germano_partials(filtered):
    hat_strain = [filtered[9 + number] for number in range(6)]
    hat_size = norm_of(hat_strain)
    cross_sum = 0.0
    square_sum = 0.0
    for number in range(6):
        index_a, index_b = PAIRS[number]
        leonard = filtered[3 + number] - filtered[index_a] * filtered[index_b]
        model_term = filtered[15 + number] - 4.0 * hat_size * hat_strain[number]
        cross_sum = cross_sum + WEIGHTS[number] * leonard * model_term
        square_sum = square_sum + WEIGHTS[number] * model_term * model_term
    return jnp.stack([jnp.sum(cross_sum, axis=-1), jnp.sum(square_sum, axis=-1)])


def forward_terms(saved_primal_fields, margin):
    center = trimmed(saved_primal_fields, 0, 0, margin)
    lap_vel = laplace(saved_primal_fields[0:3], margin)
    lap_temp = laplace(saved_primal_fields[4], margin)
    inv_rho = 1.0 / center[3]
    return (center, lap_vel, lap_temp, inv_rho)


def coef_partial(terms, strain_size, adjoint):
    center, lap_vel, lap_temp, inv_rho = terms
    work_term = (
        adjoint[0] * lap_vel[0]
        + adjoint[1] * lap_vel[1]
        + adjoint[2] * lap_vel[2]
        + adjoint[4] * lap_temp / PRANDTL_TURB
    )
    return jnp.sum(strain_size * work_term * inv_rho, axis=-1)


def adjoint_update(terms, gradient, strain_size, model_coef, adjoint_pad):
    center, lap_vel, lap_temp, inv_rho = terms
    adjoint = trimmed(adjoint_pad, 0, 0, 2)
    eddy_visc = model_coef[:, :, None] * strain_size
    mu_mom = NU_MOL + eddy_visc
    mu_heat = NU_MOL / PRANDTL + eddy_visc / PRANDTL_TURB
    advect = (
        center[0] * deriv_x(adjoint_pad, 2)
        + center[1] * deriv_y(adjoint)
        + center[2] * deriv_z(adjoint_pad, 2)
    )
    lap_adj = laplace(adjoint_pad, 2)
    source_mom = jnp.sum(gradient * adjoint[None], axis=1)
    new_mom = adjoint[0:3] + TIME_STEP * (
        advect[0:3] + mu_mom * inv_rho * lap_adj[0:3] + source_mom
    )
    work_term = (
        mu_mom * (adjoint[0] * lap_vel[0] + adjoint[1] * lap_vel[1] + adjoint[2] * lap_vel[2])
        + mu_heat * adjoint[4] * lap_temp
    )
    new_rho = adjoint[3] + TIME_STEP * (advect[3] - work_term * inv_rho * inv_rho)
    new_temp = adjoint[4] + TIME_STEP * (advect[4] + mu_heat * inv_rho * lap_adj[4])
    return jnp.concatenate([new_mom, new_rho[None], new_temp[None]], axis=0)


def local(
    saved_flow_speed_vector,
    saved_mass_concentration,
    saved_thermal_excess,
    costate_vector_subsequent,
):
    stacked = jnp.concatenate(
        [saved_flow_speed_vector, saved_mass_concentration[:, None], saved_thermal_excess[:, None]],
        axis=1,
    )
    span_cells = saved_mass_concentration.shape[3] * lax.axis_size("gz")
    partial_list = []
    gradient_list = []
    size_list = []
    term_list = []
    padded = padded_2(stacked, (("gx", 2), ("gz", 4)), 3).astype(jnp.float32)
    for march_index in range(REVERSE_MARCHES):
        saved_primal_fields = padded[march_index]
        gradient_rim = gradients(saved_primal_fields, 2)
        inputs_rim, size_rim = filter_inputs(trimmed(saved_primal_fields, 0, 0, 2), gradient_rim)
        partial_list.append(germano_partials(smooth(inputs_rim)))
        gradient_list.append(trimmed(gradient_rim, 0, 0, 1))
        size_list.append(trimmed(size_rim, 0, 0, 1))
        term_list.append(forward_terms(saved_primal_fields, 3))
    adjoint = costate_vector_subsequent
    coef_grads = []
    for march_index in range(REVERSE_MARCHES):
        germano, coef_total = lax.psum(
            (
                partial_list[march_index],
                coef_partial(term_list[march_index], size_list[march_index], adjoint),
            ),
            "gz",
        )
        model_coef = germano[0] / (germano[1] + EPSILON)
        coef_grads.append(coef_total / span_cells)
        adjoint_pad = padded_2(adjoint, (("gx", 1), ("gz", 3)), 2)
        adjoint = adjoint_update(
            term_list[march_index],
            gradient_list[march_index],
            size_list[march_index],
            model_coef,
            adjoint_pad,
        )
    return (adjoint, jnp.stack(coef_grads))


def solution(mesh):
    return jax.shard_map(
        local,
        mesh=mesh,
        in_specs=(
            P(None, None, "gx", None, "gz"),
            P(None, "gx", None, "gz"),
            P(None, "gx", None, "gz"),
            P(None, "gx", None, "gz"),
        ),
        out_specs=(P(None, "gx", None, "gz"), P(None, "gx", None)),
        check_vma=False,
    )
```

profile of v0, /device:TPU:0, one launch (start us, length us, event | category | flops | bytes accessed | tf_op | source)
XLA Modules:
  0.0 116.2 jit_solution(17379455459477184644)
XLA Ops:
  4.1 2.6 %collective-permute-start.2 = (bf16[2,5,3,32,128]{4,3,2,1,0:T(8,128)(2,1)}, bf16[2,5,3,32,128]{4,3,2,1,0:T(8,128)(2,1)}, u32[]{:S(2)}, u32[]{:S(2)}) collective-permute-start(bf16[2,5,3,32,128]{4,3,2,1,0:T(8,128)(2,1)} %get-tuple-element.88), channel_id=1, source_target_pairs={{0,2},{2,4},{4,6},{6,8},{8,10},{10,12},{12,14},{14,16},{16,18},{18... | collective-permute-start | bytes 737288 | tf_op jit(solution)/shard_map/ppermute | solution.py:24
  6.7 2.4 %collective-permute-start.3 = (bf16[2,5,3,32,128]{4,3,2,1,0:T(8,128)(2,1)}, bf16[2,5,3,32,128]{4,3,2,1,0:T(8,128)(2,1)}, u32[]{:S(2)}, u32[]{:S(2)}) collective-permute-start(bf16[2,5,3,32,128]{4,3,2,1,0:T(8,128)(2,1)} %get-tuple-element.89), channel_id=1, source_target_pairs={{2,0},{4,2},{6,4},{8,6},{10,8},{12,10},{14,12},{16,14},{18,16},{20... | collective-permute-start | bytes 737288 | tf_op jit(solution)/shard_map/ppermute | solution.py:27
  11.3 3.5 %collective-permute-done = f32[5,2,32,128]{3,2,1,0:T(8,128)S(1)} collective-permute-done((f32[5,2,32,128]{3,2,1,0:T(8,128)S(1)}, f32[5,2,32,128]{3,2,1,0:T(8,128)S(1)}, u32[]{:S(2)}, u32[]{:S(2)}) %collective-permute-start) | collective-permute-done | bytes 163872 | tf_op jit(solution)/shard_map/ppermute | solution.py:27
  16.3 2.0 %collective-permute-start.6 = (f32[5,8,32,2]{2,1,3,0:T(8,128)S(1)}, f32[5,8,32,2]{2,1,3,0:T(8,128)}, u32[]{:S(2)}, u32[]{:S(2)}) collective-permute-start(f32[5,8,32,2]{2,1,3,0:T(8,128)S(1)} %copy.42), channel_id=1, source_target_pairs={{1,0},{0,1},{3,2},{2,3},{5,4},{4,5},{7,6},{6,7},{9,8},{8,9},{11,10... | collective-permute-start | bytes 30728 | tf_op jit(solution)/shard_map/ppermute | solution.py:27
  19.2 3.4 %collective-permute-done.7 = f32[5,8,32,2]{2,1,3,0:T(8,128)S(1)} collective-permute-done((f32[5,8,32,2]{2,1,3,0:T(8,128)}, f32[5,8,32,2]{2,1,3,0:T(8,128)S(1)}, u32[]{:S(2)}, u32[]{:S(2)}) %collective-permute-start.7) | collective-permute-done | bytes 10272 | tf_op jit(solution)/shard_map/ppermute | solution.py:24
  27.1 1.8 %copy.38 = bf16[2,5,10,32,3]{3,0,4,2,1:T(2,128)(2,1)S(1)} copy(bf16[2,5,10,32,3]{4,3,2,1,0:T(8,128)(2,1)} %get-tuple-element.65) | data formatting | bytes 38400 | tf_op jit(solution)/shard_map/slice | solution.py:25
  28.9 1.8 %copy.39 = bf16[2,5,10,32,3]{3,0,4,2,1:T(2,128)(2,1)S(1)} copy(bf16[2,5,10,32,3]{4,3,2,1,0:T(8,128)(2,1)} %get-tuple-element.66) | data formatting | bytes 38400 | tf_op jit(solution)/shard_map/slice | solution.py:27
  31.0 1.8 %collective-permute-start.4 = (bf16[2,5,10,32,3]{3,0,4,2,1:T(2,128)(2,1)S(1)}, bf16[2,5,10,32,3]{3,0,4,2,1:T(2,128)(2,1)S(1)}, u32[]{:S(2)}, u32[]{:S(2)}) collective-permute-start(bf16[2,5,10,32,3]{3,0,4,2,1:T(2,128)(2,1)S(1)} %copy.38), channel_id=1, source_target_pairs={{0,1},{1,0},{2,3},{3,2},{4,5},{5,4},{6,7},{7,6},{8,9},{9,8},{10,11... | collective-permute-start | bytes 57608 | tf_op jit(solution)/shard_map/ppermute | solution.py:24
  32.8 2.3 %multiply_subtract_fusion.1 = f32[5,4,32,128]{3,2,1,0:T(8,128)} fusion(f32[5,4,32,128]{3,2,1,0:T(8,128)S(1)} %copy-done, f32[5,6,32,128]{3,2,1,0:T(8,128)} %copy-done.27, f32[5,6,32,128]{3,2,1,0:T(8,128)} %copy-done.18, f32[5,4,31,128]{3,2,1,0:T(8,128)} %get-tuple-element.83, f32[5,4,31,128]{3,2,1,0:T(8,128)S(1)} %get-tuple-element.82, ...), kind=kLoop, calls=%fused_computation.103 | loop fusion | flops 737280 | bytes 2621440 | tf_op jit(solution)/shard_map/sub | solution.py:78
  35.1 2.3 %collective-permute-done.4 = bf16[2,5,10,32,3]{3,0,4,2,1:T(2,128)(2,1)S(1)} collective-permute-done((bf16[2,5,10,32,3]{3,0,4,2,1:T(2,128)(2,1)S(1)}, bf16[2,5,10,32,3]{3,0,4,2,1:T(2,128)(2,1)S(1)}, u32[]{:S(2)}, u32[]{:S(2)}) %collective-permute-start.4) | collective-permute-done | bytes 19232 | tf_op jit(solution)/shard_map/ppermute | solution.py:24
  39.8 3.1 %maximum_convert_fusion = f32[2,5,10,32,134]{4,3,2,1,0:T(8,128)S(1)} fusion(bf16[2,5,10,32,3]{4,3,2,1,0:T(8,128)(2,1)S(1)} %copy.41, bf16[2,5,3,32,128]{4,3,2,1,0:T(8,128)(2,1)} %collective-permute-done.3, bf16[2,1,4,32,128]{4,3,2,1,0:T(8,128)(2,1)S(1)} %bitcast.588, bf16[2,1,4,32,128]{4,3,2,1,0:T(8,128)(2,1)S(1)} %bitcast.591, ...), kind=kLoop, calls=%fused_computation.12 | loop fusion | flops 6003200 | bytes 2572800 | tf_op jit(solution)/shard_map/convert_element_type | solution.py:202
  47.3 3.6 %fusion.12 = (f32[1,5,6,32,130]{4,3,2,1,0:T(8,128)S(1)}, f32[1,5,6,32,130]{4,3,2,1,0:T(8,128)S(1)}, f32[1,5,6,32,130]{4,3,2,1,0:T(8,128)S(1)}, f32[1,5,6,32,130]{4,3,2,1,0:T(8,128)S(1)}) fusion(f32[5,10,32,134]{3,2,1,0:T(8,128)S(1)} %get-tuple-element.41, f32[5,10,32,134]{3,2,1,0:T(8,128)S(1)} %get-tuple-element.40), kind=kLoop, calls=%fused_computation.31 | loop fusion | flops 2496000 | bytes 9984000 | tf_op jit(solution)/shard_map/stack | solution.py:82
  64.9 4.9 %psum.28 = f32[2,4,32]{2,1,0:T(4,128)S(1)} all-reduce(f32[2,4,32]{2,1,0:T(4,128)S(1)} %pad_maximum_fusion.26), channel_id=1, replica_groups=mesh['gx'=16,'gz'=2] {'gz'}, use_global_device_ids=true, to_apply=%region_2.0 | all-reduce | flops 256 | bytes 2048 | tf_op jit(solution)/shard_map/psum | solution.py:214
  69.9 1.8 %fusion.236 = (f32[3,4,31,128]{3,2,1,0:T(8,128)S(1)}, f32[3,4,31,128]{3,2,1,0:T(8,128)S(1)}, f32[3,4,31,128]{3,2,1,0:T(8,128)S(1)}, f32[3,4,31,128]{3,2,1,0:T(8,128)S(1)}) fusion(f32[3,10,32,134]{3,2,1,0:T(8,128)} %get-tuple-element.38, f32[3,10,32,134]{3,2,1,0:T(8,128)} %get-tuple-element.39), kind=kLoop, calls=%fused_computation.468 | loop fusion | bytes 1523712 | tf_op jit(solution)/shard_map/slice | solution.py:59
  71.8 2.0 %fusion.60 = f32[3,4,32,128]{3,2,1,0:T(8,128)S(1)} fusion(f32[3,10,32,134]{3,2,1,0:T(8,128)} %get-tuple-element.39, f32[3,4,31,128]{3,2,1,0:T(8,128)S(1)} %get-tuple-element.100, f32[3,4,31,128]{3,2,1,0:T(8,128)S(1)} %get-tuple-element.101), kind=kLoop, calls=%fused_computation.143 | loop fusion | flops 344064 | bytes 1560576 | tf_op jit(solution)/shard_map/sub | solution.py:78
  73.8 2.1 %fusion.70 = f32[3,4,32,128]{3,2,1,0:T(8,128)S(1)} fusion(f32[3,10,32,134]{3,2,1,0:T(8,128)} %get-tuple-element.38, f32[3,4,31,128]{3,2,1,0:T(8,128)S(1)} %get-tuple-element.62, f32[3,4,31,128]{3,2,1,0:T(8,128)S(1)} %get-tuple-element.61), kind=kLoop, calls=%fused_computation.164 | loop fusion | flops 344064 | bytes 1560576 | tf_op jit(solution)/shard_map/sub | solution.py:78
  76.0 1.7 %fusion.38 = f32[5,4,32,128]{3,2,1,0:T(8,128)S(1)} fusion(f32[5,8,32,128]{3,2,1,0:T(8,128)S(1)} %copy-done.6, f32[5,8,32,2]{3,2,1,0:T(8,128)S(1)} %copy-done.12, f32[5,8,32,2]{3,2,1,0:T(8,128)S(1)} %copy-done.14, f32[5,6,32,128]{3,2,1,0:T(8,128)S(1)} %copy-done.28, f32[5,6,32,128]{3,2,1,0:T(8,128)S(1)} %copy-done.19, f32[5,4,31,128]{3,2,1,0:T(8,128)S(1)} %copy-done.26, ...), kind=kLoop, calls=%fused_computation.91 | loop fusion | flops 1474560 | bytes 3145728 | tf_op jit(solution)/shard_map/add | solution.py:169
  79.7 2.0 %multiply_reduce_fusion = (f32[4,32]{1,0:T(4,128)S(1)}, f32[4,32,128]{2,1,0:T(8,128)}, f32[4,32,128]{2,1,0:T(8,128)}, f32[4,32,128]{2,1,0:T(8,128)}, f32[4,32,128]{2,1,0:T(8,128)S(1)}) fusion(f32[5,10,32,134]{3,2,1,0:T(8,128)S(1)} %get-tuple-element.41, f32[10,32,134]{2,1,0:T(8,128)S(1)} %copy-done.33, f32[4,31,128]{2,1,0:T(8,128)S(1)} %copy-done.46, ...), kind=kLoop, calls=%fused_computation.450 | loop fusion | flops 589696 | bytes 1831936 | tf_op jit(solution)/shard_map/reduce_sum | solution.py:159
  88.8 5.0 %all-reduce.16 = (f32[2,4,32]{2,1,0:T(4,128)S(1)}, f32[4,32]{1,0:T(4,128)S(1)}, f32[4,32]{1,0:T(4,128)S(1)}) all-reduce(f32[2,4,32]{2,1,0:T(4,128)S(1)} %pad_maximum_fusion.27, f32[4,32]{1,0:T(4,128)S(1)} %get-tuple-element.11, f32[4,32]{1,0:T(4,128)S(1)} %get-tuple-element.7), channel_id=1, replica_groups=mesh['gx'=16,'gz'=2] {'gz'}, use_global_device_ids=true, to_apply=%region_6.0 | all-reduce | flops 512 | bytes 4096 | tf_op jit(solution)/shard_map/psum | solution.py:214
  94.9 2.3 %fusion.9 = f32[3,4,32,128]{3,2,1,0:T(8,128)} fusion(f32[1,5,6,32,130]{4,3,2,1,0:T(8,128)S(1)} %copy-done.8, f32[1,5,6,32,130]{4,3,2,1,0:T(8,128)} %copy-done.9, f32[1,5,6,32,130]{4,3,2,1,0:T(8,128)} %copy-done.10, f32[5,4,32,128]{3,2,1,0:T(8,128)S(1)} %pad_maximum_fusion.24), kind=kLoop, calls=%fused_computation.26 | loop fusion | flops 933888 | bytes 2021888 | tf_op jit(solution)/shard_map/reduce_sum | solution.py:174
  97.2 4.3 %collective-permute-done.9 = f32[5,2,32,128]{3,2,1,0:T(8,128)S(1)} collective-permute-done((f32[5,2,32,128]{3,2,1,0:T(8,128)}, f32[5,2,32,128]{3,2,1,0:T(8,128)S(1)}, u32[]{:S(2)}, u32[]{:S(2)}) %collective-permute-start.9) | collective-permute-done | bytes 163872 | tf_op jit(solution)/shard_map/ppermute | solution.py:24
  107.1 2.0 %pad_maximum_fusion.6 = (f32[5,6,32,128]{3,2,1,0:T(8,128)}, f32[5,6,32,128]{3,2,1,0:T(8,128)}) fusion(f32[5,2,32,128]{3,2,1,0:T(8,128)S(1)} %collective-permute-done.8, f32[1,4,32,128]{3,2,1,0:T(8,128)S(1)} %bitcast.581, f32[1,4,32,128]{3,2,1,0:T(8,128)S(1)} %bitcast.576, f32[3,4,32,128]{3,2,1,0:T(8,128)S(1)} %fusion.76, f32[5,2,32,128]{3,2,1,0:T(8,128)} %copy-done.29), kind=kLoop, calls=%fused_computation.63 | loop fusion | flops 737280 | bytes 1638400 | tf_op jit(solution)/shard_map/concatenate | solution.py:28
  111.2 1.7 %multiply_subtract_fusion = f32[5,4,32,128]{3,2,1,0:T(8,128)S(1)} fusion(f32[5,6,32,128]{3,2,1,0:T(8,128)} %get-tuple-element.74, f32[5,6,32,128]{3,2,1,0:T(8,128)} %get-tuple-element.73, f32[5,4,31,128]{3,2,1,0:T(8,128)} %get-tuple-element.72, f32[5,4,31,128]{3,2,1,0:T(8,128)} %get-tuple-element.71, f32[5,8,32,2]{3,2,1,0:T(8,128)S(1)} %copy.47, ...), kind=kLoop, calls=%fused_computation.102 | loop fusion | flops 1556480 | bytes 2293760 | tf_op jit(solution)/shard_map/sub | solution.py:78
  113.0 2.2 %fusion.31 = f32[5,4,32,128]{3,2,1,0:T(8,128)S(1)} fusion(f32[5,8,32,2]{3,2,1,0:T(8,128)S(1)} %copy.49, f32[5,2,32,128]{3,2,1,0:T(8,128)S(1)} %collective-permute-done.8, f32[5,2,32,128]{3,2,1,0:T(8,128)} %copy-done.29, f32[1,4,32,128]{3,2,1,0:T(8,128)S(1)} %bitcast.583, f32[1,4,32,128]{3,2,1,0:T(8,128)S(1)} %bitcast.578, f32[3,4,32,128]{3,2,1,0:T(8,128)S(1)} %fusion.76, ...), kind=kLoop, calls=%fused_computation.70 | loop fusion | flops 2785280 | bytes 3145728 | tf_op jit(solution)/shard_map/add | solution.py:169
  (214 shorter events, 51.7 us)
Async XLA Ops:
  1.7 16.8 %copy-start = (f32[5,4,32,128]{3,2,1,0:T(8,128)S(1)}, f32[5,4,32,128]{3,2,1,0:T(8,128)}, u32[]{:S(2)}) copy-start(f32[5,4,32,128]{3,2,1,0:T(8,128)} %param.7) | copy-start | bytes 983044
  1.7 8.5 %collective-permute-start.1 = (f32[5,2,32,128]{3,2,1,0:T(8,128)S(1)}, f32[5,2,32,128]{3,2,1,0:T(8,128)S(1)}, u32[]{:S(2)}, u32[]{:S(2)}) collective-permute-start(f32[5,2,32,128]{3,2,1,0:T(8,128)S(1)} %get-tuple-element.85), channel_id=1, source_target_pairs={{0,2},{2,4},{4,6},{6,8},{8,10},{10,12},{12,14},{14,16},{16,18},{18... | collective-permute-start | bytes 491528 | tf_op jit(solution)/shard_map/ppermute | solution.py:24
  4.1 19.9 %collective-permute-start.2 = (bf16[2,5,3,32,128]{4,3,2,1,0:T(8,128)(2,1)}, bf16[2,5,3,32,128]{4,3,2,1,0:T(8,128)(2,1)}, u32[]{:S(2)}, u32[]{:S(2)}) collective-permute-start(bf16[2,5,3,32,128]{4,3,2,1,0:T(8,128)(2,1)} %get-tuple-element.88), channel_id=1, source_target_pairs={{0,2},{2,4},{4,6},{6,8},{8,10},{10,12},{12,14},{14,16},{16,18},{18... | collective-permute-start | bytes 737288 | tf_op jit(solution)/shard_map/ppermute | solution.py:24
  6.7 17.4 %collective-permute-start.3 = (bf16[2,5,3,32,128]{4,3,2,1,0:T(8,128)(2,1)}, bf16[2,5,3,32,128]{4,3,2,1,0:T(8,128)(2,1)}, u32[]{:S(2)}, u32[]{:S(2)}) collective-permute-start(bf16[2,5,3,32,128]{4,3,2,1,0:T(8,128)(2,1)} %get-tuple-element.89), channel_id=1, source_target_pairs={{2,0},{4,2},{6,4},{8,6},{10,8},{12,10},{14,12},{16,14},{18,16},{20... | collective-permute-start | bytes 737288 | tf_op jit(solution)/shard_map/ppermute | solution.py:27
  9.1 5.7 %collective-permute-start = (f32[5,2,32,128]{3,2,1,0:T(8,128)S(1)}, f32[5,2,32,128]{3,2,1,0:T(8,128)S(1)}, u32[]{:S(2)}, u32[]{:S(2)}) collective-permute-start(f32[5,2,32,128]{3,2,1,0:T(8,128)S(1)} %get-tuple-element.84), channel_id=1, source_target_pairs={{2,0},{4,2},{6,4},{8,6},{10,8},{12,10},{14,12},{16,14},{18,16},{20... | collective-permute-start | bytes 491528 | tf_op jit(solution)/shard_map/ppermute | solution.py:27
  10.2 13.9 %copy-start.39 = (bf16[2,4,32,128]{3,2,1,0:T(8,128)(2,1)S(1)}, bf16[2,4,32,128]{3,2,1,0:T(8,128)(2,1)}, u32[]{:S(2)}) copy-start(bf16[2,4,32,128]{3,2,1,0:T(8,128)(2,1)} %param.6) | copy-start | bytes 196612
  14.8 18.0 %copy-start.5 = (f32[5,8,32,128]{3,2,1,0:T(8,128)}, f32[5,8,32,128]{3,2,1,0:T(8,128)S(1)}, u32[]{:S(2)}) copy-start(f32[5,8,32,128]{3,2,1,0:T(8,128)S(1)} %get-tuple-element.90) | copy-start | bytes 1966084
  16.3 6.6 %collective-permute-start.6 = (f32[5,8,32,2]{2,1,3,0:T(8,128)S(1)}, f32[5,8,32,2]{2,1,3,0:T(8,128)}, u32[]{:S(2)}, u32[]{:S(2)}) collective-permute-start(f32[5,8,32,2]{2,1,3,0:T(8,128)S(1)} %copy.42), channel_id=1, source_target_pairs={{1,0},{0,1},{3,2},{2,3},{5,4},{4,5},{7,6},{6,7},{9,8},{8,9},{11,10... | collective-permute-start | bytes 30728 | tf_op jit(solution)/shard_map/ppermute | solution.py:27
  18.3 4.2 %collective-permute-start.7 = (f32[5,8,32,2]{2,1,3,0:T(8,128)}, f32[5,8,32,2]{2,1,3,0:T(8,128)S(1)}, u32[]{:S(2)}, u32[]{:S(2)}) collective-permute-start(f32[5,8,32,2]{2,1,3,0:T(8,128)} %copy.44), channel_id=1, source_target_pairs={{0,1},{1,0},{2,3},{3,2},{4,5},{5,4},{6,7},{7,6},{8,9},{9,8},{10,11... | collective-permute-start | bytes 30728 | tf_op jit(solution)/shard_map/ppermute | solution.py:24
  19.2 15.9 %copy-start.24 = (f32[5,4,31,128]{3,2,1,0:T(8,128)}, f32[5,4,31,128]{3,2,1,0:T(8,128)S(1)}, u32[]{:S(2)}) copy-start(f32[5,4,31,128]{3,2,1,0:T(8,128)S(1)} %get-tuple-element.82) | copy-start | bytes 952324
  22.9 12.3 %copy-start.11 = (f32[5,8,32,2]{3,2,1,0:T(8,128)}, f32[5,8,32,2]{3,2,1,0:T(8,128)S(1)}, u32[]{:S(2)}) copy-start(f32[5,8,32,2]{3,2,1,0:T(8,128)S(1)} %copy.45) | copy-start | bytes 30724
  24.0 11.1 %copy-start.13 = (f32[5,8,32,2]{3,2,1,0:T(8,128)}, f32[5,8,32,2]{3,2,1,0:T(8,128)S(1)}, u32[]{:S(2)}) copy-start(f32[5,8,32,2]{3,2,1,0:T(8,128)S(1)} %copy.43) | copy-start | bytes 30724
  27.1 12.7 %copy-start.40 = (bf16[2,4,32,128]{3,2,1,0:T(8,128)(2,1)S(1)}, bf16[2,4,32,128]{3,2,1,0:T(8,128)(2,1)}, u32[]{:S(2)}) copy-start(bf16[2,4,32,128]{3,2,1,0:T(8,128)(2,1)} %param.5) | copy-start | bytes 196612
  30.7 7.4 %collective-permute-start.5 = (bf16[2,5,10,32,3]{3,0,4,2,1:T(2,128)(2,1)S(1)}, bf16[2,5,10,32,3]{3,0,4,2,1:T(2,128)(2,1)}, u32[]{:S(2)}, u32[]{:S(2)}) collective-permute-start(bf16[2,5,10,32,3]{3,0,4,2,1:T(2,128)(2,1)S(1)} %copy.39), channel_id=1, source_target_pairs={{1,0},{0,1},{3,2},{2,3},{5,4},{4,5},{7,6},{6,7},{9,8},{8,9},{11,10... | collective-permute-start | bytes 57608 | tf_op jit(solution)/shard_map/ppermute | solution.py:27
  31.0 6.4 %collective-permute-start.4 = (bf16[2,5,10,32,3]{3,0,4,2,1:T(2,128)(2,1)S(1)}, bf16[2,5,10,32,3]{3,0,4,2,1:T(2,128)(2,1)S(1)}, u32[]{:S(2)}, u32[]{:S(2)}) collective-permute-start(bf16[2,5,10,32,3]{3,0,4,2,1:T(2,128)(2,1)S(1)} %copy.38), channel_id=1, source_target_pairs={{0,1},{1,0},{2,3},{3,2},{4,5},{5,4},{6,7},{7,6},{8,9},{9,8},{10,11... | collective-permute-start | bytes 57608 | tf_op jit(solution)/shard_map/ppermute | solution.py:24
  42.9 10.5 %copy-start.34 = (f32[10,32,134]{2,1,0:T(8,128)}, f32[10,32,134]{2,1,0:T(8,128)S(1)}, u32[]{:S(2)}) copy-start(f32[10,32,134]{2,1,0:T(8,128)S(1)} %get-tuple-element.36) | copy-start | bytes 514564
  42.9 11.3 %copy-start.32 = (f32[10,32,134]{2,1,0:T(8,128)}, f32[10,32,134]{2,1,0:T(8,128)S(1)}, u32[]{:S(2)}) copy-start(f32[10,32,134]{2,1,0:T(8,128)S(1)} %get-tuple-element.37) | copy-start | bytes 514564
  51.0 9.4 %copy-start.10 = (f32[1,5,6,32,130]{4,3,2,1,0:T(8,128)}, f32[1,5,6,32,130]{4,3,2,1,0:T(8,128)S(1)}, u32[]{:S(2)}) copy-start(f32[1,5,6,32,130]{4,3,2,1,0:T(8,128)S(1)} %get-tuple-element.51) | copy-start | bytes 1497604
  88.4 13.2 %copy-start.21 = (f32[4,32,128]{2,1,0:T(8,128)S(1)}, f32[4,32,128]{2,1,0:T(8,128)}, u32[]{:S(2)}) copy-start(f32[4,32,128]{2,1,0:T(8,128)} %copy-done.20) | copy-start | bytes 196612
  93.8 3.5 %collective-permute-start.8 = (f32[5,2,32,128]{3,2,1,0:T(8,128)}, f32[5,2,32,128]{3,2,1,0:T(8,128)S(1)}, u32[]{:S(2)}, u32[]{:S(2)}) collective-permute-start(f32[5,2,32,128]{3,2,1,0:T(8,128)} %get-tuple-element.75), channel_id=1, source_target_pairs={{2,0},{4,2},{6,4},{8,6},{10,8},{12,10},{14,12},{16,14},{18,16},{20... | collective-permute-start | bytes 491528 | tf_op jit(solution)/shard_map/ppermute | solution.py:27
  93.8 7.7 %collective-permute-start.9 = (f32[5,2,32,128]{3,2,1,0:T(8,128)}, f32[5,2,32,128]{3,2,1,0:T(8,128)S(1)}, u32[]{:S(2)}, u32[]{:S(2)}) collective-permute-start(f32[5,2,32,128]{3,2,1,0:T(8,128)} %get-tuple-element.76), channel_id=1, source_target_pairs={{0,2},{2,4},{4,6},{6,8},{8,10},{10,12},{12,14},{14,16},{16,18},{18... | collective-permute-start | bytes 491528 | tf_op jit(solution)/shard_map/ppermute | solution.py:24
  102.8 10.2 %copy-start.41 = (f32[4,32,128]{2,1,0:T(8,128)S(1)}, f32[4,32,128]{2,1,0:T(8,128)}, u32[]{:S(2)}) copy-start(f32[4,32,128]{2,1,0:T(8,128)} %get-tuple-element.47) | copy-start | bytes 196612
  105.1 5.0 %collective-permute-start.10 = (f32[5,8,32,2]{2,1,3,0:T(8,128)}, f32[5,8,32,2]{2,1,3,0:T(8,128)}, u32[]{:S(2)}, u32[]{:S(2)}) collective-permute-start(f32[5,8,32,2]{2,1,3,0:T(8,128)} %copy.46), channel_id=1, source_target_pairs={{1,0},{0,1},{3,2},{2,3},{5,4},{4,5},{7,6},{6,7},{9,8},{8,9},{11,10... | collective-permute-start | bytes 30728 | tf_op jit(solution)/shard_map/ppermute | solution.py:27
  105.7 4.0 %collective-permute-start.11 = (f32[5,8,32,2]{2,1,3,0:T(8,128)S(1)}, f32[5,8,32,2]{2,1,3,0:T(8,128)S(1)}, u32[]{:S(2)}, u32[]{:S(2)}) collective-permute-start(f32[5,8,32,2]{2,1,3,0:T(8,128)S(1)} %copy.48), channel_id=1, source_target_pairs={{0,1},{1,0},{2,3},{3,2},{4,5},{5,4},{6,7},{7,6},{8,9},{9,8},{10,11... | collective-permute-start | bytes 30728 | tf_op jit(solution)/shard_map/ppermute | solution.py:24
  (37 other events, 181.0 us)
where the time goes:
time: 117 us; the launch traced here: 116 us
  other arithmetic  49.4 us (42%)
  local copies, waits for them, and re-layouts  27.8 us (24%)
  waiting for transfers between devices  14.4 us (12%)
  starting transfers between devices  13 us (11%)
  blocking collectives  9.95 us (9%)
  between operations  1.66 us (1%)
    ppermute x6, waiting for transfers between devices, padded_2(): lax.ppermute(lax.slice_in_dim(block, block.shape[dim] - width, None, axis...  10.9 us
    psum x2, blocking collectives, local(): lax.psum((partial_list[march_index], coef_partial(term_list[march_index],...  9.95 us
    sub x4, other arithmetic, laplace(): return neighbours + shifted_up + shifted_down - 6.0 * center  8.17 us
    slice x7, local copies, waits for them, and re-layouts, padded_2(): lax.slice_in_dim(block, block.shape[dim] - width, None, axis=dim)  7.94 us
    ppermute x6, starting transfers between devices, padded_2(): lax.ppermute(lax.slice_in_dim(block, block.shape[dim] - width, None, axis...  6.85 us
    unnamed x34, other arithmetic  6.33 us
    ppermute x6, starting transfers between devices, padded_2(): lax.ppermute(lax.slice_in_dim(block, 0, width, axis=dim), axis, backward)  6.12 us
    slice x6, local copies, waits for them, and re-layouts, wall_shifts(): shifted_up = jnp.concatenate([center[..., 1:, :], zeros_row], axis=-2)  6 us
  transfers between devices with their start and end apart: 12, of which 6 were waited for; matrix products, arithmetic and copies ran while one was open for 13% of the time, Pallas kernels for 0%

commit v1 on v0

v1 whole, which is shorter than its diff:
```python
import functools

import jax
import jax.numpy as jnp
from jax import lax
from jax.experimental import pallas as pl
from jax.experimental.pallas import tpu as pltpu
from jax.sharding import PartitionSpec as P

EPSILON = 1e-06
NU_MOL = 0.05
PRANDTL = 0.72
PRANDTL_TURB = 0.9
TIME_STEP = 0.04
PAIRS = ((0, 0), (1, 1), (2, 2), (0, 1), (0, 2), (1, 2))
WEIGHTS = (1.0, 1.0, 1.0, 2.0, 2.0, 2.0)

CX = 4
ROWS = 32
LANES = 128
STRIP = 8
F32 = jnp.float32
BF16 = jnp.bfloat16
SLOT_T = 8
SLOT_PSI_HI = 10
SLOT_PSI_LO = 15


def lane_ids():
    return lax.broadcasted_iota(jnp.int32, (ROWS, LANES), 1)


def row_ids():
    return lax.broadcasted_iota(jnp.int32, (ROWS, LANES), 0)


def turn(values, shift):
    shift = shift % LANES
    return values if shift == 0 else pltpu.roll(values, shift, 1)


class Ops:
    def __init__(self):
        self.lane = lane_ids()
        row = row_ids()
        self.top = row == ROWS - 1
        self.bottom = row == 0

    def z_at(self, values, halo, step):
        if step > 0:
            return turn(jnp.where(self.lane < step, halo, values), -step)
        return turn(jnp.where(self.lane >= LANES + step, halo, values), -step)

    def y_up(self, values):
        return jnp.where(self.top, 0.0, pltpu.roll(values, ROWS - 1, 0))

    def y_down(self, values):
        return jnp.where(self.bottom, 0.0, pltpu.roll(values, 1, 0))

    def unpack(self, block, strip):
        return turn(block, LANES - 4 - STRIP * strip)


def fourth(plus, minus, plus_2, minus_2):
    return (2.0 / 3.0) * (plus - minus) - (1.0 / 12.0) * (plus_2 - minus_2)


def strain_of(grad):
    return [
        grad[0][0],
        grad[1][1],
        grad[2][2],
        0.5 * (grad[0][1] + grad[1][0]),
        0.5 * (grad[0][2] + grad[2][0]),
        0.5 * (grad[1][2] + grad[2][1]),
    ]


def size_of(strain):
    diagonal = strain[0] * strain[0] + strain[1] * strain[1] + strain[2] * strain[2]
    other = strain[3] * strain[3] + strain[4] * strain[4] + strain[5] * strain[5]
    return jnp.sqrt(2.0 * diagonal + (4.0 * other + EPSILON))


def filter_fields(velocity, strain, size):
    products = [velocity[a] * velocity[b] for a, b in PAIRS]
    return list(velocity) + products + strain + [size * part for part in strain]


def pack_strips(ops, planes):
    block = jnp.zeros((ROWS, LANES), F32)
    strip_id = ops.lane // STRIP
    for strip, values in planes.items():
        block = jnp.where(strip_id == strip, turn(values, STRIP * strip + 4), block)
    return block


def split_halves(values):
    upper = values.astype(BF16)
    lower = (values - upper.astype(F32)).astype(BF16)
    return upper, lower


def pack_kernel(flow, rho, temp, psi, packed):
    ops = Ops()
    items = []
    for t in range(2):
        items += [[flow[t, k, x].astype(F32) for x in range(CX)] for k in range(3)]
        items += [[rho[t, x].astype(F32) for x in range(CX)]]
    items += [[temp[t, x].astype(F32) for x in range(CX)] for t in range(2)]
    halves = [[split_halves(psi[k, x]) for x in range(CX)] for k in range(5)]
    for half in range(2):
        items += [[halves[k][x][half].astype(F32) for x in range(CX)] for k in range(5)]
    for number in range(5):
        planes = {}
        for slot in range(4):
            for x in range(CX):
                planes[4 * slot + x] = items[4 * number + slot][x]
        packed[number] = pack_strips(ops, planes).astype(BF16)


def message_kernel(flow, rho, temp, psi, packed, first_up, first_down, second_up, second_down):
    for t in range(2):
        for k in range(3):
            for i in range(3):
                first_up[t * 9 + k * 3 + i] = flow[t, k, 1 + i]
                first_down[t * 9 + k * 3 + i] = flow[t, k, i]
        for i in range(2):
            second_up[t * 4 + i] = rho[t, 2 + i]
            second_down[t * 4 + i] = rho[t, i]
            second_up[t * 4 + 2 + i] = temp[t, 2 + i]
            second_down[t * 4 + 2 + i] = temp[t, i]
        first_up[18 + t] = packed[t]
        first_down[18 + t] = packed[t]
    for k in range(5):
        for i in range(2):
            upper, lower = split_halves(psi[k, 2 + i])
            second_up[8 + k * 2 + i] = upper
            second_up[18 + k * 2 + i] = lower
            upper, lower = split_halves(psi[k, i])
            second_down[8 + k * 2 + i] = upper
            second_down[18 + k * 2 + i] = lower
    zero = jnp.zeros((ROWS, LANES), BF16)
    for t in range(2):
        first_up[20 + t] = zero
        first_down[20 + t] = zero


def germano_kernel(flow, left, right, own_pack, own_halo, sums, fields, edges):
    t = pl.program_id(0)
    ops = Ops()

    def plane(k, x):
        if x < 0:
            return left[t * 9 + k * 3 + x + 3].astype(F32)
        if x >= CX:
            return right[t * 9 + k * 3 + x - CX].astype(F32)
        return flow[0, k, x].astype(F32)

    own_o = own_pack[t].astype(F32)
    own_h = own_halo[t].astype(F32)
    left_o = left[18 + t].astype(F32)
    left_h = left[20 + t].astype(F32)
    right_o = right[18 + t].astype(F32)
    right_h = right[20 + t].astype(F32)

    def halo(k, x):
        if x < 0:
            return ops.unpack(left_h, 4 * k + CX + x)
        if x >= CX:
            return ops.unpack(right_h, 4 * k + x - CX)
        return ops.unpack(own_h, 4 * k + x)

    for x in range(-1, CX + 1):
        grad = [[None] * 3 for _ in range(3)]
        for k in range(3):
            center = plane(k, x)
            edge = halo(k, x)
            grad[0][k] = fourth(plane(k, x + 1), plane(k, x - 1), plane(k, x + 2), plane(k, x - 2))
            grad[1][k] = 0.5 * (ops.y_up(center) - ops.y_down(center))
            grad[2][k] = fourth(*(ops.z_at(center, edge, step) for step in (1, -1, 2, -2)))
        strain = strain_of(grad)
        size = size_of(strain)
        for number, values in enumerate(
            filter_fields([plane(k, x) for k in range(3)], strain, size)
        ):
            fields[number, x + 1] = values

    strip_id = ops.lane // STRIP
    low_half = ops.lane % STRIP < 4

    def gathered(k, from_left, own, from_right):
        own_turned = turn(own, STRIP * (3 - 4 * k))
        left_turned = turn(from_left, STRIP * (-1 - 4 * k))
        right_turned = turn(from_right, STRIP * (7 - 4 * k))
        return jnp.where(
            strip_id < 3, left_turned, jnp.where(strip_id < 7, own_turned, right_turned)
        )

    inner = [gathered(k, left_o, own_o, right_o) for k in range(3)]
    outer = [gathered(k, left_h, own_h, right_h) for k in range(3)]
    sides = []
    for side in range(2):
        velocity = [
            jnp.where(low_half, outer[k], inner[k])
            if side == 0
            else jnp.where(low_half, inner[k], outer[k])
            for k in range(3)
        ]
        grad = [[None] * 3 for _ in range(3)]
        for k in range(3):
            center = velocity[k]
            grad[0][k] = fourth(*(turn(center, -STRIP * step) for step in (1, -1, 2, -2)))
            grad[1][k] = 0.5 * (ops.y_up(center) - ops.y_down(center))
            grad[2][k] = fourth(*(turn(center, -step) for step in (1, -1, 2, -2)))
        strain = strain_of(grad)
        sides.append(filter_fields(velocity, strain, size_of(strain)))
    for number in range(21):
        both = jnp.where(low_half, sides[0][number], sides[1][number])
        edges[number] = turn(both, STRIP) + turn(both, -STRIP) + 2.0 * both

    last = ops.lane == LANES - 1
    first = ops.lane == 0
    columns = jnp.zeros((ROWS, LANES), F32)
    for x in range(CX):

        def hat(number):
            along_x = fields[number, x] + fields[number, x + 2] + 2.0 * fields[number, x + 1]
            edge = ops.unpack(edges[number], x + 3)
            before = turn(jnp.where(last, edge, along_x), 1)
            after = turn(jnp.where(first, edge, along_x), -1)
            return before + after + 2.0 * along_x

        velocity = [hat(k) for k in range(3)]
        strain = [hat(9 + number) for number in range(6)]
        diagonal = strain[0] * strain[0] + strain[1] * strain[1] + strain[2] * strain[2]
        other = strain[3] * strain[3] + strain[4] * strain[4] + strain[5] * strain[5]
        size = jnp.sqrt((2.0 / 256.0) * diagonal + ((4.0 / 256.0) * other + EPSILON))
        size = 4.0 * size
        cross = 0.0
        square = 0.0
        for number, (a, b) in enumerate(PAIRS):
            leonard = hat(3 + number) - (1.0 / 16.0) * velocity[a] * velocity[b]
            model = hat(15 + number) - size * strain[number]
            if WEIGHTS[number] != 1.0:
                weighted = WEIGHTS[number] * model
            else:
                weighted = model
            cross = cross + leonard * weighted
            square = square + model * weighted
        cross = (1.0 / 256.0) * jnp.sum(cross, axis=1, keepdims=True)
        square = (1.0 / 256.0) * jnp.sum(square, axis=1, keepdims=True)
        columns = jnp.where(ops.lane == 8 * t + x, cross, columns)
        columns = jnp.where(ops.lane == 8 * t + 4 + x, square, columns)

    @pl.when(t == 0)
    def _():
        sums[...] = columns

    @pl.when(t == 1)
    def _():
        sums[...] = sums[...] + columns


class State:
    def __init__(self, ops, t, where, flow, rho, temp, left_1, right_1, left_2, right_2, own_halo):
        self.ops, self.t, self.where = ops, t, where
        self.flow, self.rho, self.temp = flow, rho, temp
        self.left_1, self.right_1, self.left_2, self.right_2 = left_1, right_1, left_2, right_2
        self.own_halo = own_halo

    def plane(self, k, x):
        t = self.t
        if k < 3:
            if x < 0:
                return self.left_1[t * 9 + k * 3 + x + 3].astype(F32)
            if x >= CX:
                return self.right_1[t * 9 + k * 3 + x - CX].astype(F32)
            return self.flow[self.where, k, x].astype(F32)
        if x < 0:
            return self.left_2[t * 4 + (k - 3) * 2 + x + 2].astype(F32)
        if x >= CX:
            return self.right_2[t * 4 + (k - 3) * 2 + x - CX].astype(F32)
        return (self.rho if k == 3 else self.temp)[self.where, x].astype(F32)

    def halo(self, k, x):
        slot = 4 * self.t + k if k < 4 else SLOT_T + self.t
        return self.ops.unpack(self.own_halo[slot // 4].astype(F32), 4 * (slot % 4) + x)

    def terms(self, x, need_all=True):
        ops = self.ops
        grad = [[None] * 5 for _ in range(3)]
        lap = [None] * 5
        center = [self.plane(k, x) for k in range(5)]
        for k in range(5):
            if k == 3 and not need_all:
                continue
            edge = self.halo(k, x)
            up, down = ops.y_up(center[k]), ops.y_down(center[k])
            xs = [self.plane(k, x + step) for step in (1, -1, 2, -2)]
            zs = [ops.z_at(center[k], edge, step) for step in (1, -1, 2, -2)]
            if k < 3 or need_all:
                grad[0][k] = fourth(*xs)
                grad[1][k] = 0.5 * (up - down)
                grad[2][k] = fourth(*zs)
            if k != 3:
                lap[k] = xs[0] + xs[1] + zs[0] + zs[1] + up + down - 6.0 * center[k]
        size = size_of(strain_of(grad))
        return center, grad, lap, size, 1.0 / center[3]


def affine_update(ops, x, terms, psi_plane, psi_halo):
    center, grad, lap, size, inv_rho = terms
    psi = [psi_plane(k, x) for k in range(5)]
    work_mom = psi[0] * lap[0] + psi[1] * lap[1] + psi[2] * lap[2]
    work_heat = psi[4] * lap[4]
    turbulent = work_mom + work_heat * (1.0 / PRANDTL_TURB)
    inv_rho_2 = inv_rho * inv_rho
    size_rho = size * inv_rho
    first, second = [], []
    for k in range(5):
        edge = psi_halo(k, x)
        up, down = ops.y_up(psi[k]), ops.y_down(psi[k])
        xs = [psi_plane(k, x + step) for step in (1, -1, 2, -2)]
        zs = [ops.z_at(psi[k], edge, step) for step in (1, -1, 2, -2)]
        rate = (
            center[0] * fourth(*xs) + center[1] * (0.5 * (up - down)) + center[2] * fourth(*zs)
        )
        if k == 3:
            rate = rate - (NU_MOL * work_mom + (NU_MOL / PRANDTL) * work_heat) * inv_rho_2
            eddy = -(size * turbulent) * inv_rho_2
        else:
            lap_psi = xs[0] + xs[1] + zs[0] + zs[1] + up + down - 6.0 * psi[k]
            if k < 3:
                for other in range(5):
                    rate = rate + psi[other] * grad[k][other]
                rate = rate + NU_MOL * (inv_rho * lap_psi)
                eddy = size_rho * lap_psi
            else:
                rate = rate + (NU_MOL / PRANDTL) * (inv_rho * lap_psi)
                eddy = (1.0 / PRANDTL_TURB) * (size_rho * lap_psi)
        first.append(psi[k] + TIME_STEP * rate)
        second.append(TIME_STEP * eddy)
    return first, second, size_rho * turbulent


def first_kernel(
    flow, rho, temp, psi, left_1, right_1, left_2, right_2, own_halo,
    first, second, weight, sums,
):
    ops = Ops()
    state = State(ops, 0, 0, flow, rho, temp, left_1, right_1, left_2, right_2, own_halo)

    def psi_plane(k, x):
        if x < 0:
            return left_2[8 + k * 2 + x + 2].astype(F32) + left_2[18 + k * 2 + x + 2].astype(F32)
        if x >= CX:
            return right_2[8 + k * 2 + x - CX].astype(F32) + right_2[18 + k * 2 + x - CX].astype(F32)
        return psi[k, x]

    def psi_halo(k, x):
        slot = SLOT_PSI_HI + k
        upper = ops.unpack(own_halo[slot // 4].astype(F32), 4 * (slot % 4) + x)
        slot = SLOT_PSI_LO + k
        return upper + ops.unpack(own_halo[slot // 4].astype(F32), 4 * (slot % 4) + x)

    columns = jnp.zeros((ROWS, LANES), F32)
    for x in range(CX):
        new, slope, sensitivity = affine_update(ops, x, state.terms(x), psi_plane, psi_halo)
        for k in range(5):
            first[k, x] = new[k]
            second[k, x] = slope[k]
        total = jnp.sum(sensitivity, axis=1, keepdims=True)
        columns = jnp.where(ops.lane == x, total, columns)
    sums[...] = columns
    state = State(ops, 1, 1, flow, rho, temp, left_1, right_1, left_2, right_2, own_halo)
    for x in range(CX):
        _, _, lap, size, inv_rho = state.terms(x, need_all=False)
        size_rho = size * inv_rho
        for number, k in enumerate((0, 1, 2, 4)):
            scale = 1.0 if k < 3 else 1.0 / PRANDTL_TURB
            weight[number, x] = (scale * size_rho) * lap[k]


def coefficients(ops, own, other):
    total = own + other
    return total / (turn(total, -4) + EPSILON)


def middle_kernel(first, second, weight, partial, own, other, psi, up, down, packed):
    ops = Ops()
    coef = coefficients(ops, own[...], other[...])
    columns = partial[...]
    planes = [{}, {}]
    for x in range(CX):
        coef_x = jnp.broadcast_to(coef[:, x : x + 1], (ROWS, LANES))
        values = [first[k, x] + coef_x * second[k, x] for k in range(5)]
        for k in range(5):
            psi[k, x] = values[k]
            if x >= 2:
                up[k, x - 2] = values[k]
            else:
                down[k, x] = values[k]
            planes[k // 4][4 * (k % 4) + x] = values[k]
        work = weight[0, x] * values[0] + weight[1, x] * values[1]
        work = work + weight[2, x] * values[2] + weight[3, x] * values[4]
        columns = jnp.where(
            ops.lane == 4 + x, jnp.sum(work, axis=1, keepdims=True), columns
        )
    for number in range(2):
        packed[number] = pack_strips(ops, planes[number])
    packed[2] = columns


def last_kernel(
    flow, rho, temp, psi, left_1, right_1, left_2, right_2, own_halo,
    left_psi, right_psi, psi_edges, own, other, out,
):
    ops = Ops()
    coef = coefficients(ops, own[...], other[...])
    state = State(ops, 1, 0, flow, rho, temp, left_1, right_1, left_2, right_2, own_halo)

    def psi_plane(k, x):
        if x < 0:
            return left_psi[k, x + 2]
        if x >= CX:
            return right_psi[k, x - CX]
        return psi[k, x]

    def psi_halo(k, x):
        return ops.unpack(psi_edges[k // 4], 4 * (k % 4) + x)

    for x in range(CX):
        new, slope, _ = affine_update(ops, x, state.terms(x), psi_plane, psi_halo)
        coef_x = jnp.broadcast_to(coef[:, 8 + x : 9 + x], (ROWS, LANES))
        for k in range(5):
            out[k, x] = new[k] + coef_x * slope[k]


def ring(axis):
    count = lax.axis_size(axis)
    forward = [(i, (i + 1) % count) for i in range(count)]
    return forward, [(target, source) for source, target in forward]


def span_edges(block):
    forward, backward = ring("gz")
    before = lax.ppermute(block, "gz", forward)
    if lax.axis_size("gz") == 2:
        return before
    after = lax.ppermute(block, "gz", backward)
    lane = lax.broadcasted_iota(jnp.int32, block.shape, block.ndim - 1)
    return jnp.where(lane % STRIP < 4, before, after)


def span_sum(block):
    if lax.axis_size("gz") == 2:
        return block, lax.ppermute(block, "gz", ring("gz")[0])
    return lax.psum(block, "gz"), jnp.zeros_like(block)


def shape_of(dims, kind):
    return jax.ShapeDtypeStruct(dims, kind)


def whole(count):
    return [pl.BlockSpec(memory_space=pltpu.VMEM)] * count


def cost(operations, size):
    return pl.CostEstimate(flops=operations, bytes_accessed=size, transcendentals=0)


def local(flow, rho, temp, psi):
    block = (ROWS, LANES)
    forward, backward = ring("gx")
    own_pack = pl.pallas_call(
        pack_kernel,
        in_specs=whole(4),
        out_specs=whole(1)[0],
        out_shape=shape_of((5,) + block, BF16),
        cost_estimate=cost(2_000_000, 700_000),
        name="pack",
    )(flow, rho, temp, psi)
    own_halo = span_edges(own_pack)
    first_up, first_down, second_up, second_down = pl.pallas_call(
        message_kernel,
        in_specs=whole(5),
        out_specs=whole(4),
        out_shape=[shape_of((22,) + block, BF16)] * 2 + [shape_of((28,) + block, BF16)] * 2,
        cost_estimate=cost(1_000_000, 1_500_000),
        name="message",
    )(flow, rho, temp, psi, own_pack)
    first_up = lax.dynamic_update_slice(first_up, own_halo[:2], (20, 0, 0))
    first_down = lax.dynamic_update_slice(first_down, own_halo[:2], (20, 0, 0))
    left_1 = lax.ppermute(first_up, "gx", forward)
    right_1 = lax.ppermute(first_down, "gx", backward)
    left_2 = lax.ppermute(second_up, "gx", forward)
    right_2 = lax.ppermute(second_down, "gx", backward)

    def fixed(dims):
        return pl.BlockSpec(dims, lambda t: (0,) * len(dims))

    own = pl.pallas_call(
        germano_kernel,
        grid=(2,),
        in_specs=[
            pl.BlockSpec((1, 3, CX) + block, lambda t: (t, 0, 0, 0, 0)),
            fixed((22,) + block),
            fixed((22,) + block),
            fixed((5,) + block),
            fixed((5,) + block),
        ],
        out_specs=fixed(block),
        out_shape=shape_of(block, F32),
        scratch_shapes=[pltpu.VMEM((21, CX + 2) + block, F32), pltpu.VMEM((21,) + block, F32)],
        cost_estimate=cost(40_000_000, 1_000_000),
        name="germano",
    )(flow, left_1, right_1, own_pack, own_halo)
    own, other = span_sum(own)
    first, second, weight, partial = pl.pallas_call(
        first_kernel,
        in_specs=whole(9),
        out_specs=whole(4),
        out_shape=[
            shape_of((5, CX) + block, F32),
            shape_of((5, CX) + block, F32),
            shape_of((4, CX) + block, F32),
            shape_of(block, F32),
        ],
        cost_estimate=cost(20_000_000, 2_500_000),
        name="first",
    )(flow, rho, temp, psi, left_1, right_1, left_2, right_2, own_halo)
    psi, up, down, packed = pl.pallas_call(
        middle_kernel,
        in_specs=whole(6),
        out_specs=whole(4),
        out_shape=[
            shape_of((5, CX) + block, F32),
            shape_of((5, 2) + block, F32),
            shape_of((5, 2) + block, F32),
            shape_of((3,) + block, F32),
        ],
        cost_estimate=cost(1_000_000, 2_000_000),
        name="middle",
    )(first, second, weight, partial, own, other)
    left_psi = lax.ppermute(up, "gx", forward)
    right_psi = lax.ppermute(down, "gx", backward)
    psi_edges = span_edges(packed)
    if lax.axis_size("gz") == 2:
        totals = packed[2] + psi_edges[2]
    else:
        totals = lax.psum(packed[2], "gz")
    out = pl.pallas_call(
        last_kernel,
        grid=(1,),
        in_specs=[
            pl.BlockSpec((1, 3, CX) + block, lambda t: (1, 0, 0, 0, 0)),
            pl.BlockSpec((1, CX) + block, lambda t: (1, 0, 0, 0)),
            pl.BlockSpec((1, CX) + block, lambda t: (1, 0, 0, 0)),
            fixed((5, CX) + block),
            fixed((22,) + block),
            fixed((22,) + block),
            fixed((28,) + block),
            fixed((28,) + block),
            fixed((5,) + block),
            fixed((5, 2) + block),
            fixed((5, 2) + block),
            fixed((3,) + block),
            fixed(block),
            fixed(block),
        ],
        out_specs=fixed((5, CX) + block),
        out_shape=shape_of((5, CX) + block, F32),
        cost_estimate=cost(15_000_000, 2_500_000),
        name="last",
    )(
        flow, rho, temp, psi, left_1, right_1, left_2, right_2, own_halo,
        left_psi, right_psi, psi_edges, own, other,
    )
    span_cells = LANES * lax.axis_size("gz")
    coef_grad = totals[:, :8].T.reshape(2, CX, ROWS) * (1.0 / span_cells)
    return out, coef_grad


def solution(mesh):
    return jax.shard_map(
        local,
        mesh=mesh,
        in_specs=(
            P(None, None, "gx", None, "gz"),
            P(None, "gx", None, "gz"),
            P(None, "gx", None, "gz"),
            P(None, "gx", None, "gz"),
        ),
        out_specs=(P(None, "gx", None, "gz"), P(None, "gx", None)),
        check_vma=False,
    )
```

time: 117 us -> 65 us (0.56)
  other arithmetic: 49.4 us -> 0.75 us
  Pallas kernels: 0 us -> 34.6 us
  local copies, waits for them, and re-layouts: 27.8 us -> 4.67 us
  blocking collectives: 9.95 us -> 0 us
  waiting for transfers between devices: 14.4 us -> 9.54 us
  starting transfers between devices: 13 us -> 14.4 us
    pallas_call x0 -> x6, Pallas kernels: none -> 34.6 us  [the longest x1 17.1 us: local(): pl.pallas_call(germano_kernel, grid=(2,), in_specs=[pl.BlockSpec((1, 3, C...]
    slice x19 -> x0, local copies, waits for them, and re-layouts: 20.3 us -> none  [the longest x7 7.94 us: padded_2(): lax.slice_in_dim(block, block.shape[dim] - width, None, axis=dim)]
    psum x2 -> x0, blocking collectives: 9.95 us -> none  [local(): lax.psum((partial_list[march_index], coef_partial(term_list[march_index],...]
    sub x4 -> x0, other arithmetic: 8.17 us -> none  [laplace(): return neighbours + shifted_up + shifted_down - 6.0 * center]
    add x11 -> x1, other arithmetic: 8.83 us -> 0.74 us  [local(): totals = packed[2] + psi_edges[2]]
    reduce_sum x8 -> x0, other arithmetic: 7.84 us -> none  [the longest x2 3.67 us: coef_partial(): return jnp.sum(strain_size * work_term * inv_rho, axis=-1)]
    unnamed x34 -> x0, other arithmetic: 6.33 us -> none
    concatenate x6 -> x0, other arithmetic: 5.4 us -> none  [the longest x3 3.59 us: padded_2(): block = jnp.concatenate([low, block, high], axis=dim)]
  transfers between devices with their start and end apart: 12 -> 9, of which waited for: 6 -> 3; matrix products, arithmetic and copies ran while one was open for 13% -> 3% of each run, Pallas kernels for 0% -> 39%
where the time goes in v1:
time: 65 us; the launch traced here: 64.6 us
  Pallas kernels  34.6 us (53%)
  starting transfers between devices  14.4 us (22%)
  waiting for transfers between devices  9.54 us (15%)
  local copies, waits for them, and re-layouts  4.67 us (7%)
  other arithmetic  0.75 us (1%)
  between operations  0.66 us (1%)
    pallas_call x1, Pallas kernels, local(): pl.pallas_call(germano_kernel, grid=(2,), in_specs=[pl.BlockSpec((1, 3, C...  17.1 us
    pallas_call x1, Pallas kernels, local(): pl.pallas_call(first_kernel, in_specs=whole(9), out_specs=whole(4), out_s...  6.26 us
    pallas_call x1, Pallas kernels, local(): pl.pallas_call(last_kernel, grid=(1,), in_specs=[pl.BlockSpec((1, 3, CX)...  5.07 us
    ppermute x1, waiting for transfers between devices, local(): right_1 = lax.ppermute(first_down, 'gx', backward)  4.64 us
    ppermute x2, starting transfers between devices, span_edges(): before = lax.ppermute(block, 'gz', forward)  4.49 us
    ppermute x1, starting transfers between devices, local(): right_2 = lax.ppermute(second_down, 'gx', backward)  4.44 us
    ppermute x1, starting transfers between devices, local(): right_psi = lax.ppermute(down, 'gx', backward)  3.97 us
    unnamed x18, local copies, waits for them, and re-layouts  3.38 us
  transfers between devices with their start and end apart: 9, of which 3 were waited for; matrix products, arithmetic and copies ran while one was open for 3% of the time, Pallas kernels for 39%

profile of v1, /device:TPU:0, one launch (start us, length us, event | category | flops | bytes accessed | tf_op | source)
XLA Modules:
  0.0 64.6 jit_solution(14077410296458815940)
XLA Ops:
  0.6 2.0 %pack.1.packed.own_pack = bf16[5,32,128]{2,1,0:T(8,128)(2,1)} custom-call(bf16[2,3,4,32,128]{4,3,2,1,0:T(8,128)(2,1)} %flow.9, bf16[2,4,32,128]{3,2,1,0:T(8,128)(2,1)} %rho.7, bf16[2,4,32,128]{3,2,1,0:T(8,128)(2,1)} %temp.7, f32[5,4,32,128]{3,2,1,0:T(8,128)} %psi.5), custom_call_target="tpu_custom_call" | custom-call | flops 2000000 | bytes 700000 | tf_op jit(solution)/shard_map/pack/pallas_call | solution.py:477
  2.6 3.0 %collective-permute-start = (bf16[5,32,128]{2,1,0:T(8,128)(2,1)}, bf16[5,32,128]{2,1,0:T(8,128)(2,1)S(1)}, u32[]{:S(2)}, u32[]{:S(2)}) collective-permute-start(bf16[5,32,128]{2,1,0:T(8,128)(2,1)} %pack.1.packed.own_pack), channel_id=1, source_target_pairs={{0,1},{1,0},{2,3},{3,2},{4,5},{5,4},{6,7},{7,6},{8,9},{9,8},{10,11... | collective-permute-start | bytes 122888 | tf_op jit(solution)/shard_map/ppermute | solution.py:448
  5.6 2.0 %message.1 = (bf16[22,32,128]{2,1,0:T(8,128)(2,1)}, bf16[22,32,128]{2,1,0:T(8,128)(2,1)}, bf16[28,32,128]{2,1,0:T(8,128)(2,1)}, bf16[28,32,128]{2,1,0:T(8,128)(2,1)}) custom-call(bf16[2,3,4,32,128]{4,3,2,1,0:T(8,128)(2,1)} %flow.9, bf16[2,4,32,128]{3,2,1,0:T(8,128)(2,1)} %rho.7, bf16[2,4,32,128]{3,2,1,0:T(8,128)(2,1)} %temp.7, f32[5,4,32,128]{3,2,1,0:T(8,128)} %psi.5, ...), custom_call_target="tpu_custom_call" | custom-call | flops 1000000 | bytes 1500000 | tf_op jit(solution)/shard_map/message/pallas_call | solution.py:486
  7.6 4.4 %collective-permute-start.4 = (bf16[28,32,128]{2,1,0:T(8,128)(2,1)}, bf16[28,32,128]{2,1,0:T(8,128)(2,1)S(1)}, u32[]{:S(2)}, u32[]{:S(2)}) collective-permute-start(bf16[28,32,128]{2,1,0:T(8,128)(2,1)} %get-tuple-element.17), channel_id=1, source_target_pairs={{2,0},{4,2},{6,4},{8,6},{10,8},{12,10},{14,12},{16,14},{18,16},{20... | collective-permute-start | bytes 688136 | tf_op jit(solution)/shard_map/ppermute | solution.py:499
  12.0 0.6 slice_dynamic-update-slice_fusion
  12.9 0.3 collective-permute-start.1
  13.2 4.6 %collective-permute-done.2.right_1.right = bf16[22,32,128]{2,1,0:T(8,128)(2,1)S(1)} collective-permute-done((bf16[22,32,128]{2,1,0:T(8,128)(2,1)}, bf16[22,32,128]{2,1,0:T(8,128)(2,1)S(1)}, u32[]{:S(2)}, u32[]{:S(2)}) %collective-permute-start.2) | collective-permute-done | bytes 180256 | tf_op jit(solution)/shard_map/ppermute | solution.py:497
  17.8 3.0 %collective-permute-done.1.left_1.left = bf16[22,32,128]{2,1,0:T(8,128)(2,1)S(1)} collective-permute-done((bf16[22,32,128]{2,1,0:T(8,128)(2,1)}, bf16[22,32,128]{2,1,0:T(8,128)(2,1)S(1)}, u32[]{:S(2)}, u32[]{:S(2)}) %collective-permute-start.1) | collective-permute-done | bytes 180256 | tf_op jit(solution)/shard_map/ppermute | solution.py:496
  20.8 0.7 %copy-done.1 = bf16[22,32,128]{2,1,0:T(8,128)(2,1)} copy-done((bf16[22,32,128]{2,1,0:T(8,128)(2,1)}, bf16[22,32,128]{2,1,0:T(8,128)(2,1)S(1)}, u32[]{:S(2)}) %copy-start.1) | copy-done | bytes 180248
  21.5 17.1 %germano.1.own = f32[32,128]{1,0:T(8,128)} custom-call(bf16[2,3,4,32,128]{4,3,2,1,0:T(8,128)(2,1)} %flow.9, bf16[22,32,128]{2,1,0:T(8,128)(2,1)} %copy-done.1, bf16[22,32,128]{2,1,0:T(8,128)(2,1)} %copy-done, bf16[5,32,128]{2,1,0:T(8,128)(2,1)} %pack.1.packed.own_pack, bf16[5,32,128]{2,1,0:T(8,128)(2,1)} %copy-done.4), custom_call_target="tpu_custom_call" | custom-call | flops 40000000 | bytes 1000000 | tf_op jit(solution)/shard_map/germano/pallas_call | solution.py:504
  38.6 0.5 collective-permute-start.5
  39.1 0.7 %copy-done.2 = bf16[28,32,128]{2,1,0:T(8,128)(2,1)} copy-done((bf16[28,32,128]{2,1,0:T(8,128)(2,1)}, bf16[28,32,128]{2,1,0:T(8,128)(2,1)S(1)}, u32[]{:S(2)}) %copy-start.2) | copy-done | bytes 229400
  39.8 0.7 %copy-done.3 = bf16[28,32,128]{2,1,0:T(8,128)(2,1)} copy-done((bf16[28,32,128]{2,1,0:T(8,128)(2,1)}, bf16[28,32,128]{2,1,0:T(8,128)(2,1)S(1)}, u32[]{:S(2)}) %copy-start.3) | copy-done | bytes 229400
  40.5 6.3 %first.1 = (f32[5,4,32,128]{3,2,1,0:T(8,128)}, f32[5,4,32,128]{3,2,1,0:T(8,128)}, f32[4,4,32,128]{3,2,1,0:T(8,128)}, f32[32,128]{1,0:T(8,128)}) custom-call(bf16[2,3,4,32,128]{4,3,2,1,0:T(8,128)(2,1)} %flow.9, bf16[2,4,32,128]{3,2,1,0:T(8,128)(2,1)} %rho.7, bf16[2,4,32,128]{3,2,1,0:T(8,128)(2,1)} %temp.7, f32[5,4,32,128]{3,2,1,0:T(8,128)} %psi.5, ...), custom_call_target="tpu_custom_call" | custom-call | flops 20000000 | bytes 2500000 | tf_op jit(solution)/shard_map/first/pallas_call | solution.py:521
  46.7 0.6 copy-done.8
  47.3 2.2 %middle.1 = (f32[5,4,32,128]{3,2,1,0:T(8,128)}, f32[5,2,32,128]{3,2,1,0:T(8,128)}, f32[5,2,32,128]{3,2,1,0:T(8,128)}, f32[3,32,128]{2,1,0:T(8,128)}) custom-call(f32[5,4,32,128]{3,2,1,0:T(8,128)} %get-tuple-element.18.first, f32[5,4,32,128]{3,2,1,0:T(8,128)} %get-tuple-element.19.second, f32[4,4,32,128]{3,2,1,0:T(8,128)} %get-tuple-element.20.weight, ...), custom_call_target="tpu_custom_call" | custom-call | flops 1000000 | bytes 2000000 | tf_op jit(solution)/shard_map/middle/pallas_call | solution.py:534
  49.6 1.5 %collective-permute-start.8 = (f32[3,32,128]{2,1,0:T(8,128)}, f32[3,32,128]{2,1,0:T(8,128)S(1)}, u32[]{:S(2)}, u32[]{:S(2)}) collective-permute-start(f32[3,32,128]{2,1,0:T(8,128)} %get-tuple-element.25), channel_id=1, source_target_pairs={{0,1},{1,0},{2,3},{3,2},{4,5},{5,4},{6,7},{7,6},{8,9},{9,8},{10,11... | collective-permute-start | bytes 147464 | tf_op jit(solution)/shard_map/ppermute | solution.py:448
  51.1 0.5 collective-permute-start.6
  51.6 4.0 %collective-permute-start.7 = (f32[5,2,32,128]{3,2,1,0:T(8,128)}, f32[5,2,32,128]{3,2,1,0:T(8,128)S(1)}, u32[]{:S(2)}, u32[]{:S(2)}) collective-permute-start(f32[5,2,32,128]{3,2,1,0:T(8,128)} %get-tuple-element.24), channel_id=1, source_target_pairs={{2,0},{4,2},{6,4},{8,6},{10,8},{12,10},{14,12},{16,14},{18,16},{20... | collective-permute-start | bytes 491528 | tf_op jit(solution)/shard_map/ppermute | solution.py:548
  55.5 0.7 %fusion.1 = f32[32,128]{1,0:T(8,128)S(1)} fusion(f32[3,32,128]{2,1,0:T(8,128)S(1)} %collective-permute-done.8.psi_edges, f32[3,32,128]{2,1,0:T(8,128)} %get-tuple-element.25), kind=kLoop, calls=%fused_computation.3 | loop fusion | flops 4096 | bytes 49152 | tf_op jit(solution)/shard_map/add | solution.py:551
  56.3 0.7 %copy.7 = f32[8,32]{1,0:T(8,128)} copy(f32[8,32]{0,1:T(8,128)S(1)} %fusion) | data formatting | bytes 2048 | tf_op jit(solution)/shard_map/mul | solution.py:582
  56.9 1.9 %collective-permute-done.6.left_psi = f32[5,2,32,128]{3,2,1,0:T(8,128)S(1)} collective-permute-done((f32[5,2,32,128]{3,2,1,0:T(8,128)}, f32[5,2,32,128]{3,2,1,0:T(8,128)S(1)}, u32[]{:S(2)}, u32[]{:S(2)}) %collective-permute-start.6) | collective-permute-done | bytes 163872 | tf_op jit(solution)/shard_map/ppermute | solution.py:547
  58.9 0.7 %copy-done.5 = f32[5,2,32,128]{3,2,1,0:T(8,128)} copy-done((f32[5,2,32,128]{3,2,1,0:T(8,128)}, f32[5,2,32,128]{3,2,1,0:T(8,128)S(1)}, u32[]{:S(2)}) %copy-start.5) | copy-done | bytes 163864
  59.6 5.1 %last.1 = f32[5,4,32,128]{3,2,1,0:T(8,128)} custom-call(bf16[2,3,4,32,128]{4,3,2,1,0:T(8,128)(2,1)} %flow.9, bf16[2,4,32,128]{3,2,1,0:T(8,128)(2,1)} %rho.7, bf16[2,4,32,128]{3,2,1,0:T(8,128)(2,1)} %temp.7, f32[5,4,32,128]{3,2,1,0:T(8,128)} %get-tuple-element.22.psi, bf16[22,32,128]{2,1,0:T(8,128)(2,1)} %copy-done.1, bf16[22,32,128]{2,1,0:T(8,128)(2,1)} %copy-done, ...), custom_call_target="tpu_custom_call" | custom-call | flops 15000000 | bytes 2500000 | tf_op jit(solution)/shard_map/last/pallas_call | solution.py:554
  (22 shorter events, 0.3 us)
Async XLA Ops:
  2.6 9.4 %collective-permute-start = (bf16[5,32,128]{2,1,0:T(8,128)(2,1)}, bf16[5,32,128]{2,1,0:T(8,128)(2,1)S(1)}, u32[]{:S(2)}, u32[]{:S(2)}) collective-permute-start(bf16[5,32,128]{2,1,0:T(8,128)(2,1)} %pack.1.packed.own_pack), channel_id=1, source_target_pairs={{0,1},{1,0},{2,3},{3,2},{4,5},{5,4},{6,7},{7,6},{8,9},{9,8},{10,11... | collective-permute-start | bytes 122888 | tf_op jit(solution)/shard_map/ppermute | solution.py:448
  7.6 31.5 %collective-permute-start.3 = (bf16[28,32,128]{2,1,0:T(8,128)(2,1)}, bf16[28,32,128]{2,1,0:T(8,128)(2,1)S(1)}, u32[]{:S(2)}, u32[]{:S(2)}) collective-permute-start(bf16[28,32,128]{2,1,0:T(8,128)(2,1)} %get-tuple-element.16), channel_id=1, source_target_pairs={{0,2},{2,4},{4,6},{6,8},{8,10},{10,12},{12,14},{14,16},{16,18},{18... | collective-permute-start | bytes 688136 | tf_op jit(solution)/shard_map/ppermute | solution.py:498
  7.6 31.5 %collective-permute-start.4 = (bf16[28,32,128]{2,1,0:T(8,128)(2,1)}, bf16[28,32,128]{2,1,0:T(8,128)(2,1)S(1)}, u32[]{:S(2)}, u32[]{:S(2)}) collective-permute-start(bf16[28,32,128]{2,1,0:T(8,128)(2,1)} %get-tuple-element.17), channel_id=1, source_target_pairs={{2,0},{4,2},{6,4},{8,6},{10,8},{12,10},{14,12},{16,14},{18,16},{20... | collective-permute-start | bytes 688136 | tf_op jit(solution)/shard_map/ppermute | solution.py:499
  12.0 8.8 %copy-start.4 = (bf16[5,32,128]{2,1,0:T(8,128)(2,1)}, bf16[5,32,128]{2,1,0:T(8,128)(2,1)S(1)}, u32[]{:S(2)}) copy-start(bf16[5,32,128]{2,1,0:T(8,128)(2,1)S(1)} %collective-permute-done.own_halo) | copy-start | bytes 122884
  12.7 5.1 %collective-permute-start.2 = (bf16[22,32,128]{2,1,0:T(8,128)(2,1)}, bf16[22,32,128]{2,1,0:T(8,128)(2,1)S(1)}, u32[]{:S(2)}, u32[]{:S(2)}) collective-permute-start(bf16[22,32,128]{2,1,0:T(8,128)(2,1)} %get-tuple-element.28), channel_id=1, source_target_pairs={{2,0},{4,2},{6,4},{8,6},{10,8},{12,10},{14,12},{16,14},{18,16},{20... | collective-permute-start | bytes 540680 | tf_op jit(solution)/shard_map/ppermute | solution.py:497
  12.9 7.9 %collective-permute-start.1 = (bf16[22,32,128]{2,1,0:T(8,128)(2,1)}, bf16[22,32,128]{2,1,0:T(8,128)(2,1)S(1)}, u32[]{:S(2)}, u32[]{:S(2)}) collective-permute-start(bf16[22,32,128]{2,1,0:T(8,128)(2,1)} %get-tuple-element.29), channel_id=1, source_target_pairs={{0,2},{2,4},{4,6},{6,8},{8,10},{10,12},{12,14},{14,16},{16,18},{18... | collective-permute-start | bytes 540680 | tf_op jit(solution)/shard_map/ppermute | solution.py:496
  17.8 3.0 %copy-start = (bf16[22,32,128]{2,1,0:T(8,128)(2,1)}, bf16[22,32,128]{2,1,0:T(8,128)(2,1)S(1)}, u32[]{:S(2)}) copy-start(bf16[22,32,128]{2,1,0:T(8,128)(2,1)S(1)} %collective-permute-done.2.right_1.right) | copy-start | bytes 540676
  20.8 0.7 %copy-start.1 = (bf16[22,32,128]{2,1,0:T(8,128)(2,1)}, bf16[22,32,128]{2,1,0:T(8,128)(2,1)S(1)}, u32[]{:S(2)}) copy-start(bf16[22,32,128]{2,1,0:T(8,128)(2,1)S(1)} %collective-permute-done.1.left_1.left) | copy-start | bytes 540676
  38.6 8.2 %collective-permute-start.5 = (f32[32,128]{1,0:T(8,128)}, f32[32,128]{1,0:T(8,128)S(1)}, u32[]{:S(2)}, u32[]{:S(2)}) collective-permute-start(f32[32,128]{1,0:T(8,128)} %germano.1.own), channel_id=1, source_target_pairs={{0,1},{1,0},{2,3},{3,2},{4,5},{5,4},{6,7},{7,6},{8,9},{9,8},{10,11... | collective-permute-start | bytes 49160 | tf_op jit(solution)/shard_map/ppermute | solution.py:458
  39.1 0.7 %copy-start.2 = (bf16[28,32,128]{2,1,0:T(8,128)(2,1)}, bf16[28,32,128]{2,1,0:T(8,128)(2,1)S(1)}, u32[]{:S(2)}) copy-start(bf16[28,32,128]{2,1,0:T(8,128)(2,1)S(1)} %collective-permute-done.3.left_2) | copy-start | bytes 688132
  39.8 0.7 %copy-start.3 = (bf16[28,32,128]{2,1,0:T(8,128)(2,1)}, bf16[28,32,128]{2,1,0:T(8,128)(2,1)S(1)}, u32[]{:S(2)}) copy-start(bf16[28,32,128]{2,1,0:T(8,128)(2,1)S(1)} %collective-permute-done.4.right_2) | copy-start | bytes 688132
  46.7 0.6 copy-start.8
  49.6 6.0 %collective-permute-start.8 = (f32[3,32,128]{2,1,0:T(8,128)}, f32[3,32,128]{2,1,0:T(8,128)S(1)}, u32[]{:S(2)}, u32[]{:S(2)}) collective-permute-start(f32[3,32,128]{2,1,0:T(8,128)} %get-tuple-element.25), channel_id=1, source_target_pairs={{0,1},{1,0},{2,3},{3,2},{4,5},{5,4},{6,7},{7,6},{8,9},{9,8},{10,11... | collective-permute-start | bytes 147464 | tf_op jit(solution)/shard_map/ppermute | solution.py:448
  51.1 7.8 %collective-permute-start.6 = (f32[5,2,32,128]{3,2,1,0:T(8,128)}, f32[5,2,32,128]{3,2,1,0:T(8,128)S(1)}, u32[]{:S(2)}, u32[]{:S(2)}) collective-permute-start(f32[5,2,32,128]{3,2,1,0:T(8,128)} %get-tuple-element.23), channel_id=1, source_target_pairs={{0,2},{2,4},{4,6},{6,8},{8,10},{10,12},{12,14},{14,16},{16,18},{18... | collective-permute-start | bytes 491528 | tf_op jit(solution)/shard_map/ppermute | solution.py:547
  51.6 7.3 %collective-permute-start.7 = (f32[5,2,32,128]{3,2,1,0:T(8,128)}, f32[5,2,32,128]{3,2,1,0:T(8,128)S(1)}, u32[]{:S(2)}, u32[]{:S(2)}) collective-permute-start(f32[5,2,32,128]{3,2,1,0:T(8,128)} %get-tuple-element.24), channel_id=1, source_target_pairs={{2,0},{4,2},{6,4},{8,6},{10,8},{12,10},{14,12},{16,14},{18,16},{20... | collective-permute-start | bytes 491528 | tf_op jit(solution)/shard_map/ppermute | solution.py:548
  55.5 1.4 %copy-start.7 = (f32[3,32,128]{2,1,0:T(8,128)}, f32[3,32,128]{2,1,0:T(8,128)S(1)}, u32[]{:S(2)}) copy-start(f32[3,32,128]{2,1,0:T(8,128)S(1)} %collective-permute-done.8.psi_edges) | copy-start | bytes 147460
  58.8 0.7 %copy-start.5 = (f32[5,2,32,128]{3,2,1,0:T(8,128)}, f32[5,2,32,128]{3,2,1,0:T(8,128)S(1)}, u32[]{:S(2)}) copy-start(f32[5,2,32,128]{3,2,1,0:T(8,128)S(1)} %collective-permute-done.6.left_psi) | copy-start | bytes 491524
  58.8 0.7 %copy-start.6 = (f32[5,2,32,128]{3,2,1,0:T(8,128)}, f32[5,2,32,128]{3,2,1,0:T(8,128)S(1)}, u32[]{:S(2)}) copy-start(f32[5,2,32,128]{3,2,1,0:T(8,128)S(1)} %collective-permute-done.7.right_psi) | copy-start | bytes 491524

commit v2 on v1

--- a/solution.py
+++ b/solution.py
@@ -89,7 +89,7 @@
 
 def pack_strips(ops, planes):
     block = jnp.zeros((ROWS, LANES), F32)
-    strip_id = ops.lane // STRIP
+    strip_id = (ops.lane >> 3)
     for strip, values in planes.items():
         block = jnp.where(strip_id == strip, turn(values, STRIP * strip + 4), block)
     return block
@@ -146,67 +146,57 @@
         first_down[20 + t] = zero
 
 
-def germano_kernel(flow, left, right, own_pack, own_halo, sums, fields, edges):
+def germano_kernel(flow, left, right, own_pack, own_halo, sums, wide, halos, fields, edges, spread, hats):
     t = pl.program_id(0)
     ops = Ops()
-
-    def plane(k, x):
-        if x < 0:
-            return left[t * 9 + k * 3 + x + 3].astype(F32)
-        if x >= CX:
-            return right[t * 9 + k * 3 + x - CX].astype(F32)
-        return flow[0, k, x].astype(F32)
-
+    for k in range(3):
+        for i in range(3):
+            wide[k, i] = left[t * 9 + k * 3 + i].astype(F32)
+            wide[k, 7 + i] = right[t * 9 + k * 3 + i].astype(F32)
+        for x in range(CX):
+            wide[k, 3 + x] = flow[0, k, x].astype(F32)
     own_o = own_pack[t].astype(F32)
     own_h = own_halo[t].astype(F32)
     left_o = left[18 + t].astype(F32)
     left_h = left[20 + t].astype(F32)
     right_o = right[18 + t].astype(F32)
     right_h = right[20 + t].astype(F32)
-
-    def halo(k, x):
-        if x < 0:
-            return ops.unpack(left_h, 4 * k + CX + x)
-        if x >= CX:
-            return ops.unpack(right_h, 4 * k + x - CX)
-        return ops.unpack(own_h, 4 * k + x)
+    for k in range(3):
+        halos[k, 0] = ops.unpack(left_h, 4 * k + 3)
+        for x in range(CX):
+            halos[k, 1 + x] = ops.unpack(own_h, 4 * k + x)
+        halos[k, 5] = ops.unpack(right_h, 4 * k)
+    strip_id = ops.lane >> 3
+    low_half = (ops.lane & 7) < 4
+
+    def gathered(k, from_left, own, from_right):
+        own_turned = turn(own, STRIP * (3 - 4 * k))
+        left_turned = turn(from_left, STRIP * (-1 - 4 * k))
+        right_turned = turn(from_right, STRIP * (7 - 4 * k))
+        return jnp.where(strip_id < 3, left_turned, jnp.where(strip_id < 7, own_turned, right_turned))
+
+    for k in range(3):
+        inner = gathered(k, left_o, own_o, right_o)
+        outer = gathered(k, left_h, own_h, right_h)
+        edges[k] = jnp.where(low_half, outer, inner)
+        edges[3 + k] = jnp.where(low_half, inner, outer)
 
     for x in range(-1, CX + 1):
         grad = [[None] * 3 for _ in range(3)]
         for k in range(3):
-            center = plane(k, x)
-            edge = halo(k, x)
-            grad[0][k] = fourth(plane(k, x + 1), plane(k, x - 1), plane(k, x + 2), plane(k, x - 2))
+            center = wide[k, x + 3]
+            edge = halos[k, x + 1]
+            grad[0][k] = fourth(wide[k, x + 4], wide[k, x + 2], wide[k, x + 5], wide[k, x + 1])
             grad[1][k] = 0.5 * (ops.y_up(center) - ops.y_down(center))
             grad[2][k] = fourth(*(ops.z_at(center, edge, step) for step in (1, -1, 2, -2)))
         strain = strain_of(grad)
         size = size_of(strain)
-        for number, values in enumerate(
-            filter_fields([plane(k, x) for k in range(3)], strain, size)
-        ):
+        for number, values in enumerate(filter_fields([wide[k, x + 3] for k in range(3)], strain, size)):
             fields[number, x + 1] = values
 
-    strip_id = ops.lane // STRIP
-    low_half = ops.lane % STRIP < 4
-
-    def gathered(k, from_left, own, from_right):
-        own_turned = turn(own, STRIP * (3 - 4 * k))
-        left_turned = turn(from_left, STRIP * (-1 - 4 * k))
-        right_turned = turn(from_right, STRIP * (7 - 4 * k))
-        return jnp.where(
-            strip_id < 3, left_turned, jnp.where(strip_id < 7, own_turned, right_turned)
-        )
-
-    inner = [gathered(k, left_o, own_o, right_o) for k in range(3)]
-    outer = [gathered(k, left_h, own_h, right_h) for k in range(3)]
     sides = []
     for side in range(2):
-        velocity = [
-            jnp.where(low_half, outer[k], inner[k])
-            if side == 0
-            else jnp.where(low_half, inner[k], outer[k])
-            for k in range(3)
-        ]
+        velocity = [edges[3 * side + k] for k in range(3)]
         grad = [[None] * 3 for _ in range(3)]
         for k in range(3):
             center = velocity[k]
@@ -214,25 +204,30 @@
             grad[1][k] = 0.5 * (ops.y_up(center) - ops.y_down(center))
             grad[2][k] = fourth(*(turn(center, -step) for step in (1, -1, 2, -2)))
         strain = strain_of(grad)
-        sides.append(filter_fields(velocity, strain, size_of(strain)))
+        for number, values in enumerate(filter_fields(velocity, strain, size_of(strain))):
+            if side == 0:
+                spread[number] = values
+            else:
+                spread[number] = jnp.where(low_half, spread[number], values)
     for number in range(21):
-        both = jnp.where(low_half, sides[0][number], sides[1][number])
+        both = spread[number]
         edges[number] = turn(both, STRIP) + turn(both, -STRIP) + 2.0 * both
-
+    for number in range(21):
+        for x in range(CX):
+            hats[number, x] = ops.unpack(edges[number], x + 3)
     last = ops.lane == LANES - 1
     first = ops.lane == 0
-    columns = jnp.zeros((ROWS, LANES), F32)
-    for x in range(CX):
-
-        def hat(number):
+    for x in range(CX):
+        for number in range(21):
             along_x = fields[number, x] + fields[number, x + 2] + 2.0 * fields[number, x + 1]
-            edge = ops.unpack(edges[number], x + 3)
+            edge = hats[number, x]
             before = turn(jnp.where(last, edge, along_x), 1)
             after = turn(jnp.where(first, edge, along_x), -1)
-            return before + after + 2.0 * along_x
-
-        velocity = [hat(k) for k in range(3)]
-        strain = [hat(9 + number) for number in range(6)]
+            hats[number, x] = before + after + 2.0 * along_x
+    columns = jnp.zeros((ROWS, LANES), F32)
+    for x in range(CX):
+        velocity = [hats[k, x] for k in range(3)]
+        strain = [hats[9 + number, x] for number in range(6)]
         diagonal = strain[0] * strain[0] + strain[1] * strain[1] + strain[2] * strain[2]
         other = strain[3] * strain[3] + strain[4] * strain[4] + strain[5] * strain[5]
         size = jnp.sqrt((2.0 / 256.0) * diagonal + ((4.0 / 256.0) * other + EPSILON))
@@ -240,12 +235,9 @@
         cross = 0.0
         square = 0.0
         for number, (a, b) in enumerate(PAIRS):
-            leonard = hat(3 + number) - (1.0 / 16.0) * velocity[a] * velocity[b]
-            model = hat(15 + number) - size * strain[number]
-            if WEIGHTS[number] != 1.0:
-                weighted = WEIGHTS[number] * model
-            else:
-                weighted = model
+            leonard = hats[3 + number, x] - (1.0 / 16.0) * velocity[a] * velocity[b]
+            model = hats[15 + number, x] - size * strain[number]
+            weighted = WEIGHTS[number] * model if WEIGHTS[number] != 1.0 else model
             cross = cross + leonard * weighted
             square = square + model * weighted
         cross = (1.0 / 256.0) * jnp.sum(cross, axis=1, keepdims=True)
@@ -262,56 +254,50 @@
         sums[...] = sums[...] + columns
 
 
-class State:
-    def __init__(self, ops, t, where, flow, rho, temp, left_1, right_1, left_2, right_2, own_halo):
-        self.ops, self.t, self.where = ops, t, where
-        self.flow, self.rho, self.temp = flow, rho, temp
-        self.left_1, self.right_1, self.left_2, self.right_2 = left_1, right_1, left_2, right_2
-        self.own_halo = own_halo
-
-    def plane(self, k, x):
-        t = self.t
-        if k < 3:
-            if x < 0:
-                return self.left_1[t * 9 + k * 3 + x + 3].astype(F32)
-            if x >= CX:
-                return self.right_1[t * 9 + k * 3 + x - CX].astype(F32)
-            return self.flow[self.where, k, x].astype(F32)
-        if x < 0:
-            return self.left_2[t * 4 + (k - 3) * 2 + x + 2].astype(F32)
-        if x >= CX:
-            return self.right_2[t * 4 + (k - 3) * 2 + x - CX].astype(F32)
-        return (self.rho if k == 3 else self.temp)[self.where, x].astype(F32)
-
-    def halo(self, k, x):
-        slot = 4 * self.t + k if k < 4 else SLOT_T + self.t
-        return self.ops.unpack(self.own_halo[slot // 4].astype(F32), 4 * (slot % 4) + x)
-
-    def terms(self, x, need_all=True):
-        ops = self.ops
-        grad = [[None] * 5 for _ in range(3)]
-        lap = [None] * 5
-        center = [self.plane(k, x) for k in range(5)]
-        for k in range(5):
-            if k == 3 and not need_all:
-                continue
-            edge = self.halo(k, x)
-            up, down = ops.y_up(center[k]), ops.y_down(center[k])
-            xs = [self.plane(k, x + step) for step in (1, -1, 2, -2)]
-            zs = [ops.z_at(center[k], edge, step) for step in (1, -1, 2, -2)]
-            if k < 3 or need_all:
-                grad[0][k] = fourth(*xs)
-                grad[1][k] = 0.5 * (up - down)
-                grad[2][k] = fourth(*zs)
-            if k != 3:
-                lap[k] = xs[0] + xs[1] + zs[0] + zs[1] + up + down - 6.0 * center[k]
-        size = size_of(strain_of(grad))
-        return center, grad, lap, size, 1.0 / center[3]
-
-
-def affine_update(ops, x, terms, psi_plane, psi_halo):
+def spread_state(ops, t, where, flow, rho, temp, left_1, right_1, left_2, right_2, own_halo, wide, halos):
+    for k in range(3):
+        for i in range(2):
+            wide[k, i] = left_1[t * 9 + k * 3 + 1 + i].astype(F32)
+            wide[k, 2 + CX + i] = right_1[t * 9 + k * 3 + i].astype(F32)
+        for x in range(CX):
+            wide[k, 2 + x] = flow[where, k, x].astype(F32)
+    for k in range(3, 5):
+        for i in range(2):
+            wide[k, i] = left_2[t * 4 + (k - 3) * 2 + i].astype(F32)
+            wide[k, 2 + CX + i] = right_2[t * 4 + (k - 3) * 2 + i].astype(F32)
+        for x in range(CX):
+            wide[k, 2 + x] = (rho if k == 3 else temp)[where, x].astype(F32)
+    for k in range(5):
+        slot = 4 * t + k if k < 4 else SLOT_T + t
+        strips = own_halo[slot // 4].astype(F32)
+        for x in range(CX):
+            halos[k, x] = ops.unpack(strips, 4 * (slot % 4) + x)
+
+
+def state_terms(ops, wide, halos, x, need_all=True):
+    grad = [[None] * 5 for _ in range(3)]
+    lap = [None] * 5
+    center = [wide[k, x + 2] for k in range(5)]
+    for k in range(5):
+        if k == 3 and not need_all:
+            continue
+        edge = halos[k, x]
+        up, down = ops.y_up(center[k]), ops.y_down(center[k])
+        xs = [wide[k, x + 2 + step] for step in (1, -1, 2, -2)]
+        zs = [ops.z_at(center[k], edge, step) for step in (1, -1, 2, -2)]
+        if k < 3 or need_all:
+            grad[0][k] = fourth(*xs)
+            grad[1][k] = 0.5 * (up - down)
+            grad[2][k] = fourth(*zs)
+        if k != 3:
+            lap[k] = xs[0] + xs[1] + zs[0] + zs[1] + up + down - 6.0 * center[k]
+    size = size_of(strain_of(grad))
+    return center, grad, lap, size, 1.0 / center[3]
+
+
+def affine_update(ops, x, terms, psi_wide, psi_halos):
     center, grad, lap, size, inv_rho = terms
-    psi = [psi_plane(k, x) for k in range(5)]
+    psi = [psi_wide[k, x + 2] for k in range(5)]
     work_mom = psi[0] * lap[0] + psi[1] * lap[1] + psi[2] * lap[2]
     work_heat = psi[4] * lap[4]
     turbulent = work_mom + work_heat * (1.0 / PRANDTL_TURB)
@@ -319,9 +305,9 @@
     size_rho = size * inv_rho
     first, second = [], []
     for k in range(5):
-        edge = psi_halo(k, x)
+        edge = psi_halos[k, x]
         up, down = ops.y_up(psi[k]), ops.y_down(psi[k])
-        xs = [psi_plane(k, x + step) for step in (1, -1, 2, -2)]
+        xs = [psi_wide[k, x + 2 + step] for step in (1, -1, 2, -2)]
         zs = [ops.z_at(psi[k], edge, step) for step in (1, -1, 2, -2)]
         rate = (
             center[0] * fourth(*xs) + center[1] * (0.5 * (up - down)) + center[2] * fourth(*zs)
@@ -347,39 +333,48 @@
 def first_kernel(
     flow, rho, temp, psi, left_1, right_1, left_2, right_2, own_halo,
     first, second, weight, sums,
+    wide, halos, psi_wide, psi_halos, work,
 ):
     ops = Ops()
-    state = State(ops, 0, 0, flow, rho, temp, left_1, right_1, left_2, right_2, own_halo)
-
-    def psi_plane(k, x):
-        if x < 0:
-            return left_2[8 + k * 2 + x + 2].astype(F32) + left_2[18 + k * 2 + x + 2].astype(F32)
-        if x >= CX:
-            return right_2[8 + k * 2 + x - CX].astype(F32) + right_2[18 + k * 2 + x - CX].astype(F32)
-        return psi[k, x]
-
-    def psi_halo(k, x):
-        slot = SLOT_PSI_HI + k
-        upper = ops.unpack(own_halo[slot // 4].astype(F32), 4 * (slot % 4) + x)
-        slot = SLOT_PSI_LO + k
-        return upper + ops.unpack(own_halo[slot // 4].astype(F32), 4 * (slot % 4) + x)
-
-    columns = jnp.zeros((ROWS, LANES), F32)
-    for x in range(CX):
-        new, slope, sensitivity = affine_update(ops, x, state.terms(x), psi_plane, psi_halo)
+    for k in range(5):
+        for i in range(2):
+            psi_wide[k, i] = left_2[8 + k * 2 + i].astype(F32) + left_2[18 + k * 2 + i].astype(F32)
+            psi_wide[k, 2 + CX + i] = (
+                right_2[8 + k * 2 + i].astype(F32) + right_2[18 + k * 2 + i].astype(F32)
+            )
+        upper, lower = SLOT_PSI_HI + k, SLOT_PSI_LO + k
+        upper_strips = own_halo[upper // 4].astype(F32)
+        lower_strips = own_halo[lower // 4].astype(F32)
+        for x in range(CX):
+            psi_wide[k, 2 + x] = psi[k, x]
+            psi_halos[k, x] = ops.unpack(upper_strips, 4 * (upper % 4) + x) + ops.unpack(
+                lower_strips, 4 * (lower % 4) + x
+            )
+    spread_state(
+        ops, 0, 0, flow, rho, temp, left_1, right_1, left_2, right_2, own_halo,
+        wide.at[0], halos.at[0],
+    )
+    spread_state(
+        ops, 1, 1, flow, rho, temp, left_1, right_1, left_2, right_2, own_halo,
+        wide.at[1], halos.at[1],
+    )
+    for x in range(CX):
+        terms = state_terms(ops, wide.at[0], halos.at[0], x)
+        new, slope, sensitivity = affine_update(ops, x, terms, psi_wide, psi_halos)
         for k in range(5):
             first[k, x] = new[k]
             second[k, x] = slope[k]
-        total = jnp.sum(sensitivity, axis=1, keepdims=True)
-        columns = jnp.where(ops.lane == x, total, columns)
-    sums[...] = columns
-    state = State(ops, 1, 1, flow, rho, temp, left_1, right_1, left_2, right_2, own_halo)
-    for x in range(CX):
-        _, _, lap, size, inv_rho = state.terms(x, need_all=False)
+        work[x] = sensitivity
+    for x in range(CX):
+        _, _, lap, size, inv_rho = state_terms(ops, wide.at[1], halos.at[1], x, need_all=False)
         size_rho = size * inv_rho
         for number, k in enumerate((0, 1, 2, 4)):
             scale = 1.0 if k < 3 else 1.0 / PRANDTL_TURB
             weight[number, x] = (scale * size_rho) * lap[k]
+    columns = jnp.zeros((ROWS, LANES), F32)
+    for x in range(CX):
+        columns = jnp.where(ops.lane == x, jnp.sum(work[x], axis=1, keepdims=True), columns)
+    sums[...] = columns
 
 
 def coefficients(ops, own, other):
@@ -387,54 +382,61 @@
     return total / (turn(total, -4) + EPSILON)
 
 
-def middle_kernel(first, second, weight, partial, own, other, psi, up, down, packed):
+def middle_kernel(
+    first, second, weight, partial, own, other, psi, up, down, packed, coef_planes, work
+):
     ops = Ops()
     coef = coefficients(ops, own[...], other[...])
-    columns = partial[...]
-    planes = [{}, {}]
-    for x in range(CX):
-        coef_x = jnp.broadcast_to(coef[:, x : x + 1], (ROWS, LANES))
-        values = [first[k, x] + coef_x * second[k, x] for k in range(5)]
+    for x in range(CX):
+        coef_planes[x] = jnp.broadcast_to(coef[:, x : x + 1], (ROWS, LANES))
+    for x in range(CX):
+        values = [first[k, x] + coef_planes[x] * second[k, x] for k in range(5)]
         for k in range(5):
             psi[k, x] = values[k]
             if x >= 2:
                 up[k, x - 2] = values[k]
             else:
                 down[k, x] = values[k]
-            planes[k // 4][4 * (k % 4) + x] = values[k]
-        work = weight[0, x] * values[0] + weight[1, x] * values[1]
-        work = work + weight[2, x] * values[2] + weight[3, x] * values[4]
+        total = weight[0, x] * values[0] + weight[1, x] * values[1]
+        work[x] = total + weight[2, x] * values[2] + weight[3, x] * values[4]
+    for number in range(2):
+        planes = {}
+        for k in range(4 * number, min(4 * number + 4, 5)):
+            for x in range(CX):
+                planes[4 * (k % 4) + x] = psi[k, x]
+        packed[number] = pack_strips(ops, planes)
+    columns = partial[...]
+    for x in range(CX):
         columns = jnp.where(
-            ops.lane == 4 + x, jnp.sum(work, axis=1, keepdims=True), columns
+            ops.lane == 4 + x, jnp.sum(work[x], axis=1, keepdims=True), columns
         )
-    for number in range(2):
-        packed[number] = pack_strips(ops, planes[number])
     packed[2] = columns
 
 
 def last_kernel(
     flow, rho, temp, psi, left_1, right_1, left_2, right_2, own_halo,
     left_psi, right_psi, psi_edges, own, other, out,
+    wide, halos, psi_wide, psi_halos, coef_planes,
 ):
     ops = Ops()
     coef = coefficients(ops, own[...], other[...])
-    state = State(ops, 1, 0, flow, rho, temp, left_1, right_1, left_2, right_2, own_halo)
-
-    def psi_plane(k, x):
-        if x < 0:
-            return left_psi[k, x + 2]
-        if x >= CX:
-            return right_psi[k, x - CX]
-        return psi[k, x]
-
-    def psi_halo(k, x):
-        return ops.unpack(psi_edges[k // 4], 4 * (k % 4) + x)
-
-    for x in range(CX):
-        new, slope, _ = affine_update(ops, x, state.terms(x), psi_plane, psi_halo)
-        coef_x = jnp.broadcast_to(coef[:, 8 + x : 9 + x], (ROWS, LANES))
+    for x in range(CX):
+        coef_planes[x] = jnp.broadcast_to(coef[:, 8 + x : 9 + x], (ROWS, LANES))
+    for k in range(5):
+        for i in range(2):
+            psi_wide[k, i] = left_psi[k, i]
+            psi_wide[k, 2 + CX + i] = right_psi[k, i]
+        for x in range(CX):
+            psi_wide[k, 2 + x] = psi[k, x]
+            psi_halos[k, x] = ops.unpack(psi_edges[k // 4], 4 * (k % 4) + x)
+    spread_state(
+        ops, 1, 0, flow, rho, temp, left_1, right_1, left_2, right_2, own_halo, wide, halos
+    )
+    for x in range(CX):
+        terms = state_terms(ops, wide, halos, x)
+        new, slope, _ = affine_update(ops, x, terms, psi_wide, psi_halos)
         for k in range(5):
-            out[k, x] = new[k] + coef_x * slope[k]
+            out[k, x] = new[k] + coef_planes[x] * slope[k]
 
 
 def ring(axis):
@@ -465,6 +467,13 @@
 
 def whole(count):
     return [pl.BlockSpec(memory_space=pltpu.VMEM)] * count
+
+
+def scratch(*dims):
+    return [pltpu.VMEM(d + (ROWS, LANES), F32) for d in dims]
+
+
+PARAMS = pltpu.CompilerParams(vmem_limit_bytes=24 * 2**20)
 
 
 def cost(operations, size):
@@ -480,6 +489,7 @@
         out_specs=whole(1)[0],
         out_shape=shape_of((5,) + block, BF16),
         cost_estimate=cost(2_000_000, 700_000),
+        compiler_params=PARAMS,
         name="pack",
     )(flow, rho, temp, psi)
     own_halo = span_edges(own_pack)
@@ -489,12 +499,16 @@
         out_specs=whole(4),
         out_shape=[shape_of((22,) + block, BF16)] * 2 + [shape_of((28,) + block, BF16)] * 2,
         cost_estimate=cost(1_000_000, 1_500_000),
+        compiler_params=PARAMS,
         name="message",
     )(flow, rho, temp, psi, own_pack)
     first_up = lax.dynamic_update_slice(first_up, own_halo[:2], (20, 0, 0))
     first_down = lax.dynamic_update_slice(first_down, own_halo[:2], (20, 0, 0))
     left_1 = lax.ppermute(first_up, "gx", forward)
     right_1 = lax.ppermute(first_down, "gx", backward)
+    second_up, second_down, left_1, right_1 = lax.optimization_barrier(
+        (second_up, second_down, left_1, right_1)
+    )
     left_2 = lax.ppermute(second_up, "gx", forward)
     right_2 = lax.ppermute(second_down, "gx", backward)
 
@@ -513,8 +527,11 @@
         ],
         out_specs=fixed(block),
         out_shape=shape_of(block, F32),
-        scratch_shapes=[pltpu.VMEM((21, CX + 2) + block, F32), pltpu.VMEM((21,) + block, F32)],
+        scratch_shapes=scratch(
+            (3, CX + 6), (3, CX + 2), (21, CX + 2), (21,), (21,), (21, CX)
+        ),
         cost_estimate=cost(40_000_000, 1_000_000),
+        compiler_params=PARAMS,
         name="germano",
     )(flow, left_1, right_1, own_pack, own_halo)
     own, other = span_sum(own)
@@ -528,7 +545,9 @@
             shape_of((4, CX) + block, F32),
             shape_of(block, F32),
         ],
+        scratch_shapes=scratch((2, 5, CX + 4), (2, 5, CX), (5, CX + 4), (5, CX), (CX,)),
         cost_estimate=cost(20_000_000, 2_500_000),
+        compiler_params=PARAMS,
         name="first",
     )(flow, rho, temp, psi, left_1, right_1, left_2, right_2, own_halo)
     psi, up, down, packed = pl.pallas_call(
@@ -541,7 +560,9 @@
             shape_of((5, 2) + block, F32),
             shape_of((3,) + block, F32),
         ],
+        scratch_shapes=scratch((CX,), (CX,)),
         cost_estimate=cost(1_000_000, 2_000_000),
+        compiler_params=PARAMS,
         name="middle",
     )(first, second, weight, partial, own, other)
     left_psi = lax.ppermute(up, "gx", forward)
@@ -572,7 +593,9 @@
         ],
         out_specs=fixed((5, CX) + block),
         out_shape=shape_of((5, CX) + block, F32),
+        scratch_shapes=scratch((5, CX + 4), (5, CX), (5, CX + 4), (5, CX), (CX,)),
         cost_estimate=cost(15_000_000, 2_500_000),
+        compiler_params=PARAMS,
         name="last",
     )(
         flow, rho, temp, psi, left_1, right_1, left_2, right_2, own_halo,

time: 65 us -> 44.2 us (0.68)
  Pallas kernels: 34.6 us -> 8.01 us
  starting transfers between devices: 14.4 us -> 18.5 us
  waiting for transfers between devices: 9.54 us -> 12.5 us
  other arithmetic: 0.75 us -> 0.01 us
    pallas_call x1, Pallas kernels: 17.1 us -> 3.79 us  [local(): pl.pallas_call(germano_kernel, grid=(2,), in_specs=[pl.BlockSpec((1, 3, C...]
    pallas_call x1, Pallas kernels: 6.26 us -> 1.56 us  [local(): pl.pallas_call(first_kernel, in_specs=whole(9), out_specs=whole(4), out_s...]
    ppermute x1, starting transfers between devices: 0.2 us -> 3.37 us  [local(): right_1 = lax.ppermute(first_down, 'gx', backward)]
    pallas_call x1, Pallas kernels: 5.07 us -> 1.96 us  [local(): pl.pallas_call(last_kernel, grid=(1,), in_specs=[pl.BlockSpec((1, 3, CX)...]
    pallas_call x1, Pallas kernels: 1.98 us -> 0.08 us  [local(): pl.pallas_call(message_kernel, in_specs=whole(5), out_specs=whole(4), out...]
    ppermute x2, waiting for transfers between devices: 0.01 us -> 1.9 us  [span_edges(): before = lax.ppermute(block, 'gz', forward)]
    pallas_call x1, Pallas kernels: 2.25 us -> 0.38 us  [local(): pl.pallas_call(middle_kernel, in_specs=whole(6), out_specs=whole(4), out_...]
    pallas_call x1, Pallas kernels: 2 us -> 0.24 us  [local(): pl.pallas_call(pack_kernel, in_specs=whole(4), out_specs=whole(1)[0], out...]
  transfers between devices with their start and end apart: 9 -> 9, of which waited for: 3 -> 5; matrix products, arithmetic and copies ran while one was open for 3% -> 2% of each run, Pallas kernels for 39% -> 12%
where the time goes in v2:
time: 44.2 us; the launch traced here: 43.9 us
  starting transfers between devices  18.5 us (42%)
  waiting for transfers between devices  12.5 us (28%)
  Pallas kernels  8.01 us (18%)
  local copies, waits for them, and re-layouts  4.26 us (10%)
  between operations  0.7 us (2%)
    ppermute x2, starting transfers between devices, span_edges(): before = lax.ppermute(block, 'gz', forward)  4.62 us
    ppermute x1, waiting for transfers between devices, local(): left_1 = lax.ppermute(first_up, 'gx', forward)  4.6 us
    ppermute x1, starting transfers between devices, local(): right_2 = lax.ppermute(second_down, 'gx', backward)  4.44 us
    ppermute x1, starting transfers between devices, local(): right_psi = lax.ppermute(down, 'gx', backward)  4.44 us
    pallas_call x1, Pallas kernels, local(): pl.pallas_call(germano_kernel, grid=(2,), in_specs=[pl.BlockSpec((1, 3, C...  3.79 us
    unnamed x16, local copies, waits for them, and re-layouts  3.59 us
    ppermute x1, starting transfers between devices, local(): right_1 = lax.ppermute(first_down, 'gx', backward)  3.37 us
    ppermute x1, waiting for transfers between devices, local(): right_1 = lax.ppermute(first_down, 'gx', backward)  3.01 us
  transfers between devices with their start and end apart: 9, of which 5 were waited for; matrix products, arithmetic and copies ran while one was open for 2% of the time, Pallas kernels for 12%

profile of v2, /device:TPU:0, one launch (start us, length us, event | category | flops | bytes accessed | tf_op | source)
XLA Modules:
  0.0 43.9 jit_solution(13608809096703944816)
XLA Ops:
  0.6 0.0 copy-start
  0.6 0.9 %copy-done = bf16[2,3,4,32,128]{4,3,2,1,0:T(8,128)(2,1)S(1)} copy-done((bf16[2,3,4,32,128]{4,3,2,1,0:T(8,128)(2,1)S(1)}, bf16[2,3,4,32,128]{4,3,2,1,0:T(8,128)(2,1)}, u32[]{:S(2)}) %copy-start) | copy-done | bytes 196632
  1.6 1.0 %copy-done.2 = f32[5,4,32,128]{3,2,1,0:T(8,128)S(1)} copy-done((f32[5,4,32,128]{3,2,1,0:T(8,128)S(1)}, f32[5,4,32,128]{3,2,1,0:T(8,128)}, u32[]{:S(2)}) %copy-start.2) | copy-done | bytes 327704
  2.5 0.8 %copy-done.4 = bf16[2,4,32,128]{3,2,1,0:T(8,128)(2,1)S(1)} copy-done((bf16[2,4,32,128]{3,2,1,0:T(8,128)(2,1)S(1)}, bf16[2,4,32,128]{3,2,1,0:T(8,128)(2,1)}, u32[]{:S(2)}) %copy-start.4) | copy-done | bytes 65560
  3.4 0.8 %copy-done.6 = bf16[2,4,32,128]{3,2,1,0:T(8,128)(2,1)S(1)} copy-done((bf16[2,4,32,128]{3,2,1,0:T(8,128)(2,1)S(1)}, bf16[2,4,32,128]{3,2,1,0:T(8,128)(2,1)}, u32[]{:S(2)}) %copy-start.6) | copy-done | bytes 65560
  4.2 0.2 pack.1.packed.own_pack
  4.5 3.0 %collective-permute-start = (bf16[5,32,128]{2,1,0:T(8,128)(2,1)S(1)}, bf16[5,32,128]{2,1,0:T(8,128)(2,1)S(1)}, u32[]{:S(2)}, u32[]{:S(2)}) collective-permute-start(bf16[5,32,128]{2,1,0:T(8,128)(2,1)S(1)} %pack.1.packed.own_pack), channel_id=1, source_target_pairs={{0,1},{1,0},{2,3},{3,2},{4,5},{5,4},{6,7},{7,6},{8,9},{9,8},{10,11... | collective-permute-start | bytes 122888 | tf_op jit(solution)/shard_map/ppermute | solution.py:450
  7.5 0.1 message.1
  7.6 1.9 %collective-permute-done.own_halo = bf16[5,32,128]{2,1,0:T(8,128)(2,1)S(1)} collective-permute-done((bf16[5,32,128]{2,1,0:T(8,128)(2,1)S(1)}, bf16[5,32,128]{2,1,0:T(8,128)(2,1)S(1)}, u32[]{:S(2)}, u32[]{:S(2)}) %collective-permute-start) | collective-permute-done | bytes 40992 | tf_op jit(solution)/shard_map/ppermute | solution.py:450
  9.5 3.4 %collective-permute-start.2 = (bf16[22,32,128]{2,1,0:T(8,128)(2,1)S(1)}, bf16[22,32,128]{2,1,0:T(8,128)(2,1)S(1)}, u32[]{:S(2)}, u32[]{:S(2)}) collective-permute-start(bf16[22,32,128]{2,1,0:T(8,128)(2,1)S(1)} %get-tuple-element.36), channel_id=1, source_target_pairs={{2,0},{4,2},{6,4},{8,6},{10,8},{12,10},{14,12},{16,14},{18,16},{20... | collective-permute-start | bytes 540680 | tf_op jit(solution)/shard_map/ppermute | solution.py:508
  12.9 3.0 %collective-permute-done.2.right_1.right = bf16[22,32,128]{2,1,0:T(8,128)(2,1)S(1)} collective-permute-done((bf16[22,32,128]{2,1,0:T(8,128)(2,1)S(1)}, bf16[22,32,128]{2,1,0:T(8,128)(2,1)S(1)}, u32[]{:S(2)}, u32[]{:S(2)}) %collective-permute-start.2) | collective-permute-done | bytes 180256 | tf_op jit(solution)/shard_map/ppermute | solution.py:508
  15.9 4.6 %collective-permute-done.1.left_1.left = bf16[22,32,128]{2,1,0:T(8,128)(2,1)S(1)} collective-permute-done((bf16[22,32,128]{2,1,0:T(8,128)(2,1)S(1)}, bf16[22,32,128]{2,1,0:T(8,128)(2,1)S(1)}, u32[]{:S(2)}, u32[]{:S(2)}) %collective-permute-start.1) | collective-permute-done | bytes 180256 | tf_op jit(solution)/shard_map/ppermute | solution.py:507
  20.5 4.4 %collective-permute-start.4 = (bf16[28,32,128]{2,1,0:T(8,128)(2,1)S(1)}, bf16[28,32,128]{2,1,0:T(8,128)(2,1)S(1)}, u32[]{:S(2)}, u32[]{:S(2)}) collective-permute-start(bf16[28,32,128]{2,1,0:T(8,128)(2,1)S(1)} %get-tuple-element.25), channel_id=1, source_target_pairs={{2,0},{4,2},{6,4},{8,6},{10,8},{12,10},{14,12},{16,14},{18,16},{20... | collective-permute-start | bytes 688136 | tf_op jit(solution)/shard_map/ppermute | solution.py:513
  24.9 3.8 %germano.1.own = f32[32,128]{1,0:T(8,128)S(1)} custom-call(bf16[2,3,4,32,128]{4,3,2,1,0:T(8,128)(2,1)S(1)} %copy-done, bf16[22,32,128]{2,1,0:T(8,128)(2,1)S(1)} %collective-permute-done.1.left_1.left, bf16[22,32,128]{2,1,0:T(8,128)(2,1)S(1)} %collective-permute-done.2.right_1.right, bf16[5,32,128]{2,1,0:T(8,128)(2,1)S(1)} %pack.1.packed.own_pack, ...), custom_call_target="tpu_custom_call" | custom-call | flops 40000000 | bytes 1000000 | tf_op jit(solution)/shard_map/germano/pallas_call | solution.py:518
  28.7 1.6 %collective-permute-start.5 = (f32[32,128]{1,0:T(8,128)S(1)}, f32[32,128]{1,0:T(8,128)S(1)}, u32[]{:S(2)}, u32[]{:S(2)}) collective-permute-start(f32[32,128]{1,0:T(8,128)S(1)} %germano.1.own), channel_id=1, source_target_pairs={{0,1},{1,0},{2,3},{3,2},{4,5},{5,4},{6,7},{7,6},{8,9},{9,8},{10,11... | collective-permute-start | bytes 49160 | tf_op jit(solution)/shard_map/ppermute | solution.py:460
  30.3 1.6 %first.1 = (f32[5,4,32,128]{3,2,1,0:T(8,128)S(1)}, f32[5,4,32,128]{3,2,1,0:T(8,128)S(1)}, f32[4,4,32,128]{3,2,1,0:T(8,128)S(1)}, f32[32,128]{1,0:T(8,128)S(1)}) custom-call(bf16[2,3,4,32,128]{4,3,2,1,0:T(8,128)(2,1)S(1)} %copy-done, bf16[2,4,32,128]{3,2,1,0:T(8,128)(2,1)S(1)} %copy-done.5, bf16[2,4,32,128]{3,2,1,0:T(8,128)(2,1)S(1)} %copy-done.6, ...), custom_call_target="tpu_custom_call" | custom-call | flops 20000000 | bytes 2500000 | tf_op jit(solution)/shard_map/first/pallas_call | solution.py:538
  31.9 0.6 %collective-permute-done.5.other = f32[32,128]{1,0:T(8,128)S(1)} collective-permute-done((f32[32,128]{1,0:T(8,128)S(1)}, f32[32,128]{1,0:T(8,128)S(1)}, u32[]{:S(2)}, u32[]{:S(2)}) %collective-permute-start.5) | collective-permute-done | bytes 16416 | tf_op jit(solution)/shard_map/ppermute | solution.py:460
  32.5 0.4 middle.1
  32.9 0.0 copy-start.7
  32.9 1.6 %collective-permute-start.8 = (f32[3,32,128]{2,1,0:T(8,128)S(1)}, f32[3,32,128]{2,1,0:T(8,128)S(1)}, u32[]{:S(2)}, u32[]{:S(2)}) collective-permute-start(f32[3,32,128]{2,1,0:T(8,128)S(1)} %get-tuple-element.33), channel_id=1, source_target_pairs={{0,1},{1,0},{2,3},{3,2},{4,5},{5,4},{6,7},{7,6},{8,9},{9,8},{10,11... | collective-permute-start | bytes 147464 | tf_op jit(solution)/shard_map/ppermute | solution.py:450
  34.5 4.4 %collective-permute-start.7 = (f32[5,2,32,128]{3,2,1,0:T(8,128)S(1)}, f32[5,2,32,128]{3,2,1,0:T(8,128)S(1)}, u32[]{:S(2)}, u32[]{:S(2)}) collective-permute-start(f32[5,2,32,128]{3,2,1,0:T(8,128)S(1)} %get-tuple-element.32), channel_id=1, source_target_pairs={{2,0},{4,2},{6,4},{8,6},{10,8},{12,10},{14,12},{16,14},{18,16},{20... | collective-permute-start | bytes 491528 | tf_op jit(solution)/shard_map/ppermute | solution.py:569
  39.0 0.7 %copy.7 = f32[8,32]{1,0:T(8,128)} copy(f32[8,32]{0,1:T(8,128)S(1)} %fusion) | data formatting | bytes 2048 | tf_op jit(solution)/shard_map/mul | solution.py:605
  39.6 2.3 %collective-permute-done.6.left_psi = f32[5,2,32,128]{3,2,1,0:T(8,128)S(1)} collective-permute-done((f32[5,2,32,128]{3,2,1,0:T(8,128)S(1)}, f32[5,2,32,128]{3,2,1,0:T(8,128)S(1)}, u32[]{:S(2)}, u32[]{:S(2)}) %collective-permute-start.6) | collective-permute-done | bytes 163872 | tf_op jit(solution)/shard_map/ppermute | solution.py:568
  42.0 2.0 %last.1 = f32[5,4,32,128]{3,2,1,0:T(8,128)} custom-call(bf16[2,3,4,32,128]{4,3,2,1,0:T(8,128)(2,1)S(1)} %copy-done.1, bf16[2,4,32,128]{3,2,1,0:T(8,128)(2,1)S(1)} %copy-done.5, bf16[2,4,32,128]{3,2,1,0:T(8,128)(2,1)S(1)} %copy-done.7, f32[5,4,32,128]{3,2,1,0:T(8,128)S(1)} %get-tuple-element.30.psi, ...), custom_call_target="tpu_custom_call" | custom-call | flops 15000000 | bytes 2500000 | tf_op jit(solution)/shard_map/last/pallas_call | solution.py:575
  (20 shorter events, 0.1 us)
Async XLA Ops:
  0.6 0.9 %copy-start = (bf16[2,3,4,32,128]{4,3,2,1,0:T(8,128)(2,1)S(1)}, bf16[2,3,4,32,128]{4,3,2,1,0:T(8,128)(2,1)}, u32[]{:S(2)}) copy-start(bf16[2,3,4,32,128]{4,3,2,1,0:T(8,128)(2,1)} %flow.9) | copy-start | bytes 589828
  1.6 1.0 %copy-start.2 = (f32[5,4,32,128]{3,2,1,0:T(8,128)S(1)}, f32[5,4,32,128]{3,2,1,0:T(8,128)}, u32[]{:S(2)}) copy-start(f32[5,4,32,128]{3,2,1,0:T(8,128)} %psi.5) | copy-start | bytes 983044
  2.5 0.8 %copy-start.4 = (bf16[2,4,32,128]{3,2,1,0:T(8,128)(2,1)S(1)}, bf16[2,4,32,128]{3,2,1,0:T(8,128)(2,1)}, u32[]{:S(2)}) copy-start(bf16[2,4,32,128]{3,2,1,0:T(8,128)(2,1)} %rho.7) | copy-start | bytes 196612
  3.4 0.8 %copy-start.6 = (bf16[2,4,32,128]{3,2,1,0:T(8,128)(2,1)S(1)}, bf16[2,4,32,128]{3,2,1,0:T(8,128)(2,1)}, u32[]{:S(2)}) copy-start(bf16[2,4,32,128]{3,2,1,0:T(8,128)(2,1)} %temp.7) | copy-start | bytes 196612
  4.5 5.0 %collective-permute-start = (bf16[5,32,128]{2,1,0:T(8,128)(2,1)S(1)}, bf16[5,32,128]{2,1,0:T(8,128)(2,1)S(1)}, u32[]{:S(2)}, u32[]{:S(2)}) collective-permute-start(bf16[5,32,128]{2,1,0:T(8,128)(2,1)S(1)} %pack.1.packed.own_pack), channel_id=1, source_target_pairs={{0,1},{1,0},{2,3},{3,2},{4,5},{5,4},{6,7},{7,6},{8,9},{9,8},{10,11... | collective-permute-start | bytes 122888 | tf_op jit(solution)/shard_map/ppermute | solution.py:450
  9.5 6.4 %collective-permute-start.2 = (bf16[22,32,128]{2,1,0:T(8,128)(2,1)S(1)}, bf16[22,32,128]{2,1,0:T(8,128)(2,1)S(1)}, u32[]{:S(2)}, u32[]{:S(2)}) collective-permute-start(bf16[22,32,128]{2,1,0:T(8,128)(2,1)S(1)} %get-tuple-element.36), channel_id=1, source_target_pairs={{2,0},{4,2},{6,4},{8,6},{10,8},{12,10},{14,12},{16,14},{18,16},{20... | collective-permute-start | bytes 540680 | tf_op jit(solution)/shard_map/ppermute | solution.py:508
  12.9 7.6 %collective-permute-start.1 = (bf16[22,32,128]{2,1,0:T(8,128)(2,1)S(1)}, bf16[22,32,128]{2,1,0:T(8,128)(2,1)S(1)}, u32[]{:S(2)}, u32[]{:S(2)}) collective-permute-start(bf16[22,32,128]{2,1,0:T(8,128)(2,1)S(1)} %get-tuple-element.37), channel_id=1, source_target_pairs={{0,2},{2,4},{4,6},{6,8},{8,10},{10,12},{12,14},{14,16},{16,18},{18... | collective-permute-start | bytes 540680 | tf_op jit(solution)/shard_map/ppermute | solution.py:507
  20.5 9.8 %copy-start.3 = (f32[5,4,32,128]{3,2,1,0:T(8,128)S(1)}, f32[5,4,32,128]{3,2,1,0:T(8,128)}, u32[]{:S(2)}) copy-start(f32[5,4,32,128]{3,2,1,0:T(8,128)} %psi.5) | copy-start | bytes 983044
  20.5 9.8 %copy-start.5 = (bf16[2,4,32,128]{3,2,1,0:T(8,128)(2,1)S(1)}, bf16[2,4,32,128]{3,2,1,0:T(8,128)(2,1)}, u32[]{:S(2)}) copy-start(bf16[2,4,32,128]{3,2,1,0:T(8,128)(2,1)} %rho.7) | copy-start | bytes 196612
  20.5 9.8 %collective-permute-start.3 = (bf16[28,32,128]{2,1,0:T(8,128)(2,1)S(1)}, bf16[28,32,128]{2,1,0:T(8,128)(2,1)S(1)}, u32[]{:S(2)}, u32[]{:S(2)}) collective-permute-start(bf16[28,32,128]{2,1,0:T(8,128)(2,1)S(1)} %get-tuple-element.24), channel_id=1, source_target_pairs={{0,2},{2,4},{4,6},{6,8},{8,10},{10,12},{12,14},{14,16},{16,18},{18... | collective-permute-start | bytes 688136 | tf_op jit(solution)/shard_map/ppermute | solution.py:512
  20.5 9.8 %collective-permute-start.4 = (bf16[28,32,128]{2,1,0:T(8,128)(2,1)S(1)}, bf16[28,32,128]{2,1,0:T(8,128)(2,1)S(1)}, u32[]{:S(2)}, u32[]{:S(2)}) collective-permute-start(bf16[28,32,128]{2,1,0:T(8,128)(2,1)S(1)} %get-tuple-element.25), channel_id=1, source_target_pairs={{2,0},{4,2},{6,4},{8,6},{10,8},{12,10},{14,12},{16,14},{18,16},{20... | collective-permute-start | bytes 688136 | tf_op jit(solution)/shard_map/ppermute | solution.py:513
  28.7 3.8 %collective-permute-start.5 = (f32[32,128]{1,0:T(8,128)S(1)}, f32[32,128]{1,0:T(8,128)S(1)}, u32[]{:S(2)}, u32[]{:S(2)}) collective-permute-start(f32[32,128]{1,0:T(8,128)S(1)} %germano.1.own), channel_id=1, source_target_pairs={{0,1},{1,0},{2,3},{3,2},{4,5},{5,4},{6,7},{7,6},{8,9},{9,8},{10,11... | collective-permute-start | bytes 49160 | tf_op jit(solution)/shard_map/ppermute | solution.py:460
  32.5 9.4 %copy-start.1 = (bf16[2,3,4,32,128]{4,3,2,1,0:T(8,128)(2,1)S(1)}, bf16[2,3,4,32,128]{4,3,2,1,0:T(8,128)(2,1)}, u32[]{:S(2)}) copy-start(bf16[2,3,4,32,128]{4,3,2,1,0:T(8,128)(2,1)} %flow.9) | copy-start | bytes 589828
  32.9 9.0 %copy-start.7 = (bf16[2,4,32,128]{3,2,1,0:T(8,128)(2,1)S(1)}, bf16[2,4,32,128]{3,2,1,0:T(8,128)(2,1)}, u32[]{:S(2)}) copy-start(bf16[2,4,32,128]{3,2,1,0:T(8,128)(2,1)} %temp.7) | copy-start | bytes 196612
  32.9 6.0 %collective-permute-start.8 = (f32[3,32,128]{2,1,0:T(8,128)S(1)}, f32[3,32,128]{2,1,0:T(8,128)S(1)}, u32[]{:S(2)}, u32[]{:S(2)}) collective-permute-start(f32[3,32,128]{2,1,0:T(8,128)S(1)} %get-tuple-element.33), channel_id=1, source_target_pairs={{0,1},{1,0},{2,3},{3,2},{4,5},{5,4},{6,7},{7,6},{8,9},{9,8},{10,11... | collective-permute-start | bytes 147464 | tf_op jit(solution)/shard_map/ppermute | solution.py:450
  34.5 7.4 %collective-permute-start.6 = (f32[5,2,32,128]{3,2,1,0:T(8,128)S(1)}, f32[5,2,32,128]{3,2,1,0:T(8,128)S(1)}, u32[]{:S(2)}, u32[]{:S(2)}) collective-permute-start(f32[5,2,32,128]{3,2,1,0:T(8,128)S(1)} %get-tuple-element.31), channel_id=1, source_target_pairs={{0,2},{2,4},{4,6},{6,8},{8,10},{10,12},{12,14},{14,16},{16,18},{18... | collective-permute-start | bytes 491528 | tf_op jit(solution)/shard_map/ppermute | solution.py:568
  34.5 7.4 %collective-permute-start.7 = (f32[5,2,32,128]{3,2,1,0:T(8,128)S(1)}, f32[5,2,32,128]{3,2,1,0:T(8,128)S(1)}, u32[]{:S(2)}, u32[]{:S(2)}) collective-permute-start(f32[5,2,32,128]{3,2,1,0:T(8,128)S(1)} %get-tuple-element.32), channel_id=1, source_target_pairs={{2,0},{4,2},{6,4},{8,6},{10,8},{12,10},{14,12},{16,14},{18,16},{20... | collective-permute-start | bytes 491528 | tf_op jit(solution)/shard_map/ppermute | solution.py:569

commit v3 on v2

v3 whole, which is shorter than its diff:
```python
import functools
import math

import jax
import jax.numpy as jnp
from jax import lax
from jax.experimental import pallas as pl
from jax.experimental.pallas import tpu as pltpu
from jax.sharding import PartitionSpec as P

EPSILON = 1e-06
NU_MOL = 0.05
PRANDTL = 0.72
PRANDTL_TURB = 0.9
TIME_STEP = 0.04
PAIRS = ((0, 0), (1, 1), (2, 2), (0, 1), (0, 2), (1, 2))
WEIGHTS = (1.0, 1.0, 1.0, 2.0, 2.0, 2.0)

CX = 4
ROWS = 32
LANES = 128
STRIP = 8
F32 = jnp.float32
BF16 = jnp.bfloat16
SLOT_T = 8
SLOT_PSI_HI = 10
SLOT_PSI_LO = 15
BAND = 12
STRIP_BLOCKS = 5
VELOCITY = 0
SCALARS = 18
PSI_HI = 26
PSI_LO = 36
MESSAGE = 46


def lane_ids():
    return lax.broadcasted_iota(jnp.int32, (ROWS, LANES), 1)


def row_ids():
    return lax.broadcasted_iota(jnp.int32, (ROWS, LANES), 0)


def turn(values, shift):
    shift = shift % LANES
    return values if shift == 0 else pltpu.roll(values, shift, 1)


class Ops:
    def __init__(self):
        self.lane = lane_ids()
        row = row_ids()
        self.top = row == ROWS - 1
        self.bottom = row == 0

    def z_at(self, values, halo, step):
        if step > 0:
            return turn(jnp.where(self.lane < step, halo, values), -step)
        return turn(jnp.where(self.lane >= LANES + step, halo, values), -step)

    def y_up(self, values):
        return jnp.where(self.top, 0.0, pltpu.roll(values, ROWS - 1, 0))

    def y_down(self, values):
        return jnp.where(self.bottom, 0.0, pltpu.roll(values, 1, 0))

    def unpack(self, block, strip):
        return turn(block, LANES - 4 - STRIP * strip)


def fourth(plus, minus, plus_2, minus_2):
    return (2.0 / 3.0) * (plus - minus) - (1.0 / 12.0) * (plus_2 - minus_2)


def strain_of(grad):
    return [
        grad[0][0],
        grad[1][1],
        grad[2][2],
        0.5 * (grad[0][1] + grad[1][0]),
        0.5 * (grad[0][2] + grad[2][0]),
        0.5 * (grad[1][2] + grad[2][1]),
    ]


def size_of(strain):
    diagonal = strain[0] * strain[0] + strain[1] * strain[1] + strain[2] * strain[2]
    other = strain[3] * strain[3] + strain[4] * strain[4] + strain[5] * strain[5]
    return jnp.sqrt(2.0 * diagonal + (4.0 * other + EPSILON))


def filter_fields(velocity, strain, size):
    products = [velocity[a] * velocity[b] for a, b in PAIRS]
    return list(velocity) + products + strain + [size * part for part in strain]


def pack_strips(ops, planes):
    block = jnp.zeros((ROWS, LANES), F32)
    strip_id = (ops.lane >> 3)
    for strip, values in planes.items():
        block = jnp.where(strip_id == strip, turn(values, STRIP * strip + 4), block)
    return block


def split_halves(values):
    upper = values.astype(BF16)
    lower = (values - upper.astype(F32)).astype(BF16)
    return upper, lower


def spread_state(ops, t, where, flow, rho, temp, left, right, own_halo, wide, halos):
    for k in range(3):
        for i in range(2):
            wide[k, i] = left[t * 9 + k * 3 + 1 + i].astype(F32)
            wide[k, 2 + CX + i] = right[t * 9 + k * 3 + i].astype(F32)
        for x in range(CX):
            wide[k, 2 + x] = flow[where, k, x].astype(F32)
    for k in range(3, 5):
        for i in range(2):
            wide[k, i] = left[SCALARS + t * 4 + (k - 3) * 2 + i].astype(F32)
            wide[k, 2 + CX + i] = right[SCALARS + t * 4 + (k - 3) * 2 + i].astype(F32)
        for x in range(CX):
            wide[k, 2 + x] = (rho if k == 3 else temp)[where, x].astype(F32)
    for k in range(5):
        slot = 4 * t + k if k < 4 else SLOT_T + t
        strips = own_halo[slot // 4].astype(F32)
        for x in range(CX):
            halos[k, x] = ops.unpack(strips, 4 * (slot % 4) + x)


def state_terms(ops, wide, halos, x, need_all=True):
    grad = [[None] * 5 for _ in range(3)]
    lap = [None] * 5
    center = [wide[k, x + 2] for k in range(5)]
    for k in range(5):
        if k == 3 and not need_all:
            continue
        edge = halos[k, x]
        up, down = ops.y_up(center[k]), ops.y_down(center[k])
        xs = [wide[k, x + 2 + step] for step in (1, -1, 2, -2)]
        zs = [ops.z_at(center[k], edge, step) for step in (1, -1, 2, -2)]
        if k < 3 or need_all:
            grad[0][k] = fourth(*xs)
            grad[1][k] = 0.5 * (up - down)
            grad[2][k] = fourth(*zs)
        if k != 3:
            lap[k] = xs[0] + xs[1] + zs[0] + zs[1] + up + down - 6.0 * center[k]
    size = size_of(strain_of(grad))
    return center, grad, lap, size, 1.0 / center[3]


def affine_update(ops, x, terms, psi_wide, psi_halos):
    center, grad, lap, size, inv_rho = terms
    psi = [psi_wide[k, x + 2] for k in range(5)]
    work_mom = psi[0] * lap[0] + psi[1] * lap[1] + psi[2] * lap[2]
    work_heat = psi[4] * lap[4]
    turbulent = work_mom + work_heat * (1.0 / PRANDTL_TURB)
    inv_rho_2 = inv_rho * inv_rho
    size_rho = size * inv_rho
    first, second = [], []
    for k in range(5):
        edge = psi_halos[k, x]
        up, down = ops.y_up(psi[k]), ops.y_down(psi[k])
        xs = [psi_wide[k, x + 2 + step] for step in (1, -1, 2, -2)]
        zs = [ops.z_at(psi[k], edge, step) for step in (1, -1, 2, -2)]
        rate = (
            center[0] * fourth(*xs) + center[1] * (0.5 * (up - down)) + center[2] * fourth(*zs)
        )
        if k == 3:
            rate = rate - (NU_MOL * work_mom + (NU_MOL / PRANDTL) * work_heat) * inv_rho_2
            eddy = -(size * turbulent) * inv_rho_2
        else:
            lap_psi = xs[0] + xs[1] + zs[0] + zs[1] + up + down - 6.0 * psi[k]
            if k < 3:
                for other in range(5):
                    rate = rate + psi[other] * grad[k][other]
                rate = rate + NU_MOL * (inv_rho * lap_psi)
                eddy = size_rho * lap_psi
            else:
                rate = rate + (NU_MOL / PRANDTL) * (inv_rho * lap_psi)
                eddy = (1.0 / PRANDTL_TURB) * (size_rho * lap_psi)
        first.append(psi[k] + TIME_STEP * rate)
        second.append(TIME_STEP * eddy)
    return first, second, size_rho * turbulent


def band_of(lane):
    return (lane * 43) >> 9


def message_kernel(
    flow_far, rho_far, temp_far, psi_far, up, down, flow, rho, temp, psi, sems
):
    copies = [
        pltpu.make_async_copy(source, target, sems.at[i])
        for i, (source, target) in enumerate(
            ((flow_far, flow), (psi_far, psi), (rho_far, rho), (temp_far, temp))
        )
    ]
    for copy in copies:
        copy.start()
    copies[0].wait()
    for t in range(2):
        for k in range(3):
            for i in range(3):
                up[t * 9 + k * 3 + i] = flow[t, k, 1 + i]
                down[t * 9 + k * 3 + i] = flow[t, k, i]
    copies[1].wait()
    for k in range(5):
        for i in range(2):
            upper, lower = split_halves(psi[k, 2 + i])
            up[PSI_HI + k * 2 + i] = upper
            up[PSI_LO + k * 2 + i] = lower
            upper, lower = split_halves(psi[k, i])
            down[PSI_HI + k * 2 + i] = upper
            down[PSI_LO + k * 2 + i] = lower
    copies[2].wait()
    copies[3].wait()
    for t in range(2):
        for i in range(2):
            up[SCALARS + t * 4 + i] = rho[t, 2 + i]
            down[SCALARS + t * 4 + i] = rho[t, i]
            up[SCALARS + t * 4 + 2 + i] = temp[t, 2 + i]
            down[SCALARS + t * 4 + 2 + i] = temp[t, i]


def pack_kernel(flow, rho, temp, psi, packed):
    ops = Ops()
    items = []
    for t in range(2):
        items += [[flow[t, k, x].astype(F32) for x in range(CX)] for k in range(3)]
        items += [[rho[t, x].astype(F32) for x in range(CX)]]
    items += [[temp[t, x].astype(F32) for x in range(CX)] for t in range(2)]
    halves = [[split_halves(psi[k, x]) for x in range(CX)] for k in range(5)]
    for half in range(2):
        items += [[halves[k][x][half].astype(F32) for x in range(CX)] for k in range(5)]
    for number in range(STRIP_BLOCKS):
        planes = {}
        for slot in range(4):
            for x in range(CX):
                planes[4 * slot + x] = items[4 * number + slot][x]
        packed[number] = pack_strips(ops, planes).astype(BF16)
    band = band_of(ops.lane)
    for t in range(2):
        for k in range(3):
            block = jnp.zeros((ROWS, LANES), F32)
            for x in range(CX):
                moved = turn(flow[t, k, x].astype(F32), BAND * (x + 3) + 3)
                block = jnp.where(band == x + 3, moved, block)
            packed[STRIP_BLOCKS + 3 * t + k] = block.astype(BF16)


def bands_kernel(packed, left, right, out):
    ops = Ops()
    for number in range(STRIP_BLOCKS):
        out[number] = packed[number]
    band = band_of(ops.lane)
    for t in range(2):
        for k in range(3):
            block = packed[STRIP_BLOCKS + 3 * t + k].astype(F32)
            for i in range(3):
                number = VELOCITY + t * 9 + k * 3 + i
                moved = turn(left[number].astype(F32), BAND * i + 3)
                block = jnp.where(band == i, moved, block)
                moved = turn(right[number].astype(F32), BAND * (7 + i) + 3)
                block = jnp.where(band == 7 + i, moved, block)
            out[STRIP_BLOCKS + 3 * t + k] = block.astype(BF16)


def products_of(hat):
    velocity = [hat(k) for k in range(3)]
    strain = [hat(9 + number) for number in range(6)]
    diagonal = strain[0] * strain[0] + strain[1] * strain[1] + strain[2] * strain[2]
    other = strain[3] * strain[3] + strain[4] * strain[4] + strain[5] * strain[5]
    size = 4.0 * jnp.sqrt((2.0 / 256.0) * diagonal + ((4.0 / 256.0) * other + EPSILON))
    cross = 0.0
    square = 0.0
    for number, (a, b) in enumerate(PAIRS):
        leonard = hat(3 + number) - (1.0 / 16.0) * velocity[a] * velocity[b]
        model = hat(15 + number) - size * strain[number]
        weighted = WEIGHTS[number] * model if WEIGHTS[number] != 1.0 else model
        cross = cross + leonard * weighted
        square = square + model * weighted
    return cross, square


def inner_kernel(flow, left, right, inner, high, wide, fields, hats):
    ops = Ops()
    valid = (ops.lane >= 3) & (ops.lane < LANES - 3)
    band = band_of(jnp.maximum(ops.lane - 2, 0))

    def step(t, carry):
        for k in range(3):
            for i in range(3):
                wide[k, i] = left[VELOCITY + t * 9 + k * 3 + i].astype(F32)
                wide[k, 7 + i] = right[VELOCITY + t * 9 + k * 3 + i].astype(F32)
            for x in range(CX):
                wide[k, 3 + x] = flow[t, k, x].astype(F32)
        for x in range(-1, CX + 1):
            grad = [[None] * 3 for _ in range(3)]
            for k in range(3):
                center = wide[k, x + 3]
                grad[0][k] = fourth(
                    wide[k, x + 4], wide[k, x + 2], wide[k, x + 5], wide[k, x + 1]
                )
                grad[1][k] = 0.5 * (ops.y_up(center) - ops.y_down(center))
                grad[2][k] = fourth(*(turn(center, -step) for step in (1, -1, 2, -2)))
            strain = strain_of(grad)
            size = size_of(strain)
            velocity = [wide[k, x + 3] for k in range(3)]
            for number, values in enumerate(filter_fields(velocity, strain, size)):
                fields[number, x + 1] = values
        for x in range(CX):
            for number in range(21):
                along_x = (
                    fields[number, x] + fields[number, x + 2] + 2.0 * fields[number, x + 1]
                )
                hats[number, x] = turn(along_x, 1) + turn(along_x, -1) + 2.0 * along_x
        for k in range(3):
            block = jnp.zeros((ROWS, LANES), F32)
            for q in range(CX + 6):
                block = jnp.where(band == q, turn(wide[k, q], BAND * q + 11), block)
            high[t, k] = block
        for x in range(CX):
            cross, square = products_of(lambda number: hats[number, x])
            inner[t, 0, x] = jnp.where(valid, cross, 0.0)
            inner[t, 1, x] = jnp.where(valid, square, 0.0)
        return carry

    lax.fori_loop(0, 2, step, 0)


def edge_kernel(
    flow, rho, temp, psi, left, right, own_pack, own_halo, inner, high,
    first, second, message,
    wide, halos, psi_wide, psi_halos, weight, work, bands, spread, sums,
):
    ops = Ops()
    band = band_of(ops.lane)
    place = ops.lane - BAND * band
    from_low = place < 3
    from_high = (place == 11) | (place < 2)
    low_side = place < 7
    at_edge = ((place >= 3) & (place <= 5)) | ((place >= 8) & (place <= 10))
    for t in range(2):
        for k in range(3):
            number = STRIP_BLOCKS + 3 * t + k
            far = own_halo[number].astype(F32)
            bands[t, 0, k] = jnp.where(from_low, far, own_pack[number].astype(F32))
            bands[t, 1, k] = jnp.where(from_high, turn(far, 8), high[t, k])
    for k in range(5):
        for i in range(2):
            psi_wide[k, i] = left[PSI_HI + k * 2 + i].astype(F32) + left[
                PSI_LO + k * 2 + i
            ].astype(F32)
            psi_wide[k, 2 + CX + i] = right[PSI_HI + k * 2 + i].astype(F32) + right[
                PSI_LO + k * 2 + i
            ].astype(F32)
        upper, lower = SLOT_PSI_HI + k, SLOT_PSI_LO + k
        upper_strips = own_halo[upper // 4].astype(F32)
        lower_strips = own_halo[lower // 4].astype(F32)
        for x in range(CX):
            psi_wide[k, 2 + x] = psi[k, x]
            psi_halos[k, x] = ops.unpack(upper_strips, 4 * (upper % 4) + x) + ops.unpack(
                lower_strips, 4 * (lower % 4) + x
            )
    for t in range(2):
        spread_state(
            ops, t, t, flow, rho, temp, left, right, own_halo, wide.at[t], halos.at[t]
        )
    for t in range(2):
        for side in range(2):
            velocity = [bands[t, side, k] for k in range(3)]
            grad = [[None] * 3 for _ in range(3)]
            for k in range(3):
                center = velocity[k]
                grad[0][k] = fourth(*(turn(center, -BAND * step) for step in (1, -1, 2, -2)))
                grad[1][k] = 0.5 * (ops.y_up(center) - ops.y_down(center))
                grad[2][k] = fourth(*(turn(center, -step) for step in (1, -1, 2, -2)))
            strain = strain_of(grad)
            for number, values in enumerate(filter_fields(velocity, strain, size_of(strain))):
                if side == 0:
                    spread[t, number] = values
                else:
                    spread[t, number] = jnp.where(low_side, spread[t, number], values)
    for t in range(2):
        for number in range(21):
            both = spread[t, number]
            spread[t, number] = turn(both, BAND) + turn(both, -BAND) + 2.0 * both
    for t in range(2):
        for number in range(21):
            both = spread[t, number]
            spread[t, number] = turn(both, 1) + turn(both, -1) + 2.0 * both
    for x in range(CX):
        terms = state_terms(ops, wide.at[0], halos.at[0], x)
        new, slope, sensitivity = affine_update(ops, x, terms, psi_wide, psi_halos)
        for k in range(5):
            first[k, x] = new[k]
            second[k, x] = slope[k]
        work[0, x] = sensitivity
    for x in range(CX):
        _, _, lap, size, inv_rho = state_terms(ops, wide.at[1], halos.at[1], x, need_all=False)
        size_rho = size * inv_rho
        for part, source in enumerate((first, second)):
            total = lap[0] * source[0, x] + lap[1] * source[1, x] + lap[2] * source[2, x]
            work[1 + part, x] = size_rho * (
                total + (1.0 / PRANDTL_TURB) * (lap[4] * source[4, x])
            )
    for t in range(2):
        for part, values in enumerate(products_of(lambda number: spread[t, number])):
            values = jnp.where(at_edge, values, 0.0)
            for x in range(CX):
                sums[t, part, x] = inner[t, part, x] + jnp.where(band == x + 3, values, 0.0)
    columns = jnp.zeros((ROWS, LANES), F32)
    for t in range(2):
        for part in range(2):
            for x in range(CX):
                total = (1.0 / 256.0) * jnp.sum(sums[t, part, x], axis=1, keepdims=True)
                columns = jnp.where(ops.lane == 8 * t + 4 * part + x, total, columns)
    for part in range(3):
        for x in range(CX):
            total = jnp.sum(work[part, x], axis=1, keepdims=True)
            columns = jnp.where(ops.lane == 16 + 4 * part + x, total, columns)
    for number in range(3):
        planes = {}
        for slot in range(4 * number, min(4 * number + 4, 10)):
            source = first if slot < 5 else second
            for x in range(CX):
                planes[4 * (slot % 4) + x] = source[slot % 5, x]
        message[number] = pack_strips(ops, planes)
    message[3] = columns


def middle_kernel(
    add_own, first, second, own, other, psi, up, down, psi_halos, coef_planes, grads, coef_first
):
    ops = Ops()
    total = own[3] + other[3] if add_own else other[3]
    coef = total / (turn(total, -4) + EPSILON)
    after = total + turn(coef, 20) * turn(total, -4)
    grads[...] = jnp.where(ops.lane < 20, total, after)
    for x in range(CX):
        coef_first[x] = jnp.broadcast_to(coef[:, x : x + 1], (ROWS, LANES))
        coef_planes[x] = jnp.broadcast_to(coef[:, 8 + x : 9 + x], (ROWS, LANES))
    for x in range(CX):
        for k in range(5):
            values = first[k, x] + coef_first[x] * second[k, x]
            psi[k, x] = values
            if x >= 2:
                up[k, x - 2] = values
            else:
                down[k, x] = values
    for k in range(5):
        for x in range(CX):
            base = ops.unpack(other[k // 4], 4 * (k % 4) + x)
            slope = ops.unpack(other[(5 + k) // 4], 4 * ((5 + k) % 4) + x)
            psi_halos[k, x] = base + coef_first[x] * slope


def base_kernel(
    flow, rho, temp, left, right, own_halo, psi, psi_halos, coef_planes,
    base, drift, spread,
    wide, halos, psi_wide,
):
    ops = Ops()
    zero = jnp.zeros((ROWS, LANES), F32)
    for k in range(5):
        for i in range(2):
            psi_wide[k, i] = zero
            psi_wide[k, 2 + CX + i] = zero
        for x in range(CX):
            psi_wide[k, 2 + x] = psi[k, x]
    spread_state(ops, 1, 1, flow, rho, temp, left, right, own_halo, wide, halos)
    for x in range(CX):
        terms = state_terms(ops, wide, halos, x)
        new, slope, _ = affine_update(ops, x, terms, psi_wide, psi_halos)
        for k in range(5):
            base[k, x] = new[k] + coef_planes[x] * slope[k]
        center, _, _, size, inv_rho = terms
        drift[x] = TIME_STEP * center[0]
        if x in (0, CX - 1):
            eddy = coef_planes[x] * size
            scaled = TIME_STEP * inv_rho
            spread[x // (CX - 1), 0] = scaled * (NU_MOL + eddy)
            spread[x // (CX - 1), 1] = scaled * (
                NU_MOL / PRANDTL + (1.0 / PRANDTL_TURB) * eddy
            )


def last_kernel(base, drift, spread, left_psi, right_psi, out):
    for k in range(5):
        far, near = left_psi[k, 0], left_psi[k, 1]
        after, beyond = right_psi[k, 0], right_psi[k, 1]
        low = drift[0] * ((1.0 / 12.0) * far - (2.0 / 3.0) * near)
        high = drift[CX - 1] * ((2.0 / 3.0) * after - (1.0 / 12.0) * beyond)
        if k != 3:
            kind = 1 if k == 4 else 0
            low = low + spread[0, kind] * near
            high = high + spread[1, kind] * after
        out[k, 0] = base[k, 0] + low
        out[k, 1] = base[k, 1] + drift[1] * ((1.0 / 12.0) * near)
        out[k, CX - 2] = base[k, CX - 2] - drift[CX - 2] * ((1.0 / 12.0) * after)
        out[k, CX - 1] = base[k, CX - 1] + high


def ring(axis):
    count = lax.axis_size(axis)
    forward = [(i, (i + 1) % count) for i in range(count)]
    return forward, [(target, source) for source, target in forward]


def span_edges(message, strips):
    forward, backward = ring("gz")
    before = lax.ppermute(message, "gz", forward)
    if lax.axis_size("gz") == 2:
        return before
    after = lax.ppermute(message, "gz", backward)
    lane = lax.broadcasted_iota(jnp.int32, message.shape, 2)
    number = lax.broadcasted_iota(jnp.int32, message.shape, 0)
    low = jnp.where(number < strips, lane % STRIP < 4, lane % BAND < 3)
    return jnp.where(low, before, after)


def shape_of(dims, kind=F32):
    return jax.ShapeDtypeStruct(dims + (ROWS, LANES), kind)


def whole(count):
    return [pl.BlockSpec(memory_space=pltpu.VMEM)] * count


def scratch(*dims):
    return [pltpu.VMEM(d + (ROWS, LANES), F32) for d in dims]


def call(kernel, name, inputs, outputs, operations, buffers=(), in_specs=None):
    size = sum(math.prod(a.shape) * a.dtype.itemsize for a in list(inputs) + list(outputs))
    return pl.pallas_call(
        kernel,
        in_specs=in_specs or whole(len(inputs)),
        out_specs=whole(len(outputs)),
        out_shape=list(outputs),
        scratch_shapes=list(buffers),
        compiler_params=pltpu.CompilerParams(vmem_limit_bytes=24 * 2**20),
        cost_estimate=pl.CostEstimate(
            flops=operations, bytes_accessed=size, transcendentals=0
        ),
        name=name,
    )(*inputs)


def local(flow, rho, temp, psi):
    forward, backward = ring("gx")
    up, down, flow, rho, temp, psi = call(
        message_kernel,
        "message",
        (flow, rho, temp, psi),
        [shape_of((MESSAGE,), BF16)] * 2
        + [
            shape_of((2, 3, CX), BF16),
            shape_of((2, CX), BF16),
            shape_of((2, CX), BF16),
            shape_of((5, CX)),
        ],
        1_000_000,
        [pltpu.SemaphoreType.DMA((4,))],
        [pl.BlockSpec(memory_space=pltpu.MemorySpace.HBM)] * 4,
    )
    left = lax.ppermute(up, "gx", forward)
    right = lax.ppermute(down, "gx", backward)
    (packed,) = call(
        pack_kernel,
        "pack",
        (flow, rho, temp, psi),
        [shape_of((STRIP_BLOCKS + 6,), BF16)],
        2_000_000,
    )
    (packed,) = call(
        bands_kernel,
        "bands",
        (packed, left, right),
        [shape_of((STRIP_BLOCKS + 6,), BF16)],
        1_000_000,
    )
    own_halo = span_edges(packed, STRIP_BLOCKS)
    inner, high = call(
        inner_kernel,
        "inner",
        (flow, left, right),
        [shape_of((2, 2, CX)), shape_of((2, 3))],
        30_000_000,
        scratch((3, CX + 6), (21, CX + 2), (21, CX)),
    )
    first, second, message = call(
        edge_kernel,
        "edge",
        (flow, rho, temp, psi, left, right, packed, own_halo, inner, high),
        [shape_of((5, CX)), shape_of((5, CX)), shape_of((4,))],
        20_000_000,
        scratch(
            (2, 5, CX + 4), (2, 5, CX), (5, CX + 4), (5, CX), (4, CX), (3, CX),
            (2, 2, 3), (2, 21), (2, 2, CX),
        ),
    )
    other = span_edges(message, 4)
    add_own = lax.axis_size("gz") == 2
    if not add_own:
        total = lax.psum(message[3], "gz")
        other = jnp.concatenate([other[:3], total[None]], axis=0)
    psi, up, down, psi_halos, coef_planes, grads = call(
        functools.partial(middle_kernel, add_own),
        "middle",
        (first, second, message, other),
        [
            shape_of((5, CX)), shape_of((5, 2)), shape_of((5, 2)),
            shape_of((5, CX)), shape_of((CX,)), shape_of(()),
        ],
        1_000_000,
        scratch((CX,)),
    )
    left_psi = lax.ppermute(up, "gx", forward)
    right_psi = lax.ppermute(down, "gx", backward)
    base, drift, spread = call(
        base_kernel,
        "base",
        (flow, rho, temp, left, right, own_halo, psi, psi_halos, coef_planes),
        [shape_of((5, CX)), shape_of((CX,)), shape_of((2, 2))],
        15_000_000,
        scratch((5, CX + 4), (5, CX), (5, CX + 4)),
    )
    (out,) = call(
        last_kernel,
        "last",
        (base, drift, spread, left_psi, right_psi),
        [shape_of((5, CX))],
        1_000_000,
    )
    span_cells = LANES * lax.axis_size("gz")
    coef_grad = grads[:, 16:24].T.reshape(2, CX, ROWS) * (1.0 / span_cells)
    return out, coef_grad


def solution(mesh):
    return jax.shard_map(
        local,
        mesh=mesh,
        in_specs=(
            P(None, None, "gx", None, "gz"),
            P(None, "gx", None, "gz"),
            P(None, "gx", None, "gz"),
            P(None, "gx", None, "gz"),
        ),
        out_specs=(P(None, "gx", None, "gz"), P(None, "gx", None)),
        check_vma=False,
    )
```

time: 44.2 us -> 37.7 us (0.85)
  the two profiles are of different devices: /device:TPU:0 before, /device:TPU:1 now
where the time goes in v3:
time: 37.7 us; the launch traced here: 37.5 us
  waiting for transfers between devices  16.6 us (44%)
  Pallas kernels  8.39 us (22%)
  starting transfers between devices  7.46 us (20%)
  local copies, waits for them, and re-layouts  4.23 us (11%)
  between operations  0.7 us (2%)
    pallas_call x8, Pallas kernels, call(): pl.pallas_call(kernel, in_specs=in_specs or whole(len(inputs)), out_specs...  8.39 us
    ppermute x1, waiting for transfers between devices, local(): left = lax.ppermute(up, 'gx', forward)  8.29 us
    unnamed x8, local copies, waits for them, and re-layouts  3.57 us
    ppermute x1, starting transfers between devices, local(): left = lax.ppermute(up, 'gx', forward)  2.65 us
    ppermute x2, starting transfers between devices, span_edges(): before = lax.ppermute(message, 'gz', forward)  2.53 us
    ppermute x1, waiting for transfers between devices, local(): right = lax.ppermute(down, 'gx', backward)  2.48 us
    ppermute x1, starting transfers between devices, local(): left_psi = lax.ppermute(up, 'gx', forward)  2.27 us
    ppermute x1, waiting for transfers between devices, local(): right_psi = lax.ppermute(down, 'gx', backward)  1.98 us
  transfers between devices with their start and end apart: 6, of which 5 were waited for; matrix products, arithmetic and copies ran while one was open for 2% of the time, Pallas kernels for 9%

profile of v3, /device:TPU:1, one launch (start us, length us, event | category | flops | bytes accessed | tf_op | source)
XLA Modules:
  0.0 37.5 jit_solution(6668786261788005640)
XLA Ops:
  0.6 1.0 %copy-done = f32[5,4,32,128]{3,2,1,0:T(8,128)S(1)} copy-done((f32[5,4,32,128]{3,2,1,0:T(8,128)S(1)}, f32[5,4,32,128]{3,2,1,0:T(8,128)}, u32[]{:S(2)}) %copy-start) | copy-done | bytes 327704
  1.6 0.9 %copy-done.1 = bf16[2,3,4,32,128]{4,3,2,1,0:T(8,128)(2,1)S(1)} copy-done((bf16[2,3,4,32,128]{4,3,2,1,0:T(8,128)(2,1)S(1)}, bf16[2,3,4,32,128]{4,3,2,1,0:T(8,128)(2,1)}, u32[]{:S(2)}) %copy-start.1) | copy-done | bytes 196632
  2.5 0.8 %copy-done.2 = bf16[2,4,32,128]{3,2,1,0:T(8,128)(2,1)S(1)} copy-done((bf16[2,4,32,128]{3,2,1,0:T(8,128)(2,1)S(1)}, bf16[2,4,32,128]{3,2,1,0:T(8,128)(2,1)}, u32[]{:S(2)}) %copy-start.2) | copy-done | bytes 65560
  3.4 0.8 %copy-done.3 = bf16[2,4,32,128]{3,2,1,0:T(8,128)(2,1)S(1)} copy-done((bf16[2,4,32,128]{3,2,1,0:T(8,128)(2,1)S(1)}, bf16[2,4,32,128]{3,2,1,0:T(8,128)(2,1)}, u32[]{:S(2)}) %copy-start.3) | copy-done | bytes 65560
  4.2 0.6 %message.1 = (bf16[46,32,128]{2,1,0:T(8,128)(2,1)S(1)}, bf16[46,32,128]{2,1,0:T(8,128)(2,1)S(1)}, bf16[2,3,4,32,128]{4,3,2,1,0:T(8,128)(2,1)S(1)}, bf16[2,4,32,1...) custom-call(bf16[2,3,4,32,128]{4,3,2,1,0:T(8,128)(2,1)S(1)} %copy-done.1, ...), custom_call_target="tpu_custom_call" | custom-call | flops 1000000 | bytes 2064384 | tf_op jit(solution)/shard_map/message/pallas_call | solution.py:539
  4.8 2.7 %collective-permute-start = (bf16[46,32,128]{2,1,0:T(8,128)(2,1)S(1)}, bf16[46,32,128]{2,1,0:T(8,128)(2,1)S(1)}, u32[]{:S(2)}, u32[]{:S(2)}) collective-permute-start(bf16[46,32,128]{2,1,0:T(8,128)(2,1)S(1)} %get-tuple-element.25), channel_id=1, source_target_pairs={{0,2},{2,4},{4,6},{6,8},{8,10},{10,12},{12,14},{14,16},{16,18},{18... | collective-permute-start | bytes 1130504 | tf_op jit(solution)/shard_map/ppermute | solution.py:570
  7.5 0.0 collective-permute-start.1
  7.5 0.3 pack.1.packed
  7.8 8.3 %collective-permute-done.left = bf16[46,32,128]{2,1,0:T(8,128)(2,1)S(1)} collective-permute-done((bf16[46,32,128]{2,1,0:T(8,128)(2,1)S(1)}, bf16[46,32,128]{2,1,0:T(8,128)(2,1)S(1)}, u32[]{:S(2)}, u32[]{:S(2)}) %collective-permute-start) | collective-permute-done | bytes 376864 | tf_op jit(solution)/shard_map/ppermute | solution.py:570
  16.1 2.5 %collective-permute-done.1.right = bf16[46,32,128]{2,1,0:T(8,128)(2,1)S(1)} collective-permute-done((bf16[46,32,128]{2,1,0:T(8,128)(2,1)S(1)}, bf16[46,32,128]{2,1,0:T(8,128)(2,1)S(1)}, u32[]{:S(2)}, u32[]{:S(2)}) %collective-permute-start.1) | collective-permute-done | bytes 376864 | tf_op jit(solution)/shard_map/ppermute | solution.py:571
  18.5 0.1 bands.1.own_pack
  18.7 1.3 %collective-permute-start.2 = (bf16[11,32,128]{2,1,0:T(8,128)(2,1)S(1)}, bf16[11,32,128]{2,1,0:T(8,128)(2,1)S(1)}, u32[]{:S(2)}, u32[]{:S(2)}) collective-permute-start(bf16[11,32,128]{2,1,0:T(8,128)(2,1)S(1)} %bands.1.own_pack), channel_id=1, source_target_pairs={{0,1},{1,0},{2,3},{3,2},{4,5},{5,4},{6,7},{7,6},{8,9},{9,8},{10,11... | collective-permute-start | bytes 270344 | tf_op jit(solution)/shard_map/ppermute | solution.py:515
  20.0 2.2 %inner.1 = (f32[2,2,4,32,128]{4,3,2,1,0:T(8,128)S(1)}, f32[2,3,32,128]{3,2,1,0:T(8,128)S(1)}) custom-call(bf16[2,3,4,32,128]{4,3,2,1,0:T(8,128)(2,1)S(1)} %get-tuple-element.22.flow, bf16[46,32,128]{2,1,0:T(8,128)(2,1)S(1)} %collective-permute-done.left, bf16[46,32,128]{2,1,0:T(8,128)(2,1)S(1)} %collective-permute-done.1.right), custom_call_target="tpu_custom_call" | custom-call | flops 30000000 | bytes 1310720 | tf_op jit(solution)/shard_map/inner/pallas_call | solution.py:539
  22.2 2.9 %edge.1 = (f32[5,4,32,128]{3,2,1,0:T(8,128)S(1)}, f32[5,4,32,128]{3,2,1,0:T(8,128)S(1)}, f32[4,32,128]{2,1,0:T(8,128)S(1)}) custom-call(bf16[2,3,4,32,128]{4,3,2,1,0:T(8,128)(2,1)S(1)} %get-tuple-element.22.flow, bf16[2,4,32,128]{3,2,1,0:T(8,128)(2,1)S(1)} %get-tuple-element.23.rho, bf16[2,4,32,128]{3,2,1,0:T(8,128)(2,1)S(1)} %get-tuple-element.24.temp, ...), custom_call_target="tpu_custom_call" | custom-call | flops 20000000 | bytes 2670592 | tf_op jit(solution)/shard_map/edge/pallas_call | solution.py:539
  25.1 1.2 %collective-permute-start.3 = (f32[4,32,128]{2,1,0:T(8,128)S(1)}, f32[4,32,128]{2,1,0:T(8,128)S(1)}, u32[]{:S(2)}, u32[]{:S(2)}) collective-permute-start(f32[4,32,128]{2,1,0:T(8,128)S(1)} %get-tuple-element.32.own), channel_id=1, source_target_pairs={{0,1},{1,0},{2,3},{3,2},{4,5},{5,4},{6,7},{7,6},{8,9},{9,8},{10,11... | collective-permute-start | bytes 196616 | tf_op jit(solution)/shard_map/ppermute | solution.py:515
  26.4 2.0 %collective-permute-done.3.other = f32[4,32,128]{2,1,0:T(8,128)S(1)} collective-permute-done((f32[4,32,128]{2,1,0:T(8,128)S(1)}, f32[4,32,128]{2,1,0:T(8,128)S(1)}, u32[]{:S(2)}, u32[]{:S(2)}) %collective-permute-start.3) | collective-permute-done | bytes 65568 | tf_op jit(solution)/shard_map/ppermute | solution.py:515
  28.3 0.4 middle.1
  28.7 2.3 %collective-permute-start.4 = (f32[5,2,32,128]{3,2,1,0:T(8,128)S(1)}, f32[5,2,32,128]{3,2,1,0:T(8,128)S(1)}, u32[]{:S(2)}, u32[]{:S(2)}) collective-permute-start(f32[5,2,32,128]{3,2,1,0:T(8,128)S(1)} %get-tuple-element.39), channel_id=1, source_target_pairs={{0,2},{2,4},{4,6},{6,8},{8,10},{10,12},{12,14},{14,16},{16,18},{18... | collective-permute-start | bytes 491528 | tf_op jit(solution)/shard_map/ppermute | solution.py:622
  31.0 0.1 multiply_bitcast_fusion
  31.0 0.7 %copy.7 = f32[8,32]{1,0:T(8,128)} copy(f32[8,32]{0,1:T(8,128)S(1)} %multiply_bitcast_fusion) | data formatting | bytes 2048 | tf_op jit(solution)/shard_map/mul | solution.py:640
  31.7 1.1 %base.1 = (f32[5,4,32,128]{3,2,1,0:T(8,128)S(1)}, f32[4,32,128]{2,1,0:T(8,128)S(1)}, f32[2,2,32,128]{3,2,1,0:T(8,128)S(1)}) custom-call(bf16[2,3,4,32,128]{4,3,2,1,0:T(8,128)(2,1)S(1)} %get-tuple-element.22.flow, bf16[2,4,32,128]{3,2,1,0:T(8,128)(2,1)S(1)} %get-tuple-element.23.rho, bf16[2,4,32,128]{3,2,1,0:T(8,128)(2,1)S(1)} %get-tuple-element.24.temp, ...), custom_call_target="tpu_custom_call" | custom-call | flops 15000000 | bytes 2351104 | tf_op jit(solution)/shard_map/base/pallas_call | solution.py:539
  32.8 1.9 %collective-permute-done.4.left_psi = f32[5,2,32,128]{3,2,1,0:T(8,128)S(1)} collective-permute-done((f32[5,2,32,128]{3,2,1,0:T(8,128)S(1)}, f32[5,2,32,128]{3,2,1,0:T(8,128)S(1)}, u32[]{:S(2)}, u32[]{:S(2)}) %collective-permute-start.4) | collective-permute-done | bytes 163872 | tf_op jit(solution)/shard_map/ppermute | solution.py:622
  34.7 2.0 %collective-permute-done.5.right_psi = f32[5,2,32,128]{3,2,1,0:T(8,128)S(1)} collective-permute-done((f32[5,2,32,128]{3,2,1,0:T(8,128)S(1)}, f32[5,2,32,128]{3,2,1,0:T(8,128)S(1)}, u32[]{:S(2)}, u32[]{:S(2)}) %collective-permute-start.5) | collective-permute-done | bytes 163872 | tf_op jit(solution)/shard_map/ppermute | solution.py:623
  36.7 0.8 %last.1 = f32[5,4,32,128]{3,2,1,0:T(8,128)} custom-call(f32[5,4,32,128]{3,2,1,0:T(8,128)S(1)} %get-tuple-element.36.base, f32[4,32,128]{2,1,0:T(8,128)S(1)} %get-tuple-element.37.drift, f32[2,2,32,128]{3,2,1,0:T(8,128)S(1)} %get-tuple-element.38.spread, f32[5,2,32,128]{3,2,1,0:T(8,128)S(1)} %collective-permute-done.4.left_psi, ...), custom_call_target="tpu_custom_call" | custom-call | flops 1000000 | bytes 1114112 | tf_op jit(solution)/shard_map/last/pallas_call | solution.py:539
  (6 shorter events, 0.0 us)
Async XLA Ops:
  0.6 1.0 %copy-start = (f32[5,4,32,128]{3,2,1,0:T(8,128)S(1)}, f32[5,4,32,128]{3,2,1,0:T(8,128)}, u32[]{:S(2)}) copy-start(f32[5,4,32,128]{3,2,1,0:T(8,128)} %psi_far.1) | copy-start | bytes 983044
  1.6 0.9 %copy-start.1 = (bf16[2,3,4,32,128]{4,3,2,1,0:T(8,128)(2,1)S(1)}, bf16[2,3,4,32,128]{4,3,2,1,0:T(8,128)(2,1)}, u32[]{:S(2)}) copy-start(bf16[2,3,4,32,128]{4,3,2,1,0:T(8,128)(2,1)} %flow_far.1) | copy-start | bytes 589828
  2.5 0.8 %copy-start.2 = (bf16[2,4,32,128]{3,2,1,0:T(8,128)(2,1)S(1)}, bf16[2,4,32,128]{3,2,1,0:T(8,128)(2,1)}, u32[]{:S(2)}) copy-start(bf16[2,4,32,128]{3,2,1,0:T(8,128)(2,1)} %rho_far.1) | copy-start | bytes 196612
  3.4 0.8 %copy-start.3 = (bf16[2,4,32,128]{3,2,1,0:T(8,128)(2,1)S(1)}, bf16[2,4,32,128]{3,2,1,0:T(8,128)(2,1)}, u32[]{:S(2)}) copy-start(bf16[2,4,32,128]{3,2,1,0:T(8,128)(2,1)} %temp_far.1) | copy-start | bytes 196612
  4.8 11.2 %collective-permute-start = (bf16[46,32,128]{2,1,0:T(8,128)(2,1)S(1)}, bf16[46,32,128]{2,1,0:T(8,128)(2,1)S(1)}, u32[]{:S(2)}, u32[]{:S(2)}) collective-permute-start(bf16[46,32,128]{2,1,0:T(8,128)(2,1)S(1)} %get-tuple-element.25), channel_id=1, source_target_pairs={{0,2},{2,4},{4,6},{6,8},{8,10},{10,12},{12,14},{14,16},{16,18},{18... | collective-permute-start | bytes 1130504 | tf_op jit(solution)/shard_map/ppermute | solution.py:570
  7.5 11.1 %collective-permute-start.1 = (bf16[46,32,128]{2,1,0:T(8,128)(2,1)S(1)}, bf16[46,32,128]{2,1,0:T(8,128)(2,1)S(1)}, u32[]{:S(2)}, u32[]{:S(2)}) collective-permute-start(bf16[46,32,128]{2,1,0:T(8,128)(2,1)S(1)} %get-tuple-element.26), channel_id=1, source_target_pairs={{2,0},{4,2},{6,4},{8,6},{10,8},{12,10},{14,12},{16,14},{18,16},{20... | collective-permute-start | bytes 1130504 | tf_op jit(solution)/shard_map/ppermute | solution.py:571
  18.7 3.5 %collective-permute-start.2 = (bf16[11,32,128]{2,1,0:T(8,128)(2,1)S(1)}, bf16[11,32,128]{2,1,0:T(8,128)(2,1)S(1)}, u32[]{:S(2)}, u32[]{:S(2)}) collective-permute-start(bf16[11,32,128]{2,1,0:T(8,128)(2,1)S(1)} %bands.1.own_pack), channel_id=1, source_target_pairs={{0,1},{1,0},{2,3},{3,2},{4,5},{5,4},{6,7},{7,6},{8,9},{9,8},{10,11... | collective-permute-start | bytes 270344 | tf_op jit(solution)/shard_map/ppermute | solution.py:515
  25.1 3.2 %collective-permute-start.3 = (f32[4,32,128]{2,1,0:T(8,128)S(1)}, f32[4,32,128]{2,1,0:T(8,128)S(1)}, u32[]{:S(2)}, u32[]{:S(2)}) collective-permute-start(f32[4,32,128]{2,1,0:T(8,128)S(1)} %get-tuple-element.32.own), channel_id=1, source_target_pairs={{0,1},{1,0},{2,3},{3,2},{4,5},{5,4},{6,7},{7,6},{8,9},{9,8},{10,11... | collective-permute-start | bytes 196616 | tf_op jit(solution)/shard_map/ppermute | solution.py:515
  28.7 6.0 %collective-permute-start.4 = (f32[5,2,32,128]{3,2,1,0:T(8,128)S(1)}, f32[5,2,32,128]{3,2,1,0:T(8,128)S(1)}, u32[]{:S(2)}, u32[]{:S(2)}) collective-permute-start(f32[5,2,32,128]{3,2,1,0:T(8,128)S(1)} %get-tuple-element.39), channel_id=1, source_target_pairs={{0,2},{2,4},{4,6},{6,8},{8,10},{10,12},{12,14},{14,16},{16,18},{18... | collective-permute-start | bytes 491528 | tf_op jit(solution)/shard_map/ppermute | solution.py:622
  31.0 5.7 %collective-permute-start.5 = (f32[5,2,32,128]{3,2,1,0:T(8,128)S(1)}, f32[5,2,32,128]{3,2,1,0:T(8,128)S(1)}, u32[]{:S(2)}, u32[]{:S(2)}) collective-permute-start(f32[5,2,32,128]{3,2,1,0:T(8,128)S(1)} %get-tuple-element.40), channel_id=1, source_target_pairs={{2,0},{4,2},{6,4},{8,6},{10,8},{12,10},{14,12},{16,14},{18,16},{20... | collective-permute-start | bytes 491528 | tf_op jit(solution)/shard_map/ppermute | solution.py:623

commit v4 on v3

--- a/solution.py
+++ b/solution.py
@@ -23,15 +23,13 @@
 F32 = jnp.float32
 BF16 = jnp.bfloat16
 SLOT_T = 8
-SLOT_PSI_HI = 10
-SLOT_PSI_LO = 15
+SLOT_PSI = 10
 BAND = 12
-STRIP_BLOCKS = 5
+STRIP_BLOCKS = 4
 VELOCITY = 0
 SCALARS = 18
-PSI_HI = 26
-PSI_LO = 36
-MESSAGE = 46
+PSI = 26
+MESSAGE = 36
 
 
 def lane_ids():
@@ -103,25 +101,7 @@
     return block
 
 
-def split_halves(values):
-    upper = values.astype(BF16)
-    lower = (values - upper.astype(F32)).astype(BF16)
-    return upper, lower
-
-
-def spread_state(ops, t, where, flow, rho, temp, left, right, own_halo, wide, halos):
-    for k in range(3):
-        for i in range(2):
-            wide[k, i] = left[t * 9 + k * 3 + 1 + i].astype(F32)
-            wide[k, 2 + CX + i] = right[t * 9 + k * 3 + i].astype(F32)
-        for x in range(CX):
-            wide[k, 2 + x] = flow[where, k, x].astype(F32)
-    for k in range(3, 5):
-        for i in range(2):
-            wide[k, i] = left[SCALARS + t * 4 + (k - 3) * 2 + i].astype(F32)
-            wide[k, 2 + CX + i] = right[SCALARS + t * 4 + (k - 3) * 2 + i].astype(F32)
-        for x in range(CX):
-            wide[k, 2 + x] = (rho if k == 3 else temp)[where, x].astype(F32)
+def place_halos(ops, t, own_halo, halos):
     for k in range(5):
         slot = 4 * t + k if k < 4 else SLOT_T + t
         strips = own_halo[slot // 4].astype(F32)
@@ -132,13 +112,13 @@
 def state_terms(ops, wide, halos, x, need_all=True):
     grad = [[None] * 5 for _ in range(3)]
     lap = [None] * 5
-    center = [wide[k, x + 2] for k in range(5)]
+    center = [wide[k, x + 3] for k in range(5)]
     for k in range(5):
         if k == 3 and not need_all:
             continue
         edge = halos[k, x]
         up, down = ops.y_up(center[k]), ops.y_down(center[k])
-        xs = [wide[k, x + 2 + step] for step in (1, -1, 2, -2)]
+        xs = [wide[k, x + 3 + step] for step in (1, -1, 2, -2)]
         zs = [ops.z_at(center[k], edge, step) for step in (1, -1, 2, -2)]
         if k < 3 or need_all:
             grad[0][k] = fourth(*xs)
@@ -189,8 +169,12 @@
     return (lane * 43) >> 9
 
 
+def is_even():
+    return lax.rem(lax.axis_index("gx"), 2) == 0
+
+
 def message_kernel(
-    flow_far, rho_far, temp_far, psi_far, up, down, flow, rho, temp, psi, sems
+    flow_far, rho_far, temp_far, psi_far, near, far, flow, rho, temp, psi, sems
 ):
     copies = [
         pltpu.make_async_copy(source, target, sems.at[i])
@@ -200,29 +184,26 @@
     ]
     for copy in copies:
         copy.start()
+    even = is_even().astype(jnp.int32)
+    sides = ((near, even), (far, 1 - even))
     copies[0].wait()
-    for t in range(2):
-        for k in range(3):
-            for i in range(3):
-                up[t * 9 + k * 3 + i] = flow[t, k, 1 + i]
-                down[t * 9 + k * 3 + i] = flow[t, k, i]
+    for out, side in sides:
+        for t in range(2):
+            for k in range(3):
+                for i in range(3):
+                    out[t * 9 + k * 3 + i] = flow[t, k, side + i]
     copies[1].wait()
-    for k in range(5):
-        for i in range(2):
-            upper, lower = split_halves(psi[k, 2 + i])
-            up[PSI_HI + k * 2 + i] = upper
-            up[PSI_LO + k * 2 + i] = lower
-            upper, lower = split_halves(psi[k, i])
-            down[PSI_HI + k * 2 + i] = upper
-            down[PSI_LO + k * 2 + i] = lower
+    for out, side in sides:
+        for k in range(5):
+            for i in range(2):
+                out[PSI + k * 2 + i] = psi[k, 2 * side + i].astype(BF16)
     copies[2].wait()
     copies[3].wait()
-    for t in range(2):
-        for i in range(2):
-            up[SCALARS + t * 4 + i] = rho[t, 2 + i]
-            down[SCALARS + t * 4 + i] = rho[t, i]
-            up[SCALARS + t * 4 + 2 + i] = temp[t, 2 + i]
-            down[SCALARS + t * 4 + 2 + i] = temp[t, i]
+    for out, side in sides:
+        for t in range(2):
+            for i in range(2):
+                out[SCALARS + t * 4 + i] = rho[t, 2 * side + i]
+                out[SCALARS + t * 4 + 2 + i] = temp[t, 2 * side + i]
 
 
 def pack_kernel(flow, rho, temp, psi, packed):
@@ -232,14 +213,12 @@
         items += [[flow[t, k, x].astype(F32) for x in range(CX)] for k in range(3)]
         items += [[rho[t, x].astype(F32) for x in range(CX)]]
     items += [[temp[t, x].astype(F32) for x in range(CX)] for t in range(2)]
-    halves = [[split_halves(psi[k, x]) for x in range(CX)] for k in range(5)]
-    for half in range(2):
-        items += [[halves[k][x][half].astype(F32) for x in range(CX)] for k in range(5)]
+    items += [[psi[k, x] for x in range(CX)] for k in range(5)]
     for number in range(STRIP_BLOCKS):
         planes = {}
-        for slot in range(4):
+        for slot, item in enumerate(items[4 * number : 4 * number + 4]):
             for x in range(CX):
-                planes[4 * slot + x] = items[4 * number + slot][x]
+                planes[4 * slot + x] = item[x]
         packed[number] = pack_strips(ops, planes).astype(BF16)
     band = band_of(ops.lane)
     for t in range(2):
@@ -251,8 +230,9 @@
             packed[STRIP_BLOCKS + 3 * t + k] = block.astype(BF16)
 
 
-def bands_kernel(packed, left, right, out):
+def bands_kernel(packed, near, far, out):
     ops = Ops()
+    even = is_even()
     for number in range(STRIP_BLOCKS):
         out[number] = packed[number]
     band = band_of(ops.lane)
@@ -261,9 +241,10 @@
             block = packed[STRIP_BLOCKS + 3 * t + k].astype(F32)
             for i in range(3):
                 number = VELOCITY + t * 9 + k * 3 + i
-                moved = turn(left[number].astype(F32), BAND * i + 3)
+                one, two = near[number].astype(F32), far[number].astype(F32)
+                moved = turn(jnp.where(even, two, one), BAND * i + 3)
                 block = jnp.where(band == i, moved, block)
-                moved = turn(right[number].astype(F32), BAND * (7 + i) + 3)
+                moved = turn(jnp.where(even, one, two), BAND * (7 + i) + 3)
                 block = jnp.where(band == 7 + i, moved, block)
             out[STRIP_BLOCKS + 3 * t + k] = block.astype(BF16)
 
@@ -285,30 +266,49 @@
     return cross, square
 
 
-def inner_kernel(flow, left, right, inner, high, wide, fields, hats):
+def inner_kernel(
+    flow, rho, temp, psi, near, far, inner, high, wide, psi_wide, fields, hats
+):
     ops = Ops()
+    even = is_even()
     valid = (ops.lane >= 3) & (ops.lane < LANES - 3)
     band = band_of(jnp.maximum(ops.lane - 2, 0))
+
+    def sides(number):
+        one, two = near[number].astype(F32), far[number].astype(F32)
+        return jnp.where(even, two, one), jnp.where(even, one, two)
+
+    for k in range(5):
+        for i in range(2):
+            psi_wide[k, i], psi_wide[k, 2 + CX + i] = sides(PSI + k * 2 + i)
+        for x in range(CX):
+            psi_wide[k, 2 + x] = psi[k, x]
 
     def step(t, carry):
         for k in range(3):
             for i in range(3):
-                wide[k, i] = left[VELOCITY + t * 9 + k * 3 + i].astype(F32)
-                wide[k, 7 + i] = right[VELOCITY + t * 9 + k * 3 + i].astype(F32)
+                wide[t, k, i], wide[t, k, 7 + i] = sides(VELOCITY + t * 9 + k * 3 + i)
             for x in range(CX):
-                wide[k, 3 + x] = flow[t, k, x].astype(F32)
+                wide[t, k, 3 + x] = flow[t, k, x].astype(F32)
+        for k, source in ((3, rho), (4, temp)):
+            for i in range(2):
+                wide[t, k, 1 + i], wide[t, k, 7 + i] = sides(
+                    SCALARS + t * 4 + (k - 3) * 2 + i
+                )
+            for x in range(CX):
+                wide[t, k, 3 + x] = source[t, x].astype(F32)
         for x in range(-1, CX + 1):
             grad = [[None] * 3 for _ in range(3)]
             for k in range(3):
-                center = wide[k, x + 3]
+                center = wide[t, k, x + 3]
                 grad[0][k] = fourth(
-                    wide[k, x + 4], wide[k, x + 2], wide[k, x + 5], wide[k, x + 1]
+                    wide[t, k, x + 4], wide[t, k, x + 2], wide[t, k, x + 5], wide[t, k, x + 1]
                 )
                 grad[1][k] = 0.5 * (ops.y_up(center) - ops.y_down(center))
                 grad[2][k] = fourth(*(turn(center, -step) for step in (1, -1, 2, -2)))
             strain = strain_of(grad)
             size = size_of(strain)
-            velocity = [wide[k, x + 3] for k in range(3)]
+            velocity = [wide[t, k, x + 3] for k in range(3)]
             for number, values in enumerate(filter_fields(velocity, strain, size)):
                 fields[number, x + 1] = values
         for x in range(CX):
@@ -320,7 +320,7 @@
         for k in range(3):
             block = jnp.zeros((ROWS, LANES), F32)
             for q in range(CX + 6):
-                block = jnp.where(band == q, turn(wide[k, q], BAND * q + 11), block)
+                block = jnp.where(band == q, turn(wide[t, k, q], BAND * q + 11), block)
             high[t, k] = block
         for x in range(CX):
             cross, square = products_of(lambda number: hats[number, x])
@@ -332,9 +332,9 @@
 
 
 def edge_kernel(
-    flow, rho, temp, psi, left, right, own_pack, own_halo, inner, high,
+    wide, psi_wide, own_pack, own_halo, inner, high,
     first, second, message,
-    wide, halos, psi_wide, psi_halos, weight, work, bands, spread, sums,
+    halos, psi_halos, work, bands, spread, sums,
 ):
     ops = Ops()
     band = band_of(ops.lane)
@@ -350,25 +350,11 @@
             bands[t, 0, k] = jnp.where(from_low, far, own_pack[number].astype(F32))
             bands[t, 1, k] = jnp.where(from_high, turn(far, 8), high[t, k])
     for k in range(5):
-        for i in range(2):
-            psi_wide[k, i] = left[PSI_HI + k * 2 + i].astype(F32) + left[
-                PSI_LO + k * 2 + i
-            ].astype(F32)
-            psi_wide[k, 2 + CX + i] = right[PSI_HI + k * 2 + i].astype(F32) + right[
-                PSI_LO + k * 2 + i
-            ].astype(F32)
-        upper, lower = SLOT_PSI_HI + k, SLOT_PSI_LO + k
-        upper_strips = own_halo[upper // 4].astype(F32)
-        lower_strips = own_halo[lower // 4].astype(F32)
-        for x in range(CX):
-            psi_wide[k, 2 + x] = psi[k, x]
-            psi_halos[k, x] = ops.unpack(upper_strips, 4 * (upper % 4) + x) + ops.unpack(
-                lower_strips, 4 * (lower % 4) + x
-            )
-    for t in range(2):
-        spread_state(
-            ops, t, t, flow, rho, temp, left, right, own_halo, wide.at[t], halos.at[t]
-        )
+        strips = own_halo[(SLOT_PSI + k) // 4].astype(F32)
+        for x in range(CX):
+            psi_halos[k, x] = ops.unpack(strips, 4 * ((SLOT_PSI + k) % 4) + x)
+    for t in range(2):
+        place_halos(ops, t, own_halo, halos.at[t])
     for t in range(2):
         for side in range(2):
             velocity = [bands[t, side, k] for k in range(3)]
@@ -433,7 +419,7 @@
 
 
 def middle_kernel(
-    add_own, first, second, own, other, psi, up, down, psi_halos, coef_planes, grads, coef_first
+    add_own, first, second, own, other, psi, near, far, psi_halos, coef_planes, grads, coef_first
 ):
     ops = Ops()
     total = own[3] + other[3] if add_own else other[3]
@@ -447,21 +433,22 @@
         for k in range(5):
             values = first[k, x] + coef_first[x] * second[k, x]
             psi[k, x] = values
-            if x >= 2:
-                up[k, x - 2] = values
-            else:
-                down[k, x] = values
     for k in range(5):
         for x in range(CX):
             base = ops.unpack(other[k // 4], 4 * (k % 4) + x)
             slope = ops.unpack(other[(5 + k) // 4], 4 * ((5 + k) % 4) + x)
             psi_halos[k, x] = base + coef_first[x] * slope
+    even = is_even().astype(jnp.int32)
+    for out, side in ((near, even), (far, 1 - even)):
+        for k in range(5):
+            for i in range(2):
+                out[k, i] = psi[k, 2 * side + i].astype(BF16)
 
 
 def base_kernel(
-    flow, rho, temp, left, right, own_halo, psi, psi_halos, coef_planes,
+    wide, own_halo, psi, psi_halos, coef_planes,
     base, drift, spread,
-    wide, halos, psi_wide,
+    halos, psi_wide,
 ):
     ops = Ops()
     zero = jnp.zeros((ROWS, LANES), F32)
@@ -471,9 +458,9 @@
             psi_wide[k, 2 + CX + i] = zero
         for x in range(CX):
             psi_wide[k, 2 + x] = psi[k, x]
-    spread_state(ops, 1, 1, flow, rho, temp, left, right, own_halo, wide, halos)
+    place_halos(ops, 1, own_halo, halos)
     for x in range(CX):
-        terms = state_terms(ops, wide, halos, x)
+        terms = state_terms(ops, wide.at[1], halos, x)
         new, slope, _ = affine_update(ops, x, terms, psi_wide, psi_halos)
         for k in range(5):
             base[k, x] = new[k] + coef_planes[x] * slope[k]
@@ -488,10 +475,13 @@
             )
 
 
-def last_kernel(base, drift, spread, left_psi, right_psi, out):
-    for k in range(5):
-        far, near = left_psi[k, 0], left_psi[k, 1]
-        after, beyond = right_psi[k, 0], right_psi[k, 1]
+def last_kernel(base, drift, spread, near_psi, far_psi, out):
+    even = is_even()
+    for k in range(5):
+        ones = [near_psi[k, i].astype(F32) for i in range(2)]
+        twos = [far_psi[k, i].astype(F32) for i in range(2)]
+        far, near = (jnp.where(even, two, one) for one, two in zip(ones, twos))
+        after, beyond = (jnp.where(even, one, two) for one, two in zip(ones, twos))
         low = drift[0] * ((1.0 / 12.0) * far - (2.0 / 3.0) * near)
         high = drift[CX - 1] * ((2.0 / 3.0) * after - (1.0 / 12.0) * beyond)
         if k != 3:
@@ -508,6 +498,15 @@
     count = lax.axis_size(axis)
     forward = [(i, (i + 1) % count) for i in range(count)]
     return forward, [(target, source) for source, target in forward]
+
+
+def pairs():
+    count = lax.axis_size("gx")
+    if count % 2:
+        raise ValueError("odd gx")
+    inside = [(i, i ^ 1) for i in range(count)]
+    across = [(i, (i + 1 if i % 2 else i - 1) % count) for i in range(count)]
+    return inside, across
 
 
 def span_edges(message, strips):
@@ -551,11 +550,14 @@
 
 
 def local(flow, rho, temp, psi):
-    forward, backward = ring("gx")
-    up, down, flow, rho, temp, psi = call(
+    inside, across = pairs()
+    near, far, flow, rho, temp, psi = call(
         message_kernel,
         "message",
-        (flow, rho, temp, psi),
+        tuple(
+            pltpu.with_memory_space_constraint(a, pltpu.MemorySpace.HBM)
+            for a in (flow, rho, temp, psi)
+        ),
         [shape_of((MESSAGE,), BF16)] * 2
         + [
             shape_of((2, 3, CX), BF16),
@@ -567,8 +569,8 @@
         [pltpu.SemaphoreType.DMA((4,))],
         [pl.BlockSpec(memory_space=pltpu.MemorySpace.HBM)] * 4,
     )
-    left = lax.ppermute(up, "gx", forward)
-    right = lax.ppermute(down, "gx", backward)
+    far = lax.ppermute(far, "gx", across)
+    near = lax.ppermute(near, "gx", inside)
     (packed,) = call(
         pack_kernel,
         "pack",
@@ -579,28 +581,30 @@
     (packed,) = call(
         bands_kernel,
         "bands",
-        (packed, left, right),
+        (packed, near, far),
         [shape_of((STRIP_BLOCKS + 6,), BF16)],
         1_000_000,
     )
     own_halo = span_edges(packed, STRIP_BLOCKS)
-    inner, high = call(
+    inner, high, wide, psi_wide = call(
         inner_kernel,
         "inner",
-        (flow, left, right),
-        [shape_of((2, 2, CX)), shape_of((2, 3))],
+        (flow, rho, temp, psi, near, far),
+        [
+            shape_of((2, 2, CX)), shape_of((2, 3)),
+            shape_of((2, 5, CX + 6)), shape_of((5, CX + 4)),
+        ],
         30_000_000,
-        scratch((3, CX + 6), (21, CX + 2), (21, CX)),
+        scratch((21, CX + 2), (21, CX)),
     )
     first, second, message = call(
         edge_kernel,
         "edge",
-        (flow, rho, temp, psi, left, right, packed, own_halo, inner, high),
+        (wide, psi_wide, packed, own_halo, inner, high),
         [shape_of((5, CX)), shape_of((5, CX)), shape_of((4,))],
         20_000_000,
         scratch(
-            (2, 5, CX + 4), (2, 5, CX), (5, CX + 4), (5, CX), (4, CX), (3, CX),
-            (2, 2, 3), (2, 21), (2, 2, CX),
+            (2, 5, CX), (5, CX), (3, CX), (2, 2, 3), (2, 21), (2, 2, CX)
         ),
     )
     other = span_edges(message, 4)
@@ -608,31 +612,31 @@
     if not add_own:
         total = lax.psum(message[3], "gz")
         other = jnp.concatenate([other[:3], total[None]], axis=0)
-    psi, up, down, psi_halos, coef_planes, grads = call(
+    psi, near, far, psi_halos, coef_planes, grads = call(
         functools.partial(middle_kernel, add_own),
         "middle",
         (first, second, message, other),
         [
-            shape_of((5, CX)), shape_of((5, 2)), shape_of((5, 2)),
+            shape_of((5, CX)), shape_of((5, 2), BF16), shape_of((5, 2), BF16),
             shape_of((5, CX)), shape_of((CX,)), shape_of(()),
         ],
         1_000_000,
         scratch((CX,)),
     )
-    left_psi = lax.ppermute(up, "gx", forward)
-    right_psi = lax.ppermute(down, "gx", backward)
+    far = lax.ppermute(far, "gx", across)
+    near = lax.ppermute(near, "gx", inside)
     base, drift, spread = call(
         base_kernel,
         "base",
-        (flow, rho, temp, left, right, own_halo, psi, psi_halos, coef_planes),
+        (wide, own_halo, psi, psi_halos, coef_planes),
         [shape_of((5, CX)), shape_of((CX,)), shape_of((2, 2))],
         15_000_000,
-        scratch((5, CX + 4), (5, CX), (5, CX + 4)),
+        scratch((5, CX), (5, CX + 4)),
     )
     (out,) = call(
         last_kernel,
         "last",
-        (base, drift, spread, left_psi, right_psi),
+        (base, drift, spread, near, far),
         [shape_of((5, CX))],
         1_000_000,
     )

time: 37.7 us -> 32.6 us (0.86)
  the two profiles are of different devices: /device:TPU:1 before, /device:TPU:0 now
where the time goes in v4:
time: 32.6 us; the launch traced here: 32.5 us
  starting transfers between devices  13.3 us (41%)
  waiting for transfers between devices  8.91 us (27%)
  Pallas kernels  8.8 us (27%)
  between operations  0.71 us (2%)
  local copies, waits for them, and re-layouts  0.66 us (2%)
    ppermute x2, starting transfers between devices, local(): far = lax.ppermute(far, 'gx', across)  9.36 us
    pallas_call x8, Pallas kernels, call(): pl.pallas_call(kernel, in_specs=in_specs or whole(len(inputs)), out_specs...  8.8 us
    ppermute x2, waiting for transfers between devices, local(): far = lax.ppermute(far, 'gx', across)  5.42 us
    ppermute x2, waiting for transfers between devices, span_edges(): before = lax.ppermute(message, 'gz', forward)  3.48 us
    ppermute x2, starting transfers between devices, span_edges(): before = lax.ppermute(message, 'gz', forward)  3.39 us
    mul x1, local copies, waits for them, and re-layouts, local(): coef_grad = grads[:, 16:24].T.reshape(2, CX, ROWS) * (1.0 / span_cells)  0.66 us
  transfers between devices with their start and end apart: 6, of which 4 were waited for; matrix products, arithmetic and copies ran while one was open for 2% of the time, Pallas kernels for 11%

profile of v4, /device:TPU:0, one launch (start us, length us, event | category | flops | bytes accessed | tf_op | source)
XLA Modules:
  0.0 32.5 jit_solution(1762944884643636115)
XLA Ops:
  0.6 1.1 %message.1 = (bf16[36,32,128]{2,1,0:T(8,128)(2,1)S(1)}, bf16[36,32,128]{2,1,0:T(8,128)(2,1)S(1)}, bf16[2,3,4,32,128]{4,3,2,1,0:T(8,128)(2,1)S(1)}, bf16[2,4,32,1...) custom-call(bf16[2,3,4,32,128]{4,3,2,1,0:T(8,128)(2,1)} %flow_far.1, ...), custom_call_target="tpu_custom_call" | custom-call | flops 1000000 | bytes 1900544 | tf_op jit(solution)/shard_map/message/pallas_call | solution.py:538
  1.8 0.5 %collective-permute-start = (bf16[36,32,128]{2,1,0:T(8,128)(2,1)S(1)}, bf16[36,32,128]{2,1,0:T(8,128)(2,1)S(1)}, u32[]{:S(2)}, u32[]{:S(2)}) collective-permute-start(bf16[36,32,128]{2,1,0:T(8,128)(2,1)S(1)} %get-tuple-element.28), channel_id=1, source_target_pairs={{0,2},{2,0},{4,6},{6,4},{8,10},{10,8},{12,14},{14,12},{16,18},{18,... | collective-permute-start | bytes 884744 | tf_op jit(solution)/shard_map/ppermute | solution.py:573
  2.3 5.6 %collective-permute-start.1 = (bf16[36,32,128]{2,1,0:T(8,128)(2,1)S(1)}, bf16[36,32,128]{2,1,0:T(8,128)(2,1)S(1)}, u32[]{:S(2)}, u32[]{:S(2)}) collective-permute-start(bf16[36,32,128]{2,1,0:T(8,128)(2,1)S(1)} %get-tuple-element.29), channel_id=1, source_target_pairs={{0,30},{2,4},{4,2},{6,8},{8,6},{10,12},{12,10},{14,16},{16,14},{18... | collective-permute-start | bytes 884744 | tf_op jit(solution)/shard_map/ppermute | solution.py:572
  7.9 0.2 pack.1.packed
  8.2 0.0 collective-permute-done.near
  8.2 4.3 %collective-permute-done.1.far = bf16[36,32,128]{2,1,0:T(8,128)(2,1)S(1)} collective-permute-done((bf16[36,32,128]{2,1,0:T(8,128)(2,1)S(1)}, bf16[36,32,128]{2,1,0:T(8,128)(2,1)S(1)}, u32[]{:S(2)}, u32[]{:S(2)}) %collective-permute-start.1) | collective-permute-done | bytes 294944 | tf_op jit(solution)/shard_map/ppermute | solution.py:572
  12.5 0.2 bands.1.own_pack
  12.6 1.6 %collective-permute-start.2 = (bf16[10,32,128]{2,1,0:T(8,128)(2,1)S(1)}, bf16[10,32,128]{2,1,0:T(8,128)(2,1)S(1)}, u32[]{:S(2)}, u32[]{:S(2)}) collective-permute-start(bf16[10,32,128]{2,1,0:T(8,128)(2,1)S(1)} %bands.1.own_pack), channel_id=1, source_target_pairs={{0,1},{1,0},{2,3},{3,2},{4,5},{5,4},{6,7},{7,6},{8,9},{9,8},{10,11... | collective-permute-start | bytes 245768 | tf_op jit(solution)/shard_map/ppermute | solution.py:514
  14.2 2.3 %inner.1 = (f32[2,2,4,32,128]{4,3,2,1,0:T(8,128)S(1)}, f32[2,3,32,128]{3,2,1,0:T(8,128)S(1)}, f32[2,5,10,32,128]{4,3,2,1,0:T(8,128)S(1)}, f32[5,8,32,128]{3,2,1,0:T(8,128)S(1)}) custom-call(bf16[2,3,4,32,128]{4,3,2,1,0:T(8,128)(2,1)S(1)} %get-tuple-element.24.flow, bf16[2,4,32,128]{3,2,1,0:T(8,128)(2,1)S(1)} %get-tuple-element.25.rho, ...), custom_call_target="tpu_custom_call" | custom-call | flops 30000000 | bytes 3899392 | tf_op jit(solution)/shard_map/inner/pallas_call | solution.py:538
  16.5 1.0 %collective-permute-done.2.own_halo = bf16[10,32,128]{2,1,0:T(8,128)(2,1)S(1)} collective-permute-done((bf16[10,32,128]{2,1,0:T(8,128)(2,1)S(1)}, bf16[10,32,128]{2,1,0:T(8,128)(2,1)S(1)}, u32[]{:S(2)}, u32[]{:S(2)}) %collective-permute-start.2) | collective-permute-done | bytes 81952 | tf_op jit(solution)/shard_map/ppermute | solution.py:514
  17.5 2.8 %edge.1 = (f32[5,4,32,128]{3,2,1,0:T(8,128)S(1)}, f32[5,4,32,128]{3,2,1,0:T(8,128)S(1)}, f32[4,32,128]{2,1,0:T(8,128)S(1)}) custom-call(f32[2,5,10,32,128]{4,3,2,1,0:T(8,128)S(1)} %get-tuple-element.30.wide, f32[5,8,32,128]{3,2,1,0:T(8,128)S(1)} %get-tuple-element.31.psi_wide, bf16[10,32,128]{2,1,0:T(8,128)(2,1)S(1)} %bands.1.own_pack, ...), custom_call_target="tpu_custom_call" | custom-call | flops 20000000 | bytes 3538944 | tf_op jit(solution)/shard_map/edge/pallas_call | solution.py:538
  20.3 1.8 %collective-permute-start.3 = (f32[4,32,128]{2,1,0:T(8,128)S(1)}, f32[4,32,128]{2,1,0:T(8,128)S(1)}, u32[]{:S(2)}, u32[]{:S(2)}) collective-permute-start(f32[4,32,128]{2,1,0:T(8,128)S(1)} %get-tuple-element.36.own), channel_id=1, source_target_pairs={{0,1},{1,0},{2,3},{3,2},{4,5},{5,4},{6,7},{7,6},{8,9},{9,8},{10,11... | collective-permute-start | bytes 196616 | tf_op jit(solution)/shard_map/ppermute | solution.py:514
  22.1 2.5 %collective-permute-done.3.other = f32[4,32,128]{2,1,0:T(8,128)S(1)} collective-permute-done((f32[4,32,128]{2,1,0:T(8,128)S(1)}, f32[4,32,128]{2,1,0:T(8,128)S(1)}, u32[]{:S(2)}, u32[]{:S(2)}) %collective-permute-start.3) | collective-permute-done | bytes 65568 | tf_op jit(solution)/shard_map/ppermute | solution.py:514
  24.6 0.4 %middle.1 = (f32[5,4,32,128]{3,2,1,0:T(8,128)S(1)}, bf16[5,2,32,128]{3,2,1,0:T(8,128)(2,1)S(1)}, bf16[5,2,32,128]{3,2,1,0:T(8,128)(2,1)S(1)}, f32[5,4,32,128]{3,...) custom-call(f32[5,4,32,128]{3,2,1,0:T(8,128)S(1)} %get-tuple-element.34.first, ...), custom_call_target="tpu_custom_call" | custom-call | flops 1000000 | bytes 1687552 | tf_op jit(solution)/shard_map/middle/pallas_call | solution.py:538
  25.0 0.1 collective-permute-start.4
  25.1 3.7 %collective-permute-start.5 = (bf16[5,2,32,128]{3,2,1,0:T(8,128)(2,1)S(1)}, bf16[5,2,32,128]{3,2,1,0:T(8,128)(2,1)S(1)}, u32[]{:S(2)}, u32[]{:S(2)}) collective-permute-start(bf16[5,2,32,128]{3,2,1,0:T(8,128)(2,1)S(1)} %get-tuple-element.44), channel_id=1, source_target_pairs={{0,30},{2,4},{4,2},{6,8},{8,6},{10,12},{12,10},{14,16},{16,14},{18... | collective-permute-start | bytes 245768 | tf_op jit(solution)/shard_map/ppermute | solution.py:626
  28.8 0.1 multiply_bitcast_fusion
  28.8 0.7 %copy.7 = f32[8,32]{1,0:T(8,128)} copy(f32[8,32]{0,1:T(8,128)S(1)} %multiply_bitcast_fusion) | data formatting | bytes 2048 | tf_op jit(solution)/shard_map/mul | solution.py:644
  29.5 1.0 %base.1 = (f32[5,4,32,128]{3,2,1,0:T(8,128)S(1)}, f32[4,32,128]{2,1,0:T(8,128)S(1)}, f32[2,2,32,128]{3,2,1,0:T(8,128)S(1)}) custom-call(f32[2,5,10,32,128]{4,3,2,1,0:T(8,128)S(1)} %get-tuple-element.30.wide, bf16[10,32,128]{2,1,0:T(8,128)(2,1)S(1)} %collective-permute-done.2.own_halo, f32[5,4,32,128]{3,2,1,0:T(8,128)S(1)} %get-tuple-element.37.psi, ...), custom_call_target="tpu_custom_call" | custom-call | flops 15000000 | bytes 2899968 | tf_op jit(solution)/shard_map/base/pallas_call | solution.py:538
  30.5 0.0 collective-permute-done.4.near_psi
  30.5 1.2 %collective-permute-done.5.far_psi = bf16[5,2,32,128]{3,2,1,0:T(8,128)(2,1)S(1)} collective-permute-done((bf16[5,2,32,128]{3,2,1,0:T(8,128)(2,1)S(1)}, bf16[5,2,32,128]{3,2,1,0:T(8,128)(2,1)S(1)}, u32[]{:S(2)}, u32[]{:S(2)}) %collective-permute-start.5) | collective-permute-done | bytes 81952 | tf_op jit(solution)/shard_map/ppermute | solution.py:626
  31.7 0.8 %last.1 = f32[5,4,32,128]{3,2,1,0:T(8,128)} custom-call(f32[5,4,32,128]{3,2,1,0:T(8,128)S(1)} %get-tuple-element.40.base, f32[4,32,128]{2,1,0:T(8,128)S(1)} %get-tuple-element.41.drift, f32[2,2,32,128]{3,2,1,0:T(8,128)S(1)} %get-tuple-element.42.spread, bf16[5,2,32,128]{3,2,1,0:T(8,128)(2,1)S(1)} %collective-permute-done.4.near_psi, ...), custom_call_target="tpu_custom_call" | custom-call | flops 1000000 | bytes 950272 | tf_op jit(solution)/shard_map/last/pallas_call | solution.py:538
Async XLA Ops:
  1.8 6.4 %collective-permute-start = (bf16[36,32,128]{2,1,0:T(8,128)(2,1)S(1)}, bf16[36,32,128]{2,1,0:T(8,128)(2,1)S(1)}, u32[]{:S(2)}, u32[]{:S(2)}) collective-permute-start(bf16[36,32,128]{2,1,0:T(8,128)(2,1)S(1)} %get-tuple-element.28), channel_id=1, source_target_pairs={{0,2},{2,0},{4,6},{6,4},{8,10},{10,8},{12,14},{14,12},{16,18},{18,... | collective-permute-start | bytes 884744 | tf_op jit(solution)/shard_map/ppermute | solution.py:573
  2.3 10.2 %collective-permute-start.1 = (bf16[36,32,128]{2,1,0:T(8,128)(2,1)S(1)}, bf16[36,32,128]{2,1,0:T(8,128)(2,1)S(1)}, u32[]{:S(2)}, u32[]{:S(2)}) collective-permute-start(bf16[36,32,128]{2,1,0:T(8,128)(2,1)S(1)} %get-tuple-element.29), channel_id=1, source_target_pairs={{0,30},{2,4},{4,2},{6,8},{8,6},{10,12},{12,10},{14,16},{16,14},{18... | collective-permute-start | bytes 884744 | tf_op jit(solution)/shard_map/ppermute | solution.py:572
  12.6 4.9 %collective-permute-start.2 = (bf16[10,32,128]{2,1,0:T(8,128)(2,1)S(1)}, bf16[10,32,128]{2,1,0:T(8,128)(2,1)S(1)}, u32[]{:S(2)}, u32[]{:S(2)}) collective-permute-start(bf16[10,32,128]{2,1,0:T(8,128)(2,1)S(1)} %bands.1.own_pack), channel_id=1, source_target_pairs={{0,1},{1,0},{2,3},{3,2},{4,5},{5,4},{6,7},{7,6},{8,9},{9,8},{10,11... | collective-permute-start | bytes 245768 | tf_op jit(solution)/shard_map/ppermute | solution.py:514
  20.3 4.3 %collective-permute-start.3 = (f32[4,32,128]{2,1,0:T(8,128)S(1)}, f32[4,32,128]{2,1,0:T(8,128)S(1)}, u32[]{:S(2)}, u32[]{:S(2)}) collective-permute-start(f32[4,32,128]{2,1,0:T(8,128)S(1)} %get-tuple-element.36.own), channel_id=1, source_target_pairs={{0,1},{1,0},{2,3},{3,2},{4,5},{5,4},{6,7},{7,6},{8,9},{9,8},{10,11... | collective-permute-start | bytes 196616 | tf_op jit(solution)/shard_map/ppermute | solution.py:514
  25.0 5.5 %collective-permute-start.4 = (bf16[5,2,32,128]{3,2,1,0:T(8,128)(2,1)S(1)}, bf16[5,2,32,128]{3,2,1,0:T(8,128)(2,1)S(1)}, u32[]{:S(2)}, u32[]{:S(2)}) collective-permute-start(bf16[5,2,32,128]{3,2,1,0:T(8,128)(2,1)S(1)} %get-tuple-element.43), channel_id=1, source_target_pairs={{0,2},{2,0},{4,6},{6,4},{8,10},{10,8},{12,14},{14,12},{16,18},{18,... | collective-permute-start | bytes 245768 | tf_op jit(solution)/shard_map/ppermute | solution.py:627
  25.1 6.6 %collective-permute-start.5 = (bf16[5,2,32,128]{3,2,1,0:T(8,128)(2,1)S(1)}, bf16[5,2,32,128]{3,2,1,0:T(8,128)(2,1)S(1)}, u32[]{:S(2)}, u32[]{:S(2)}) collective-permute-start(bf16[5,2,32,128]{3,2,1,0:T(8,128)(2,1)S(1)} %get-tuple-element.44), channel_id=1, source_target_pairs={{0,30},{2,4},{4,2},{6,8},{8,6},{10,12},{12,10},{14,16},{16,14},{18... | collective-permute-start | bytes 245768 | tf_op jit(solution)/shard_map/ppermute | solution.py:626

commit v5 on v4

--- a/solution.py
+++ b/solution.py
@@ -19,13 +19,13 @@
 CX = 4
 ROWS = 32
 LANES = 128
-STRIP = 8
+STRIP = 4
 F32 = jnp.float32
 BF16 = jnp.bfloat16
-SLOT_T = 8
-SLOT_PSI = 10
+SLOT_PSI = 4
 BAND = 12
-STRIP_BLOCKS = 4
+STRIP_BLOCKS = 2
+BAND_BLOCKS = 3
 VELOCITY = 0
 SCALARS = 18
 PSI = 26
@@ -63,8 +63,8 @@
     def y_down(self, values):
         return jnp.where(self.bottom, 0.0, pltpu.roll(values, 1, 0))
 
-    def unpack(self, block, strip):
-        return turn(block, LANES - 4 - STRIP * strip)
+    def strip(self, blocks, slot, x):
+        return turn(blocks[slot // 8], -(STRIP * (4 * (slot % 8) + x) + 2))
 
 
 def fourth(plus, minus, plus_2, minus_2):
@@ -93,46 +93,54 @@
     return list(velocity) + products + strain + [size * part for part in strain]
 
 
-def pack_strips(ops, planes):
+def pack_strips(ops, items):
     block = jnp.zeros((ROWS, LANES), F32)
-    strip_id = (ops.lane >> 3)
-    for strip, values in planes.items():
-        block = jnp.where(strip_id == strip, turn(values, STRIP * strip + 4), block)
+    strip_id = ops.lane >> 2
+    for slot, planes in enumerate(items):
+        for x in range(CX):
+            number = 4 * slot + x
+            block = jnp.where(strip_id == number, turn(planes[x], STRIP * number + 2), block)
     return block
 
 
 def place_halos(ops, t, own_halo, halos):
-    for k in range(5):
-        slot = 4 * t + k if k < 4 else SLOT_T + t
-        strips = own_halo[slot // 4].astype(F32)
-        for x in range(CX):
-            halos[k, x] = ops.unpack(strips, 4 * (slot % 4) + x)
-
-
-def state_terms(ops, wide, halos, x, need_all=True):
+    strips = [own_halo[number].astype(F32) for number in range(STRIP_BLOCKS)]
+    for k in range(3):
+        number = 3 * t + k
+        bands = own_halo[STRIP_BLOCKS + number // 2].astype(F32)
+        for x in range(CX):
+            halos[k, x] = turn(bands, -(BAND * (x + 3) + 3 + 6 * (number % 2)))
+    for k in range(3, 5):
+        for x in range(CX):
+            halos[k, x] = ops.strip(strips, 2 * t + k - 3, x)
+
+
+def plane_terms(ops, values, xs):
+    up, down = ops.y_up(values), ops.y_down(values)
+    lap = xs[0] + xs[1] + up + down - 6.0 * values
+    return fourth(*xs), 0.5 * (up - down), lap
+
+
+def state_terms(ops, wide, grad_xy, lap_xy, halos, x, need_all=True):
     grad = [[None] * 5 for _ in range(3)]
     lap = [None] * 5
     center = [wide[k, x + 3] for k in range(5)]
     for k in range(5):
         if k == 3 and not need_all:
             continue
-        edge = halos[k, x]
-        up, down = ops.y_up(center[k]), ops.y_down(center[k])
-        xs = [wide[k, x + 3 + step] for step in (1, -1, 2, -2)]
-        zs = [ops.z_at(center[k], edge, step) for step in (1, -1, 2, -2)]
+        zs = [ops.z_at(center[k], halos[k, x], step) for step in (1, -1, 2, -2)]
         if k < 3 or need_all:
-            grad[0][k] = fourth(*xs)
-            grad[1][k] = 0.5 * (up - down)
+            grad[0][k] = grad_xy[k, 0, x]
+            grad[1][k] = grad_xy[k, 1, x]
             grad[2][k] = fourth(*zs)
         if k != 3:
-            lap[k] = xs[0] + xs[1] + zs[0] + zs[1] + up + down - 6.0 * center[k]
+            lap[k] = lap_xy[k, x] + (zs[0] + zs[1])
     size = size_of(strain_of(grad))
     return center, grad, lap, size, 1.0 / center[3]
 
 
-def affine_update(ops, x, terms, psi_wide, psi_halos):
+def affine_update(ops, x, terms, psi, rate_xy, lap_psi_xy, psi_halos):
     center, grad, lap, size, inv_rho = terms
-    psi = [psi_wide[k, x + 2] for k in range(5)]
     work_mom = psi[0] * lap[0] + psi[1] * lap[1] + psi[2] * lap[2]
     work_heat = psi[4] * lap[4]
     turbulent = work_mom + work_heat * (1.0 / PRANDTL_TURB)
@@ -140,18 +148,13 @@
     size_rho = size * inv_rho
     first, second = [], []
     for k in range(5):
-        edge = psi_halos[k, x]
-        up, down = ops.y_up(psi[k]), ops.y_down(psi[k])
-        xs = [psi_wide[k, x + 2 + step] for step in (1, -1, 2, -2)]
-        zs = [ops.z_at(psi[k], edge, step) for step in (1, -1, 2, -2)]
-        rate = (
-            center[0] * fourth(*xs) + center[1] * (0.5 * (up - down)) + center[2] * fourth(*zs)
-        )
+        zs = [ops.z_at(psi[k], psi_halos[k, x], step) for step in (1, -1, 2, -2)]
+        rate = rate_xy[k] + center[2] * fourth(*zs)
         if k == 3:
             rate = rate - (NU_MOL * work_mom + (NU_MOL / PRANDTL) * work_heat) * inv_rho_2
             eddy = -(size * turbulent) * inv_rho_2
         else:
-            lap_psi = xs[0] + xs[1] + zs[0] + zs[1] + up + down - 6.0 * psi[k]
+            lap_psi = lap_psi_xy[k] + (zs[0] + zs[1])
             if k < 3:
                 for other in range(5):
                     rate = rate + psi[other] * grad[k][other]
@@ -206,20 +209,15 @@
                 out[SCALARS + t * 4 + 2 + i] = temp[t, 2 * side + i]
 
 
-def pack_kernel(flow, rho, temp, psi, packed):
+def pack_kernel(flow, rho, temp, psi, strips, low):
     ops = Ops()
     items = []
     for t in range(2):
-        items += [[flow[t, k, x].astype(F32) for x in range(CX)] for k in range(3)]
-        items += [[rho[t, x].astype(F32) for x in range(CX)]]
-    items += [[temp[t, x].astype(F32) for x in range(CX)] for t in range(2)]
+        for source in (rho, temp):
+            items.append([source[t, x].astype(F32) for x in range(CX)])
     items += [[psi[k, x] for x in range(CX)] for k in range(5)]
     for number in range(STRIP_BLOCKS):
-        planes = {}
-        for slot, item in enumerate(items[4 * number : 4 * number + 4]):
-            for x in range(CX):
-                planes[4 * slot + x] = item[x]
-        packed[number] = pack_strips(ops, planes).astype(BF16)
+        strips[number] = pack_strips(ops, items[8 * number : 8 * number + 8]).astype(BF16)
     band = band_of(ops.lane)
     for t in range(2):
         for k in range(3):
@@ -227,18 +225,18 @@
             for x in range(CX):
                 moved = turn(flow[t, k, x].astype(F32), BAND * (x + 3) + 3)
                 block = jnp.where(band == x + 3, moved, block)
-            packed[STRIP_BLOCKS + 3 * t + k] = block.astype(BF16)
-
-
-def bands_kernel(packed, near, far, out):
+            low[3 * t + k] = block
+
+
+def bands_kernel(strips, own_low, near, far, message, low):
     ops = Ops()
     even = is_even()
     for number in range(STRIP_BLOCKS):
-        out[number] = packed[number]
+        message[number] = strips[number]
     band = band_of(ops.lane)
     for t in range(2):
         for k in range(3):
-            block = packed[STRIP_BLOCKS + 3 * t + k].astype(F32)
+            block = own_low[3 * t + k]
             for i in range(3):
                 number = VELOCITY + t * 9 + k * 3 + i
                 one, two = near[number].astype(F32), far[number].astype(F32)
@@ -246,7 +244,11 @@
                 block = jnp.where(band == i, moved, block)
                 moved = turn(jnp.where(even, one, two), BAND * (7 + i) + 3)
                 block = jnp.where(band == 7 + i, moved, block)
-            out[STRIP_BLOCKS + 3 * t + k] = block.astype(BF16)
+            low[3 * t + k] = block
+    lower = ops.lane - BAND * band < 6
+    for number in range(BAND_BLOCKS):
+        both = jnp.where(lower, low[2 * number], turn(low[2 * number + 1], 6))
+        message[STRIP_BLOCKS + number] = both.astype(BF16)
 
 
 def products_of(hat):
@@ -267,7 +269,9 @@
 
 
 def inner_kernel(
-    flow, rho, temp, psi, near, far, inner, high, wide, psi_wide, fields, hats
+    flow, rho, temp, psi, near, far,
+    inner, high, wide_0, wide_1, grad_0, grad_1, lap_0, lap_1, psi_rate, psi_lap,
+    psi_wide, fields, hats,
 ):
     ops = Ops()
     even = is_even()
@@ -284,31 +288,31 @@
         for x in range(CX):
             psi_wide[k, 2 + x] = psi[k, x]
 
-    def step(t, carry):
+    for t, wide, grad_xy, lap_xy in ((0, wide_0, grad_0, lap_0), (1, wide_1, grad_1, lap_1)):
         for k in range(3):
             for i in range(3):
-                wide[t, k, i], wide[t, k, 7 + i] = sides(VELOCITY + t * 9 + k * 3 + i)
+                wide[k, i], wide[k, 7 + i] = sides(VELOCITY + t * 9 + k * 3 + i)
             for x in range(CX):
-                wide[t, k, 3 + x] = flow[t, k, x].astype(F32)
+                wide[k, 3 + x] = flow[t, k, x].astype(F32)
         for k, source in ((3, rho), (4, temp)):
             for i in range(2):
-                wide[t, k, 1 + i], wide[t, k, 7 + i] = sides(
+                wide[k, 1 + i], wide[k, 7 + i] = sides(
                     SCALARS + t * 4 + (k - 3) * 2 + i
                 )
             for x in range(CX):
-                wide[t, k, 3 + x] = source[t, x].astype(F32)
+                wide[k, 3 + x] = source[t, x].astype(F32)
         for x in range(-1, CX + 1):
             grad = [[None] * 3 for _ in range(3)]
             for k in range(3):
-                center = wide[t, k, x + 3]
+                center = wide[k, x + 3]
                 grad[0][k] = fourth(
-                    wide[t, k, x + 4], wide[t, k, x + 2], wide[t, k, x + 5], wide[t, k, x + 1]
+                    wide[k, x + 4], wide[k, x + 2], wide[k, x + 5], wide[k, x + 1]
                 )
                 grad[1][k] = 0.5 * (ops.y_up(center) - ops.y_down(center))
                 grad[2][k] = fourth(*(turn(center, -step) for step in (1, -1, 2, -2)))
             strain = strain_of(grad)
             size = size_of(strain)
-            velocity = [wide[t, k, x + 3] for k in range(3)]
+            velocity = [wide[k, x + 3] for k in range(3)]
             for number, values in enumerate(filter_fields(velocity, strain, size)):
                 fields[number, x + 1] = values
         for x in range(CX):
@@ -320,20 +324,29 @@
         for k in range(3):
             block = jnp.zeros((ROWS, LANES), F32)
             for q in range(CX + 6):
-                block = jnp.where(band == q, turn(wide[t, k, q], BAND * q + 11), block)
+                block = jnp.where(band == q, turn(wide[k, q], BAND * q + 11), block)
             high[t, k] = block
+        for x in range(CX):
+            for k in range(5):
+                grad_xy[k, 0, x], grad_xy[k, 1, x], lap_xy[k, x] = plane_terms(
+                    ops, wide[k, x + 3], [wide[k, x + 3 + i] for i in (1, -1, 2, -2)]
+                )
         for x in range(CX):
             cross, square = products_of(lambda number: hats[number, x])
             inner[t, 0, x] = jnp.where(valid, cross, 0.0)
             inner[t, 1, x] = jnp.where(valid, square, 0.0)
-        return carry
-
-    lax.fori_loop(0, 2, step, 0)
+    for x in range(CX):
+        for k in range(5):
+            along_x, along_y, lap = plane_terms(
+                ops, psi_wide[k, x + 2], [psi_wide[k, x + 2 + i] for i in (1, -1, 2, -2)]
+            )
+            psi_rate[k, x] = wide_0[0, x + 3] * along_x + wide_0[1, x + 3] * along_y
+            psi_lap[k, x] = lap
 
 
 def edge_kernel(
-    wide, psi_wide, own_pack, own_halo, inner, high,
-    first, second, message,
+    psi, low, high, own_halo, inner, wide_0, wide_1, grad_0, grad_1, lap_0, lap_1, psi_rate, psi_lap,
+    first, second, message, columns,
     halos, psi_halos, work, bands, spread, sums,
 ):
     ops = Ops()
@@ -345,14 +358,15 @@
     at_edge = ((place >= 3) & (place <= 5)) | ((place >= 8) & (place <= 10))
     for t in range(2):
         for k in range(3):
-            number = STRIP_BLOCKS + 3 * t + k
-            far = own_halo[number].astype(F32)
-            bands[t, 0, k] = jnp.where(from_low, far, own_pack[number].astype(F32))
-            bands[t, 1, k] = jnp.where(from_high, turn(far, 8), high[t, k])
+            number = 3 * t + k
+            far = own_halo[STRIP_BLOCKS + number // 2].astype(F32)
+            shift = 6 * (number % 2)
+            bands[t, 0, k] = jnp.where(from_low, turn(far, -shift), low[number])
+            bands[t, 1, k] = jnp.where(from_high, turn(far, 8 - shift), high[t, k])
+    strips = [own_halo[number].astype(F32) for number in range(STRIP_BLOCKS)]
     for k in range(5):
-        strips = own_halo[(SLOT_PSI + k) // 4].astype(F32)
-        for x in range(CX):
-            psi_halos[k, x] = ops.unpack(strips, 4 * ((SLOT_PSI + k) % 4) + x)
+        for x in range(CX):
+            psi_halos[k, x] = ops.strip(strips, SLOT_PSI + k, x)
     for t in range(2):
         place_halos(ops, t, own_halo, halos.at[t])
     for t in range(2):
@@ -379,14 +393,22 @@
             both = spread[t, number]
             spread[t, number] = turn(both, 1) + turn(both, -1) + 2.0 * both
     for x in range(CX):
-        terms = state_terms(ops, wide.at[0], halos.at[0], x)
-        new, slope, sensitivity = affine_update(ops, x, terms, psi_wide, psi_halos)
+        terms = state_terms(ops, wide_0, grad_0, lap_0, halos.at[0], x)
+        new, slope, sensitivity = affine_update(
+            ops, x, terms,
+            [psi[k, x] for k in range(5)],
+            [psi_rate[k, x] for k in range(5)],
+            [psi_lap[k, x] for k in range(5)],
+            psi_halos,
+        )
         for k in range(5):
             first[k, x] = new[k]
             second[k, x] = slope[k]
         work[0, x] = sensitivity
     for x in range(CX):
-        _, _, lap, size, inv_rho = state_terms(ops, wide.at[1], halos.at[1], x, need_all=False)
+        _, _, lap, size, inv_rho = state_terms(
+            ops, wide_1, grad_1, lap_1, halos.at[1], x, need_all=False
+        )
         size_rho = size * inv_rho
         for part, source in enumerate((first, second)):
             total = lap[0] * source[0, x] + lap[1] * source[1, x] + lap[2] * source[2, x]
@@ -398,31 +420,36 @@
             values = jnp.where(at_edge, values, 0.0)
             for x in range(CX):
                 sums[t, part, x] = inner[t, part, x] + jnp.where(band == x + 3, values, 0.0)
-    columns = jnp.zeros((ROWS, LANES), F32)
+    total = jnp.zeros((ROWS, LANES), F32)
     for t in range(2):
         for part in range(2):
             for x in range(CX):
-                total = (1.0 / 256.0) * jnp.sum(sums[t, part, x], axis=1, keepdims=True)
-                columns = jnp.where(ops.lane == 8 * t + 4 * part + x, total, columns)
+                value = (1.0 / 256.0) * jnp.sum(sums[t, part, x], axis=1, keepdims=True)
+                total = jnp.where(ops.lane == 8 * t + 4 * part + x, value, total)
     for part in range(3):
         for x in range(CX):
-            total = jnp.sum(work[part, x], axis=1, keepdims=True)
-            columns = jnp.where(ops.lane == 16 + 4 * part + x, total, columns)
-    for number in range(3):
-        planes = {}
-        for slot in range(4 * number, min(4 * number + 4, 10)):
-            source = first if slot < 5 else second
-            for x in range(CX):
-                planes[4 * (slot % 4) + x] = source[slot % 5, x]
-        message[number] = pack_strips(ops, planes)
-    message[3] = columns
+            value = jnp.sum(work[part, x], axis=1, keepdims=True)
+            total = jnp.where(ops.lane == 16 + 4 * part + x, value, total)
+    columns[...] = total
+    items = [[part[k, x] for x in range(CX)] for part in (first, second) for k in range(5)]
+    message[0] = pack_strips(ops, items[:8]).astype(BF16)
+    upper = total.astype(BF16).astype(F32)
+    rest = total - upper
+    middle = rest.astype(BF16).astype(F32)
+    block = pack_strips(ops, items[8:])
+    for number, part in enumerate((upper, middle, rest - middle)):
+        block = jnp.where(ops.lane >> 5 == 1 + number, turn(part, 32 * (1 + number)), block)
+    message[1] = block.astype(BF16)
 
 
 def middle_kernel(
-    add_own, first, second, own, other, psi, near, far, psi_halos, coef_planes, grads, coef_first
+    add_other, first, second, columns, other, psi, near, far, psi_halos, coef_planes, grads, coef_first
 ):
     ops = Ops()
-    total = own[3] + other[3] if add_own else other[3]
+    total = columns[...]
+    if add_other:
+        parts = other[1].astype(F32)
+        total = total + ((turn(parts, -32) + turn(parts, -64)) + turn(parts, -96))
     coef = total / (turn(total, -4) + EPSILON)
     after = total + turn(coef, 20) * turn(total, -4)
     grads[...] = jnp.where(ops.lane < 20, total, after)
@@ -433,11 +460,13 @@
         for k in range(5):
             values = first[k, x] + coef_first[x] * second[k, x]
             psi[k, x] = values
+    strips = [other[number].astype(F32) for number in range(2)]
     for k in range(5):
         for x in range(CX):
-            base = ops.unpack(other[k // 4], 4 * (k % 4) + x)
-            slope = ops.unpack(other[(5 + k) // 4], 4 * ((5 + k) % 4) + x)
-            psi_halos[k, x] = base + coef_first[x] * slope
+            psi_halos[k, x] = ops.strip(strips, k, x)
+    for k in range(5):
+        for x in range(CX):
+            psi_halos[k, x] = psi_halos[k, x] + coef_first[x] * ops.strip(strips, 5 + k, x)
     even = is_even().astype(jnp.int32)
     for out, side in ((near, even), (far, 1 - even)):
         for k in range(5):
@@ -446,11 +475,14 @@
 
 
 def base_kernel(
-    wide, own_halo, psi, psi_halos, coef_planes,
-    base, drift, spread,
+    span_cells, wide, grad_xy, lap_xy, own_halo, psi, psi_halos, coef_planes, grads,
+    base, drift, spread, coef_grad,
     halos, psi_wide,
 ):
     ops = Ops()
+    turned = jnp.concatenate([grads[...]] * (LANES // ROWS), axis=0).T * (1.0 / span_cells)
+    for t in range(2):
+        coef_grad[t] = turned[16 + 4 * t : 20 + 4 * t, :ROWS]
     zero = jnp.zeros((ROWS, LANES), F32)
     for k in range(5):
         for i in range(2):
@@ -460,11 +492,21 @@
             psi_wide[k, 2 + x] = psi[k, x]
     place_halos(ops, 1, own_halo, halos)
     for x in range(CX):
-        terms = state_terms(ops, wide.at[1], halos, x)
-        new, slope, _ = affine_update(ops, x, terms, psi_wide, psi_halos)
+        terms = state_terms(ops, wide, grad_xy, lap_xy, halos, x)
+        center = terms[0]
+        rates, laps = [], []
+        for k in range(5):
+            along_x, along_y, lap = plane_terms(
+                ops, psi_wide[k, x + 2], [psi_wide[k, x + 2 + i] for i in (1, -1, 2, -2)]
+            )
+            rates.append(center[0] * along_x + center[1] * along_y)
+            laps.append(lap)
+        new, slope, _ = affine_update(
+            ops, x, terms, [psi[k, x] for k in range(5)], rates, laps, psi_halos
+        )
         for k in range(5):
             base[k, x] = new[k] + coef_planes[x] * slope[k]
-        center, _, _, size, inv_rho = terms
+        size, inv_rho = terms[3:]
         drift[x] = TIME_STEP * center[0]
         if x in (0, CX - 1):
             eddy = coef_planes[x] * size
@@ -517,7 +559,7 @@
     after = lax.ppermute(message, "gz", backward)
     lane = lax.broadcasted_iota(jnp.int32, message.shape, 2)
     number = lax.broadcasted_iota(jnp.int32, message.shape, 0)
-    low = jnp.where(number < strips, lane % STRIP < 4, lane % BAND < 3)
+    low = jnp.where(number < strips, lane % STRIP < 2, lane % 6 < 3)
     return jnp.where(low, before, after)
 
 
@@ -534,6 +576,8 @@
 
 
 def call(kernel, name, inputs, outputs, operations, buffers=(), in_specs=None):
+    space = pltpu.MemorySpace.HBM if in_specs else pltpu.MemorySpace.VMEM
+    inputs = [pltpu.with_memory_space_constraint(a, space) for a in inputs]
     size = sum(math.prod(a.shape) * a.dtype.itemsize for a in list(inputs) + list(outputs))
     return pl.pallas_call(
         kernel,
@@ -541,7 +585,7 @@
         out_specs=whole(len(outputs)),
         out_shape=list(outputs),
         scratch_shapes=list(buffers),
-        compiler_params=pltpu.CompilerParams(vmem_limit_bytes=24 * 2**20),
+        compiler_params=pltpu.CompilerParams(vmem_limit_bytes=8 * 2**20),
         cost_estimate=pl.CostEstimate(
             flops=operations, bytes_accessed=size, transcendentals=0
         ),
@@ -554,10 +598,7 @@
     near, far, flow, rho, temp, psi = call(
         message_kernel,
         "message",
-        tuple(
-            pltpu.with_memory_space_constraint(a, pltpu.MemorySpace.HBM)
-            for a in (flow, rho, temp, psi)
-        ),
+        (flow, rho, temp, psi),
         [shape_of((MESSAGE,), BF16)] * 2
         + [
             shape_of((2, 3, CX), BF16),
@@ -569,53 +610,56 @@
         [pltpu.SemaphoreType.DMA((4,))],
         [pl.BlockSpec(memory_space=pltpu.MemorySpace.HBM)] * 4,
     )
+    near = lax.ppermute(near, "gx", inside)
     far = lax.ppermute(far, "gx", across)
-    near = lax.ppermute(near, "gx", inside)
-    (packed,) = call(
+    strips, own_low = call(
         pack_kernel,
         "pack",
         (flow, rho, temp, psi),
-        [shape_of((STRIP_BLOCKS + 6,), BF16)],
+        [shape_of((STRIP_BLOCKS,), BF16), shape_of((6,))],
         2_000_000,
     )
-    (packed,) = call(
+    message, low = call(
         bands_kernel,
         "bands",
-        (packed, near, far),
-        [shape_of((STRIP_BLOCKS + 6,), BF16)],
+        (strips, own_low, near, far),
+        [shape_of((STRIP_BLOCKS + BAND_BLOCKS,), BF16), shape_of((6,))],
         1_000_000,
     )
-    own_halo = span_edges(packed, STRIP_BLOCKS)
-    inner, high, wide, psi_wide = call(
+    own_halo = span_edges(message, STRIP_BLOCKS)
+    inner, high, wide_0, wide_1, grad_0, grad_1, lap_0, lap_1, psi_rate, psi_lap = call(
         inner_kernel,
         "inner",
         (flow, rho, temp, psi, near, far),
         [
             shape_of((2, 2, CX)), shape_of((2, 3)),
-            shape_of((2, 5, CX + 6)), shape_of((5, CX + 4)),
+            shape_of((5, CX + 6)), shape_of((5, CX + 6)),
+            shape_of((5, 2, CX)), shape_of((5, 2, CX)),
+            shape_of((5, CX)), shape_of((5, CX)),
+            shape_of((5, CX)), shape_of((5, CX)),
         ],
         30_000_000,
-        scratch((21, CX + 2), (21, CX)),
-    )
-    first, second, message = call(
+        scratch((5, CX + 4), (21, CX + 2), (21, CX)),
+    )
+    first, second, message, columns = call(
         edge_kernel,
         "edge",
-        (wide, psi_wide, packed, own_halo, inner, high),
-        [shape_of((5, CX)), shape_of((5, CX)), shape_of((4,))],
+        (
+            psi, low, high, own_halo, inner,
+            wide_0, wide_1, grad_0, grad_1, lap_0, lap_1, psi_rate, psi_lap,
+        ),
+        [shape_of((5, CX)), shape_of((5, CX)), shape_of((2,), BF16), shape_of(())],
         20_000_000,
-        scratch(
-            (2, 5, CX), (5, CX), (3, CX), (2, 2, 3), (2, 21), (2, 2, CX)
-        ),
-    )
-    other = span_edges(message, 4)
-    add_own = lax.axis_size("gz") == 2
-    if not add_own:
-        total = lax.psum(message[3], "gz")
-        other = jnp.concatenate([other[:3], total[None]], axis=0)
+        scratch((2, 5, CX), (5, CX), (3, CX), (2, 2, 3), (2, 21), (2, 2, CX)),
+    )
+    other = span_edges(message, 2)
+    add_other = lax.axis_size("gz") == 2
+    if not add_other:
+        columns = lax.psum(columns, "gz")
     psi, near, far, psi_halos, coef_planes, grads = call(
-        functools.partial(middle_kernel, add_own),
+        functools.partial(middle_kernel, add_other),
         "middle",
-        (first, second, message, other),
+        (first, second, columns, other),
         [
             shape_of((5, CX)), shape_of((5, 2), BF16), shape_of((5, 2), BF16),
             shape_of((5, CX)), shape_of((CX,)), shape_of(()),
@@ -623,13 +667,16 @@
         1_000_000,
         scratch((CX,)),
     )
+    near = lax.ppermute(near, "gx", inside)
     far = lax.ppermute(far, "gx", across)
-    near = lax.ppermute(near, "gx", inside)
-    base, drift, spread = call(
-        base_kernel,
+    base, drift, spread, coef_grad = call(
+        functools.partial(base_kernel, LANES * lax.axis_size("gz")),
         "base",
-        (wide, own_halo, psi, psi_halos, coef_planes),
-        [shape_of((5, CX)), shape_of((CX,)), shape_of((2, 2))],
+        (wide_1, grad_1, lap_1, own_halo, psi, psi_halos, coef_planes, grads),
+        [
+            shape_of((5, CX)), shape_of((CX,)), shape_of((2, 2)),
+            jax.ShapeDtypeStruct((2, CX, ROWS), F32),
+        ],
         15_000_000,
         scratch((5, CX), (5, CX + 4)),
     )
@@ -640,8 +687,6 @@
         [shape_of((5, CX))],
         1_000_000,
     )
-    span_cells = LANES * lax.axis_size("gz")
-    coef_grad = grads[:, 16:24].T.reshape(2, CX, ROWS) * (1.0 / span_cells)
     return out, coef_grad
 
 

time: 32.6 us -> 31.3 us (0.960)
  waiting for transfers between devices: 8.91 us -> 8.17 us
  local copies, waits for them, and re-layouts: 0.66 us -> 0 us
  Pallas kernels: 8.8 us -> 9.34 us
  starting transfers between devices: 13.3 us -> 12.9 us
    ppermute x2, waiting for transfers between devices: 3.48 us -> 2.28 us  [span_edges(): before = lax.ppermute(message, 'gz', forward)]
    mul x1 -> x0, local copies, waits for them, and re-layouts: 0.66 us -> none  [local(): coef_grad = grads[:, 16:24].T.reshape(2, CX, ROWS) * (1.0 / span_cells)]
    pallas_call x8, Pallas kernels: 8.8 us -> 9.34 us  [call(): pl.pallas_call(kernel, in_specs=in_specs or whole(len(inputs)), out_specs...]
    ppermute x2, waiting for transfers between devices: 5.42 us -> 5.89 us  [local(): far = lax.ppermute(far, 'gx', across)]
  transfers between devices with their start and end apart: 6 -> 6, of which waited for: 4 -> 3; matrix products, arithmetic and copies ran while one was open for 2% -> 0% of each run, Pallas kernels for 11% -> 14%
where the time goes in v5:
time: 31.3 us; the launch traced here: 31.1 us
  starting transfers between devices  12.9 us (41%)
  Pallas kernels  9.34 us (30%)
  waiting for transfers between devices  8.17 us (26%)
  between operations  0.7 us (2%)
    pallas_call x8, Pallas kernels, call(): pl.pallas_call(kernel, in_specs=in_specs or whole(len(inputs)), out_specs...  9.34 us
    ppermute x2, starting transfers between devices, local(): far = lax.ppermute(far, 'gx', across)  9.26 us
    ppermute x2, waiting for transfers between devices, local(): far = lax.ppermute(far, 'gx', across)  5.89 us
    ppermute x2, starting transfers between devices, span_edges(): before = lax.ppermute(message, 'gz', forward)  3.09 us
    ppermute x2, waiting for transfers between devices, span_edges(): before = lax.ppermute(message, 'gz', forward)  2.28 us
  transfers between devices with their start and end apart: 6, of which 3 were waited for; matrix products, arithmetic and copies ran while one was open for 0% of the time, Pallas kernels for 14%

profile of v5, /device:TPU:0, one launch (start us, length us, event | category | flops | bytes accessed | tf_op | source)
XLA Modules:
  0.0 31.1 jit_solution(11346042459344543032)
XLA Ops:
  0.6 1.1 %message.1 = (bf16[36,32,128]{2,1,0:T(8,128)(2,1)S(1)}, bf16[36,32,128]{2,1,0:T(8,128)(2,1)S(1)}, bf16[2,3,4,32,128]{4,3,2,1,0:T(8,128)(2,1)S(1)}, bf16[2,4,32,1...) custom-call(bf16[2,3,4,32,128]{4,3,2,1,0:T(8,128)(2,1)} %flow_far.1, ...), custom_call_target="tpu_custom_call" | custom-call | flops 1000000 | bytes 1900544 | tf_op jit(solution)/shard_map/message/pallas_call | solution.py:582
  1.8 0.5 %collective-permute-start = (bf16[36,32,128]{2,1,0:T(8,128)(2,1)S(1)}, bf16[36,32,128]{2,1,0:T(8,128)(2,1)S(1)}, u32[]{:S(2)}, u32[]{:S(2)}) collective-permute-start(bf16[36,32,128]{2,1,0:T(8,128)(2,1)S(1)} %get-tuple-element.40), channel_id=1, source_target_pairs={{0,2},{2,0},{4,6},{6,4},{8,10},{10,8},{12,14},{14,12},{16,18},{18,... | collective-permute-start | bytes 884744 | tf_op jit(solution)/shard_map/ppermute | solution.py:613
  2.3 5.6 %collective-permute-start.1 = (bf16[36,32,128]{2,1,0:T(8,128)(2,1)S(1)}, bf16[36,32,128]{2,1,0:T(8,128)(2,1)S(1)}, u32[]{:S(2)}, u32[]{:S(2)}) collective-permute-start(bf16[36,32,128]{2,1,0:T(8,128)(2,1)S(1)} %get-tuple-element.41), channel_id=1, source_target_pairs={{0,30},{2,4},{4,2},{6,8},{8,6},{10,12},{12,10},{14,16},{16,14},{18... | collective-permute-start | bytes 884744 | tf_op jit(solution)/shard_map/ppermute | solution.py:614
  7.9 0.2 pack.1
  8.1 0.0 collective-permute-done.near
  8.1 4.3 %collective-permute-done.1.far = bf16[36,32,128]{2,1,0:T(8,128)(2,1)S(1)} collective-permute-done((bf16[36,32,128]{2,1,0:T(8,128)(2,1)S(1)}, bf16[36,32,128]{2,1,0:T(8,128)(2,1)S(1)}, u32[]{:S(2)}, u32[]{:S(2)}) %collective-permute-start.1) | collective-permute-done | bytes 294944 | tf_op jit(solution)/shard_map/ppermute | solution.py:614
  12.5 0.2 bands.1
  12.7 1.5 %collective-permute-start.2 = (bf16[5,32,128]{2,1,0:T(8,128)(2,1)S(1)}, bf16[5,32,128]{2,1,0:T(8,128)(2,1)S(1)}, u32[]{:S(2)}, u32[]{:S(2)}) collective-permute-start(bf16[5,32,128]{2,1,0:T(8,128)(2,1)S(1)} %get-tuple-element.47), channel_id=1, source_target_pairs={{0,1},{1,0},{2,3},{3,2},{4,5},{5,4},{6,7},{7,6},{8,9},{9,8},{10,11... | collective-permute-start | bytes 122888 | tf_op jit(solution)/shard_map/ppermute | solution.py:556
  14.2 2.6 %inner.1 = (f32[2,2,4,32,128]{4,3,2,1,0:T(8,128)S(1)}, f32[2,3,32,128]{3,2,1,0:T(8,128)S(1)}, f32[5,10,32,128]{3,2,1,0:T(8,128)S(1)}, f32[5,10,32,128]{3,2,1,0:T...) custom-call(bf16[2,3,4,32,128]{4,3,2,1,0:T(8,128)(2,1)S(1)} %get-tup, ...), custom_call_target="tpu_custom_call" | custom-call | flops 30000000 | bytes 5865472 | tf_op jit(solution)/shard_map/inner/pallas_call | solution.py:582
  16.8 0.0 collective-permute-done.2.own_halo
  16.8 2.6 %edge.1 = (f32[5,4,32,128]{3,2,1,0:T(8,128)S(1)}, f32[5,4,32,128]{3,2,1,0:T(8,128)S(1)}, bf16[2,32,128]{2,1,0:T(8,128)(2,1)S(1)}, f32[32,128]{1,0:T(8,128)S(1)}) custom-call(f32[5,4,32,128]{3,2,1,0:T(8,128)S(1)} %get-tuple-element.39.psi, f32[6,32,128]{2,1,0:T(8,128)S(1)} %get-tuple-element.48.low, f32[2,3,32,128]{3,2,1,0:T(8,128)S(1)} %get-tuple-element.49.high, ...), custom_call_target="tpu_custom_call" | custom-call | flops 20000000 | bytes 5775360 | tf_op jit(solution)/shard_map/edge/pallas_call | solution.py:582
  19.5 1.5 %collective-permute-start.3 = (bf16[2,32,128]{2,1,0:T(8,128)(2,1)S(1)}, bf16[2,32,128]{2,1,0:T(8,128)(2,1)S(1)}, u32[]{:S(2)}, u32[]{:S(2)}) collective-permute-start(bf16[2,32,128]{2,1,0:T(8,128)(2,1)S(1)} %get-tuple-element.59), channel_id=1, source_target_pairs={{0,1},{1,0},{2,3},{3,2},{4,5},{5,4},{6,7},{7,6},{8,9},{9,8},{10,11... | collective-permute-start | bytes 49160 | tf_op jit(solution)/shard_map/ppermute | solution.py:556
  21.0 2.3 %collective-permute-done.3.other = bf16[2,32,128]{2,1,0:T(8,128)(2,1)S(1)} collective-permute-done((bf16[2,32,128]{2,1,0:T(8,128)(2,1)S(1)}, bf16[2,32,128]{2,1,0:T(8,128)(2,1)S(1)}, u32[]{:S(2)}, u32[]{:S(2)}) %collective-permute-start.3) | collective-permute-done | bytes 16416 | tf_op jit(solution)/shard_map/ppermute | solution.py:556
  23.3 0.3 %middle.1 = (f32[5,4,32,128]{3,2,1,0:T(8,128)S(1)}, bf16[5,2,32,128]{3,2,1,0:T(8,128)(2,1)S(1)}, bf16[5,2,32,128]{3,2,1,0:T(8,128)(2,1)S(1)}, f32[5,4,32,128]{3,...) custom-call(f32[5,4,32,128]{3,2,1,0:T(8,128)S(1)} %get-tuple-element.56.first, ...), custom_call_target="tpu_custom_call" | custom-call | flops 1000000 | bytes 1589248 | tf_op jit(solution)/shard_map/middle/pallas_call | solution.py:582
  23.6 0.1 collective-permute-start.4
  23.7 3.6 %collective-permute-start.5 = (bf16[5,2,32,128]{3,2,1,0:T(8,128)(2,1)S(1)}, bf16[5,2,32,128]{3,2,1,0:T(8,128)(2,1)S(1)}, u32[]{:S(2)}, u32[]{:S(2)}) collective-permute-start(bf16[5,2,32,128]{3,2,1,0:T(8,128)(2,1)S(1)} %get-tuple-element.68), channel_id=1, source_target_pairs={{0,30},{2,4},{4,2},{6,8},{8,6},{10,12},{12,10},{14,16},{16,14},{18... | collective-permute-start | bytes 245768 | tf_op jit(solution)/shard_map/ppermute | solution.py:671
  27.3 1.4 %base.1 = (f32[5,4,32,128]{3,2,1,0:T(8,128)S(1)}, f32[4,32,128]{2,1,0:T(8,128)S(1)}, f32[2,2,32,128]{3,2,1,0:T(8,128)S(1)}, f32[2,4,32]{2,1,0:T(4,128)}) custom-call(f32[5,10,32,128]{3,2,1,0:T(8,128)S(1)} %get-tuple-element.42.wide_1.wide, f32[5,2,4,32,128]{4,3,2,1,0:T(8,128)S(1)} %get-tuple-element.43.grad_1.grad_xy, ...), custom_call_target="tpu_custom_call" | custom-call | flops 15000000 | bytes 3040256 | tf_op jit(solution)/shard_map/base/pallas_call | solution.py:582
  28.8 0.0 collective-permute-done.4.near_psi
  28.8 1.6 %collective-permute-done.5.far_psi = bf16[5,2,32,128]{3,2,1,0:T(8,128)(2,1)S(1)} collective-permute-done((bf16[5,2,32,128]{3,2,1,0:T(8,128)(2,1)S(1)}, bf16[5,2,32,128]{3,2,1,0:T(8,128)(2,1)S(1)}, u32[]{:S(2)}, u32[]{:S(2)}) %collective-permute-start.5) | collective-permute-done | bytes 81952 | tf_op jit(solution)/shard_map/ppermute | solution.py:671
  30.3 0.8 %last.1 = f32[5,4,32,128]{3,2,1,0:T(8,128)} custom-call(f32[5,4,32,128]{3,2,1,0:T(8,128)S(1)} %get-tuple-element.64.base, f32[4,32,128]{2,1,0:T(8,128)S(1)} %get-tuple-element.65.drift, f32[2,2,32,128]{3,2,1,0:T(8,128)S(1)} %get-tuple-element.66.spread, bf16[5,2,32,128]{3,2,1,0:T(8,128)(2,1)S(1)} %collective-permute-done.4.near_psi, ...), custom_call_target="tpu_custom_call" | custom-call | flops 1000000 | bytes 950272 | tf_op jit(solution)/shard_map/last/pallas_call | solution.py:582
Async XLA Ops:
  1.8 6.4 %collective-permute-start = (bf16[36,32,128]{2,1,0:T(8,128)(2,1)S(1)}, bf16[36,32,128]{2,1,0:T(8,128)(2,1)S(1)}, u32[]{:S(2)}, u32[]{:S(2)}) collective-permute-start(bf16[36,32,128]{2,1,0:T(8,128)(2,1)S(1)} %get-tuple-element.40), channel_id=1, source_target_pairs={{0,2},{2,0},{4,6},{6,4},{8,10},{10,8},{12,14},{14,12},{16,18},{18,... | collective-permute-start | bytes 884744 | tf_op jit(solution)/shard_map/ppermute | solution.py:613
  2.3 10.2 %collective-permute-start.1 = (bf16[36,32,128]{2,1,0:T(8,128)(2,1)S(1)}, bf16[36,32,128]{2,1,0:T(8,128)(2,1)S(1)}, u32[]{:S(2)}, u32[]{:S(2)}) collective-permute-start(bf16[36,32,128]{2,1,0:T(8,128)(2,1)S(1)} %get-tuple-element.41), channel_id=1, source_target_pairs={{0,30},{2,4},{4,2},{6,8},{8,6},{10,12},{12,10},{14,16},{16,14},{18... | collective-permute-start | bytes 884744 | tf_op jit(solution)/shard_map/ppermute | solution.py:614
  12.7 4.2 %collective-permute-start.2 = (bf16[5,32,128]{2,1,0:T(8,128)(2,1)S(1)}, bf16[5,32,128]{2,1,0:T(8,128)(2,1)S(1)}, u32[]{:S(2)}, u32[]{:S(2)}) collective-permute-start(bf16[5,32,128]{2,1,0:T(8,128)(2,1)S(1)} %get-tuple-element.47), channel_id=1, source_target_pairs={{0,1},{1,0},{2,3},{3,2},{4,5},{5,4},{6,7},{7,6},{8,9},{9,8},{10,11... | collective-permute-start | bytes 122888 | tf_op jit(solution)/shard_map/ppermute | solution.py:556
  19.5 3.8 %collective-permute-start.3 = (bf16[2,32,128]{2,1,0:T(8,128)(2,1)S(1)}, bf16[2,32,128]{2,1,0:T(8,128)(2,1)S(1)}, u32[]{:S(2)}, u32[]{:S(2)}) collective-permute-start(bf16[2,32,128]{2,1,0:T(8,128)(2,1)S(1)} %get-tuple-element.59), channel_id=1, source_target_pairs={{0,1},{1,0},{2,3},{3,2},{4,5},{5,4},{6,7},{7,6},{8,9},{9,8},{10,11... | collective-permute-start | bytes 49160 | tf_op jit(solution)/shard_map/ppermute | solution.py:556
  23.6 5.1 %collective-permute-start.4 = (bf16[5,2,32,128]{3,2,1,0:T(8,128)(2,1)S(1)}, bf16[5,2,32,128]{3,2,1,0:T(8,128)(2,1)S(1)}, u32[]{:S(2)}, u32[]{:S(2)}) collective-permute-start(bf16[5,2,32,128]{3,2,1,0:T(8,128)(2,1)S(1)} %get-tuple-element.67), channel_id=1, source_target_pairs={{0,2},{2,0},{4,6},{6,4},{8,10},{10,8},{12,14},{14,12},{16,18},{18,... | collective-permute-start | bytes 245768 | tf_op jit(solution)/shard_map/ppermute | solution.py:670
  23.7 6.6 %collective-permute-start.5 = (bf16[5,2,32,128]{3,2,1,0:T(8,128)(2,1)S(1)}, bf16[5,2,32,128]{3,2,1,0:T(8,128)(2,1)S(1)}, u32[]{:S(2)}, u32[]{:S(2)}) collective-permute-start(bf16[5,2,32,128]{3,2,1,0:T(8,128)(2,1)S(1)} %get-tuple-element.68), channel_id=1, source_target_pairs={{0,30},{2,4},{4,2},{6,8},{8,6},{10,12},{12,10},{14,16},{16,14},{18... | collective-permute-start | bytes 245768 | tf_op jit(solution)/shard_map/ppermute | solution.py:671

commit v6 on v5

--- a/solution.py
+++ b/solution.py
@@ -176,9 +176,20 @@
     return lax.rem(lax.axis_index("gx"), 2) == 0
 
 
-def message_kernel(
-    flow_far, rho_far, temp_far, psi_far, near, far, flow, rho, temp, psi, sems
-):
+def fill_message(out, side, flow, rho, temp, psi):
+    for t in range(2):
+        for k in range(3):
+            for i in range(3):
+                out[VELOCITY + t * 9 + k * 3 + i] = flow[t, k, side + i]
+        for i in range(2):
+            out[SCALARS + t * 4 + i] = rho[t, 2 * side + i]
+            out[SCALARS + t * 4 + 2 + i] = temp[t, 2 * side + i]
+    for k in range(5):
+        for i in range(2):
+            out[PSI + k * 2 + i] = psi[k, 2 * side + i].astype(BF16)
+
+
+def message_kernel(flow_far, rho_far, temp_far, psi_far, far, flow, rho, temp, psi, sems):
     copies = [
         pltpu.make_async_copy(source, target, sems.at[i])
         for i, (source, target) in enumerate(
@@ -187,30 +198,15 @@
     ]
     for copy in copies:
         copy.start()
-    even = is_even().astype(jnp.int32)
-    sides = ((near, even), (far, 1 - even))
-    copies[0].wait()
-    for out, side in sides:
-        for t in range(2):
-            for k in range(3):
-                for i in range(3):
-                    out[t * 9 + k * 3 + i] = flow[t, k, side + i]
-    copies[1].wait()
-    for out, side in sides:
-        for k in range(5):
-            for i in range(2):
-                out[PSI + k * 2 + i] = psi[k, 2 * side + i].astype(BF16)
-    copies[2].wait()
-    copies[3].wait()
-    for out, side in sides:
-        for t in range(2):
-            for i in range(2):
-                out[SCALARS + t * 4 + i] = rho[t, 2 * side + i]
-                out[SCALARS + t * 4 + 2 + i] = temp[t, 2 * side + i]
-
-
-def pack_kernel(flow, rho, temp, psi, strips, low):
+    side = 1 - is_even().astype(jnp.int32)
+    for copy in copies:
+        copy.wait()
+    fill_message(far, side, flow, rho, temp, psi)
+
+
+def pack_kernel(flow, rho, temp, psi, near, strips, low):
     ops = Ops()
+    fill_message(near, is_even().astype(jnp.int32), flow, rho, temp, psi)
     items = []
     for t in range(2):
         for source in (rho, temp):
@@ -268,132 +264,161 @@
     return cross, square
 
 
-def inner_kernel(
-    flow, rho, temp, psi, near, far,
-    inner, high, wide_0, wide_1, grad_0, grad_1, lap_0, lap_1, psi_rate, psi_lap,
-    psi_wide, fields, hats,
-):
-    ops = Ops()
+def widen(k, source, number, count, even, near, far, wide):
+    for i in range(count):
+        one, two = near[number + i].astype(F32), far[number + i].astype(F32)
+        wide[k, 3 - count + i] = jnp.where(even, two, one)
+        wide[k, 3 + CX + i] = jnp.where(even, one, two)
+    for x in range(CX):
+        wide[k, 3 + x] = source(x).astype(F32)
+
+
+def inner_products(ops, t, flow, rho, temp, near, far, sums, high, wide, grad_xy, lap_xy, fields, hats):
     even = is_even()
     valid = (ops.lane >= 3) & (ops.lane < LANES - 3)
     band = band_of(jnp.maximum(ops.lane - 2, 0))
-
-    def sides(number):
-        one, two = near[number].astype(F32), far[number].astype(F32)
-        return jnp.where(even, two, one), jnp.where(even, one, two)
-
-    for k in range(5):
-        for i in range(2):
-            psi_wide[k, i], psi_wide[k, 2 + CX + i] = sides(PSI + k * 2 + i)
-        for x in range(CX):
-            psi_wide[k, 2 + x] = psi[k, x]
-
-    for t, wide, grad_xy, lap_xy in ((0, wide_0, grad_0, lap_0), (1, wide_1, grad_1, lap_1)):
+    for k in range(3):
+        widen(k, lambda x: flow[t, k, x], VELOCITY + t * 9 + k * 3, 3, even, near, far, wide)
+    for k, source in ((3, rho), (4, temp)):
+        number = SCALARS + t * 4 + (k - 3) * 2
+        widen(k, lambda x: source[t, x], number, 2, even, near, far, wide)
+    for x in range(-1, CX + 1):
+        grad = [[None] * 3 for _ in range(3)]
         for k in range(3):
-            for i in range(3):
-                wide[k, i], wide[k, 7 + i] = sides(VELOCITY + t * 9 + k * 3 + i)
-            for x in range(CX):
-                wide[k, 3 + x] = flow[t, k, x].astype(F32)
-        for k, source in ((3, rho), (4, temp)):
-            for i in range(2):
-                wide[k, 1 + i], wide[k, 7 + i] = sides(
-                    SCALARS + t * 4 + (k - 3) * 2 + i
-                )
-            for x in range(CX):
-                wide[k, 3 + x] = source[t, x].astype(F32)
-        for x in range(-1, CX + 1):
-            grad = [[None] * 3 for _ in range(3)]
-            for k in range(3):
-                center = wide[k, x + 3]
-                grad[0][k] = fourth(
-                    wide[k, x + 4], wide[k, x + 2], wide[k, x + 5], wide[k, x + 1]
-                )
-                grad[1][k] = 0.5 * (ops.y_up(center) - ops.y_down(center))
-                grad[2][k] = fourth(*(turn(center, -step) for step in (1, -1, 2, -2)))
-            strain = strain_of(grad)
-            size = size_of(strain)
-            velocity = [wide[k, x + 3] for k in range(3)]
-            for number, values in enumerate(filter_fields(velocity, strain, size)):
-                fields[number, x + 1] = values
-        for x in range(CX):
-            for number in range(21):
-                along_x = (
-                    fields[number, x] + fields[number, x + 2] + 2.0 * fields[number, x + 1]
-                )
-                hats[number, x] = turn(along_x, 1) + turn(along_x, -1) + 2.0 * along_x
-        for k in range(3):
-            block = jnp.zeros((ROWS, LANES), F32)
-            for q in range(CX + 6):
-                block = jnp.where(band == q, turn(wide[k, q], BAND * q + 11), block)
-            high[t, k] = block
-        for x in range(CX):
-            for k in range(5):
-                grad_xy[k, 0, x], grad_xy[k, 1, x], lap_xy[k, x] = plane_terms(
-                    ops, wide[k, x + 3], [wide[k, x + 3 + i] for i in (1, -1, 2, -2)]
-                )
-        for x in range(CX):
-            cross, square = products_of(lambda number: hats[number, x])
-            inner[t, 0, x] = jnp.where(valid, cross, 0.0)
-            inner[t, 1, x] = jnp.where(valid, square, 0.0)
-    for x in range(CX):
-        for k in range(5):
+            center = wide[k, x + 3]
             along_x, along_y, lap = plane_terms(
-                ops, psi_wide[k, x + 2], [psi_wide[k, x + 2 + i] for i in (1, -1, 2, -2)]
+                ops, center, [wide[k, x + 3 + i] for i in (1, -1, 2, -2)]
             )
-            psi_rate[k, x] = wide_0[0, x + 3] * along_x + wide_0[1, x + 3] * along_y
-            psi_lap[k, x] = lap
-
-
-def edge_kernel(
-    psi, low, high, own_halo, inner, wide_0, wide_1, grad_0, grad_1, lap_0, lap_1, psi_rate, psi_lap,
-    first, second, message, columns,
-    halos, psi_halos, work, bands, spread, sums,
-):
-    ops = Ops()
+            grad[0][k], grad[1][k] = along_x, along_y
+            grad[2][k] = fourth(*(turn(center, -step) for step in (1, -1, 2, -2)))
+            if 0 <= x < CX:
+                grad_xy[k, 0, x], grad_xy[k, 1, x], lap_xy[k, x] = along_x, along_y, lap
+        strain = strain_of(grad)
+        size = size_of(strain)
+        velocity = [wide[k, x + 3] for k in range(3)]
+        for number, values in enumerate(filter_fields(velocity, strain, size)):
+            fields[number, x + 1] = values
+    for x in range(CX):
+        for number in range(21):
+            along_x = fields[number, x] + fields[number, x + 2] + 2.0 * fields[number, x + 1]
+            hats[number, x] = turn(along_x, 1) + turn(along_x, -1) + 2.0 * along_x
+    for k in range(3):
+        block = jnp.zeros((ROWS, LANES), F32)
+        for q in range(CX + 6):
+            block = jnp.where(band == q, turn(wide[k, q], BAND * q + 11), block)
+        high[k] = block
+    for x in range(CX):
+        for k in range(3, 5):
+            grad_xy[k, 0, x], grad_xy[k, 1, x], lap_xy[k, x] = plane_terms(
+                ops, wide[k, x + 3], [wide[k, x + 3 + i] for i in (1, -1, 2, -2)]
+            )
+    for x in range(CX):
+        cross, square = products_of(lambda number: hats[number, x])
+        sums[0, x] = jnp.where(valid, cross, 0.0)
+        sums[1, x] = jnp.where(valid, square, 0.0)
+
+
+def edge_products(ops, t, low, high, own_halo, sums, bands, spread):
     band = band_of(ops.lane)
     place = ops.lane - BAND * band
     from_low = place < 3
     from_high = (place == 11) | (place < 2)
     low_side = place < 7
     at_edge = ((place >= 3) & (place <= 5)) | ((place >= 8) & (place <= 10))
-    for t in range(2):
+    for k in range(3):
+        number = 3 * t + k
+        far = own_halo[STRIP_BLOCKS + number // 2].astype(F32)
+        shift = 6 * (number % 2)
+        bands[0, k] = jnp.where(from_low, turn(far, -shift), low[number])
+        bands[1, k] = jnp.where(from_high, turn(far, 8 - shift), high[k])
+    for side in range(2):
+        velocity = [bands[side, k] for k in range(3)]
+        grad = [[None] * 3 for _ in range(3)]
         for k in range(3):
-            number = 3 * t + k
-            far = own_halo[STRIP_BLOCKS + number // 2].astype(F32)
-            shift = 6 * (number % 2)
-            bands[t, 0, k] = jnp.where(from_low, turn(far, -shift), low[number])
-            bands[t, 1, k] = jnp.where(from_high, turn(far, 8 - shift), high[t, k])
+            center = velocity[k]
+            grad[0][k] = fourth(*(turn(center, -BAND * step) for step in (1, -1, 2, -2)))
+            grad[1][k] = 0.5 * (ops.y_up(center) - ops.y_down(center))
+            grad[2][k] = fourth(*(turn(center, -step) for step in (1, -1, 2, -2)))
+        strain = strain_of(grad)
+        for number, values in enumerate(filter_fields(velocity, strain, size_of(strain))):
+            if side == 0:
+                spread[number] = values
+            else:
+                spread[number] = jnp.where(low_side, spread[number], values)
+    for number in range(21):
+        both = spread[number]
+        spread[number] = turn(both, BAND) + turn(both, -BAND) + 2.0 * both
+    for number in range(21):
+        both = spread[number]
+        spread[number] = turn(both, 1) + turn(both, -1) + 2.0 * both
+    for part, values in enumerate(products_of(lambda number: spread[number])):
+        values = jnp.where(at_edge, values, 0.0)
+        for x in range(CX):
+            sums[part, x] = sums[part, x] + jnp.where(band == x + 3, values, 0.0)
+
+
+def add_columns(ops, total, first_lane, planes, scale=1.0):
+    for x in range(CX):
+        value = scale * jnp.sum(planes(x), axis=1, keepdims=True)
+        total = jnp.where(ops.lane == first_lane + x, value, total)
+    return total
+
+
+def add_parts(ops, block, total):
+    upper = total.astype(BF16).astype(F32)
+    rest = total - upper
+    middle = rest.astype(BF16).astype(F32)
+    for number, part in enumerate((upper, middle, rest - middle)):
+        block = jnp.where(ops.lane >> 5 == 1 + number, turn(part, 32 * (1 + number)), block)
+    return block
+
+
+def span_total(add_other, columns, other):
+    total = columns[...]
+    if add_other:
+        parts = other.astype(F32)
+        total = total + ((turn(parts, -32) + turn(parts, -64)) + turn(parts, -96))
+    return total
+
+
+def inner_kernel(
+    flow, rho, temp, psi, near, far,
+    sums, high, wide, grad_xy, lap_xy, psi_rate, psi_lap,
+    psi_wide, fields, hats,
+):
+    ops = Ops()
+    even = is_even()
+    for k in range(5):
+        widen(k, lambda x: psi[k, x], PSI + k * 2, 2, even, near, far, psi_wide)
+    inner_products(
+        ops, 0, flow, rho, temp, near, far, sums, high, wide, grad_xy, lap_xy, fields, hats
+    )
+    for x in range(CX):
+        for k in range(5):
+            along_x, along_y, lap = plane_terms(
+                ops, psi_wide[k, x + 3], [psi_wide[k, x + 3 + i] for i in (1, -1, 2, -2)]
+            )
+            psi_rate[k, x] = wide[0, x + 3] * along_x + wide[1, x + 3] * along_y
+            psi_lap[k, x] = lap
+
+
+def edge_kernel(
+    psi, low, high, own_halo, inner, wide, grad_xy, lap_xy, psi_rate, psi_lap,
+    first, second, message, columns,
+    halos, psi_halos, work, bands, spread, sums,
+):
+    ops = Ops()
     strips = [own_halo[number].astype(F32) for number in range(STRIP_BLOCKS)]
     for k in range(5):
         for x in range(CX):
             psi_halos[k, x] = ops.strip(strips, SLOT_PSI + k, x)
-    for t in range(2):
-        place_halos(ops, t, own_halo, halos.at[t])
-    for t in range(2):
-        for side in range(2):
-            velocity = [bands[t, side, k] for k in range(3)]
-            grad = [[None] * 3 for _ in range(3)]
-            for k in range(3):
-                center = velocity[k]
-                grad[0][k] = fourth(*(turn(center, -BAND * step) for step in (1, -1, 2, -2)))
-                grad[1][k] = 0.5 * (ops.y_up(center) - ops.y_down(center))
-                grad[2][k] = fourth(*(turn(center, -step) for step in (1, -1, 2, -2)))
-            strain = strain_of(grad)
-            for number, values in enumerate(filter_fields(velocity, strain, size_of(strain))):
-                if side == 0:
-                    spread[t, number] = values
-                else:
-                    spread[t, number] = jnp.where(low_side, spread[t, number], values)
-    for t in range(2):
-        for number in range(21):
-            both = spread[t, number]
-            spread[t, number] = turn(both, BAND) + turn(both, -BAND) + 2.0 * both
-    for t in range(2):
-        for number in range(21):
-            both = spread[t, number]
-            spread[t, number] = turn(both, 1) + turn(both, -1) + 2.0 * both
-    for x in range(CX):
-        terms = state_terms(ops, wide_0, grad_0, lap_0, halos.at[0], x)
+    place_halos(ops, 0, own_halo, halos)
+    for part in range(2):
+        for x in range(CX):
+            sums[part, x] = inner[part, x]
+    edge_products(ops, 0, low, high, own_halo, sums, bands, spread)
+    for x in range(CX):
+        terms = state_terms(ops, wide, grad_xy, lap_xy, halos, x)
         new, slope, sensitivity = affine_update(
             ops, x, terms,
             [psi[k, x] for k in range(5)],
@@ -404,85 +429,97 @@
         for k in range(5):
             first[k, x] = new[k]
             second[k, x] = slope[k]
-        work[0, x] = sensitivity
+        work[x] = sensitivity
+    total = jnp.zeros((ROWS, LANES), F32)
+    for part in range(2):
+        total = add_columns(ops, total, 4 * part, lambda x: sums[part, x], 1.0 / 256.0)
+    total = add_columns(ops, total, 16, lambda x: work[x])
+    columns[...] = total
+    items = [[part[k, x] for x in range(CX)] for part in (first, second) for k in range(5)]
+    message[0] = pack_strips(ops, items[:8]).astype(BF16)
+    message[1] = add_parts(ops, pack_strips(ops, items[8:]), total).astype(BF16)
+
+
+def later_kernel(
+    flow, rho, temp, near, far, low, own_halo, first, second,
+    wide, grad_xy, lap_xy, message, columns,
+    high, halos, fields, hats, work, bands, spread, sums,
+):
+    ops = Ops()
+    place_halos(ops, 1, own_halo, halos)
+    inner_products(
+        ops, 1, flow, rho, temp, near, far, sums, high, wide, grad_xy, lap_xy, fields, hats
+    )
+    edge_products(ops, 1, low, high, own_halo, sums, bands, spread)
     for x in range(CX):
         _, _, lap, size, inv_rho = state_terms(
-            ops, wide_1, grad_1, lap_1, halos.at[1], x, need_all=False
+            ops, wide, grad_xy, lap_xy, halos, x, need_all=False
         )
         size_rho = size * inv_rho
         for part, source in enumerate((first, second)):
             total = lap[0] * source[0, x] + lap[1] * source[1, x] + lap[2] * source[2, x]
-            work[1 + part, x] = size_rho * (
+            work[part, x] = size_rho * (
                 total + (1.0 / PRANDTL_TURB) * (lap[4] * source[4, x])
             )
-    for t in range(2):
-        for part, values in enumerate(products_of(lambda number: spread[t, number])):
-            values = jnp.where(at_edge, values, 0.0)
-            for x in range(CX):
-                sums[t, part, x] = inner[t, part, x] + jnp.where(band == x + 3, values, 0.0)
     total = jnp.zeros((ROWS, LANES), F32)
-    for t in range(2):
-        for part in range(2):
-            for x in range(CX):
-                value = (1.0 / 256.0) * jnp.sum(sums[t, part, x], axis=1, keepdims=True)
-                total = jnp.where(ops.lane == 8 * t + 4 * part + x, value, total)
-    for part in range(3):
-        for x in range(CX):
-            value = jnp.sum(work[part, x], axis=1, keepdims=True)
-            total = jnp.where(ops.lane == 16 + 4 * part + x, value, total)
+    for part in range(2):
+        total = add_columns(ops, total, 8 + 4 * part, lambda x: sums[part, x], 1.0 / 256.0)
+        total = add_columns(ops, total, 20 + 4 * part, lambda x: work[part, x])
     columns[...] = total
-    items = [[part[k, x] for x in range(CX)] for part in (first, second) for k in range(5)]
-    message[0] = pack_strips(ops, items[:8]).astype(BF16)
-    upper = total.astype(BF16).astype(F32)
-    rest = total - upper
-    middle = rest.astype(BF16).astype(F32)
-    block = pack_strips(ops, items[8:])
-    for number, part in enumerate((upper, middle, rest - middle)):
-        block = jnp.where(ops.lane >> 5 == 1 + number, turn(part, 32 * (1 + number)), block)
-    message[1] = block.astype(BF16)
-
-
-def middle_kernel(
-    add_other, first, second, columns, other, psi, near, far, psi_halos, coef_planes, grads, coef_first
+    message[0] = add_parts(ops, jnp.zeros((ROWS, LANES), F32), total).astype(BF16)
+
+
+def coefficients(ops, total):
+    return total / (turn(total, -4) + EPSILON)
+
+
+def middle_kernel(add_other, first, second, columns, other, psi, far, coef_first):
+    ops = Ops()
+    coef = coefficients(ops, span_total(add_other, columns, other[1]))
+    for x in range(CX):
+        coef_first[x] = jnp.broadcast_to(coef[:, x : x + 1], (ROWS, LANES))
+    for x in range(CX):
+        for k in range(5):
+            psi[k, x] = first[k, x] + coef_first[x] * second[k, x]
+    side = 1 - is_even().astype(jnp.int32)
+    for k in range(5):
+        for i in range(2):
+            far[k, i] = psi[k, 2 * side + i].astype(BF16)
+
+
+def near_kernel(psi, _, near):
+    side = is_even().astype(jnp.int32)
+    for k in range(5):
+        for i in range(2):
+            near[k, i] = psi[k, 2 * side + i].astype(BF16)
+
+
+def base_kernel(
+    add_other, span_cells,
+    wide, grad_xy, lap_xy, own_halo, psi, coef_first, columns, other, later, later_other,
+    base, drift, spread, coef_grad,
+    halos, psi_halos, psi_wide, coef_planes,
 ):
     ops = Ops()
-    total = columns[...]
-    if add_other:
-        parts = other[1].astype(F32)
-        total = total + ((turn(parts, -32) + turn(parts, -64)) + turn(parts, -96))
-    coef = total / (turn(total, -4) + EPSILON)
+    place_halos(ops, 1, own_halo, halos)
+    strips = [other[number].astype(F32) for number in range(2)]
+    for k in range(5):
+        for x in range(CX):
+            psi_halos[k, x] = ops.strip(strips, k, x)
+    total = span_total(add_other, columns, other[1]) + span_total(
+        add_other, later, later_other[0]
+    )
+    coef = coefficients(ops, total)
     after = total + turn(coef, 20) * turn(total, -4)
-    grads[...] = jnp.where(ops.lane < 20, total, after)
-    for x in range(CX):
-        coef_first[x] = jnp.broadcast_to(coef[:, x : x + 1], (ROWS, LANES))
-        coef_planes[x] = jnp.broadcast_to(coef[:, 8 + x : 9 + x], (ROWS, LANES))
-    for x in range(CX):
-        for k in range(5):
-            values = first[k, x] + coef_first[x] * second[k, x]
-            psi[k, x] = values
-    strips = [other[number].astype(F32) for number in range(2)]
-    for k in range(5):
-        for x in range(CX):
-            psi_halos[k, x] = ops.strip(strips, k, x)
-    for k in range(5):
-        for x in range(CX):
-            psi_halos[k, x] = psi_halos[k, x] + coef_first[x] * ops.strip(strips, 5 + k, x)
-    even = is_even().astype(jnp.int32)
-    for out, side in ((near, even), (far, 1 - even)):
-        for k in range(5):
-            for i in range(2):
-                out[k, i] = psi[k, 2 * side + i].astype(BF16)
-
-
-def base_kernel(
-    span_cells, wide, grad_xy, lap_xy, own_halo, psi, psi_halos, coef_planes, grads,
-    base, drift, spread, coef_grad,
-    halos, psi_wide,
-):
-    ops = Ops()
-    turned = jnp.concatenate([grads[...]] * (LANES // ROWS), axis=0).T * (1.0 / span_cells)
+    grads = jnp.where(ops.lane < 20, total, after) * (1.0 / span_cells)
+    turned = jnp.concatenate([grads] * (LANES // ROWS), axis=0).T
     for t in range(2):
         coef_grad[t] = turned[16 + 4 * t : 20 + 4 * t, :ROWS]
+    for x in range(CX):
+        coef_planes[x] = jnp.broadcast_to(coef[:, 8 + x : 9 + x], (ROWS, LANES))
+    for k in range(5):
+        for x in range(CX):
+            psi_halos[k, x] = psi_halos[k, x] + coef_first[x] * ops.strip(strips, 5 + k, x)
     zero = jnp.zeros((ROWS, LANES), F32)
     for k in range(5):
         for i in range(2):
@@ -490,7 +527,6 @@
             psi_wide[k, 2 + CX + i] = zero
         for x in range(CX):
             psi_wide[k, 2 + x] = psi[k, x]
-    place_halos(ops, 1, own_halo, halos)
     for x in range(CX):
         terms = state_terms(ops, wide, grad_xy, lap_xy, halos, x)
         center = terms[0]
@@ -517,6 +553,12 @@
             )
 
 
+def widen_kernel(far, out):
+    for k in range(5):
+        for i in range(2):
+            out[k, i] = far[k, i].astype(F32)
+
+
 def last_kernel(base, drift, spread, near_psi, far_psi, out):
     even = is_even()
     for k in range(5):
@@ -593,32 +635,40 @@
     )(*inputs)
 
 
+def span_sums(columns):
+    if lax.axis_size("gz") == 2:
+        return columns
+    return lax.psum(columns, "gz")
+
+
 def local(flow, rho, temp, psi):
     inside, across = pairs()
-    near, far, flow, rho, temp, psi = call(
+    add_other = lax.axis_size("gz") == 2
+    field, planes, edges = shape_of((5, CX)), shape_of((5, CX + 6)), shape_of((5, 2), BF16)
+    far, flow, rho, temp, psi = call(
         message_kernel,
         "message",
         (flow, rho, temp, psi),
-        [shape_of((MESSAGE,), BF16)] * 2
-        + [
+        [
+            shape_of((MESSAGE,), BF16),
             shape_of((2, 3, CX), BF16),
             shape_of((2, CX), BF16),
             shape_of((2, CX), BF16),
-            shape_of((5, CX)),
+            field,
         ],
         1_000_000,
         [pltpu.SemaphoreType.DMA((4,))],
         [pl.BlockSpec(memory_space=pltpu.MemorySpace.HBM)] * 4,
     )
-    near = lax.ppermute(near, "gx", inside)
     far = lax.ppermute(far, "gx", across)
-    strips, own_low = call(
+    near, strips, own_low = call(
         pack_kernel,
         "pack",
         (flow, rho, temp, psi),
-        [shape_of((STRIP_BLOCKS,), BF16), shape_of((6,))],
+        [shape_of((MESSAGE,), BF16), shape_of((STRIP_BLOCKS,), BF16), shape_of((6,))],
         2_000_000,
     )
+    near = lax.ppermute(near, "gx", inside)
     message, low = call(
         bands_kernel,
         "bands",
@@ -627,66 +677,61 @@
         1_000_000,
     )
     own_halo = span_edges(message, STRIP_BLOCKS)
-    inner, high, wide_0, wide_1, grad_0, grad_1, lap_0, lap_1, psi_rate, psi_lap = call(
+    inner, high, wide, grad_xy, lap_xy, psi_rate, psi_lap = call(
         inner_kernel,
         "inner",
         (flow, rho, temp, psi, near, far),
-        [
-            shape_of((2, 2, CX)), shape_of((2, 3)),
-            shape_of((5, CX + 6)), shape_of((5, CX + 6)),
-            shape_of((5, 2, CX)), shape_of((5, 2, CX)),
-            shape_of((5, CX)), shape_of((5, CX)),
-            shape_of((5, CX)), shape_of((5, CX)),
-        ],
-        30_000_000,
-        scratch((5, CX + 4), (21, CX + 2), (21, CX)),
+        [shape_of((2, CX)), shape_of((3,)), planes, shape_of((5, 2, CX)), field, field, field],
+        20_000_000,
+        scratch((5, CX + 6), (21, CX + 2), (21, CX)),
     )
     first, second, message, columns = call(
         edge_kernel,
         "edge",
-        (
-            psi, low, high, own_halo, inner,
-            wide_0, wide_1, grad_0, grad_1, lap_0, lap_1, psi_rate, psi_lap,
-        ),
-        [shape_of((5, CX)), shape_of((5, CX)), shape_of((2,), BF16), shape_of(())],
+        (psi, low, high, own_halo, inner, wide, grad_xy, lap_xy, psi_rate, psi_lap),
+        [field, field, shape_of((2,), BF16), shape_of(())],
         20_000_000,
-        scratch((2, 5, CX), (5, CX), (3, CX), (2, 2, 3), (2, 21), (2, 2, CX)),
+        scratch((5, CX), (5, CX), (CX,), (2, 3), (21,), (2, CX)),
     )
     other = span_edges(message, 2)
-    add_other = lax.axis_size("gz") == 2
-    if not add_other:
-        columns = lax.psum(columns, "gz")
-    psi, near, far, psi_halos, coef_planes, grads = call(
+    columns = span_sums(columns)
+    wide, grad_xy, lap_xy, message, later = call(
+        later_kernel,
+        "later",
+        (flow, rho, temp, near, far, low, own_halo, first, second),
+        [planes, shape_of((5, 2, CX)), field, shape_of((1,), BF16), shape_of(())],
+        20_000_000,
+        scratch((3,), (5, CX), (21, CX + 2), (21, CX), (2, CX), (2, 3), (21,), (2, CX)),
+    )
+    later_other = span_edges(message, 1)
+    later = span_sums(later)
+    first, later = lax.optimization_barrier((first, later))
+    psi, far, coef_first = call(
         functools.partial(middle_kernel, add_other),
         "middle",
         (first, second, columns, other),
+        [field, edges, shape_of((CX,))],
+        1_000_000,
+    )
+    far = lax.ppermute(far, "gx", across)
+    (near,) = call(near_kernel, "near", (psi, later_other), [edges], 100_000)
+    near = lax.ppermute(near, "gx", inside)
+    base, drift, spread, coef_grad = call(
+        functools.partial(base_kernel, add_other, LANES * lax.axis_size("gz")),
+        "base",
+        (
+            wide, grad_xy, lap_xy, own_halo, psi, coef_first,
+            columns, other, later, later_other,
+        ),
         [
-            shape_of((5, CX)), shape_of((5, 2), BF16), shape_of((5, 2), BF16),
-            shape_of((5, CX)), shape_of((CX,)), shape_of(()),
-        ],
-        1_000_000,
-        scratch((CX,)),
-    )
-    near = lax.ppermute(near, "gx", inside)
-    far = lax.ppermute(far, "gx", across)
-    base, drift, spread, coef_grad = call(
-        functools.partial(base_kernel, LANES * lax.axis_size("gz")),
-        "base",
-        (wide_1, grad_1, lap_1, own_halo, psi, psi_halos, coef_planes, grads),
-        [
-            shape_of((5, CX)), shape_of((CX,)), shape_of((2, 2)),
+            field, shape_of((CX,)), shape_of((2, 2)),
             jax.ShapeDtypeStruct((2, CX, ROWS), F32),
         ],
         15_000_000,
-        scratch((5, CX), (5, CX + 4)),
-    )
-    (out,) = call(
-        last_kernel,
-        "last",
-        (base, drift, spread, near, far),
-        [shape_of((5, CX))],
-        1_000_000,
-    )
+        scratch((5, CX), (5, CX), (5, CX + 4), (CX,)),
+    )
+    (far,) = call(widen_kernel, "widen", (far,), [shape_of((5, 2))], 100_000)
+    (out,) = call(last_kernel, "last", (base, drift, spread, near, far), [field], 1_000_000)
     return out, coef_grad
 
 

time: 31.3 us -> 30.1 us (0.962)
  waiting for transfers between devices: 8.17 us -> 7.22 us
  starting transfers between devices: 12.9 us -> 12.4 us
    ppermute x2, starting transfers between devices: 9.26 us -> 8.12 us  [local(): far = lax.ppermute(far, 'gx', across)]
    ppermute x2 -> x3, starting transfers between devices: 3.09 us -> 4.16 us  [span_edges(): before = lax.ppermute(message, 'gz', forward)]
    ppermute x2 -> x3, waiting for transfers between devices: 2.28 us -> 1.3 us  [span_edges(): before = lax.ppermute(message, 'gz', forward)]
    ppermute x2, starting transfers between devices: 0.59 us -> 0.14 us  [local(): near = lax.ppermute(near, 'gx', inside)]
    pallas_call x8 -> x11, Pallas kernels: 9.34 us -> 9.64 us  [call(): pl.pallas_call(kernel, in_specs=in_specs or whole(len(inputs)), out_specs...]
  transfers between devices with their start and end apart: 6 -> 7, of which waited for: 3 -> 4; matrix products, arithmetic and copies ran while one was open for 0% -> 0% of each run, Pallas kernels for 14% -> 19%
where the time goes in v6:
time: 30.1 us; the launch traced here: 30 us
  starting transfers between devices  12.4 us (41%)
  Pallas kernels  9.64 us (32%)
  waiting for transfers between devices  7.22 us (24%)
  between operations  0.71 us (2%)
    pallas_call x11, Pallas kernels, call(): pl.pallas_call(kernel, in_specs=in_specs or whole(len(inputs)), out_specs...  9.64 us
    ppermute x2, starting transfers between devices, local(): far = lax.ppermute(far, 'gx', across)  8.12 us
    ppermute x2, waiting for transfers between devices, local(): far = lax.ppermute(far, 'gx', across)  5.91 us
    ppermute x3, starting transfers between devices, span_edges(): before = lax.ppermute(message, 'gz', forward)  4.16 us
    ppermute x3, waiting for transfers between devices, span_edges(): before = lax.ppermute(message, 'gz', forward)  1.3 us
  transfers between devices with their start and end apart: 7, of which 4 were waited for; matrix products, arithmetic and copies ran while one was open for 0% of the time, Pallas kernels for 19%

profile of v6, /device:TPU:0, one launch (start us, length us, event | category | flops | bytes accessed | tf_op | source)
XLA Modules:
  0.0 30.0 jit_solution(903760757953804027)
XLA Ops:
  0.6 1.1 %message.1 = (bf16[36,32,128]{2,1,0:T(8,128)(2,1)S(1)}, bf16[2,3,4,32,128]{4,3,2,1,0:T(8,128)(2,1)S(1)}, bf16[2,4,32,128]{3,2,1,0:T(8,128)(2,1)S(1)}, bf16[2,4,3...) custom-call(bf16[2,3,4,32,128]{4,3,2,1,0:T(8,128)(2,1)} %flow_far.1, bf16[2,4,32,128]{3,2,1,0:T(8,128)(2,1)} %rho_far.1, ...), custom_call_target="tpu_custom_call" | custom-call | flops 1000000 | bytes 1605632 | tf_op jit(solution)/shard_map/message/pallas_call | solution.py:624
  1.8 5.5 %collective-permute-start.1 = (bf16[36,32,128]{2,1,0:T(8,128)(2,1)S(1)}, bf16[36,32,128]{2,1,0:T(8,128)(2,1)S(1)}, u32[]{:S(2)}, u32[]{:S(2)}) collective-permute-start(bf16[36,32,128]{2,1,0:T(8,128)(2,1)S(1)} %get-tuple-element.42), channel_id=1, source_target_pairs={{0,30},{2,4},{4,2},{6,8},{8,6},{10,12},{12,10},{14,16},{16,14},{18... | collective-permute-start | bytes 884744 | tf_op jit(solution)/shard_map/ppermute | solution.py:663
  7.3 0.2 pack.1
  7.5 0.1 collective-permute-start
  7.5 4.2 %collective-permute-done.1.far = bf16[36,32,128]{2,1,0:T(8,128)(2,1)S(1)} collective-permute-done((bf16[36,32,128]{2,1,0:T(8,128)(2,1)S(1)}, bf16[36,32,128]{2,1,0:T(8,128)(2,1)S(1)}, u32[]{:S(2)}, u32[]{:S(2)}) %collective-permute-start.1) | collective-permute-done | bytes 294944 | tf_op jit(solution)/shard_map/ppermute | solution.py:663
  11.8 0.0 collective-permute-done.near
  11.8 0.2 bands.1
  12.0 2.0 %collective-permute-start.2 = (bf16[5,32,128]{2,1,0:T(8,128)(2,1)S(1)}, bf16[5,32,128]{2,1,0:T(8,128)(2,1)S(1)}, u32[]{:S(2)}, u32[]{:S(2)}) collective-permute-start(bf16[5,32,128]{2,1,0:T(8,128)(2,1)S(1)} %get-tuple-element.46), channel_id=1, source_target_pairs={{0,1},{1,0},{2,3},{3,2},{4,5},{5,4},{6,7},{7,6},{8,9},{9,8},{10,11... | collective-permute-start | bytes 122888 | tf_op jit(solution)/shard_map/ppermute | solution.py:598
  14.0 1.4 %inner.1 = (f32[2,4,32,128]{3,2,1,0:T(8,128)S(1)}, f32[3,32,128]{2,1,0:T(8,128)S(1)}, f32[5,10,32,128]{3,2,1,0:T(8,128)S(1)}, f32[5,2,4,32,128]{4,3,2,1,0:T(8,12...) custom-call(bf16[2,3,4,32,128]{4,3,2,1,0:T(8,128)(2,1)S(1)} %get-tuple-element.3, ...), custom_call_target="tpu_custom_call" | custom-call | flops 20000000 | bytes 3883008 | tf_op jit(solution)/shard_map/inner/pallas_call | solution.py:624
  15.4 0.8 %collective-permute-done.2.own_halo = bf16[5,32,128]{2,1,0:T(8,128)(2,1)S(1)} collective-permute-done((bf16[5,32,128]{2,1,0:T(8,128)(2,1)S(1)}, bf16[5,32,128]{2,1,0:T(8,128)(2,1)S(1)}, u32[]{:S(2)}, u32[]{:S(2)}) %collective-permute-start.2) | collective-permute-done | bytes 40992 | tf_op jit(solution)/shard_map/ppermute | solution.py:598
  16.2 1.7 %edge.1 = (f32[5,4,32,128]{3,2,1,0:T(8,128)S(1)}, f32[5,4,32,128]{3,2,1,0:T(8,128)S(1)}, bf16[2,32,128]{2,1,0:T(8,128)(2,1)S(1)}, f32[32,128]{1,0:T(8,128)S(1)}) custom-call(f32[5,4,32,128]{3,2,1,0:T(8,128)S(1)} %get-tuple-element.40.psi, f32[6,32,128]{2,1,0:T(8,128)S(1)} %get-tuple-element.45.low, f32[3,32,128]{2,1,0:T(8,128)S(1)} %get-tuple-element.47.high, ...), custom_call_target="tpu_custom_call" | custom-call | flops 20000000 | bytes 3792896 | tf_op jit(solution)/shard_map/edge/pallas_call | solution.py:624
  17.9 1.9 %collective-permute-start.3 = (bf16[2,32,128]{2,1,0:T(8,128)(2,1)S(1)}, bf16[2,32,128]{2,1,0:T(8,128)(2,1)S(1)}, u32[]{:S(2)}, u32[]{:S(2)}) collective-permute-start(bf16[2,32,128]{2,1,0:T(8,128)(2,1)S(1)} %get-tuple-element.62), channel_id=1, source_target_pairs={{0,1},{1,0},{2,3},{3,2},{4,5},{5,4},{6,7},{7,6},{8,9},{9,8},{10,11... | collective-permute-start | bytes 49160 | tf_op jit(solution)/shard_map/ppermute | solution.py:598
  19.8 2.2 %later.1 = (f32[5,10,32,128]{3,2,1,0:T(8,128)S(1)}, f32[5,2,4,32,128]{4,3,2,1,0:T(8,128)S(1)}, f32[5,4,32,128]{3,2,1,0:T(8,128)S(1)}, bf16[1,32,128]{2,1,0:T(8,128)(2,1)S(1)}, f32[32,128]{1,0:T(8,128)S(1)}) custom-call(bf16[2,3,4,32,128]{4,3,2,1,0:T(8,128)(2,1)S(1)} %get-tuple-element.37.flow, bf16[2,4,32,128]{3,2,1,0:T(8,128)(2,1)S(1)} %get-tuple-element.38.rho, ...), custom_call_target="tpu_custom_call" | custom-call | flops 20000000 | bytes 3538944 | tf_op jit(solution)/shard_map/later/pallas_call | solution.py:624
  22.0 0.2 collective-permute-start.4
  22.2 0.0 collective-permute-done.3.other
  22.2 0.3 middle.1
  22.5 2.6 %collective-permute-start.6 = (bf16[5,2,32,128]{3,2,1,0:T(8,128)(2,1)S(1)}, bf16[5,2,32,128]{3,2,1,0:T(8,128)(2,1)S(1)}, u32[]{:S(2)}, u32[]{:S(2)}) collective-permute-start(bf16[5,2,32,128]{3,2,1,0:T(8,128)(2,1)S(1)} %get-tuple-element.70), channel_id=1, source_target_pairs={{0,30},{2,4},{4,2},{6,8},{8,6},{10,12},{12,10},{14,16},{16,14},{18... | collective-permute-start | bytes 245768 | tf_op jit(solution)/shard_map/ppermute | solution.py:716
  25.1 0.5 %collective-permute-done.4.later_other._ = bf16[1,32,128]{2,1,0:T(8,128)(2,1)S(1)} collective-permute-done((bf16[1,32,128]{2,1,0:T(8,128)(2,1)S(1)}, bf16[1,32,128]{2,1,0:T(8,128)(2,1)S(1)}, u32[]{:S(2)}, u32[]{:S(2)}) %collective-permute-start.4) | collective-permute-done | bytes 8224 | tf_op jit(solution)/shard_map/ppermute | solution.py:598
  25.7 0.1 collective-permute-start.5
  25.8 1.7 %base.1 = (f32[5,4,32,128]{3,2,1,0:T(8,128)S(1)}, f32[4,32,128]{2,1,0:T(8,128)S(1)}, f32[2,2,32,128]{3,2,1,0:T(8,128)S(1)}, f32[2,4,32]{2,1,0:T(4,128)}) custom-call(f32[5,10,32,128]{3,2,1,0:T(8,128)S(1)} %get-tuple-element.56.wide, f32[5,2,4,32,128]{4,3,2,1,0:T(8,128)S(1)} %get-tuple-element.57.grad_xy, f32[5,4,32,128]{3,2,1,0:T(8,128)S(1)} %get-tuple-element.58.lap_xy, ...), custom_call_target="tpu_custom_call" | custom-call | flops 15000000 | bytes 2753536 | tf_op jit(solution)/shard_map/base/pallas_call | solution.py:624
  27.4 1.7 %collective-permute-done.6.far = bf16[5,2,32,128]{3,2,1,0:T(8,128)(2,1)S(1)} collective-permute-done((bf16[5,2,32,128]{3,2,1,0:T(8,128)(2,1)S(1)}, bf16[5,2,32,128]{3,2,1,0:T(8,128)(2,1)S(1)}, u32[]{:S(2)}, u32[]{:S(2)}) %collective-permute-start.6) | collective-permute-done | bytes 81952 | tf_op jit(solution)/shard_map/ppermute | solution.py:716
  29.1 0.0 collective-permute-done.5.near_psi
  29.2 0.8 %last.1 = f32[5,4,32,128]{3,2,1,0:T(8,128)} custom-call(f32[5,4,32,128]{3,2,1,0:T(8,128)S(1)} %get-tuple-element.67.base, f32[4,32,128]{2,1,0:T(8,128)S(1)} %get-tuple-element.68.drift, f32[2,2,32,128]{3,2,1,0:T(8,128)S(1)} %get-tuple-element.69.spread, bf16[5,2,32,128]{3,2,1,0:T(8,128)(2,1)S(1)} %collective-permute-done.5.near_psi, ...), custom_call_target="tpu_custom_call" | custom-call | flops 1000000 | bytes 1032192 | tf_op jit(solution)/shard_map/last/pallas_call | solution.py:624
  (2 shorter events, 0.0 us)
Async XLA Ops:
  1.8 10.0 %collective-permute-start.1 = (bf16[36,32,128]{2,1,0:T(8,128)(2,1)S(1)}, bf16[36,32,128]{2,1,0:T(8,128)(2,1)S(1)}, u32[]{:S(2)}, u32[]{:S(2)}) collective-permute-start(bf16[36,32,128]{2,1,0:T(8,128)(2,1)S(1)} %get-tuple-element.42), channel_id=1, source_target_pairs={{0,30},{2,4},{4,2},{6,8},{8,6},{10,12},{12,10},{14,16},{16,14},{18... | collective-permute-start | bytes 884744 | tf_op jit(solution)/shard_map/ppermute | solution.py:663
  7.5 4.3 %collective-permute-start = (bf16[36,32,128]{2,1,0:T(8,128)(2,1)S(1)}, bf16[36,32,128]{2,1,0:T(8,128)(2,1)S(1)}, u32[]{:S(2)}, u32[]{:S(2)}) collective-permute-start(bf16[36,32,128]{2,1,0:T(8,128)(2,1)S(1)} %get-tuple-element.41), channel_id=1, source_target_pairs={{0,2},{2,0},{4,6},{6,4},{8,10},{10,8},{12,14},{14,12},{16,18},{18,... | collective-permute-start | bytes 884744 | tf_op jit(solution)/shard_map/ppermute | solution.py:671
  12.0 4.2 %collective-permute-start.2 = (bf16[5,32,128]{2,1,0:T(8,128)(2,1)S(1)}, bf16[5,32,128]{2,1,0:T(8,128)(2,1)S(1)}, u32[]{:S(2)}, u32[]{:S(2)}) collective-permute-start(bf16[5,32,128]{2,1,0:T(8,128)(2,1)S(1)} %get-tuple-element.46), channel_id=1, source_target_pairs={{0,1},{1,0},{2,3},{3,2},{4,5},{5,4},{6,7},{7,6},{8,9},{9,8},{10,11... | collective-permute-start | bytes 122888 | tf_op jit(solution)/shard_map/ppermute | solution.py:598
  17.9 4.4 %collective-permute-start.3 = (bf16[2,32,128]{2,1,0:T(8,128)(2,1)S(1)}, bf16[2,32,128]{2,1,0:T(8,128)(2,1)S(1)}, u32[]{:S(2)}, u32[]{:S(2)}) collective-permute-start(bf16[2,32,128]{2,1,0:T(8,128)(2,1)S(1)} %get-tuple-element.62), channel_id=1, source_target_pairs={{0,1},{1,0},{2,3},{3,2},{4,5},{5,4},{6,7},{7,6},{8,9},{9,8},{10,11... | collective-permute-start | bytes 49160 | tf_op jit(solution)/shard_map/ppermute | solution.py:598
  22.0 3.7 %collective-permute-start.4 = (bf16[1,32,128]{2,1,0:T(8,128)(2,1)S(1)}, bf16[1,32,128]{2,1,0:T(8,128)(2,1)S(1)}, u32[]{:S(2)}, u32[]{:S(2)}) collective-permute-start(bf16[1,32,128]{2,1,0:T(8,128)(2,1)S(1)} %get-tuple-element.66), channel_id=1, source_target_pairs={{0,1},{1,0},{2,3},{3,2},{4,5},{5,4},{6,7},{7,6},{8,9},{9,8},{10,11... | collective-permute-start | bytes 24584 | tf_op jit(solution)/shard_map/ppermute | solution.py:598
  22.5 6.6 %collective-permute-start.6 = (bf16[5,2,32,128]{3,2,1,0:T(8,128)(2,1)S(1)}, bf16[5,2,32,128]{3,2,1,0:T(8,128)(2,1)S(1)}, u32[]{:S(2)}, u32[]{:S(2)}) collective-permute-start(bf16[5,2,32,128]{3,2,1,0:T(8,128)(2,1)S(1)} %get-tuple-element.70), channel_id=1, source_target_pairs={{0,30},{2,4},{4,2},{6,8},{8,6},{10,12},{12,10},{14,16},{16,14},{18... | collective-permute-start | bytes 245768 | tf_op jit(solution)/shard_map/ppermute | solution.py:716
  25.7 3.5 %collective-permute-start.5 = (bf16[5,2,32,128]{3,2,1,0:T(8,128)(2,1)S(1)}, bf16[5,2,32,128]{3,2,1,0:T(8,128)(2,1)S(1)}, u32[]{:S(2)}, u32[]{:S(2)}) collective-permute-start(bf16[5,2,32,128]{3,2,1,0:T(8,128)(2,1)S(1)} %near.1), channel_id=1, source_target_pairs={{0,2},{2,0},{4,6},{6,4},{8,10},{10,8},{12,14},{14,12},{16,18},{18,... | collective-permute-start | bytes 245768 | tf_op jit(solution)/shard_map/ppermute | solution.py:718

commit v7 on v6

--- a/solution.py
+++ b/solution.py
@@ -115,31 +115,28 @@
             halos[k, x] = ops.strip(strips, 2 * t + k - 3, x)
 
 
-def plane_terms(ops, values, xs):
+def across_terms(ops, values, halo):
     up, down = ops.y_up(values), ops.y_down(values)
-    lap = xs[0] + xs[1] + up + down - 6.0 * values
-    return fourth(*xs), 0.5 * (up - down), lap
-
-
-def state_terms(ops, wide, grad_xy, lap_xy, halos, x, need_all=True):
+    zs = [ops.z_at(values, halo, step) for step in (1, -1, 2, -2)]
+    lap = (up + down) + (zs[0] + zs[1]) - 6.0 * values
+    return 0.5 * (up - down), fourth(*zs), lap
+
+
+def state_terms(wide, grad_yz, lap_yz, x):
     grad = [[None] * 5 for _ in range(3)]
     lap = [None] * 5
     center = [wide[k, x + 3] for k in range(5)]
     for k in range(5):
-        if k == 3 and not need_all:
-            continue
-        zs = [ops.z_at(center[k], halos[k, x], step) for step in (1, -1, 2, -2)]
-        if k < 3 or need_all:
-            grad[0][k] = grad_xy[k, 0, x]
-            grad[1][k] = grad_xy[k, 1, x]
-            grad[2][k] = fourth(*zs)
+        xs = [wide[k, x + 3 + step] for step in (1, -1, 2, -2)]
+        grad[0][k] = fourth(*xs)
+        grad[1][k], grad[2][k] = grad_yz[k, 0, x], grad_yz[k, 1, x]
         if k != 3:
-            lap[k] = lap_xy[k, x] + (zs[0] + zs[1])
+            lap[k] = lap_yz[k, x] + (xs[0] + xs[1])
     size = size_of(strain_of(grad))
     return center, grad, lap, size, 1.0 / center[3]
 
 
-def affine_update(ops, x, terms, psi, rate_xy, lap_psi_xy, psi_halos):
+def affine_update(terms, psi, rates, laps):
     center, grad, lap, size, inv_rho = terms
     work_mom = psi[0] * lap[0] + psi[1] * lap[1] + psi[2] * lap[2]
     work_heat = psi[4] * lap[4]
@@ -148,13 +145,12 @@
     size_rho = size * inv_rho
     first, second = [], []
     for k in range(5):
-        zs = [ops.z_at(psi[k], psi_halos[k, x], step) for step in (1, -1, 2, -2)]
-        rate = rate_xy[k] + center[2] * fourth(*zs)
+        rate = rates[k]
         if k == 3:
             rate = rate - (NU_MOL * work_mom + (NU_MOL / PRANDTL) * work_heat) * inv_rho_2
             eddy = -(size * turbulent) * inv_rho_2
         else:
-            lap_psi = lap_psi_xy[k] + (zs[0] + zs[1])
+            lap_psi = laps[k]
             if k < 3:
                 for other in range(5):
                     rate = rate + psi[other] * grad[k][other]
@@ -189,7 +185,40 @@
             out[PSI + k * 2 + i] = psi[k, 2 * side + i].astype(BF16)
 
 
-def message_kernel(flow_far, rho_far, temp_far, psi_far, far, flow, rho, temp, psi, sems):
+def message_kernel(flow_far, rho_far, temp_far, psi_far, far, outer, sems):
+    side = 1 - is_even().astype(jnp.int32)
+    pieces = [(psi_far.at[:, pl.ds(2 * side, 2)], outer)]
+    for t in range(2):
+        for k in range(3):
+            target = far.at[pl.ds(VELOCITY + t * 9 + k * 3, 3)]
+            pieces.append((flow_far.at[t, k, pl.ds(side, 3)], target))
+        for number, source in enumerate((rho_far, temp_far)):
+            target = far.at[pl.ds(SCALARS + t * 4 + 2 * number, 2)]
+            pieces.append((source.at[t, pl.ds(2 * side, 2)], target))
+    copies = [
+        pltpu.make_async_copy(source, target, sems.at[number])
+        for number, (source, target) in enumerate(pieces)
+    ]
+    for copy in copies:
+        copy.start()
+    copies[0].wait()
+    for k in range(5):
+        for i in range(2):
+            far[PSI + k * 2 + i] = outer[k, i].astype(BF16)
+    for copy in copies[1:]:
+        copy.wait()
+
+
+def merge_bands(ops, low, message, first):
+    lower = ops.lane - BAND * band_of(ops.lane) < 6
+    for number in range(BAND_BLOCKS):
+        both = jnp.where(lower, low[2 * number], turn(low[2 * number + 1], 6))
+        message[first + number] = both.astype(BF16)
+
+
+def pack_kernel(
+    flow_far, rho_far, temp_far, psi_far, _, near, message, low, flow, rho, temp, psi, sems
+):
     copies = [
         pltpu.make_async_copy(source, target, sems.at[i])
         for i, (source, target) in enumerate(
@@ -198,14 +227,9 @@
     ]
     for copy in copies:
         copy.start()
-    side = 1 - is_even().astype(jnp.int32)
+    ops = Ops()
     for copy in copies:
         copy.wait()
-    fill_message(far, side, flow, rho, temp, psi)
-
-
-def pack_kernel(flow, rho, temp, psi, near, strips, low):
-    ops = Ops()
     fill_message(near, is_even().astype(jnp.int32), flow, rho, temp, psi)
     items = []
     for t in range(2):
@@ -213,7 +237,7 @@
             items.append([source[t, x].astype(F32) for x in range(CX)])
     items += [[psi[k, x] for x in range(CX)] for k in range(5)]
     for number in range(STRIP_BLOCKS):
-        strips[number] = pack_strips(ops, items[8 * number : 8 * number + 8]).astype(BF16)
+        message[number] = pack_strips(ops, items[8 * number : 8 * number + 8]).astype(BF16)
     band = band_of(ops.lane)
     for t in range(2):
         for k in range(3):
@@ -222,13 +246,37 @@
                 moved = turn(flow[t, k, x].astype(F32), BAND * (x + 3) + 3)
                 block = jnp.where(band == x + 3, moved, block)
             low[3 * t + k] = block
-
-
-def bands_kernel(strips, own_low, near, far, message, low):
+    merge_bands(ops, low, message, STRIP_BLOCKS)
+
+
+def own_kernel(
+    flow, rho, temp, psi, own_halo, grad_0, grad_1, lap_0, lap_1, psi_rate, psi_lap, halos, psi_halos
+):
+    ops = Ops()
+    for t in range(2):
+        place_halos(ops, t, own_halo, halos.at[t])
+    strips = [own_halo[number].astype(F32) for number in range(STRIP_BLOCKS)]
+    for k in range(5):
+        for x in range(CX):
+            psi_halos[k, x] = ops.strip(strips, SLOT_PSI + k, x)
+    for t, grad_yz, lap_yz in ((0, grad_0, lap_0), (1, grad_1, lap_1)):
+        for k in range(5):
+            for x in range(CX):
+                values = flow[t, k, x] if k < 3 else (rho if k == 3 else temp)[t, x]
+                grad_yz[k, 0, x], grad_yz[k, 1, x], lap_yz[k, x] = across_terms(
+                    ops, values.astype(F32), halos[t, k, x]
+                )
+    for x in range(CX):
+        along_y, along_z = flow[0, 1, x].astype(F32), flow[0, 2, x].astype(F32)
+        for k in range(5):
+            by_y, by_z, lap = across_terms(ops, psi[k, x], psi_halos[k, x])
+            psi_rate[k, x] = along_y * by_y + along_z * by_z
+            psi_lap[k, x] = lap
+
+
+def bands_kernel(own_low, near, far, _, message, low):
     ops = Ops()
     even = is_even()
-    for number in range(STRIP_BLOCKS):
-        message[number] = strips[number]
     band = band_of(ops.lane)
     for t in range(2):
         for k in range(3):
@@ -241,10 +289,7 @@
                 moved = turn(jnp.where(even, one, two), BAND * (7 + i) + 3)
                 block = jnp.where(band == 7 + i, moved, block)
             low[3 * t + k] = block
-    lower = ops.lane - BAND * band < 6
-    for number in range(BAND_BLOCKS):
-        both = jnp.where(lower, low[2 * number], turn(low[2 * number + 1], 6))
-        message[STRIP_BLOCKS + number] = both.astype(BF16)
+    merge_bands(ops, low, message, 0)
 
 
 def products_of(hat):
@@ -273,7 +318,7 @@
         wide[k, 3 + x] = source(x).astype(F32)
 
 
-def inner_products(ops, t, flow, rho, temp, near, far, sums, high, wide, grad_xy, lap_xy, fields, hats):
+def inner_products(ops, t, flow, rho, temp, near, far, grad_yz, sums, high, wide, fields, hats):
     even = is_even()
     valid = (ops.lane >= 3) & (ops.lane < LANES - 3)
     band = band_of(jnp.maximum(ops.lane - 2, 0))
@@ -286,13 +331,12 @@
         grad = [[None] * 3 for _ in range(3)]
         for k in range(3):
             center = wide[k, x + 3]
-            along_x, along_y, lap = plane_terms(
-                ops, center, [wide[k, x + 3 + i] for i in (1, -1, 2, -2)]
-            )
-            grad[0][k], grad[1][k] = along_x, along_y
-            grad[2][k] = fourth(*(turn(center, -step) for step in (1, -1, 2, -2)))
+            grad[0][k] = fourth(*(wide[k, x + 3 + step] for step in (1, -1, 2, -2)))
             if 0 <= x < CX:
-                grad_xy[k, 0, x], grad_xy[k, 1, x], lap_xy[k, x] = along_x, along_y, lap
+                grad[1][k], grad[2][k] = grad_yz[k, 0, x], grad_yz[k, 1, x]
+            else:
+                grad[1][k] = 0.5 * (ops.y_up(center) - ops.y_down(center))
+                grad[2][k] = fourth(*(turn(center, -step) for step in (1, -1, 2, -2)))
         strain = strain_of(grad)
         size = size_of(strain)
         velocity = [wide[k, x + 3] for k in range(3)]
@@ -308,17 +352,12 @@
             block = jnp.where(band == q, turn(wide[k, q], BAND * q + 11), block)
         high[k] = block
     for x in range(CX):
-        for k in range(3, 5):
-            grad_xy[k, 0, x], grad_xy[k, 1, x], lap_xy[k, x] = plane_terms(
-                ops, wide[k, x + 3], [wide[k, x + 3 + i] for i in (1, -1, 2, -2)]
-            )
-    for x in range(CX):
         cross, square = products_of(lambda number: hats[number, x])
         sums[0, x] = jnp.where(valid, cross, 0.0)
         sums[1, x] = jnp.where(valid, square, 0.0)
 
 
-def edge_products(ops, t, low, high, own_halo, sums, bands, spread):
+def edge_products(ops, t, low, high, halo, sums, bands, spread):
     band = band_of(ops.lane)
     place = ops.lane - BAND * band
     from_low = place < 3
@@ -327,7 +366,7 @@
     at_edge = ((place >= 3) & (place <= 5)) | ((place >= 8) & (place <= 10))
     for k in range(3):
         number = 3 * t + k
-        far = own_halo[STRIP_BLOCKS + number // 2].astype(F32)
+        far = halo[number // 2].astype(F32)
         shift = 6 * (number % 2)
         bands[0, k] = jnp.where(from_low, turn(far, -shift), low[number])
         bands[1, k] = jnp.where(from_high, turn(far, 8 - shift), high[k])
@@ -381,80 +420,71 @@
     return total
 
 
+def psi_terms(psi_wide, rate_yz, lap_yz, velocity, x):
+    rates, laps = [], []
+    for k in range(5):
+        xs = [psi_wide[k, x + 3 + step] for step in (1, -1, 2, -2)]
+        rates.append(rate_yz[k, x] + velocity * fourth(*xs))
+        laps.append(lap_yz[k, x] + (xs[0] + xs[1]))
+    return rates, laps
+
+
 def inner_kernel(
-    flow, rho, temp, psi, near, far,
-    sums, high, wide, grad_xy, lap_xy, psi_rate, psi_lap,
-    psi_wide, fields, hats,
+    flow, rho, temp, psi, near, far, grad_yz, lap_yz, psi_rate, psi_lap,
+    sums, high, first, second, message, columns,
+    wide, psi_wide, fields, hats, work,
 ):
     ops = Ops()
     even = is_even()
     for k in range(5):
         widen(k, lambda x: psi[k, x], PSI + k * 2, 2, even, near, far, psi_wide)
     inner_products(
-        ops, 0, flow, rho, temp, near, far, sums, high, wide, grad_xy, lap_xy, fields, hats
-    )
-    for x in range(CX):
-        for k in range(5):
-            along_x, along_y, lap = plane_terms(
-                ops, psi_wide[k, x + 3], [psi_wide[k, x + 3 + i] for i in (1, -1, 2, -2)]
-            )
-            psi_rate[k, x] = wide[0, x + 3] * along_x + wide[1, x + 3] * along_y
-            psi_lap[k, x] = lap
-
-
-def edge_kernel(
-    psi, low, high, own_halo, inner, wide, grad_xy, lap_xy, psi_rate, psi_lap,
-    first, second, message, columns,
-    halos, psi_halos, work, bands, spread, sums,
-):
-    ops = Ops()
-    strips = [own_halo[number].astype(F32) for number in range(STRIP_BLOCKS)]
-    for k in range(5):
-        for x in range(CX):
-            psi_halos[k, x] = ops.strip(strips, SLOT_PSI + k, x)
-    place_halos(ops, 0, own_halo, halos)
-    for part in range(2):
-        for x in range(CX):
-            sums[part, x] = inner[part, x]
-    edge_products(ops, 0, low, high, own_halo, sums, bands, spread)
-    for x in range(CX):
-        terms = state_terms(ops, wide, grad_xy, lap_xy, halos, x)
+        ops, 0, flow, rho, temp, near, far, grad_yz, sums, high, wide, fields, hats
+    )
+    for x in range(CX):
+        terms = state_terms(wide, grad_yz, lap_yz, x)
+        rates, laps = psi_terms(psi_wide, psi_rate, psi_lap, terms[0][0], x)
         new, slope, sensitivity = affine_update(
-            ops, x, terms,
-            [psi[k, x] for k in range(5)],
-            [psi_rate[k, x] for k in range(5)],
-            [psi_lap[k, x] for k in range(5)],
-            psi_halos,
+            terms, [psi[k, x] for k in range(5)], rates, laps
         )
         for k in range(5):
             first[k, x] = new[k]
             second[k, x] = slope[k]
         work[x] = sensitivity
-    total = jnp.zeros((ROWS, LANES), F32)
+    columns[...] = add_columns(ops, jnp.zeros((ROWS, LANES), F32), 16, lambda x: work[x])
+    items = [[part[k, x] for x in range(CX)] for part in (first, second) for k in range(5)]
+    for number in range(2):
+        message[number] = pack_strips(ops, items[8 * number : 8 * number + 8])
+
+
+def edge_kernel(
+    low, high, halo, inner, strips, sensitivity, message, columns, bands, spread, sums
+):
+    ops = Ops()
+    for part in range(2):
+        for x in range(CX):
+            sums[part, x] = inner[part, x]
+    edge_products(ops, 0, low, high, halo, sums, bands, spread)
+    total = sensitivity[...]
     for part in range(2):
         total = add_columns(ops, total, 4 * part, lambda x: sums[part, x], 1.0 / 256.0)
-    total = add_columns(ops, total, 16, lambda x: work[x])
     columns[...] = total
-    items = [[part[k, x] for x in range(CX)] for part in (first, second) for k in range(5)]
-    message[0] = pack_strips(ops, items[:8]).astype(BF16)
-    message[1] = add_parts(ops, pack_strips(ops, items[8:]), total).astype(BF16)
+    message[0] = strips[0].astype(BF16)
+    message[1] = add_parts(ops, strips[1], total).astype(BF16)
 
 
 def later_kernel(
-    flow, rho, temp, near, far, low, own_halo, first, second,
-    wide, grad_xy, lap_xy, message, columns,
-    high, halos, fields, hats, work, bands, spread, sums,
+    flow, rho, temp, near, far, grad_yz, lap_yz, low, halo, first, second,
+    wide, message, columns,
+    high, fields, hats, work, bands, spread, sums,
 ):
     ops = Ops()
-    place_halos(ops, 1, own_halo, halos)
     inner_products(
-        ops, 1, flow, rho, temp, near, far, sums, high, wide, grad_xy, lap_xy, fields, hats
-    )
-    edge_products(ops, 1, low, high, own_halo, sums, bands, spread)
-    for x in range(CX):
-        _, _, lap, size, inv_rho = state_terms(
-            ops, wide, grad_xy, lap_xy, halos, x, need_all=False
-        )
+        ops, 1, flow, rho, temp, near, far, grad_yz, sums, high, wide, fields, hats
+    )
+    edge_products(ops, 1, low, high, halo, sums, bands, spread)
+    for x in range(CX):
+        _, _, lap, size, inv_rho = state_terms(wide, grad_yz, lap_yz, x)
         size_rho = size * inv_rho
         for part, source in enumerate((first, second)):
             total = lap[0] * source[0, x] + lap[1] * source[1, x] + lap[2] * source[2, x]
@@ -487,21 +517,17 @@
             far[k, i] = psi[k, 2 * side + i].astype(BF16)
 
 
-def near_kernel(psi, _, near):
+def base_kernel(
+    add_other, span_cells,
+    wide, grad_yz, lap_yz, psi, coef_first, columns, other, later, later_other,
+    base, drift, spread, coef_grad, near,
+    psi_halos, psi_wide, coef_planes, psi_rate, psi_lap,
+):
+    ops = Ops()
     side = is_even().astype(jnp.int32)
     for k in range(5):
         for i in range(2):
             near[k, i] = psi[k, 2 * side + i].astype(BF16)
-
-
-def base_kernel(
-    add_other, span_cells,
-    wide, grad_xy, lap_xy, own_halo, psi, coef_first, columns, other, later, later_other,
-    base, drift, spread, coef_grad,
-    halos, psi_halos, psi_wide, coef_planes,
-):
-    ops = Ops()
-    place_halos(ops, 1, own_halo, halos)
     strips = [other[number].astype(F32) for number in range(2)]
     for k in range(5):
         for x in range(CX):
@@ -523,23 +549,20 @@
     zero = jnp.zeros((ROWS, LANES), F32)
     for k in range(5):
         for i in range(2):
-            psi_wide[k, i] = zero
-            psi_wide[k, 2 + CX + i] = zero
-        for x in range(CX):
-            psi_wide[k, 2 + x] = psi[k, x]
-    for x in range(CX):
-        terms = state_terms(ops, wide, grad_xy, lap_xy, halos, x)
+            psi_wide[k, 1 + i] = zero
+            psi_wide[k, 3 + CX + i] = zero
+        for x in range(CX):
+            psi_wide[k, 3 + x] = psi[k, x]
+    for x in range(CX):
+        for k in range(5):
+            by_y, by_z, lap = across_terms(ops, psi[k, x], psi_halos[k, x])
+            psi_rate[k, x] = wide[1, x + 3] * by_y + wide[2, x + 3] * by_z
+            psi_lap[k, x] = lap
+    for x in range(CX):
+        terms = state_terms(wide, grad_yz, lap_yz, x)
         center = terms[0]
-        rates, laps = [], []
-        for k in range(5):
-            along_x, along_y, lap = plane_terms(
-                ops, psi_wide[k, x + 2], [psi_wide[k, x + 2 + i] for i in (1, -1, 2, -2)]
-            )
-            rates.append(center[0] * along_x + center[1] * along_y)
-            laps.append(lap)
-        new, slope, _ = affine_update(
-            ops, x, terms, [psi[k, x] for k in range(5)], rates, laps, psi_halos
-        )
+        rates, laps = psi_terms(psi_wide, psi_rate, psi_lap, center[0], x)
+        new, slope, _ = affine_update(terms, [psi[k, x] for k in range(5)], rates, laps)
         for k in range(5):
             base[k, x] = new[k] + coef_planes[x] * slope[k]
         size, inv_rho = terms[3:]
@@ -618,8 +641,11 @@
 
 
 def call(kernel, name, inputs, outputs, operations, buffers=(), in_specs=None):
-    space = pltpu.MemorySpace.HBM if in_specs else pltpu.MemorySpace.VMEM
-    inputs = [pltpu.with_memory_space_constraint(a, space) for a in inputs]
+    inputs = list(inputs)
+    if in_specs:
+        inputs[:4] = [
+            pltpu.with_memory_space_constraint(a, pltpu.MemorySpace.HBM) for a in inputs[:4]
+        ]
     size = sum(math.prod(a.shape) * a.dtype.itemsize for a in list(inputs) + list(outputs))
     return pl.pallas_call(
         kernel,
@@ -641,67 +667,83 @@
     return lax.psum(columns, "gz")
 
 
-def local(flow, rho, temp, psi):
+def local(flow_far, rho_far, temp_far, psi_far):
     inside, across = pairs()
     add_other = lax.axis_size("gz") == 2
     field, planes, edges = shape_of((5, CX)), shape_of((5, CX + 6)), shape_of((5, 2), BF16)
-    far, flow, rho, temp, psi = call(
+    slopes = shape_of((5, 2, CX))
+    inputs = (flow_far, rho_far, temp_far, psi_far)
+    stay = [pl.BlockSpec(memory_space=pltpu.MemorySpace.HBM)] * 4
+    far, outer = call(
         message_kernel,
         "message",
-        (flow, rho, temp, psi),
+        inputs,
+        [shape_of((MESSAGE,), BF16), shape_of((5, 2))],
+        1_000_000,
+        [pltpu.SemaphoreType.DMA((11,))],
+        stay,
+    )
+    far = lax.ppermute(far, "gx", across)
+    near, message, own_low, flow, rho, temp, psi = call(
+        pack_kernel,
+        "pack",
+        inputs + (outer,),
         [
             shape_of((MESSAGE,), BF16),
+            shape_of((STRIP_BLOCKS + BAND_BLOCKS,), BF16),
+            shape_of((6,)),
             shape_of((2, 3, CX), BF16),
             shape_of((2, CX), BF16),
             shape_of((2, CX), BF16),
             field,
         ],
-        1_000_000,
+        2_000_000,
         [pltpu.SemaphoreType.DMA((4,))],
-        [pl.BlockSpec(memory_space=pltpu.MemorySpace.HBM)] * 4,
-    )
-    far = lax.ppermute(far, "gx", across)
-    near, strips, own_low = call(
-        pack_kernel,
-        "pack",
-        (flow, rho, temp, psi),
-        [shape_of((MESSAGE,), BF16), shape_of((STRIP_BLOCKS,), BF16), shape_of((6,))],
-        2_000_000,
+        stay + whole(1),
     )
     near = lax.ppermute(near, "gx", inside)
+    own_halo = span_edges(message, STRIP_BLOCKS)
+    grad_0, grad_1, lap_0, lap_1, psi_rate, psi_lap = call(
+        own_kernel,
+        "own",
+        (flow, rho, temp, psi, own_halo),
+        [slopes, slopes, field, field, field, field],
+        5_000_000,
+        scratch((2, 5, CX), (5, CX)),
+    )
     message, low = call(
         bands_kernel,
         "bands",
-        (strips, own_low, near, far),
-        [shape_of((STRIP_BLOCKS + BAND_BLOCKS,), BF16), shape_of((6,))],
+        (own_low, near, far, psi_lap),
+        [shape_of((BAND_BLOCKS,), BF16), shape_of((6,))],
         1_000_000,
     )
-    own_halo = span_edges(message, STRIP_BLOCKS)
-    inner, high, wide, grad_xy, lap_xy, psi_rate, psi_lap = call(
+    halo = span_edges(message, 0)
+    inner, high, first, second, strips, sensitivity = call(
         inner_kernel,
         "inner",
-        (flow, rho, temp, psi, near, far),
-        [shape_of((2, CX)), shape_of((3,)), planes, shape_of((5, 2, CX)), field, field, field],
+        (flow, rho, temp, psi, near, far, grad_0, lap_0, psi_rate, psi_lap),
+        [shape_of((2, CX)), shape_of((3,)), field, field, shape_of((2,)), shape_of(())],
         20_000_000,
-        scratch((5, CX + 6), (21, CX + 2), (21, CX)),
-    )
-    first, second, message, columns = call(
+        scratch((5, CX + 6), (5, CX + 6), (21, CX + 2), (21, CX), (CX,)),
+    )
+    message, columns = call(
         edge_kernel,
         "edge",
-        (psi, low, high, own_halo, inner, wide, grad_xy, lap_xy, psi_rate, psi_lap),
-        [field, field, shape_of((2,), BF16), shape_of(())],
+        (low, high, halo, inner, strips, sensitivity),
+        [shape_of((2,), BF16), shape_of(())],
         20_000_000,
-        scratch((5, CX), (5, CX), (CX,), (2, 3), (21,), (2, CX)),
+        scratch((2, 3), (21,), (2, CX)),
     )
     other = span_edges(message, 2)
     columns = span_sums(columns)
-    wide, grad_xy, lap_xy, message, later = call(
+    wide, message, later = call(
         later_kernel,
         "later",
-        (flow, rho, temp, near, far, low, own_halo, first, second),
-        [planes, shape_of((5, 2, CX)), field, shape_of((1,), BF16), shape_of(())],
+        (flow, rho, temp, near, far, grad_1, lap_1, low, halo, first, second),
+        [planes, shape_of((1,), BF16), shape_of(())],
         20_000_000,
-        scratch((3,), (5, CX), (21, CX + 2), (21, CX), (2, CX), (2, 3), (21,), (2, CX)),
+        scratch((3,), (21, CX + 2), (21, CX), (2, CX), (2, 3), (21,), (2, CX)),
     )
     later_other = span_edges(message, 1)
     later = span_sums(later)
@@ -714,22 +756,18 @@
         1_000_000,
     )
     far = lax.ppermute(far, "gx", across)
-    (near,) = call(near_kernel, "near", (psi, later_other), [edges], 100_000)
-    near = lax.ppermute(near, "gx", inside)
-    base, drift, spread, coef_grad = call(
+    base, drift, spread, coef_grad, near = call(
         functools.partial(base_kernel, add_other, LANES * lax.axis_size("gz")),
         "base",
-        (
-            wide, grad_xy, lap_xy, own_halo, psi, coef_first,
-            columns, other, later, later_other,
-        ),
+        (wide, grad_1, lap_1, psi, coef_first, columns, other, later, later_other),
         [
             field, shape_of((CX,)), shape_of((2, 2)),
-            jax.ShapeDtypeStruct((2, CX, ROWS), F32),
+            jax.ShapeDtypeStruct((2, CX, ROWS), F32), edges,
         ],
         15_000_000,
-        scratch((5, CX), (5, CX), (5, CX + 4), (CX,)),
-    )
+        scratch((5, CX), (5, CX + 6), (CX,), (5, CX), (5, CX)),
+    )
+    near = lax.ppermute(near, "gx", inside)
     (far,) = call(widen_kernel, "widen", (far,), [shape_of((5, 2))], 100_000)
     (out,) = call(last_kernel, "last", (base, drift, spread, near, far), [field], 1_000_000)
     return out, coef_grad

time: 30.1 us -> 30.7 us (1.020)
  Pallas kernels: 9.64 us -> 10.4 us
  starting transfers between devices: 12.4 us -> 11.7 us
  waiting for transfers between devices: 7.22 us -> 7.71 us
    ppermute x3 -> x4, waiting for transfers between devices: 1.3 us -> 5.12 us  [span_edges(): before = lax.ppermute(message, 'gz', forward)]
    ppermute x2, waiting for transfers between devices: 5.91 us -> 2.59 us  [local(): far = lax.ppermute(far, 'gx', across)]
    ppermute x2, starting transfers between devices: 8.12 us -> 6.38 us  [local(): far = lax.ppermute(far, 'gx', across)]
    ppermute x3 -> x4, starting transfers between devices: 4.16 us -> 5.27 us  [span_edges(): before = lax.ppermute(message, 'gz', forward)]
    pallas_call x11, Pallas kernels: 9.64 us -> 10.4 us  [call(): pl.pallas_call(kernel, in_specs=in_specs or whole(len(inputs)), out_specs...]
  transfers between devices with their start and end apart: 7 -> 8, of which waited for: 4 -> 4; matrix products, arithmetic and copies ran while one was open for 0% -> 0% of each run, Pallas kernels for 19% -> 24%
where the time goes in v7:
time: 30.7 us; the launch traced here: 30.5 us
  starting transfers between devices  11.7 us (38%)
  Pallas kernels  10.4 us (34%)
  waiting for transfers between devices  7.71 us (25%)
  between operations  0.71 us (2%)
    pallas_call x11, Pallas kernels, call(): pl.pallas_call(kernel, in_specs=in_specs or whole(len(inputs)), out_specs...  10.4 us
    ppermute x2, starting transfers between devices, local(): far = lax.ppermute(far, 'gx', across)  6.38 us
    ppermute x4, starting transfers between devices, span_edges(): before = lax.ppermute(message, 'gz', forward)  5.27 us
    ppermute x4, waiting for transfers between devices, span_edges(): before = lax.ppermute(message, 'gz', forward)  5.12 us
    ppermute x2, waiting for transfers between devices, local(): far = lax.ppermute(far, 'gx', across)  2.59 us
  transfers between devices with their start and end apart: 8, of which 4 were waited for; matrix products, arithmetic and copies ran while one was open for 0% of the time, Pallas kernels for 24%

profile of v7, /device:TPU:0, one launch (start us, length us, event | category | flops | bytes accessed | tf_op | source)
XLA Modules:
  0.0 30.5 jit_solution(8398532130152510905)
XLA Ops:
  0.6 1.1 %message.1 = (bf16[36,32,128]{2,1,0:T(8,128)(2,1)S(1)}, f32[5,2,32,128]{3,2,1,0:T(8,128)S(1)}) custom-call(bf16[2,3,4,32,128]{4,3,2,1,0:T(8,128)(2,1)} %flow_far.3, bf16[2,4,32,128]{3,2,1,0:T(8,128)(2,1)} %rho_far.3, bf16[2,4,32,128]{3,2,1,0:T(8,128)(2,1)} %temp_far.3, f32[5,4,32,128]{3,2,1,0:T(8,128)} %psi_far.3), custom_call_target="tpu_custom_call" | custom-call | flops 1000000 | bytes 1114112 | tf_op jit(solution)/shard_map/message/pallas_call | solution.py:650
  1.7 5.5 %collective-permute-start.1 = (bf16[36,32,128]{2,1,0:T(8,128)(2,1)S(1)}, bf16[36,32,128]{2,1,0:T(8,128)(2,1)S(1)}, u32[]{:S(2)}, u32[]{:S(2)}) collective-permute-start(bf16[36,32,128]{2,1,0:T(8,128)(2,1)S(1)} %get-tuple-element.45), channel_id=1, source_target_pairs={{0,30},{2,4},{4,2},{6,8},{8,6},{10,12},{12,10},{14,16},{16,14},{18... | collective-permute-start | bytes 884744 | tf_op jit(solution)/shard_map/ppermute | solution.py:686
  7.2 1.4 %pack.1 = (bf16[36,32,128]{2,1,0:T(8,128)(2,1)S(1)}, bf16[5,32,128]{2,1,0:T(8,128)(2,1)S(1)}, f32[6,32,128]{2,1,0:T(8,128)S(1)}, bf16[2,3,4,32,128]{4,3,2,1,0:T(...) custom-call(bf16[2,3,4,32,128]{4,3,2,1,0:T(8,128)(2,1)} %flow_far.3,, ...), custom_call_target="tpu_custom_call" | custom-call | flops 2000000 | bytes 1908736 | tf_op jit(solution)/shard_map/pack/pallas_call | solution.py:650
  8.6 0.1 collective-permute-start
  8.6 1.6 %collective-permute-start.2 = (bf16[5,32,128]{2,1,0:T(8,128)(2,1)S(1)}, bf16[5,32,128]{2,1,0:T(8,128)(2,1)S(1)}, u32[]{:S(2)}, u32[]{:S(2)}) collective-permute-start(bf16[5,32,128]{2,1,0:T(8,128)(2,1)S(1)} %get-tuple-element.47), channel_id=1, source_target_pairs={{0,1},{1,0},{2,3},{3,2},{4,5},{5,4},{6,7},{7,6},{8,9},{9,8},{10,11... | collective-permute-start | bytes 122888 | tf_op jit(solution)/shard_map/ppermute | solution.py:621
  10.2 2.5 %collective-permute-done.2.own_halo = bf16[5,32,128]{2,1,0:T(8,128)(2,1)S(1)} collective-permute-done((bf16[5,32,128]{2,1,0:T(8,128)(2,1)S(1)}, bf16[5,32,128]{2,1,0:T(8,128)(2,1)S(1)}, u32[]{:S(2)}, u32[]{:S(2)}) %collective-permute-start.2) | collective-permute-done | bytes 40992 | tf_op jit(solution)/shard_map/ppermute | solution.py:621
  12.7 1.1 %own.1 = (f32[5,2,4,32,128]{4,3,2,1,0:T(8,128)S(1)}, f32[5,2,4,32,128]{4,3,2,1,0:T(8,128)S(1)}, f32[5,4,32,128]{3,2,1,0:T(8,128)S(1)}, f32[5,4,32,128]{3,2,1,0:T...) custom-call(bf16[2,3,4,32,128]{4,3,2,1,0:T(8,128)(2,1)S(1)} %get-tuple-element.41.flow, ...), custom_call_target="tpu_custom_call" | custom-call | flops 5000000 | bytes 3317760 | tf_op jit(solution)/shard_map/own/pallas_call | solution.py:650
  13.8 0.0 collective-permute-done.1.far
  13.8 0.0 collective-permute-done.near
  13.8 0.2 bands.1
  14.0 1.5 %collective-permute-start.3 = (bf16[3,32,128]{2,1,0:T(8,128)(2,1)S(1)}, bf16[3,32,128]{2,1,0:T(8,128)(2,1)S(1)}, u32[]{:S(2)}, u32[]{:S(2)}) collective-permute-start(bf16[3,32,128]{2,1,0:T(8,128)(2,1)S(1)} %get-tuple-element.53), channel_id=1, source_target_pairs={{0,1},{1,0},{2,3},{3,2},{4,5},{5,4},{6,7},{7,6},{8,9},{9,8},{10,11... | collective-permute-start | bytes 73736 | tf_op jit(solution)/shard_map/ppermute | solution.py:621
  15.6 1.6 %inner.1 = (f32[2,4,32,128]{3,2,1,0:T(8,128)S(1)}, f32[3,32,128]{2,1,0:T(8,128)S(1)}, f32[5,4,32,128]{3,2,1,0:T(8,128)S(1)}, f32[5,4,32,128]{3,2,1,0:T(8,128)S(1...) custom-call(bf16[2,3,4,32,128]{4,3,2,1,0:T(8,128)(2,1)S(1)} %get-tuple-element.41.flow, ...), custom_call_target="tpu_custom_call" | custom-call | flops 20000000 | bytes 3768320 | tf_op jit(solution)/shard_map/inner/pallas_call | solution.py:650
  17.2 0.7 %collective-permute-done.3.halo = bf16[3,32,128]{2,1,0:T(8,128)(2,1)S(1)} collective-permute-done((bf16[3,32,128]{2,1,0:T(8,128)(2,1)S(1)}, bf16[3,32,128]{2,1,0:T(8,128)(2,1)S(1)}, u32[]{:S(2)}, u32[]{:S(2)}) %collective-permute-start.3) | collective-permute-done | bytes 24608 | tf_op jit(solution)/shard_map/ppermute | solution.py:621
  17.9 0.9 %edge.1 = (bf16[2,32,128]{2,1,0:T(8,128)(2,1)S(1)}, f32[32,128]{1,0:T(8,128)S(1)}) custom-call(f32[6,32,128]{2,1,0:T(8,128)S(1)} %get-tuple-element.52.low, f32[3,32,128]{2,1,0:T(8,128)S(1)} %get-tuple-element.62.high, bf16[3,32,128]{2,1,0:T(8,128)(2,1)S(1)} %collective-permute-done.3.halo, f32[2,4,32,128]{3,2,1,0:T(8,128)S(1)} %get-tuple-element.63.inner, ...), custom_call_target="tpu_custom_call" | custom-call | flops 20000000 | bytes 385024 | tf_op jit(solution)/shard_map/edge/pallas_call | solution.py:650
  18.7 1.6 %collective-permute-start.4 = (bf16[2,32,128]{2,1,0:T(8,128)(2,1)S(1)}, bf16[2,32,128]{2,1,0:T(8,128)(2,1)S(1)}, u32[]{:S(2)}, u32[]{:S(2)}) collective-permute-start(bf16[2,32,128]{2,1,0:T(8,128)(2,1)S(1)} %get-tuple-element.67), channel_id=1, source_target_pairs={{0,1},{1,0},{2,3},{3,2},{4,5},{5,4},{6,7},{7,6},{8,9},{9,8},{10,11... | collective-permute-start | bytes 49160 | tf_op jit(solution)/shard_map/ppermute | solution.py:621
  20.3 1.9 %later.1 = (f32[5,10,32,128]{3,2,1,0:T(8,128)S(1)}, bf16[1,32,128]{2,1,0:T(8,128)(2,1)S(1)}, f32[32,128]{1,0:T(8,128)S(1)}) custom-call(bf16[2,3,4,32,128]{4,3,2,1,0:T(8,128)(2,1)S(1)} %get-tuple-element.41.flow, bf16[2,4,32,128]{3,2,1,0:T(8,128)(2,1)S(1)} %get-tuple-element.42.rho, bf16[2,4,32,128]{3,2,1,0:T(8,128)(2,1)S(1)} %get-tuple-element.43.temp, ...), custom_call_target="tpu_custom_call" | custom-call | flops 20000000 | bytes 3522560 | tf_op jit(solution)/shard_map/later/pallas_call | solution.py:650
  22.2 0.6 %collective-permute-start.5 = (bf16[1,32,128]{2,1,0:T(8,128)(2,1)S(1)}, bf16[1,32,128]{2,1,0:T(8,128)(2,1)S(1)}, u32[]{:S(2)}, u32[]{:S(2)}) collective-permute-start(bf16[1,32,128]{2,1,0:T(8,128)(2,1)S(1)} %get-tuple-element.71), channel_id=1, source_target_pairs={{0,1},{1,0},{2,3},{3,2},{4,5},{5,4},{6,7},{7,6},{8,9},{9,8},{10,11... | collective-permute-start | bytes 24584 | tf_op jit(solution)/shard_map/ppermute | solution.py:621
  22.7 0.3 middle.1
  23.0 0.9 %collective-permute-start.7 = (bf16[5,2,32,128]{3,2,1,0:T(8,128)(2,1)S(1)}, bf16[5,2,32,128]{3,2,1,0:T(8,128)(2,1)S(1)}, u32[]{:S(2)}, u32[]{:S(2)}) collective-permute-start(bf16[5,2,32,128]{3,2,1,0:T(8,128)(2,1)S(1)} %get-tuple-element.76), channel_id=1, source_target_pairs={{0,30},{2,4},{4,2},{6,8},{8,6},{10,12},{12,10},{14,16},{16,14},{18... | collective-permute-start | bytes 245768 | tf_op jit(solution)/shard_map/ppermute | solution.py:758
  23.9 2.0 %collective-permute-done.5.later_other = bf16[1,32,128]{2,1,0:T(8,128)(2,1)S(1)} collective-permute-done((bf16[1,32,128]{2,1,0:T(8,128)(2,1)S(1)}, bf16[1,32,128]{2,1,0:T(8,128)(2,1)S(1)}, u32[]{:S(2)}, u32[]{:S(2)}) %collective-permute-start.5) | collective-permute-done | bytes 8224 | tf_op jit(solution)/shard_map/ppermute | solution.py:621
  25.9 1.2 %base.1 = (f32[5,4,32,128]{3,2,1,0:T(8,128)S(1)}, f32[4,32,128]{2,1,0:T(8,128)S(1)}, f32[2,2,32,128]{3,2,1,0:T(8,128)S(1)}, f32[2,4,32]{2,1,0:T(4,128)}, bf16[5,2,32,128]{3,2,1,0:T(8,128)(2,1)S(1)}) custom-call(f32[5,10,32,128]{3,2,1,0:T(8,128)S(1)} %get-tuple-element.59.wide, f32[5,2,4,32,128]{4,3,2,1,0:T(8,128)S(1)} %get-tuple-element.48.grad_yz, ...), custom_call_target="tpu_custom_call" | custom-call | flops 15000000 | bytes 2794496 | tf_op jit(solution)/shard_map/base/pallas_call | solution.py:650
  27.1 2.6 %collective-permute-done.7.far = bf16[5,2,32,128]{3,2,1,0:T(8,128)(2,1)S(1)} collective-permute-done((bf16[5,2,32,128]{3,2,1,0:T(8,128)(2,1)S(1)}, bf16[5,2,32,128]{3,2,1,0:T(8,128)(2,1)S(1)}, u32[]{:S(2)}, u32[]{:S(2)}) %collective-permute-start.7) | collective-permute-done | bytes 81952 | tf_op jit(solution)/shard_map/ppermute | solution.py:758
  29.7 0.0 collective-permute-done.6.near_psi
  29.7 0.8 %last.1 = f32[5,4,32,128]{3,2,1,0:T(8,128)} custom-call(f32[5,4,32,128]{3,2,1,0:T(8,128)S(1)} %get-tuple-element.72.base, f32[4,32,128]{2,1,0:T(8,128)S(1)} %get-tuple-element.73.drift, f32[2,2,32,128]{3,2,1,0:T(8,128)S(1)} %get-tuple-element.74.spread, bf16[5,2,32,128]{3,2,1,0:T(8,128)(2,1)S(1)} %collective-permute-done.6.near_psi, ...), custom_call_target="tpu_custom_call" | custom-call | flops 1000000 | bytes 1032192 | tf_op jit(solution)/shard_map/last/pallas_call | solution.py:650
  (3 shorter events, 0.0 us)
Async XLA Ops:
  1.7 12.1 %collective-permute-start.1 = (bf16[36,32,128]{2,1,0:T(8,128)(2,1)S(1)}, bf16[36,32,128]{2,1,0:T(8,128)(2,1)S(1)}, u32[]{:S(2)}, u32[]{:S(2)}) collective-permute-start(bf16[36,32,128]{2,1,0:T(8,128)(2,1)S(1)} %get-tuple-element.45), channel_id=1, source_target_pairs={{0,30},{2,4},{4,2},{6,8},{8,6},{10,12},{12,10},{14,16},{16,14},{18... | collective-permute-start | bytes 884744 | tf_op jit(solution)/shard_map/ppermute | solution.py:686
  8.6 5.2 %collective-permute-start = (bf16[36,32,128]{2,1,0:T(8,128)(2,1)S(1)}, bf16[36,32,128]{2,1,0:T(8,128)(2,1)S(1)}, u32[]{:S(2)}, u32[]{:S(2)}) collective-permute-start(bf16[36,32,128]{2,1,0:T(8,128)(2,1)S(1)} %get-tuple-element.44), channel_id=1, source_target_pairs={{0,2},{2,0},{4,6},{6,4},{8,10},{10,8},{12,14},{14,12},{16,18},{18,... | collective-permute-start | bytes 884744 | tf_op jit(solution)/shard_map/ppermute | solution.py:704
  8.6 4.1 %collective-permute-start.2 = (bf16[5,32,128]{2,1,0:T(8,128)(2,1)S(1)}, bf16[5,32,128]{2,1,0:T(8,128)(2,1)S(1)}, u32[]{:S(2)}, u32[]{:S(2)}) collective-permute-start(bf16[5,32,128]{2,1,0:T(8,128)(2,1)S(1)} %get-tuple-element.47), channel_id=1, source_target_pairs={{0,1},{1,0},{2,3},{3,2},{4,5},{5,4},{6,7},{7,6},{8,9},{9,8},{10,11... | collective-permute-start | bytes 122888 | tf_op jit(solution)/shard_map/ppermute | solution.py:621
  14.0 3.8 %collective-permute-start.3 = (bf16[3,32,128]{2,1,0:T(8,128)(2,1)S(1)}, bf16[3,32,128]{2,1,0:T(8,128)(2,1)S(1)}, u32[]{:S(2)}, u32[]{:S(2)}) collective-permute-start(bf16[3,32,128]{2,1,0:T(8,128)(2,1)S(1)} %get-tuple-element.53), channel_id=1, source_target_pairs={{0,1},{1,0},{2,3},{3,2},{4,5},{5,4},{6,7},{7,6},{8,9},{9,8},{10,11... | collective-permute-start | bytes 73736 | tf_op jit(solution)/shard_map/ppermute | solution.py:621
  18.7 4.0 %collective-permute-start.4 = (bf16[2,32,128]{2,1,0:T(8,128)(2,1)S(1)}, bf16[2,32,128]{2,1,0:T(8,128)(2,1)S(1)}, u32[]{:S(2)}, u32[]{:S(2)}) collective-permute-start(bf16[2,32,128]{2,1,0:T(8,128)(2,1)S(1)} %get-tuple-element.67), channel_id=1, source_target_pairs={{0,1},{1,0},{2,3},{3,2},{4,5},{5,4},{6,7},{7,6},{8,9},{9,8},{10,11... | collective-permute-start | bytes 49160 | tf_op jit(solution)/shard_map/ppermute | solution.py:621
  22.2 3.7 %collective-permute-start.5 = (bf16[1,32,128]{2,1,0:T(8,128)(2,1)S(1)}, bf16[1,32,128]{2,1,0:T(8,128)(2,1)S(1)}, u32[]{:S(2)}, u32[]{:S(2)}) collective-permute-start(bf16[1,32,128]{2,1,0:T(8,128)(2,1)S(1)} %get-tuple-element.71), channel_id=1, source_target_pairs={{0,1},{1,0},{2,3},{3,2},{4,5},{5,4},{6,7},{7,6},{8,9},{9,8},{10,11... | collective-permute-start | bytes 24584 | tf_op jit(solution)/shard_map/ppermute | solution.py:621
  23.0 6.6 %collective-permute-start.7 = (bf16[5,2,32,128]{3,2,1,0:T(8,128)(2,1)S(1)}, bf16[5,2,32,128]{3,2,1,0:T(8,128)(2,1)S(1)}, u32[]{:S(2)}, u32[]{:S(2)}) collective-permute-start(bf16[5,2,32,128]{3,2,1,0:T(8,128)(2,1)S(1)} %get-tuple-element.76), channel_id=1, source_target_pairs={{0,30},{2,4},{4,2},{6,8},{8,6},{10,12},{12,10},{14,16},{16,14},{18... | collective-permute-start | bytes 245768 | tf_op jit(solution)/shard_map/ppermute | solution.py:758
  27.1 2.6 %collective-permute-start.6 = (bf16[5,2,32,128]{3,2,1,0:T(8,128)(2,1)S(1)}, bf16[5,2,32,128]{3,2,1,0:T(8,128)(2,1)S(1)}, u32[]{:S(2)}, u32[]{:S(2)}) collective-permute-start(bf16[5,2,32,128]{3,2,1,0:T(8,128)(2,1)S(1)} %get-tuple-element.75), channel_id=1, source_target_pairs={{0,2},{2,0},{4,6},{6,4},{8,10},{10,8},{12,14},{14,12},{16,18},{18,... | collective-permute-start | bytes 245768 | tf_op jit(solution)/shard_map/ppermute | solution.py:770

commit v8 on v7

--- a/solution.py
+++ b/solution.py
@@ -178,8 +178,8 @@
             for i in range(3):
                 out[VELOCITY + t * 9 + k * 3 + i] = flow[t, k, side + i]
         for i in range(2):
-            out[SCALARS + t * 4 + i] = rho[t, 2 * side + i]
-            out[SCALARS + t * 4 + 2 + i] = temp[t, 2 * side + i]
+            out[SCALARS + 2 * t + i] = rho[t, 2 * side + i]
+            out[SCALARS + 4 + 2 * t + i] = temp[t, 2 * side + i]
     for k in range(5):
         for i in range(2):
             out[PSI + k * 2 + i] = psi[k, 2 * side + i].astype(BF16)
@@ -187,14 +187,19 @@
 
 def message_kernel(flow_far, rho_far, temp_far, psi_far, far, outer, sems):
     side = 1 - is_even().astype(jnp.int32)
-    pieces = [(psi_far.at[:, pl.ds(2 * side, 2)], outer)]
-    for t in range(2):
-        for k in range(3):
-            target = far.at[pl.ds(VELOCITY + t * 9 + k * 3, 3)]
-            pieces.append((flow_far.at[t, k, pl.ds(side, 3)], target))
-        for number, source in enumerate((rho_far, temp_far)):
-            target = far.at[pl.ds(SCALARS + t * 4 + 2 * number, 2)]
-            pieces.append((source.at[t, pl.ds(2 * side, 2)], target))
+    block = (ROWS, LANES)
+    pieces = [
+        (psi_far.at[:, pl.ds(2 * side, 2)], outer),
+        (
+            flow_far.at[:, :, pl.ds(side, 3)],
+            far.at[pl.ds(VELOCITY, 18)].reshape((2, 3, 3) + block),
+        ),
+        (rho_far.at[:, pl.ds(2 * side, 2)], far.at[pl.ds(SCALARS, 4)].reshape((2, 2) + block)),
+        (
+            temp_far.at[:, pl.ds(2 * side, 2)],
+            far.at[pl.ds(SCALARS + 4, 4)].reshape((2, 2) + block),
+        ),
+    ]
     copies = [
         pltpu.make_async_copy(source, target, sems.at[number])
         for number, (source, target) in enumerate(pieces)
@@ -274,6 +279,10 @@
             psi_lap[k, x] = lap
 
 
+def token_kernel(far, out):
+    out[...] = far[0].astype(F32)
+
+
 def bands_kernel(own_low, near, far, _, message, low):
     ops = Ops()
     even = is_even()
@@ -325,7 +334,7 @@
     for k in range(3):
         widen(k, lambda x: flow[t, k, x], VELOCITY + t * 9 + k * 3, 3, even, near, far, wide)
     for k, source in ((3, rho), (4, temp)):
-        number = SCALARS + t * 4 + (k - 3) * 2
+        number = SCALARS + (k - 3) * 4 + 2 * t
         widen(k, lambda x: source[t, x], number, 2, even, near, far, wide)
     for x in range(-1, CX + 1):
         grad = [[None] * 3 for _ in range(3)]
@@ -680,7 +689,7 @@
         inputs,
         [shape_of((MESSAGE,), BF16), shape_of((5, 2))],
         1_000_000,
-        [pltpu.SemaphoreType.DMA((11,))],
+        [pltpu.SemaphoreType.DMA((4,))],
         stay,
     )
     far = lax.ppermute(far, "gx", across)
@@ -711,10 +720,11 @@
         5_000_000,
         scratch((2, 5, CX), (5, CX)),
     )
+    (token,) = call(token_kernel, "token", (far,), [shape_of(())], 100_000)
     message, low = call(
         bands_kernel,
         "bands",
-        (own_low, near, far, psi_lap),
+        (own_low, near, far, token),
         [shape_of((BAND_BLOCKS,), BF16), shape_of((6,))],
         1_000_000,
     )

time: 30.7 us -> 29.4 us (0.958)
  waiting for transfers between devices: 7.71 us -> 3.73 us
  starting transfers between devices: 11.7 us -> 14.5 us
    ppermute x4, waiting for transfers between devices: 5.12 us -> 0.01 us  [span_edges(): before = lax.ppermute(message, 'gz', forward)]
    ppermute x2, starting transfers between devices: 6.38 us -> 8.68 us  [local(): far = lax.ppermute(far, 'gx', across)]
    ppermute x2, waiting for transfers between devices: 2.59 us -> 3.71 us  [local(): far = lax.ppermute(far, 'gx', across)]
    ppermute x4, starting transfers between devices: 5.27 us -> 5.74 us  [span_edges(): before = lax.ppermute(message, 'gz', forward)]
    pallas_call x11 -> x12, Pallas kernels: 10.4 us -> 10.4 us  [call(): pl.pallas_call(kernel, in_specs=in_specs or whole(len(inputs)), out_specs...]
  transfers between devices with their start and end apart: 8 -> 8, of which waited for: 4 -> 2; matrix products, arithmetic and copies ran while one was open for 0% -> 0% of each run, Pallas kernels for 24% -> 26%
where the time goes in v8:
time: 29.4 us; the launch traced here: 29.3 us
  starting transfers between devices  14.5 us (49%)
  Pallas kernels  10.4 us (35%)
  waiting for transfers between devices  3.73 us (13%)
  between operations  0.7 us (2%)
    pallas_call x12, Pallas kernels, call(): pl.pallas_call(kernel, in_specs=in_specs or whole(len(inputs)), out_specs...  10.4 us
    ppermute x2, starting transfers between devices, local(): far = lax.ppermute(far, 'gx', across)  8.68 us
    ppermute x4, starting transfers between devices, span_edges(): before = lax.ppermute(message, 'gz', forward)  5.74 us
    ppermute x2, waiting for transfers between devices, local(): far = lax.ppermute(far, 'gx', across)  3.71 us
  transfers between devices with their start and end apart: 8, of which 2 were waited for; matrix products, arithmetic and copies ran while one was open for 0% of the time, Pallas kernels for 26%

profile of v8, /device:TPU:0, one launch (start us, length us, event | category | flops | bytes accessed | tf_op | source)
XLA Modules:
  0.0 29.3 jit_solution(6464198414789800806)
XLA Ops:
  0.6 1.0 %message.1 = (bf16[36,32,128]{2,1,0:T(8,128)(2,1)S(1)}, f32[5,2,32,128]{3,2,1,0:T(8,128)S(1)}) custom-call(bf16[2,3,4,32,128]{4,3,2,1,0:T(8,128)(2,1)} %flow_far.3, bf16[2,4,32,128]{3,2,1,0:T(8,128)(2,1)} %rho_far.3, bf16[2,4,32,128]{3,2,1,0:T(8,128)(2,1)} %temp_far.3, f32[5,4,32,128]{3,2,1,0:T(8,128)} %psi_far.3), custom_call_target="tpu_custom_call" | custom-call | flops 1000000 | bytes 1114112 | tf_op jit(solution)/shard_map/message/pallas_call | solution.py:659
  1.7 5.5 %collective-permute-start.1 = (bf16[36,32,128]{2,1,0:T(8,128)(2,1)S(1)}, bf16[36,32,128]{2,1,0:T(8,128)(2,1)S(1)}, u32[]{:S(2)}, u32[]{:S(2)}) collective-permute-start(bf16[36,32,128]{2,1,0:T(8,128)(2,1)S(1)} %get-tuple-element.45), channel_id=1, source_target_pairs={{0,30},{2,4},{4,2},{6,8},{8,6},{10,12},{12,10},{14,16},{16,14},{18... | collective-permute-start | bytes 884744 | tf_op jit(solution)/shard_map/ppermute | solution.py:695
  7.2 1.4 %pack.1 = (bf16[36,32,128]{2,1,0:T(8,128)(2,1)S(1)}, bf16[5,32,128]{2,1,0:T(8,128)(2,1)S(1)}, f32[6,32,128]{2,1,0:T(8,128)S(1)}, bf16[2,3,4,32,128]{4,3,2,1,0:T(...) custom-call(bf16[2,3,4,32,128]{4,3,2,1,0:T(8,128)(2,1)} %flow_far.3,, ...), custom_call_target="tpu_custom_call" | custom-call | flops 2000000 | bytes 1908736 | tf_op jit(solution)/shard_map/pack/pallas_call | solution.py:659
  8.5 0.1 collective-permute-start
  8.6 1.6 %collective-permute-start.2 = (bf16[5,32,128]{2,1,0:T(8,128)(2,1)S(1)}, bf16[5,32,128]{2,1,0:T(8,128)(2,1)S(1)}, u32[]{:S(2)}, u32[]{:S(2)}) collective-permute-start(bf16[5,32,128]{2,1,0:T(8,128)(2,1)S(1)} %get-tuple-element.47), channel_id=1, source_target_pairs={{0,1},{1,0},{2,3},{3,2},{4,5},{5,4},{6,7},{7,6},{8,9},{9,8},{10,11... | collective-permute-start | bytes 122888 | tf_op jit(solution)/shard_map/ppermute | solution.py:630
  10.2 1.5 %collective-permute-done.1.far = bf16[36,32,128]{2,1,0:T(8,128)(2,1)S(1)} collective-permute-done((bf16[36,32,128]{2,1,0:T(8,128)(2,1)S(1)}, bf16[36,32,128]{2,1,0:T(8,128)(2,1)S(1)}, u32[]{:S(2)}, u32[]{:S(2)}) %collective-permute-start.1) | collective-permute-done | bytes 294944 | tf_op jit(solution)/shard_map/ppermute | solution.py:695
  11.7 0.0 collective-permute-done.near
  11.7 0.2 bands.1
  11.9 2.0 %collective-permute-start.3 = (bf16[3,32,128]{2,1,0:T(8,128)(2,1)S(1)}, bf16[3,32,128]{2,1,0:T(8,128)(2,1)S(1)}, u32[]{:S(2)}, u32[]{:S(2)}) collective-permute-start(bf16[3,32,128]{2,1,0:T(8,128)(2,1)S(1)} %get-tuple-element.52), channel_id=1, source_target_pairs={{0,1},{1,0},{2,3},{3,2},{4,5},{5,4},{6,7},{7,6},{8,9},{9,8},{10,11... | collective-permute-start | bytes 73736 | tf_op jit(solution)/shard_map/ppermute | solution.py:630
  13.9 0.0 collective-permute-done.2.own_halo
  13.9 1.1 %own.1 = (f32[5,2,4,32,128]{4,3,2,1,0:T(8,128)S(1)}, f32[5,2,4,32,128]{4,3,2,1,0:T(8,128)S(1)}, f32[5,4,32,128]{3,2,1,0:T(8,128)S(1)}, f32[5,4,32,128]{3,2,1,0:T...) custom-call(bf16[2,3,4,32,128]{4,3,2,1,0:T(8,128)(2,1)S(1)} %get-tuple-element.41.flow, ...), custom_call_target="tpu_custom_call" | custom-call | flops 5000000 | bytes 3317760 | tf_op jit(solution)/shard_map/own/pallas_call | solution.py:659
  15.0 1.6 %inner.1 = (f32[2,4,32,128]{3,2,1,0:T(8,128)S(1)}, f32[3,32,128]{2,1,0:T(8,128)S(1)}, f32[5,4,32,128]{3,2,1,0:T(8,128)S(1)}, f32[5,4,32,128]{3,2,1,0:T(8,128)S(1...) custom-call(bf16[2,3,4,32,128]{4,3,2,1,0:T(8,128)(2,1)S(1)} %get-tuple-element.41.flow, ...), custom_call_target="tpu_custom_call" | custom-call | flops 20000000 | bytes 3768320 | tf_op jit(solution)/shard_map/inner/pallas_call | solution.py:659
  16.6 0.0 collective-permute-done.3.halo
  16.6 0.9 %edge.1 = (bf16[2,32,128]{2,1,0:T(8,128)(2,1)S(1)}, f32[32,128]{1,0:T(8,128)S(1)}) custom-call(f32[6,32,128]{2,1,0:T(8,128)S(1)} %get-tuple-element.51.low, f32[3,32,128]{2,1,0:T(8,128)S(1)} %get-tuple-element.62.high, bf16[3,32,128]{2,1,0:T(8,128)(2,1)S(1)} %collective-permute-done.3.halo, f32[2,4,32,128]{3,2,1,0:T(8,128)S(1)} %get-tuple-element.63.inner, ...), custom_call_target="tpu_custom_call" | custom-call | flops 20000000 | bytes 385024 | tf_op jit(solution)/shard_map/edge/pallas_call | solution.py:659
  17.5 1.2 %collective-permute-start.4 = (bf16[2,32,128]{2,1,0:T(8,128)(2,1)S(1)}, bf16[2,32,128]{2,1,0:T(8,128)(2,1)S(1)}, u32[]{:S(2)}, u32[]{:S(2)}) collective-permute-start(bf16[2,32,128]{2,1,0:T(8,128)(2,1)S(1)} %get-tuple-element.67), channel_id=1, source_target_pairs={{0,1},{1,0},{2,3},{3,2},{4,5},{5,4},{6,7},{7,6},{8,9},{9,8},{10,11... | collective-permute-start | bytes 49160 | tf_op jit(solution)/shard_map/ppermute | solution.py:630
  18.7 1.9 %later.1 = (f32[5,10,32,128]{3,2,1,0:T(8,128)S(1)}, bf16[1,32,128]{2,1,0:T(8,128)(2,1)S(1)}, f32[32,128]{1,0:T(8,128)S(1)}) custom-call(bf16[2,3,4,32,128]{4,3,2,1,0:T(8,128)(2,1)S(1)} %get-tuple-element.41.flow, bf16[2,4,32,128]{3,2,1,0:T(8,128)(2,1)S(1)} %get-tuple-element.42.rho, bf16[2,4,32,128]{3,2,1,0:T(8,128)(2,1)S(1)} %get-tuple-element.43.temp, ...), custom_call_target="tpu_custom_call" | custom-call | flops 20000000 | bytes 3522560 | tf_op jit(solution)/shard_map/later/pallas_call | solution.py:659
  20.5 1.0 %collective-permute-start.5 = (bf16[1,32,128]{2,1,0:T(8,128)(2,1)S(1)}, bf16[1,32,128]{2,1,0:T(8,128)(2,1)S(1)}, u32[]{:S(2)}, u32[]{:S(2)}) collective-permute-start(bf16[1,32,128]{2,1,0:T(8,128)(2,1)S(1)} %get-tuple-element.71), channel_id=1, source_target_pairs={{0,1},{1,0},{2,3},{3,2},{4,5},{5,4},{6,7},{7,6},{8,9},{9,8},{10,11... | collective-permute-start | bytes 24584 | tf_op jit(solution)/shard_map/ppermute | solution.py:630
  21.5 0.3 middle.1
  21.8 3.2 %collective-permute-start.7 = (bf16[5,2,32,128]{3,2,1,0:T(8,128)(2,1)S(1)}, bf16[5,2,32,128]{3,2,1,0:T(8,128)(2,1)S(1)}, u32[]{:S(2)}, u32[]{:S(2)}) collective-permute-start(bf16[5,2,32,128]{3,2,1,0:T(8,128)(2,1)S(1)} %get-tuple-element.76), channel_id=1, source_target_pairs={{0,30},{2,4},{4,2},{6,8},{8,6},{10,12},{12,10},{14,16},{16,14},{18... | collective-permute-start | bytes 245768 | tf_op jit(solution)/shard_map/ppermute | solution.py:768
  25.0 1.2 %base.1 = (f32[5,4,32,128]{3,2,1,0:T(8,128)S(1)}, f32[4,32,128]{2,1,0:T(8,128)S(1)}, f32[2,2,32,128]{3,2,1,0:T(8,128)S(1)}, f32[2,4,32]{2,1,0:T(4,128)}, bf16[5,2,32,128]{3,2,1,0:T(8,128)(2,1)S(1)}) custom-call(f32[5,10,32,128]{3,2,1,0:T(8,128)S(1)} %get-tuple-element.59.wide, f32[5,2,4,32,128]{4,3,2,1,0:T(8,128)S(1)} %get-tuple-element.48.grad_yz, ...), custom_call_target="tpu_custom_call" | custom-call | flops 15000000 | bytes 2794496 | tf_op jit(solution)/shard_map/base/pallas_call | solution.py:659
  26.2 0.0 collective-permute-start.6
  26.2 2.2 %collective-permute-done.7.far = bf16[5,2,32,128]{3,2,1,0:T(8,128)(2,1)S(1)} collective-permute-done((bf16[5,2,32,128]{3,2,1,0:T(8,128)(2,1)S(1)}, bf16[5,2,32,128]{3,2,1,0:T(8,128)(2,1)S(1)}, u32[]{:S(2)}, u32[]{:S(2)}) %collective-permute-start.7) | collective-permute-done | bytes 81952 | tf_op jit(solution)/shard_map/ppermute | solution.py:768
  28.4 0.0 collective-permute-done.6.near_psi
  28.5 0.8 %last.1 = f32[5,4,32,128]{3,2,1,0:T(8,128)} custom-call(f32[5,4,32,128]{3,2,1,0:T(8,128)S(1)} %get-tuple-element.72.base, f32[4,32,128]{2,1,0:T(8,128)S(1)} %get-tuple-element.73.drift, f32[2,2,32,128]{3,2,1,0:T(8,128)S(1)} %get-tuple-element.74.spread, bf16[5,2,32,128]{3,2,1,0:T(8,128)(2,1)S(1)} %collective-permute-done.6.near_psi, ...), custom_call_target="tpu_custom_call" | custom-call | flops 1000000 | bytes 1032192 | tf_op jit(solution)/shard_map/last/pallas_call | solution.py:659
  (4 shorter events, 0.0 us)
Async XLA Ops:
  1.7 10.0 %collective-permute-start.1 = (bf16[36,32,128]{2,1,0:T(8,128)(2,1)S(1)}, bf16[36,32,128]{2,1,0:T(8,128)(2,1)S(1)}, u32[]{:S(2)}, u32[]{:S(2)}) collective-permute-start(bf16[36,32,128]{2,1,0:T(8,128)(2,1)S(1)} %get-tuple-element.45), channel_id=1, source_target_pairs={{0,30},{2,4},{4,2},{6,8},{8,6},{10,12},{12,10},{14,16},{16,14},{18... | collective-permute-start | bytes 884744 | tf_op jit(solution)/shard_map/ppermute | solution.py:695
  8.5 3.1 %collective-permute-start = (bf16[36,32,128]{2,1,0:T(8,128)(2,1)S(1)}, bf16[36,32,128]{2,1,0:T(8,128)(2,1)S(1)}, u32[]{:S(2)}, u32[]{:S(2)}) collective-permute-start(bf16[36,32,128]{2,1,0:T(8,128)(2,1)S(1)} %get-tuple-element.44), channel_id=1, source_target_pairs={{0,2},{2,0},{4,6},{6,4},{8,10},{10,8},{12,14},{14,12},{16,18},{18,... | collective-permute-start | bytes 884744 | tf_op jit(solution)/shard_map/ppermute | solution.py:713
  8.6 5.3 %collective-permute-start.2 = (bf16[5,32,128]{2,1,0:T(8,128)(2,1)S(1)}, bf16[5,32,128]{2,1,0:T(8,128)(2,1)S(1)}, u32[]{:S(2)}, u32[]{:S(2)}) collective-permute-start(bf16[5,32,128]{2,1,0:T(8,128)(2,1)S(1)} %get-tuple-element.47), channel_id=1, source_target_pairs={{0,1},{1,0},{2,3},{3,2},{4,5},{5,4},{6,7},{7,6},{8,9},{9,8},{10,11... | collective-permute-start | bytes 122888 | tf_op jit(solution)/shard_map/ppermute | solution.py:630
  11.9 4.7 %collective-permute-start.3 = (bf16[3,32,128]{2,1,0:T(8,128)(2,1)S(1)}, bf16[3,32,128]{2,1,0:T(8,128)(2,1)S(1)}, u32[]{:S(2)}, u32[]{:S(2)}) collective-permute-start(bf16[3,32,128]{2,1,0:T(8,128)(2,1)S(1)} %get-tuple-element.52), channel_id=1, source_target_pairs={{0,1},{1,0},{2,3},{3,2},{4,5},{5,4},{6,7},{7,6},{8,9},{9,8},{10,11... | collective-permute-start | bytes 73736 | tf_op jit(solution)/shard_map/ppermute | solution.py:630
  17.5 4.0 %collective-permute-start.4 = (bf16[2,32,128]{2,1,0:T(8,128)(2,1)S(1)}, bf16[2,32,128]{2,1,0:T(8,128)(2,1)S(1)}, u32[]{:S(2)}, u32[]{:S(2)}) collective-permute-start(bf16[2,32,128]{2,1,0:T(8,128)(2,1)S(1)} %get-tuple-element.67), channel_id=1, source_target_pairs={{0,1},{1,0},{2,3},{3,2},{4,5},{5,4},{6,7},{7,6},{8,9},{9,8},{10,11... | collective-permute-start | bytes 49160 | tf_op jit(solution)/shard_map/ppermute | solution.py:630
  20.5 4.5 %collective-permute-start.5 = (bf16[1,32,128]{2,1,0:T(8,128)(2,1)S(1)}, bf16[1,32,128]{2,1,0:T(8,128)(2,1)S(1)}, u32[]{:S(2)}, u32[]{:S(2)}) collective-permute-start(bf16[1,32,128]{2,1,0:T(8,128)(2,1)S(1)} %get-tuple-element.71), channel_id=1, source_target_pairs={{0,1},{1,0},{2,3},{3,2},{4,5},{5,4},{6,7},{7,6},{8,9},{9,8},{10,11... | collective-permute-start | bytes 24584 | tf_op jit(solution)/shard_map/ppermute | solution.py:630
  21.8 6.6 %collective-permute-start.7 = (bf16[5,2,32,128]{3,2,1,0:T(8,128)(2,1)S(1)}, bf16[5,2,32,128]{3,2,1,0:T(8,128)(2,1)S(1)}, u32[]{:S(2)}, u32[]{:S(2)}) collective-permute-start(bf16[5,2,32,128]{3,2,1,0:T(8,128)(2,1)S(1)} %get-tuple-element.76), channel_id=1, source_target_pairs={{0,30},{2,4},{4,2},{6,8},{8,6},{10,12},{12,10},{14,16},{16,14},{18... | collective-permute-start | bytes 245768 | tf_op jit(solution)/shard_map/ppermute | solution.py:768
  26.2 2.3 %collective-permute-start.6 = (bf16[5,2,32,128]{3,2,1,0:T(8,128)(2,1)S(1)}, bf16[5,2,32,128]{3,2,1,0:T(8,128)(2,1)S(1)}, u32[]{:S(2)}, u32[]{:S(2)}) collective-permute-start(bf16[5,2,32,128]{3,2,1,0:T(8,128)(2,1)S(1)} %get-tuple-element.75), channel_id=1, source_target_pairs={{0,2},{2,0},{4,6},{6,4},{8,10},{10,8},{12,14},{14,12},{16,18},{18,... | collective-permute-start | bytes 245768 | tf_op jit(solution)/shard_map/ppermute | solution.py:780

commit v9 on v8

--- a/solution.py
+++ b/solution.py
@@ -28,8 +28,8 @@
 BAND_BLOCKS = 3
 VELOCITY = 0
 SCALARS = 18
-PSI = 26
-MESSAGE = 36
+PSI = 8
+SCALAR_PLANES = 18
 
 
 def lane_ids():
@@ -172,46 +172,14 @@
     return lax.rem(lax.axis_index("gx"), 2) == 0
 
 
-def fill_message(out, side, flow, rho, temp, psi):
+def fill_scalars(out, side, rho, temp, psi):
     for t in range(2):
-        for k in range(3):
-            for i in range(3):
-                out[VELOCITY + t * 9 + k * 3 + i] = flow[t, k, side + i]
         for i in range(2):
-            out[SCALARS + 2 * t + i] = rho[t, 2 * side + i]
-            out[SCALARS + 4 + 2 * t + i] = temp[t, 2 * side + i]
+            out[2 * t + i] = rho[t, 2 * side + i]
+            out[4 + 2 * t + i] = temp[t, 2 * side + i]
     for k in range(5):
         for i in range(2):
             out[PSI + k * 2 + i] = psi[k, 2 * side + i].astype(BF16)
-
-
-def message_kernel(flow_far, rho_far, temp_far, psi_far, far, outer, sems):
-    side = 1 - is_even().astype(jnp.int32)
-    block = (ROWS, LANES)
-    pieces = [
-        (psi_far.at[:, pl.ds(2 * side, 2)], outer),
-        (
-            flow_far.at[:, :, pl.ds(side, 3)],
-            far.at[pl.ds(VELOCITY, 18)].reshape((2, 3, 3) + block),
-        ),
-        (rho_far.at[:, pl.ds(2 * side, 2)], far.at[pl.ds(SCALARS, 4)].reshape((2, 2) + block)),
-        (
-            temp_far.at[:, pl.ds(2 * side, 2)],
-            far.at[pl.ds(SCALARS + 4, 4)].reshape((2, 2) + block),
-        ),
-    ]
-    copies = [
-        pltpu.make_async_copy(source, target, sems.at[number])
-        for number, (source, target) in enumerate(pieces)
-    ]
-    for copy in copies:
-        copy.start()
-    copies[0].wait()
-    for k in range(5):
-        for i in range(2):
-            far[PSI + k * 2 + i] = outer[k, i].astype(BF16)
-    for copy in copies[1:]:
-        copy.wait()
 
 
 def merge_bands(ops, low, message, first):
@@ -221,8 +189,19 @@
         message[first + number] = both.astype(BF16)
 
 
+def message_kernel(flow_far, rho_far, temp_far, psi_far, far, ahead, sem):
+    side = 1 - is_even().astype(jnp.int32)
+    copy = pltpu.make_async_copy(
+        flow_far.at[:, :, pl.ds(side, 3)], far.reshape((2, 3, 3, ROWS, LANES)), sem
+    )
+    copy.start()
+    ahead[...] = jnp.zeros((ROWS, LANES), F32)
+    copy.wait()
+
+
 def pack_kernel(
-    flow_far, rho_far, temp_far, psi_far, _, near, message, low, flow, rho, temp, psi, sems
+    flow_far, rho_far, temp_far, psi_far, _,
+    near, near_scalars, far_scalars, message, low, flow, rho, temp, psi, sems,
 ):
     copies = [
         pltpu.make_async_copy(source, target, sems.at[i])
@@ -235,7 +214,13 @@
     ops = Ops()
     for copy in copies:
         copy.wait()
-    fill_message(near, is_even().astype(jnp.int32), flow, rho, temp, psi)
+    side = is_even().astype(jnp.int32)
+    for t in range(2):
+        for k in range(3):
+            for i in range(3):
+                near[VELOCITY + t * 9 + k * 3 + i] = flow[t, k, side + i]
+    fill_scalars(near_scalars, side, rho, temp, psi)
+    fill_scalars(far_scalars, 1 - side, rho, temp, psi)
     items = []
     for t in range(2):
         for source in (rho, temp):
@@ -318,24 +303,39 @@
     return cross, square
 
 
-def widen(k, source, number, count, even, near, far, wide):
+def widen(k, source, near, far, count, even, wide):
     for i in range(count):
-        one, two = near[number + i].astype(F32), far[number + i].astype(F32)
+        one, two = near(i), far(i)
         wide[k, 3 - count + i] = jnp.where(even, two, one)
         wide[k, 3 + CX + i] = jnp.where(even, one, two)
     for x in range(CX):
         wide[k, 3 + x] = source(x).astype(F32)
 
 
-def inner_products(ops, t, flow, rho, temp, near, far, grad_yz, sums, high, wide, fields, hats):
+def widen_scalars(t, rho, temp, near, far, even, wide):
+    for k, source in ((3, rho), (4, temp)):
+        number = (k - 3) * 4 + 2 * t
+        widen(
+            k,
+            lambda x: source[t, x],
+            lambda i: near[number + i].astype(F32),
+            lambda i: far[number + i].astype(F32),
+            2, even, wide,
+        )
+
+
+def inner_products(ops, t, flow, near, far, grad_yz, sums, high, wide, fields, hats):
     even = is_even()
     valid = (ops.lane >= 3) & (ops.lane < LANES - 3)
     band = band_of(jnp.maximum(ops.lane - 2, 0))
     for k in range(3):
-        widen(k, lambda x: flow[t, k, x], VELOCITY + t * 9 + k * 3, 3, even, near, far, wide)
-    for k, source in ((3, rho), (4, temp)):
-        number = SCALARS + (k - 3) * 4 + 2 * t
-        widen(k, lambda x: source[t, x], number, 2, even, near, far, wide)
+        widen(
+            k,
+            lambda x: flow[t, k, x],
+            lambda i: near[VELOCITY + t * 9 + k * 3 + i].astype(F32),
+            lambda i: far[VELOCITY + t * 9 + k * 3 + i].astype(F32),
+            3, even, wide,
+        )
     for x in range(-1, CX + 1):
         grad = [[None] * 3 for _ in range(3)]
         for k in range(3):
@@ -438,18 +438,29 @@
     return rates, laps
 
 
-def inner_kernel(
-    flow, rho, temp, psi, near, far, grad_yz, lap_yz, psi_rate, psi_lap,
-    sums, high, first, second, message, columns,
-    wide, psi_wide, fields, hats, work,
+def inner_kernel(flow, near, far, grad_yz, sums, high, wide, fields, hats):
+    inner_products(Ops(), 0, flow, near, far, grad_yz, sums, high, wide, fields, hats)
+
+
+def first_kernel(
+    rho, temp, psi, near, far, velocity, grad_yz, lap_yz, psi_rate, psi_lap,
+    first, second, message, columns,
+    wide, psi_wide, work,
 ):
     ops = Ops()
     even = is_even()
-    for k in range(5):
-        widen(k, lambda x: psi[k, x], PSI + k * 2, 2, even, near, far, psi_wide)
-    inner_products(
-        ops, 0, flow, rho, temp, near, far, grad_yz, sums, high, wide, fields, hats
-    )
+    for k in range(3):
+        for i in range(1, CX + 5):
+            wide[k, i] = velocity[k, i]
+    widen_scalars(0, rho, temp, near, far, even, wide)
+    for k in range(5):
+        widen(
+            k,
+            lambda x: psi[k, x],
+            lambda i: near[PSI + k * 2 + i].astype(F32),
+            lambda i: far[PSI + k * 2 + i].astype(F32),
+            2, even, psi_wide,
+        )
     for x in range(CX):
         terms = state_terms(wide, grad_yz, lap_yz, x)
         rates, laps = psi_terms(psi_wide, psi_rate, psi_lap, terms[0][0], x)
@@ -483,14 +494,14 @@
 
 
 def later_kernel(
-    flow, rho, temp, near, far, grad_yz, lap_yz, low, halo, first, second,
+    flow, rho, temp, near, far, near_scalars, far_scalars,
+    grad_yz, lap_yz, low, halo, first, second,
     wide, message, columns,
     high, fields, hats, work, bands, spread, sums,
 ):
     ops = Ops()
-    inner_products(
-        ops, 1, flow, rho, temp, near, far, grad_yz, sums, high, wide, fields, hats
-    )
+    inner_products(ops, 1, flow, near, far, grad_yz, sums, high, wide, fields, hats)
+    widen_scalars(1, rho, temp, near_scalars, far_scalars, is_even(), wide)
     edge_products(ops, 1, low, high, halo, sums, bands, spread)
     for x in range(CX):
         _, _, lap, size, inv_rho = state_terms(wide, grad_yz, lap_yz, x)
@@ -683,22 +694,24 @@
     slopes = shape_of((5, 2, CX))
     inputs = (flow_far, rho_far, temp_far, psi_far)
     stay = [pl.BlockSpec(memory_space=pltpu.MemorySpace.HBM)] * 4
-    far, outer = call(
+    far, ahead = call(
         message_kernel,
         "message",
         inputs,
-        [shape_of((MESSAGE,), BF16), shape_of((5, 2))],
+        [shape_of((SCALARS,), BF16), shape_of(())],
         1_000_000,
-        [pltpu.SemaphoreType.DMA((4,))],
+        [pltpu.SemaphoreType.DMA(())],
         stay,
     )
     far = lax.ppermute(far, "gx", across)
-    near, message, own_low, flow, rho, temp, psi = call(
+    near, near_scalars, far_scalars, message, own_low, flow, rho, temp, psi = call(
         pack_kernel,
         "pack",
-        inputs + (outer,),
+        inputs + (ahead,),
         [
-            shape_of((MESSAGE,), BF16),
+            shape_of((SCALARS,), BF16),
+            shape_of((SCALAR_PLANES,), BF16),
+            shape_of((SCALAR_PLANES,), BF16),
             shape_of((STRIP_BLOCKS + BAND_BLOCKS,), BF16),
             shape_of((6,)),
             shape_of((2, 3, CX), BF16),
@@ -710,7 +723,9 @@
         [pltpu.SemaphoreType.DMA((4,))],
         stay + whole(1),
     )
+    far_scalars = lax.ppermute(far_scalars, "gx", across)
     near = lax.ppermute(near, "gx", inside)
+    near_scalars = lax.ppermute(near_scalars, "gx", inside)
     own_halo = span_edges(message, STRIP_BLOCKS)
     grad_0, grad_1, lap_0, lap_1, psi_rate, psi_lap = call(
         own_kernel,
@@ -729,13 +744,21 @@
         1_000_000,
     )
     halo = span_edges(message, 0)
-    inner, high, first, second, strips, sensitivity = call(
+    inner, high, velocity = call(
         inner_kernel,
         "inner",
-        (flow, rho, temp, psi, near, far, grad_0, lap_0, psi_rate, psi_lap),
-        [shape_of((2, CX)), shape_of((3,)), field, field, shape_of((2,)), shape_of(())],
+        (flow, near, far, grad_0),
+        [shape_of((2, CX)), shape_of((3,)), shape_of((3, CX + 6))],
         20_000_000,
-        scratch((5, CX + 6), (5, CX + 6), (21, CX + 2), (21, CX), (CX,)),
+        scratch((21, CX + 2), (21, CX)),
+    )
+    first, second, strips, sensitivity = call(
+        first_kernel,
+        "first",
+        (rho, temp, psi, near_scalars, far_scalars, velocity, grad_0, lap_0, psi_rate, psi_lap),
+        [field, field, shape_of((2,)), shape_of(())],
+        10_000_000,
+        scratch((5, CX + 6), (5, CX + 6), (CX,)),
     )
     message, columns = call(
         edge_kernel,
@@ -750,7 +773,10 @@
     wide, message, later = call(
         later_kernel,
         "later",
-        (flow, rho, temp, near, far, grad_1, lap_1, low, halo, first, second),
+        (
+            flow, rho, temp, near, far, near_scalars, far_scalars,
+            grad_1, lap_1, low, halo, first, second,
+        ),
         [planes, shape_of((1,), BF16), shape_of(())],
         20_000_000,
         scratch((3,), (21, CX + 2), (21, CX), (2, CX), (2, 3), (21,), (2, CX)),

time: 29.4 us -> 29.9 us (1.017)
  waiting for transfers between devices: 3.73 us -> 5.5 us
  starting transfers between devices: 14.5 us -> 13.2 us
    ppermute x4, waiting for transfers between devices: 0.01 us -> 2.03 us  [span_edges(): before = lax.ppermute(message, 'gz', forward)]
    ppermute x2, waiting for transfers between devices: 3.71 us -> 2.59 us  [local(): far = lax.ppermute(far, 'gx', across)]
    ppermute x2, starting transfers between devices: 8.68 us -> 7.59 us  [local(): far = lax.ppermute(far, 'gx', across)]
    ppermute x4, starting transfers between devices: 5.74 us -> 4.73 us  [span_edges(): before = lax.ppermute(message, 'gz', forward)]
    ppermute x0 -> x2, waiting for transfers between devices: none -> 0.87 us  [the longest x1 0.86 us: local(): far_scalars = lax.ppermute(far_scalars, 'gx', across)]
    ppermute x0 -> x2, starting transfers between devices: none -> 0.76 us  [the longest x1 0.5 us: local(): near_scalars = lax.ppermute(near_scalars, 'gx', inside)]
    pallas_call x12 -> x13, Pallas kernels: 10.4 us -> 10.4 us  [call(): pl.pallas_call(kernel, in_specs=in_specs or whole(len(inputs)), out_specs...]
  transfers between devices with their start and end apart: 8 -> 10, of which waited for: 2 -> 4; matrix products, arithmetic and copies ran while one was open for 0% -> 0% of each run, Pallas kernels for 26% -> 26%
where the time goes in v9:
time: 29.9 us; the launch traced here: 29.7 us
  starting transfers between devices  13.2 us (44%)
  Pallas kernels  10.4 us (35%)
  waiting for transfers between devices  5.5 us (18%)
  between operations  0.72 us (2%)
    pallas_call x13, Pallas kernels, call(): pl.pallas_call(kernel, in_specs=in_specs or whole(len(inputs)), out_specs...  10.4 us
    ppermute x2, starting transfers between devices, local(): far = lax.ppermute(far, 'gx', across)  7.59 us
    ppermute x4, starting transfers between devices, span_edges(): before = lax.ppermute(message, 'gz', forward)  4.73 us
    ppermute x2, waiting for transfers between devices, local(): far = lax.ppermute(far, 'gx', across)  2.59 us
    ppermute x4, waiting for transfers between devices, span_edges(): before = lax.ppermute(message, 'gz', forward)  2.03 us
    ppermute x1, waiting for transfers between devices, local(): far_scalars = lax.ppermute(far_scalars, 'gx', across)  0.86 us
  transfers between devices with their start and end apart: 10, of which 4 were waited for; matrix products, arithmetic and copies ran while one was open for 0% of the time, Pallas kernels for 26%

profile of v9, /device:TPU:0, one launch (start us, length us, event | category | flops | bytes accessed | tf_op | source)
XLA Modules:
  0.0 29.7 jit_solution(9153454907336363409)
XLA Ops:
  0.6 0.9 %message.1 = (bf16[18,32,128]{2,1,0:T(8,128)(2,1)S(1)}, f32[32,128]{1,0:T(8,128)S(1)}) custom-call(bf16[2,3,4,32,128]{4,3,2,1,0:T(8,128)(2,1)} %flow_far.3, bf16[2,4,32,128]{3,2,1,0:T(8,128)(2,1)} %rho_far.3, bf16[2,4,32,128]{3,2,1,0:T(8,128)(2,1)} %temp_far.3, f32[5,4,32,128]{3,2,1,0:T(8,128)} %psi_far.3), custom_call_target="tpu_custom_call" | custom-call | flops 1000000 | bytes 819200 | tf_op jit(solution)/shard_map/message/pallas_call | solution.py:670
  1.6 5.5 %collective-permute-start.1 = (bf16[18,32,128]{2,1,0:T(8,128)(2,1)S(1)}, bf16[18,32,128]{2,1,0:T(8,128)(2,1)S(1)}, u32[]{:S(2)}, u32[]{:S(2)}) collective-permute-start(bf16[18,32,128]{2,1,0:T(8,128)(2,1)S(1)} %get-tuple-element.48), channel_id=1, source_target_pairs={{0,30},{2,4},{4,2},{6,8},{8,6},{10,12},{12,10},{14,16},{16,14},{18... | collective-permute-start | bytes 442376 | tf_op jit(solution)/shard_map/ppermute | solution.py:706
  7.1 1.4 %pack.1 = (bf16[18,32,128]{2,1,0:T(8,128)(2,1)S(1)}, bf16[18,32,128]{2,1,0:T(8,128)(2,1)S(1)}, bf16[18,32,128]{2,1,0:T(8,128)(2,1)S(1)}, bf16[5,32,128]{2,1,0:T(...) custom-call(bf16[2,3,4,32,128]{4,3,2,1,0:T(8,128)(2,1)} %flow_far.3,, ...), custom_call_target="tpu_custom_call" | custom-call | flops 2000000 | bytes 1908736 | tf_op jit(solution)/shard_map/pack/pallas_call | solution.py:670
  8.4 0.1 collective-permute-start
  8.5 0.5 %collective-permute-start.2 = (bf16[18,32,128]{2,1,0:T(8,128)(2,1)S(1)}, bf16[18,32,128]{2,1,0:T(8,128)(2,1)S(1)}, u32[]{:S(2)}, u32[]{:S(2)}) collective-permute-start(bf16[18,32,128]{2,1,0:T(8,128)(2,1)S(1)} %get-tuple-element.49), channel_id=1, source_target_pairs={{0,2},{2,0},{4,6},{6,4},{8,10},{10,8},{12,14},{14,12},{16,18},{18,... | collective-permute-start | bytes 442376 | tf_op jit(solution)/shard_map/ppermute | solution.py:728
  9.0 0.3 collective-permute-start.3
  9.3 1.7 %collective-permute-start.4 = (bf16[5,32,128]{2,1,0:T(8,128)(2,1)S(1)}, bf16[5,32,128]{2,1,0:T(8,128)(2,1)S(1)}, u32[]{:S(2)}, u32[]{:S(2)}) collective-permute-start(bf16[5,32,128]{2,1,0:T(8,128)(2,1)S(1)} %get-tuple-element.52), channel_id=1, source_target_pairs={{0,1},{1,0},{2,3},{3,2},{4,5},{5,4},{6,7},{7,6},{8,9},{9,8},{10,11... | collective-permute-start | bytes 122888 | tf_op jit(solution)/shard_map/ppermute | solution.py:641
  11.0 0.2 bands.1
  11.2 0.9 %collective-permute-start.5 = (bf16[3,32,128]{2,1,0:T(8,128)(2,1)S(1)}, bf16[3,32,128]{2,1,0:T(8,128)(2,1)S(1)}, u32[]{:S(2)}, u32[]{:S(2)}) collective-permute-start(bf16[3,32,128]{2,1,0:T(8,128)(2,1)S(1)} %get-tuple-element.57), channel_id=1, source_target_pairs={{0,1},{1,0},{2,3},{3,2},{4,5},{5,4},{6,7},{7,6},{8,9},{9,8},{10,11... | collective-permute-start | bytes 73736 | tf_op jit(solution)/shard_map/ppermute | solution.py:641
  12.1 1.3 %collective-permute-done.4.own_halo = bf16[5,32,128]{2,1,0:T(8,128)(2,1)S(1)} collective-permute-done((bf16[5,32,128]{2,1,0:T(8,128)(2,1)S(1)}, bf16[5,32,128]{2,1,0:T(8,128)(2,1)S(1)}, u32[]{:S(2)}, u32[]{:S(2)}) %collective-permute-start.4) | collective-permute-done | bytes 40992 | tf_op jit(solution)/shard_map/ppermute | solution.py:641
  13.4 1.1 %own.1 = (f32[5,2,4,32,128]{4,3,2,1,0:T(8,128)S(1)}, f32[5,2,4,32,128]{4,3,2,1,0:T(8,128)S(1)}, f32[5,4,32,128]{3,2,1,0:T(8,128)S(1)}, f32[5,4,32,128]{3,2,1,0:T...) custom-call(bf16[2,3,4,32,128]{4,3,2,1,0:T(8,128)(2,1)S(1)} %get-tuple-element.44.flow, ...), custom_call_target="tpu_custom_call" | custom-call | flops 5000000 | bytes 3317760 | tf_op jit(solution)/shard_map/own/pallas_call | solution.py:670
  14.5 1.0 %inner.1 = (f32[2,4,32,128]{3,2,1,0:T(8,128)S(1)}, f32[3,32,128]{2,1,0:T(8,128)S(1)}, f32[3,10,32,128]{3,2,1,0:T(8,128)S(1)}) custom-call(bf16[2,3,4,32,128]{4,3,2,1,0:T(8,128)(2,1)S(1)} %get-tuple-element.44.flow, bf16[18,32,128]{2,1,0:T(8,128)(2,1)S(1)} %collective-permute-done.near, bf16[18,32,128]{2,1,0:T(8,128)(2,1)S(1)} %collective-permute-done.1.far, ...), custom_call_target="tpu_custom_call" | custom-call | flops 20000000 | bytes 1818624 | tf_op jit(solution)/shard_map/inner/pallas_call | solution.py:670
  15.4 0.9 %collective-permute-done.3.far.far_scalars = bf16[18,32,128]{2,1,0:T(8,128)(2,1)S(1)} collective-permute-done((bf16[18,32,128]{2,1,0:T(8,128)(2,1)S(1)}, bf16[18,32,128]{2,1,0:T(8,128)(2,1)S(1)}, u32[]{:S(2)}, u32[]{:S(2)}) %collective-permute-start.3) | collective-permute-done | bytes 147488 | tf_op jit(solution)/shard_map/ppermute | solution.py:726
  16.3 0.8 %first.1 = (f32[5,4,32,128]{3,2,1,0:T(8,128)S(1)}, f32[5,4,32,128]{3,2,1,0:T(8,128)S(1)}, f32[2,32,128]{2,1,0:T(8,128)S(1)}, f32[32,128]{1,0:T(8,128)S(1)}) custom-call(bf16[2,4,32,128]{3,2,1,0:T(8,128)(2,1)S(1)} %get-tuple-element.45.rho, bf16[2,4,32,128]{3,2,1,0:T(8,128)(2,1)S(1)} %get-tuple-element.46.temp, f32[5,4,32,128]{3,2,1,0:T(8,128)S(1)} %get-tuple-element.51.psi, ...), custom_call_target="tpu_custom_call" | custom-call | flops 10000000 | bytes 3588096 | tf_op jit(solution)/shard_map/first/pallas_call | solution.py:670
  17.1 0.9 %edge.1 = (bf16[2,32,128]{2,1,0:T(8,128)(2,1)S(1)}, f32[32,128]{1,0:T(8,128)S(1)}) custom-call(f32[6,32,128]{2,1,0:T(8,128)S(1)} %get-tuple-element.56.low, f32[3,32,128]{2,1,0:T(8,128)S(1)} %get-tuple-element.68.high, bf16[3,32,128]{2,1,0:T(8,128)(2,1)S(1)} %collective-permute-done.5.halo, f32[2,4,32,128]{3,2,1,0:T(8,128)S(1)} %get-tuple-element.69.inner, ...), custom_call_target="tpu_custom_call" | custom-call | flops 20000000 | bytes 385024 | tf_op jit(solution)/shard_map/edge/pallas_call | solution.py:670
  18.0 1.6 %collective-permute-start.6 = (bf16[2,32,128]{2,1,0:T(8,128)(2,1)S(1)}, bf16[2,32,128]{2,1,0:T(8,128)(2,1)S(1)}, u32[]{:S(2)}, u32[]{:S(2)}) collective-permute-start(bf16[2,32,128]{2,1,0:T(8,128)(2,1)S(1)} %get-tuple-element.73), channel_id=1, source_target_pairs={{0,1},{1,0},{2,3},{3,2},{4,5},{5,4},{6,7},{7,6},{8,9},{9,8},{10,11... | collective-permute-start | bytes 49160 | tf_op jit(solution)/shard_map/ppermute | solution.py:641
  19.6 1.9 %later.1 = (f32[5,10,32,128]{3,2,1,0:T(8,128)S(1)}, bf16[1,32,128]{2,1,0:T(8,128)(2,1)S(1)}, f32[32,128]{1,0:T(8,128)S(1)}) custom-call(bf16[2,3,4,32,128]{4,3,2,1,0:T(8,128)(2,1)S(1)} %get-tuple-element.44.flow, bf16[2,4,32,128]{3,2,1,0:T(8,128)(2,1)S(1)} %get-tuple-element.45.rho, bf16[2,4,32,128]{3,2,1,0:T(8,128)(2,1)S(1)} %get-tuple-element.46.temp, ...), custom_call_target="tpu_custom_call" | custom-call | flops 20000000 | bytes 3522560 | tf_op jit(solution)/shard_map/later/pallas_call | solution.py:670
  21.4 0.6 %collective-permute-start.7 = (bf16[1,32,128]{2,1,0:T(8,128)(2,1)S(1)}, bf16[1,32,128]{2,1,0:T(8,128)(2,1)S(1)}, u32[]{:S(2)}, u32[]{:S(2)}) collective-permute-start(bf16[1,32,128]{2,1,0:T(8,128)(2,1)S(1)} %get-tuple-element.77), channel_id=1, source_target_pairs={{0,1},{1,0},{2,3},{3,2},{4,5},{5,4},{6,7},{7,6},{8,9},{9,8},{10,11... | collective-permute-start | bytes 24584 | tf_op jit(solution)/shard_map/ppermute | solution.py:641
  22.0 0.3 middle.1
  22.3 2.1 %collective-permute-start.9 = (bf16[5,2,32,128]{3,2,1,0:T(8,128)(2,1)S(1)}, bf16[5,2,32,128]{3,2,1,0:T(8,128)(2,1)S(1)}, u32[]{:S(2)}, u32[]{:S(2)}) collective-permute-start(bf16[5,2,32,128]{3,2,1,0:T(8,128)(2,1)S(1)} %get-tuple-element.82), channel_id=1, source_target_pairs={{0,30},{2,4},{4,2},{6,8},{8,6},{10,12},{12,10},{14,16},{16,14},{18... | collective-permute-start | bytes 245768 | tf_op jit(solution)/shard_map/ppermute | solution.py:794
  24.4 0.8 %collective-permute-done.7.later_other = bf16[1,32,128]{2,1,0:T(8,128)(2,1)S(1)} collective-permute-done((bf16[1,32,128]{2,1,0:T(8,128)(2,1)S(1)}, bf16[1,32,128]{2,1,0:T(8,128)(2,1)S(1)}, u32[]{:S(2)}, u32[]{:S(2)}) %collective-permute-start.7) | collective-permute-done | bytes 8224 | tf_op jit(solution)/shard_map/ppermute | solution.py:641
  25.1 1.2 %base.1 = (f32[5,4,32,128]{3,2,1,0:T(8,128)S(1)}, f32[4,32,128]{2,1,0:T(8,128)S(1)}, f32[2,2,32,128]{3,2,1,0:T(8,128)S(1)}, f32[2,4,32]{2,1,0:T(4,128)}, bf16[5,2,32,128]{3,2,1,0:T(8,128)(2,1)S(1)}) custom-call(f32[5,10,32,128]{3,2,1,0:T(8,128)S(1)} %get-tuple-element.65.wide, f32[5,2,4,32,128]{4,3,2,1,0:T(8,128)S(1)} %get-tuple-element.53.grad_yz, ...), custom_call_target="tpu_custom_call" | custom-call | flops 15000000 | bytes 2794496 | tf_op jit(solution)/shard_map/base/pallas_call | solution.py:670
  26.3 2.6 %collective-permute-done.9.far = bf16[5,2,32,128]{3,2,1,0:T(8,128)(2,1)S(1)} collective-permute-done((bf16[5,2,32,128]{3,2,1,0:T(8,128)(2,1)S(1)}, bf16[5,2,32,128]{3,2,1,0:T(8,128)(2,1)S(1)}, u32[]{:S(2)}, u32[]{:S(2)}) %collective-permute-start.9) | collective-permute-done | bytes 81952 | tf_op jit(solution)/shard_map/ppermute | solution.py:794
  28.9 0.8 %last.1 = f32[5,4,32,128]{3,2,1,0:T(8,128)} custom-call(f32[5,4,32,128]{3,2,1,0:T(8,128)S(1)} %get-tuple-element.78.base, f32[4,32,128]{2,1,0:T(8,128)S(1)} %get-tuple-element.79.drift, f32[2,2,32,128]{3,2,1,0:T(8,128)S(1)} %get-tuple-element.80.spread, bf16[5,2,32,128]{3,2,1,0:T(8,128)(2,1)S(1)} %collective-permute-done.8.near_psi, ...), custom_call_target="tpu_custom_call" | custom-call | flops 1000000 | bytes 1032192 | tf_op jit(solution)/shard_map/last/pallas_call | solution.py:670
  (9 shorter events, 0.0 us)
Async XLA Ops:
  1.6 9.4 %collective-permute-start.1 = (bf16[18,32,128]{2,1,0:T(8,128)(2,1)S(1)}, bf16[18,32,128]{2,1,0:T(8,128)(2,1)S(1)}, u32[]{:S(2)}, u32[]{:S(2)}) collective-permute-start(bf16[18,32,128]{2,1,0:T(8,128)(2,1)S(1)} %get-tuple-element.48), channel_id=1, source_target_pairs={{0,30},{2,4},{4,2},{6,8},{8,6},{10,12},{12,10},{14,16},{16,14},{18... | collective-permute-start | bytes 442376 | tf_op jit(solution)/shard_map/ppermute | solution.py:706
  8.4 2.6 %collective-permute-start = (bf16[18,32,128]{2,1,0:T(8,128)(2,1)S(1)}, bf16[18,32,128]{2,1,0:T(8,128)(2,1)S(1)}, u32[]{:S(2)}, u32[]{:S(2)}) collective-permute-start(bf16[18,32,128]{2,1,0:T(8,128)(2,1)S(1)} %get-tuple-element.47), channel_id=1, source_target_pairs={{0,2},{2,0},{4,6},{6,4},{8,10},{10,8},{12,14},{14,12},{16,18},{18,... | collective-permute-start | bytes 442376 | tf_op jit(solution)/shard_map/ppermute | solution.py:727
  8.5 6.9 %collective-permute-start.2 = (bf16[18,32,128]{2,1,0:T(8,128)(2,1)S(1)}, bf16[18,32,128]{2,1,0:T(8,128)(2,1)S(1)}, u32[]{:S(2)}, u32[]{:S(2)}) collective-permute-start(bf16[18,32,128]{2,1,0:T(8,128)(2,1)S(1)} %get-tuple-element.49), channel_id=1, source_target_pairs={{0,2},{2,0},{4,6},{6,4},{8,10},{10,8},{12,14},{14,12},{16,18},{18,... | collective-permute-start | bytes 442376 | tf_op jit(solution)/shard_map/ppermute | solution.py:728
  9.0 7.3 %collective-permute-start.3 = (bf16[18,32,128]{2,1,0:T(8,128)(2,1)S(1)}, bf16[18,32,128]{2,1,0:T(8,128)(2,1)S(1)}, u32[]{:S(2)}, u32[]{:S(2)}) collective-permute-start(bf16[18,32,128]{2,1,0:T(8,128)(2,1)S(1)} %get-tuple-element.50), channel_id=1, source_target_pairs={{0,30},{2,4},{4,2},{6,8},{8,6},{10,12},{12,10},{14,16},{16,14},{18... | collective-permute-start | bytes 442376 | tf_op jit(solution)/shard_map/ppermute | solution.py:726
  9.3 4.1 %collective-permute-start.4 = (bf16[5,32,128]{2,1,0:T(8,128)(2,1)S(1)}, bf16[5,32,128]{2,1,0:T(8,128)(2,1)S(1)}, u32[]{:S(2)}, u32[]{:S(2)}) collective-permute-start(bf16[5,32,128]{2,1,0:T(8,128)(2,1)S(1)} %get-tuple-element.52), channel_id=1, source_target_pairs={{0,1},{1,0},{2,3},{3,2},{4,5},{5,4},{6,7},{7,6},{8,9},{9,8},{10,11... | collective-permute-start | bytes 122888 | tf_op jit(solution)/shard_map/ppermute | solution.py:641
  11.2 5.9 %collective-permute-start.5 = (bf16[3,32,128]{2,1,0:T(8,128)(2,1)S(1)}, bf16[3,32,128]{2,1,0:T(8,128)(2,1)S(1)}, u32[]{:S(2)}, u32[]{:S(2)}) collective-permute-start(bf16[3,32,128]{2,1,0:T(8,128)(2,1)S(1)} %get-tuple-element.57), channel_id=1, source_target_pairs={{0,1},{1,0},{2,3},{3,2},{4,5},{5,4},{6,7},{7,6},{8,9},{9,8},{10,11... | collective-permute-start | bytes 73736 | tf_op jit(solution)/shard_map/ppermute | solution.py:641
  18.0 4.0 %collective-permute-start.6 = (bf16[2,32,128]{2,1,0:T(8,128)(2,1)S(1)}, bf16[2,32,128]{2,1,0:T(8,128)(2,1)S(1)}, u32[]{:S(2)}, u32[]{:S(2)}) collective-permute-start(bf16[2,32,128]{2,1,0:T(8,128)(2,1)S(1)} %get-tuple-element.73), channel_id=1, source_target_pairs={{0,1},{1,0},{2,3},{3,2},{4,5},{5,4},{6,7},{7,6},{8,9},{9,8},{10,11... | collective-permute-start | bytes 49160 | tf_op jit(solution)/shard_map/ppermute | solution.py:641
  21.4 3.7 %collective-permute-start.7 = (bf16[1,32,128]{2,1,0:T(8,128)(2,1)S(1)}, bf16[1,32,128]{2,1,0:T(8,128)(2,1)S(1)}, u32[]{:S(2)}, u32[]{:S(2)}) collective-permute-start(bf16[1,32,128]{2,1,0:T(8,128)(2,1)S(1)} %get-tuple-element.77), channel_id=1, source_target_pairs={{0,1},{1,0},{2,3},{3,2},{4,5},{5,4},{6,7},{7,6},{8,9},{9,8},{10,11... | collective-permute-start | bytes 24584 | tf_op jit(solution)/shard_map/ppermute | solution.py:641
  22.3 6.6 %collective-permute-start.9 = (bf16[5,2,32,128]{3,2,1,0:T(8,128)(2,1)S(1)}, bf16[5,2,32,128]{3,2,1,0:T(8,128)(2,1)S(1)}, u32[]{:S(2)}, u32[]{:S(2)}) collective-permute-start(bf16[5,2,32,128]{3,2,1,0:T(8,128)(2,1)S(1)} %get-tuple-element.82), channel_id=1, source_target_pairs={{0,30},{2,4},{4,2},{6,8},{8,6},{10,12},{12,10},{14,16},{16,14},{18... | collective-permute-start | bytes 245768 | tf_op jit(solution)/shard_map/ppermute | solution.py:794
  26.3 2.6 %collective-permute-start.8 = (bf16[5,2,32,128]{3,2,1,0:T(8,128)(2,1)S(1)}, bf16[5,2,32,128]{3,2,1,0:T(8,128)(2,1)S(1)}, u32[]{:S(2)}, u32[]{:S(2)}) collective-permute-start(bf16[5,2,32,128]{3,2,1,0:T(8,128)(2,1)S(1)} %get-tuple-element.81), channel_id=1, source_target_pairs={{0,2},{2,0},{4,6},{6,4},{8,10},{10,8},{12,14},{14,12},{16,18},{18,... | collective-permute-start | bytes 245768 | tf_op jit(solution)/shard_map/ppermute | solution.py:806

commit v10 on v9

--- a/solution.py
+++ b/solution.py
@@ -115,11 +115,14 @@
             halos[k, x] = ops.strip(strips, 2 * t + k - 3, x)
 
 
-def across_terms(ops, values, halo):
+def y_terms(ops, values):
     up, down = ops.y_up(values), ops.y_down(values)
+    return 0.5 * (up - down), (up + down) - 6.0 * values
+
+
+def z_terms(ops, values, halo):
     zs = [ops.z_at(values, halo, step) for step in (1, -1, 2, -2)]
-    lap = (up + down) + (zs[0] + zs[1]) - 6.0 * values
-    return 0.5 * (up - down), fourth(*zs), lap
+    return fourth(*zs), zs[0] + zs[1]
 
 
 def state_terms(wide, grad_yz, lap_yz, x):
@@ -189,38 +192,38 @@
         message[first + number] = both.astype(BF16)
 
 
-def message_kernel(flow_far, rho_far, temp_far, psi_far, far, ahead, sem):
+def message_kernel(
+    flow_far, rho_far, temp_far, psi_far, far, far_scalars, flow, rho, temp, psi, sems
+):
     side = 1 - is_even().astype(jnp.int32)
-    copy = pltpu.make_async_copy(
-        flow_far.at[:, :, pl.ds(side, 3)], far.reshape((2, 3, 3, ROWS, LANES)), sem
-    )
-    copy.start()
-    ahead[...] = jnp.zeros((ROWS, LANES), F32)
-    copy.wait()
-
-
-def pack_kernel(
-    flow_far, rho_far, temp_far, psi_far, _,
-    near, near_scalars, far_scalars, message, low, flow, rho, temp, psi, sems,
-):
+    pieces = (
+        (flow_far.at[:, :, pl.ds(side, 3)], far.reshape((2, 3, 3, ROWS, LANES))),
+        (psi_far, psi),
+        (rho_far, rho),
+        (temp_far, temp),
+        (flow_far, flow),
+    )
     copies = [
-        pltpu.make_async_copy(source, target, sems.at[i])
-        for i, (source, target) in enumerate(
-            ((flow_far, flow), (psi_far, psi), (rho_far, rho), (temp_far, temp))
-        )
+        pltpu.make_async_copy(source, target, sems.at[number])
+        for number, (source, target) in enumerate(pieces)
     ]
     for copy in copies:
         copy.start()
+    for copy in copies[1:4]:
+        copy.wait()
+    fill_scalars(far_scalars, side, rho, temp, psi)
+    copies[0].wait()
+    copies[4].wait()
+
+
+def pack_kernel(flow, rho, temp, psi, near, near_scalars, message, low):
     ops = Ops()
-    for copy in copies:
-        copy.wait()
     side = is_even().astype(jnp.int32)
     for t in range(2):
         for k in range(3):
             for i in range(3):
                 near[VELOCITY + t * 9 + k * 3 + i] = flow[t, k, side + i]
     fill_scalars(near_scalars, side, rho, temp, psi)
-    fill_scalars(far_scalars, 1 - side, rho, temp, psi)
     items = []
     for t in range(2):
         for source in (rho, temp):
@@ -239,8 +242,24 @@
     merge_bands(ops, low, message, STRIP_BLOCKS)
 
 
+def rows_kernel(flow, rho, temp, psi, grad_0, grad_1, lap_0, lap_1, psi_rate, psi_lap):
+    ops = Ops()
+    for t, grad_y, lap_y in ((0, grad_0, lap_0), (1, grad_1, lap_1)):
+        for k in range(5):
+            for x in range(CX):
+                values = flow[t, k, x] if k < 3 else (rho if k == 3 else temp)[t, x]
+                grad_y[k, x], lap_y[k, x] = y_terms(ops, values.astype(F32))
+    for x in range(CX):
+        along_y = flow[0, 1, x].astype(F32)
+        for k in range(5):
+            by_y, psi_lap[k, x] = y_terms(ops, psi[k, x])
+            psi_rate[k, x] = along_y * by_y
+
+
 def own_kernel(
-    flow, rho, temp, psi, own_halo, grad_0, grad_1, lap_0, lap_1, psi_rate, psi_lap, halos, psi_halos
+    flow, rho, temp, psi, own_halo, grad_y_0, grad_y_1, lap_y_0, lap_y_1, rate_y, psi_lap_y,
+    grad_0, grad_1, lap_0, lap_1, psi_rate, psi_lap,
+    halos, psi_halos,
 ):
     ops = Ops()
     for t in range(2):
@@ -249,19 +268,22 @@
     for k in range(5):
         for x in range(CX):
             psi_halos[k, x] = ops.strip(strips, SLOT_PSI + k, x)
-    for t, grad_yz, lap_yz in ((0, grad_0, lap_0), (1, grad_1, lap_1)):
+    for t, grad_y, lap_y, grad_yz, lap_yz in (
+        (0, grad_y_0, lap_y_0, grad_0, lap_0),
+        (1, grad_y_1, lap_y_1, grad_1, lap_1),
+    ):
         for k in range(5):
             for x in range(CX):
                 values = flow[t, k, x] if k < 3 else (rho if k == 3 else temp)[t, x]
-                grad_yz[k, 0, x], grad_yz[k, 1, x], lap_yz[k, x] = across_terms(
-                    ops, values.astype(F32), halos[t, k, x]
-                )
-    for x in range(CX):
-        along_y, along_z = flow[0, 1, x].astype(F32), flow[0, 2, x].astype(F32)
+                by_z, both = z_terms(ops, values.astype(F32), halos[t, k, x])
+                grad_yz[k, 0, x], grad_yz[k, 1, x] = grad_y[k, x], by_z
+                lap_yz[k, x] = lap_y[k, x] + both
+    for x in range(CX):
+        along_z = flow[0, 2, x].astype(F32)
         for k in range(5):
-            by_y, by_z, lap = across_terms(ops, psi[k, x], psi_halos[k, x])
-            psi_rate[k, x] = along_y * by_y + along_z * by_z
-            psi_lap[k, x] = lap
+            by_z, both = z_terms(ops, psi[k, x], psi_halos[k, x])
+            psi_rate[k, x] = rate_y[k, x] + along_z * by_z
+            psi_lap[k, x] = psi_lap_y[k, x] + both
 
 
 def token_kernel(far, out):
@@ -575,9 +597,10 @@
             psi_wide[k, 3 + x] = psi[k, x]
     for x in range(CX):
         for k in range(5):
-            by_y, by_z, lap = across_terms(ops, psi[k, x], psi_halos[k, x])
+            by_y, lap = y_terms(ops, psi[k, x])
+            by_z, both = z_terms(ops, psi[k, x], psi_halos[k, x])
             psi_rate[k, x] = wide[1, x + 3] * by_y + wide[2, x + 3] * by_z
-            psi_lap[k, x] = lap
+            psi_lap[k, x] = lap + both
     for x in range(CX):
         terms = state_terms(wide, grad_yz, lap_yz, x)
         center = terms[0]
@@ -694,43 +717,50 @@
     slopes = shape_of((5, 2, CX))
     inputs = (flow_far, rho_far, temp_far, psi_far)
     stay = [pl.BlockSpec(memory_space=pltpu.MemorySpace.HBM)] * 4
-    far, ahead = call(
+    far, far_scalars, flow, rho, temp, psi = call(
         message_kernel,
         "message",
         inputs,
-        [shape_of((SCALARS,), BF16), shape_of(())],
-        1_000_000,
-        [pltpu.SemaphoreType.DMA(())],
-        stay,
-    )
-    far = lax.ppermute(far, "gx", across)
-    near, near_scalars, far_scalars, message, own_low, flow, rho, temp, psi = call(
-        pack_kernel,
-        "pack",
-        inputs + (ahead,),
         [
             shape_of((SCALARS,), BF16),
             shape_of((SCALAR_PLANES,), BF16),
-            shape_of((SCALAR_PLANES,), BF16),
-            shape_of((STRIP_BLOCKS + BAND_BLOCKS,), BF16),
-            shape_of((6,)),
             shape_of((2, 3, CX), BF16),
             shape_of((2, CX), BF16),
             shape_of((2, CX), BF16),
             field,
         ],
+        1_000_000,
+        [pltpu.SemaphoreType.DMA((5,))],
+        stay,
+    )
+    far = lax.ppermute(far, "gx", across)
+    near, near_scalars, message, own_low = call(
+        pack_kernel,
+        "pack",
+        (flow, rho, temp, psi),
+        [
+            shape_of((SCALARS,), BF16),
+            shape_of((SCALAR_PLANES,), BF16),
+            shape_of((STRIP_BLOCKS + BAND_BLOCKS,), BF16),
+            shape_of((6,)),
+        ],
         2_000_000,
-        [pltpu.SemaphoreType.DMA((4,))],
-        stay + whole(1),
     )
     far_scalars = lax.ppermute(far_scalars, "gx", across)
     near = lax.ppermute(near, "gx", inside)
     near_scalars = lax.ppermute(near_scalars, "gx", inside)
     own_halo = span_edges(message, STRIP_BLOCKS)
+    rows = call(
+        rows_kernel,
+        "rows",
+        (flow, rho, temp, psi),
+        [field] * 6,
+        3_000_000,
+    )
     grad_0, grad_1, lap_0, lap_1, psi_rate, psi_lap = call(
         own_kernel,
         "own",
-        (flow, rho, temp, psi, own_halo),
+        (flow, rho, temp, psi, own_halo, *rows),
         [slopes, slopes, field, field, field, field],
         5_000_000,
         scratch((2, 5, CX), (5, CX)),

time: 29.9 us -> 29.1 us (0.973)
  waiting for transfers between devices: 5.5 us -> 3.53 us
  starting transfers between devices: 13.2 us -> 14.8 us
  Pallas kernels: 10.4 us -> 9.91 us
    ppermute x4, waiting for transfers between devices: 2.03 us -> 0.22 us  [span_edges(): before = lax.ppermute(message, 'gz', forward)]
    ppermute x4, starting transfers between devices: 4.73 us -> 5.88 us  [span_edges(): before = lax.ppermute(message, 'gz', forward)]
    ppermute x2, starting transfers between devices: 7.59 us -> 8.11 us  [local(): far = lax.ppermute(far, 'gx', across)]
    pallas_call x13 -> x14, Pallas kernels: 10.4 us -> 9.91 us  [call(): pl.pallas_call(kernel, in_specs=in_specs or whole(len(inputs)), out_specs...]
  transfers between devices with their start and end apart: 10 -> 10, of which waited for: 4 -> 3; matrix products, arithmetic and copies ran while one was open for 0% -> 0% of each run, Pallas kernels for 26% -> 24%
where the time goes in v10:
time: 29.1 us; the launch traced here: 28.9 us
  starting transfers between devices  14.8 us (51%)
  Pallas kernels  9.91 us (34%)
  waiting for transfers between devices  3.53 us (12%)
  between operations  0.72 us (2%)
    pallas_call x14, Pallas kernels, call(): pl.pallas_call(kernel, in_specs=in_specs or whole(len(inputs)), out_specs...  9.91 us
    ppermute x2, starting transfers between devices, local(): far = lax.ppermute(far, 'gx', across)  8.11 us
    ppermute x4, starting transfers between devices, span_edges(): before = lax.ppermute(message, 'gz', forward)  5.88 us
    ppermute x2, waiting for transfers between devices, local(): far = lax.ppermute(far, 'gx', across)  2.61 us
    ppermute x1, waiting for transfers between devices, local(): far_scalars = lax.ppermute(far_scalars, 'gx', across)  0.68 us
  transfers between devices with their start and end apart: 10, of which 3 were waited for; matrix products, arithmetic and copies ran while one was open for 0% of the time, Pallas kernels for 24%

profile of v10, /device:TPU:0, one launch (start us, length us, event | category | flops | bytes accessed | tf_op | source)
XLA Modules:
  0.0 28.9 jit_solution(14196518104592935196)
XLA Ops:
  0.6 1.2 %message.1 = (bf16[18,32,128]{2,1,0:T(8,128)(2,1)S(1)}, bf16[18,32,128]{2,1,0:T(8,128)(2,1)S(1)}, bf16[2,3,4,32,128]{4,3,2,1,0:T(8,128)(2,1)S(1)}, bf16[2,4,32,1...) custom-call(bf16[2,3,4,32,128]{4,3,2,1,0:T(8,128)(2,1)} %flow_far.1, ...), custom_call_target="tpu_custom_call" | custom-call | flops 1000000 | bytes 1605632 | tf_op jit(solution)/shard_map/message/pallas_call | solution.py:693
  1.9 5.5 %collective-permute-start.1 = (bf16[18,32,128]{2,1,0:T(8,128)(2,1)S(1)}, bf16[18,32,128]{2,1,0:T(8,128)(2,1)S(1)}, u32[]{:S(2)}, u32[]{:S(2)}) collective-permute-start(bf16[18,32,128]{2,1,0:T(8,128)(2,1)S(1)} %get-tuple-element.53), channel_id=1, source_target_pairs={{0,30},{2,4},{4,2},{6,8},{8,6},{10,12},{12,10},{14,16},{16,14},{18... | collective-permute-start | bytes 442376 | tf_op jit(solution)/shard_map/ppermute | solution.py:736
  7.3 0.3 pack.1
  7.6 0.5 %collective-permute-start.2 = (bf16[18,32,128]{2,1,0:T(8,128)(2,1)S(1)}, bf16[18,32,128]{2,1,0:T(8,128)(2,1)S(1)}, u32[]{:S(2)}, u32[]{:S(2)}) collective-permute-start(bf16[18,32,128]{2,1,0:T(8,128)(2,1)S(1)} %get-tuple-element.54), channel_id=1, source_target_pairs={{0,2},{2,0},{4,6},{6,4},{8,10},{10,8},{12,14},{14,12},{16,18},{18,... | collective-permute-start | bytes 442376 | tf_op jit(solution)/shard_map/ppermute | solution.py:751
  8.1 0.3 collective-permute-start.3
  8.4 1.7 %collective-permute-start.4 = (bf16[5,32,128]{2,1,0:T(8,128)(2,1)S(1)}, bf16[5,32,128]{2,1,0:T(8,128)(2,1)S(1)}, u32[]{:S(2)}, u32[]{:S(2)}) collective-permute-start(bf16[5,32,128]{2,1,0:T(8,128)(2,1)S(1)} %get-tuple-element.56), channel_id=1, source_target_pairs={{0,1},{1,0},{2,3},{3,2},{4,5},{5,4},{6,7},{7,6},{8,9},{9,8},{10,11... | collective-permute-start | bytes 122888 | tf_op jit(solution)/shard_map/ppermute | solution.py:664
  10.1 0.0 collective-permute-done.1.far
  10.2 0.2 bands.1
  10.4 2.0 %collective-permute-start.5 = (bf16[3,32,128]{2,1,0:T(8,128)(2,1)S(1)}, bf16[3,32,128]{2,1,0:T(8,128)(2,1)S(1)}, u32[]{:S(2)}, u32[]{:S(2)}) collective-permute-start(bf16[3,32,128]{2,1,0:T(8,128)(2,1)S(1)} %get-tuple-element.67), channel_id=1, source_target_pairs={{0,1},{1,0},{2,3},{3,2},{4,5},{5,4},{6,7},{7,6},{8,9},{9,8},{10,11... | collective-permute-start | bytes 73736 | tf_op jit(solution)/shard_map/ppermute | solution.py:664
  12.4 0.3 %rows.1 = (f32[5,4,32,128]{3,2,1,0:T(8,128)S(1)}, f32[5,4,32,128]{3,2,1,0:T(8,128)S(1)}, f32[5,4,32,128]{3,2,1,0:T(8,128)S(1)}, f32[5,4,32,128]{3,2,1,0:T(8,128)...) custom-call(bf16[2,3,4,32,128]{4,3,2,1,0:T(8,128)(2,1)S(1)} %get-tuple-element.48.flow, ...), custom_call_target="tpu_custom_call" | custom-call | flops 3000000 | bytes 2621440 | tf_op jit(solution)/shard_map/rows/pallas_call | solution.py:693
  12.7 0.9 %own.1 = (f32[5,2,4,32,128]{4,3,2,1,0:T(8,128)S(1)}, f32[5,2,4,32,128]{4,3,2,1,0:T(8,128)S(1)}, f32[5,4,32,128]{3,2,1,0:T(8,128)S(1)}, f32[5,4,32,128]{3,2,1,0:T...) custom-call(bf16[2,3,4,32,128]{4,3,2,1,0:T(8,128)(2,1)S(1)} %get-tuple-element.48.flow, ...), custom_call_target="tpu_custom_call" | custom-call | flops 5000000 | bytes 5283840 | tf_op jit(solution)/shard_map/own/pallas_call | solution.py:693
  13.7 1.0 %inner.1 = (f32[2,4,32,128]{3,2,1,0:T(8,128)S(1)}, f32[3,32,128]{2,1,0:T(8,128)S(1)}, f32[3,10,32,128]{3,2,1,0:T(8,128)S(1)}) custom-call(bf16[2,3,4,32,128]{4,3,2,1,0:T(8,128)(2,1)S(1)} %get-tuple-element.48.flow, bf16[18,32,128]{2,1,0:T(8,128)(2,1)S(1)} %collective-permute-done.near, bf16[18,32,128]{2,1,0:T(8,128)(2,1)S(1)} %collective-permute-done.1.far, ...), custom_call_target="tpu_custom_call" | custom-call | flops 20000000 | bytes 1818624 | tf_op jit(solution)/shard_map/inner/pallas_call | solution.py:693
  14.7 0.7 %collective-permute-done.3.far.far_scalars = bf16[18,32,128]{2,1,0:T(8,128)(2,1)S(1)} collective-permute-done((bf16[18,32,128]{2,1,0:T(8,128)(2,1)S(1)}, bf16[18,32,128]{2,1,0:T(8,128)(2,1)S(1)}, u32[]{:S(2)}, u32[]{:S(2)}) %collective-permute-start.3) | collective-permute-done | bytes 147488 | tf_op jit(solution)/shard_map/ppermute | solution.py:749
  15.4 0.8 %first.1 = (f32[5,4,32,128]{3,2,1,0:T(8,128)S(1)}, f32[5,4,32,128]{3,2,1,0:T(8,128)S(1)}, f32[2,32,128]{2,1,0:T(8,128)S(1)}, f32[32,128]{1,0:T(8,128)S(1)}) custom-call(bf16[2,4,32,128]{3,2,1,0:T(8,128)(2,1)S(1)} %get-tuple-element.49.rho, bf16[2,4,32,128]{3,2,1,0:T(8,128)(2,1)S(1)} %get-tuple-element.50.temp, f32[5,4,32,128]{3,2,1,0:T(8,128)S(1)} %get-tuple-element.51.psi, ...), custom_call_target="tpu_custom_call" | custom-call | flops 10000000 | bytes 3588096 | tf_op jit(solution)/shard_map/first/pallas_call | solution.py:693
  16.2 0.9 %edge.1 = (bf16[2,32,128]{2,1,0:T(8,128)(2,1)S(1)}, f32[32,128]{1,0:T(8,128)S(1)}) custom-call(f32[6,32,128]{2,1,0:T(8,128)S(1)} %get-tuple-element.66.low, f32[3,32,128]{2,1,0:T(8,128)S(1)} %get-tuple-element.78.high, bf16[3,32,128]{2,1,0:T(8,128)(2,1)S(1)} %collective-permute-done.5.halo, f32[2,4,32,128]{3,2,1,0:T(8,128)S(1)} %get-tuple-element.79.inner, ...), custom_call_target="tpu_custom_call" | custom-call | flops 20000000 | bytes 385024 | tf_op jit(solution)/shard_map/edge/pallas_call | solution.py:693
  17.1 1.6 %collective-permute-start.6 = (bf16[2,32,128]{2,1,0:T(8,128)(2,1)S(1)}, bf16[2,32,128]{2,1,0:T(8,128)(2,1)S(1)}, u32[]{:S(2)}, u32[]{:S(2)}) collective-permute-start(bf16[2,32,128]{2,1,0:T(8,128)(2,1)S(1)} %get-tuple-element.83), channel_id=1, source_target_pairs={{0,1},{1,0},{2,3},{3,2},{4,5},{5,4},{6,7},{7,6},{8,9},{9,8},{10,11... | collective-permute-start | bytes 49160 | tf_op jit(solution)/shard_map/ppermute | solution.py:664
  18.7 1.9 %later.1 = (f32[5,10,32,128]{3,2,1,0:T(8,128)S(1)}, bf16[1,32,128]{2,1,0:T(8,128)(2,1)S(1)}, f32[32,128]{1,0:T(8,128)S(1)}) custom-call(bf16[2,3,4,32,128]{4,3,2,1,0:T(8,128)(2,1)S(1)} %get-tuple-element.48.flow, bf16[2,4,32,128]{3,2,1,0:T(8,128)(2,1)S(1)} %get-tuple-element.49.rho, bf16[2,4,32,128]{3,2,1,0:T(8,128)(2,1)S(1)} %get-tuple-element.50.temp, ...), custom_call_target="tpu_custom_call" | custom-call | flops 20000000 | bytes 3522560 | tf_op jit(solution)/shard_map/later/pallas_call | solution.py:693
  20.6 0.6 %collective-permute-start.7 = (bf16[1,32,128]{2,1,0:T(8,128)(2,1)S(1)}, bf16[1,32,128]{2,1,0:T(8,128)(2,1)S(1)}, u32[]{:S(2)}, u32[]{:S(2)}) collective-permute-start(bf16[1,32,128]{2,1,0:T(8,128)(2,1)S(1)} %get-tuple-element.87), channel_id=1, source_target_pairs={{0,1},{1,0},{2,3},{3,2},{4,5},{5,4},{6,7},{7,6},{8,9},{9,8},{10,11... | collective-permute-start | bytes 24584 | tf_op jit(solution)/shard_map/ppermute | solution.py:664
  21.2 0.3 %middle.1 = (f32[5,4,32,128]{3,2,1,0:T(8,128)S(1)}, bf16[5,2,32,128]{3,2,1,0:T(8,128)(2,1)S(1)}, f32[4,32,128]{2,1,0:T(8,128)S(1)}) custom-call(f32[5,4,32,128]{3,2,1,0:T(8,128)S(1)} %get-tuple-element.77.first, f32[5,4,32,128]{3,2,1,0:T(8,128)S(1)} %get-tuple-element.74.second, f32[32,128]{1,0:T(8,128)S(1)} %get-tuple-element.82.columns, ...), custom_call_target="tpu_custom_call" | custom-call | flops 1000000 | bytes 1163264 | tf_op jit(solution)/shard_map/middle/pallas_call | solution.py:693
  21.5 2.6 %collective-permute-start.9 = (bf16[5,2,32,128]{3,2,1,0:T(8,128)(2,1)S(1)}, bf16[5,2,32,128]{3,2,1,0:T(8,128)(2,1)S(1)}, u32[]{:S(2)}, u32[]{:S(2)}) collective-permute-start(bf16[5,2,32,128]{3,2,1,0:T(8,128)(2,1)S(1)} %get-tuple-element.92), channel_id=1, source_target_pairs={{0,30},{2,4},{4,2},{6,8},{8,6},{10,12},{12,10},{14,16},{16,14},{18... | collective-permute-start | bytes 245768 | tf_op jit(solution)/shard_map/ppermute | solution.py:824
  24.1 0.2 collective-permute-done.7.later_other
  24.3 1.2 %base.1 = (f32[5,4,32,128]{3,2,1,0:T(8,128)S(1)}, f32[4,32,128]{2,1,0:T(8,128)S(1)}, f32[2,2,32,128]{3,2,1,0:T(8,128)S(1)}, f32[2,4,32]{2,1,0:T(4,128)}, bf16[5,2,32,128]{3,2,1,0:T(8,128)(2,1)S(1)}) custom-call(f32[5,10,32,128]{3,2,1,0:T(8,128)S(1)} %get-tuple-element.75.wide, f32[5,2,4,32,128]{4,3,2,1,0:T(8,128)S(1)} %get-tuple-element.63.grad_yz, ...), custom_call_target="tpu_custom_call" | custom-call | flops 15000000 | bytes 2794496 | tf_op jit(solution)/shard_map/base/pallas_call | solution.py:693
  25.5 2.6 %collective-permute-done.9.far = bf16[5,2,32,128]{3,2,1,0:T(8,128)(2,1)S(1)} collective-permute-done((bf16[5,2,32,128]{3,2,1,0:T(8,128)(2,1)S(1)}, bf16[5,2,32,128]{3,2,1,0:T(8,128)(2,1)S(1)}, u32[]{:S(2)}, u32[]{:S(2)}) %collective-permute-start.9) | collective-permute-done | bytes 81952 | tf_op jit(solution)/shard_map/ppermute | solution.py:824
  28.1 0.8 %last.1 = f32[5,4,32,128]{3,2,1,0:T(8,128)} custom-call(f32[5,4,32,128]{3,2,1,0:T(8,128)S(1)} %get-tuple-element.88.base, f32[4,32,128]{2,1,0:T(8,128)S(1)} %get-tuple-element.89.drift, f32[2,2,32,128]{3,2,1,0:T(8,128)S(1)} %get-tuple-element.90.spread, bf16[5,2,32,128]{3,2,1,0:T(8,128)(2,1)S(1)} %collective-permute-done.8.near_psi, ...), custom_call_target="tpu_custom_call" | custom-call | flops 1000000 | bytes 1032192 | tf_op jit(solution)/shard_map/last/pallas_call | solution.py:693
  (10 shorter events, 0.1 us)
Async XLA Ops:
  1.9 8.3 %collective-permute-start.1 = (bf16[18,32,128]{2,1,0:T(8,128)(2,1)S(1)}, bf16[18,32,128]{2,1,0:T(8,128)(2,1)S(1)}, u32[]{:S(2)}, u32[]{:S(2)}) collective-permute-start(bf16[18,32,128]{2,1,0:T(8,128)(2,1)S(1)} %get-tuple-element.53), channel_id=1, source_target_pairs={{0,30},{2,4},{4,2},{6,8},{8,6},{10,12},{12,10},{14,16},{16,14},{18... | collective-permute-start | bytes 442376 | tf_op jit(solution)/shard_map/ppermute | solution.py:736
  7.6 2.6 %collective-permute-start = (bf16[18,32,128]{2,1,0:T(8,128)(2,1)S(1)}, bf16[18,32,128]{2,1,0:T(8,128)(2,1)S(1)}, u32[]{:S(2)}, u32[]{:S(2)}) collective-permute-start(bf16[18,32,128]{2,1,0:T(8,128)(2,1)S(1)} %get-tuple-element.52), channel_id=1, source_target_pairs={{0,2},{2,0},{4,6},{6,4},{8,10},{10,8},{12,14},{14,12},{16,18},{18,... | collective-permute-start | bytes 442376 | tf_op jit(solution)/shard_map/ppermute | solution.py:750
  7.6 7.1 %collective-permute-start.2 = (bf16[18,32,128]{2,1,0:T(8,128)(2,1)S(1)}, bf16[18,32,128]{2,1,0:T(8,128)(2,1)S(1)}, u32[]{:S(2)}, u32[]{:S(2)}) collective-permute-start(bf16[18,32,128]{2,1,0:T(8,128)(2,1)S(1)} %get-tuple-element.54), channel_id=1, source_target_pairs={{0,2},{2,0},{4,6},{6,4},{8,10},{10,8},{12,14},{14,12},{16,18},{18,... | collective-permute-start | bytes 442376 | tf_op jit(solution)/shard_map/ppermute | solution.py:751
  8.1 7.3 %collective-permute-start.3 = (bf16[18,32,128]{2,1,0:T(8,128)(2,1)S(1)}, bf16[18,32,128]{2,1,0:T(8,128)(2,1)S(1)}, u32[]{:S(2)}, u32[]{:S(2)}) collective-permute-start(bf16[18,32,128]{2,1,0:T(8,128)(2,1)S(1)} %get-tuple-element.55), channel_id=1, source_target_pairs={{0,30},{2,4},{4,2},{6,8},{8,6},{10,12},{12,10},{14,16},{16,14},{18... | collective-permute-start | bytes 442376 | tf_op jit(solution)/shard_map/ppermute | solution.py:749
  8.4 4.3 %collective-permute-start.4 = (bf16[5,32,128]{2,1,0:T(8,128)(2,1)S(1)}, bf16[5,32,128]{2,1,0:T(8,128)(2,1)S(1)}, u32[]{:S(2)}, u32[]{:S(2)}) collective-permute-start(bf16[5,32,128]{2,1,0:T(8,128)(2,1)S(1)} %get-tuple-element.56), channel_id=1, source_target_pairs={{0,1},{1,0},{2,3},{3,2},{4,5},{5,4},{6,7},{7,6},{8,9},{9,8},{10,11... | collective-permute-start | bytes 122888 | tf_op jit(solution)/shard_map/ppermute | solution.py:664
  10.4 5.8 %collective-permute-start.5 = (bf16[3,32,128]{2,1,0:T(8,128)(2,1)S(1)}, bf16[3,32,128]{2,1,0:T(8,128)(2,1)S(1)}, u32[]{:S(2)}, u32[]{:S(2)}) collective-permute-start(bf16[3,32,128]{2,1,0:T(8,128)(2,1)S(1)} %get-tuple-element.67), channel_id=1, source_target_pairs={{0,1},{1,0},{2,3},{3,2},{4,5},{5,4},{6,7},{7,6},{8,9},{9,8},{10,11... | collective-permute-start | bytes 73736 | tf_op jit(solution)/shard_map/ppermute | solution.py:664
  17.1 4.1 %collective-permute-start.6 = (bf16[2,32,128]{2,1,0:T(8,128)(2,1)S(1)}, bf16[2,32,128]{2,1,0:T(8,128)(2,1)S(1)}, u32[]{:S(2)}, u32[]{:S(2)}) collective-permute-start(bf16[2,32,128]{2,1,0:T(8,128)(2,1)S(1)} %get-tuple-element.83), channel_id=1, source_target_pairs={{0,1},{1,0},{2,3},{3,2},{4,5},{5,4},{6,7},{7,6},{8,9},{9,8},{10,11... | collective-permute-start | bytes 49160 | tf_op jit(solution)/shard_map/ppermute | solution.py:664
  20.6 3.7 %collective-permute-start.7 = (bf16[1,32,128]{2,1,0:T(8,128)(2,1)S(1)}, bf16[1,32,128]{2,1,0:T(8,128)(2,1)S(1)}, u32[]{:S(2)}, u32[]{:S(2)}) collective-permute-start(bf16[1,32,128]{2,1,0:T(8,128)(2,1)S(1)} %get-tuple-element.87), channel_id=1, source_target_pairs={{0,1},{1,0},{2,3},{3,2},{4,5},{5,4},{6,7},{7,6},{8,9},{9,8},{10,11... | collective-permute-start | bytes 24584 | tf_op jit(solution)/shard_map/ppermute | solution.py:664
  21.5 6.6 %collective-permute-start.9 = (bf16[5,2,32,128]{3,2,1,0:T(8,128)(2,1)S(1)}, bf16[5,2,32,128]{3,2,1,0:T(8,128)(2,1)S(1)}, u32[]{:S(2)}, u32[]{:S(2)}) collective-permute-start(bf16[5,2,32,128]{3,2,1,0:T(8,128)(2,1)S(1)} %get-tuple-element.92), channel_id=1, source_target_pairs={{0,30},{2,4},{4,2},{6,8},{8,6},{10,12},{12,10},{14,16},{16,14},{18... | collective-permute-start | bytes 245768 | tf_op jit(solution)/shard_map/ppermute | solution.py:824
  25.5 2.6 %collective-permute-start.8 = (bf16[5,2,32,128]{3,2,1,0:T(8,128)(2,1)S(1)}, bf16[5,2,32,128]{3,2,1,0:T(8,128)(2,1)S(1)}, u32[]{:S(2)}, u32[]{:S(2)}) collective-permute-start(bf16[5,2,32,128]{3,2,1,0:T(8,128)(2,1)S(1)} %get-tuple-element.91), channel_id=1, source_target_pairs={{0,2},{2,0},{4,6},{6,4},{8,10},{10,8},{12,14},{14,12},{16,18},{18,... | collective-permute-start | bytes 245768 | tf_op jit(solution)/shard_map/ppermute | solution.py:836

commit v11 on v10

--- a/solution.py
+++ b/solution.py
@@ -125,18 +125,19 @@
     return fourth(*zs), zs[0] + zs[1]
 
 
-def state_terms(wide, grad_yz, lap_yz, x):
+def state_terms(wide, grad_x, grad_yz, lap_velocity, lap_yz, sizes, x):
     grad = [[None] * 5 for _ in range(3)]
     lap = [None] * 5
     center = [wide[k, x + 3] for k in range(5)]
     for k in range(5):
-        xs = [wide[k, x + 3 + step] for step in (1, -1, 2, -2)]
-        grad[0][k] = fourth(*xs)
+        if k < 3:
+            grad[0][k], lap[k] = grad_x[k, x], lap_velocity[k, x]
+        else:
+            xs = [wide[k, x + 3 + step] for step in (1, -1, 2, -2)]
+            grad[0][k] = fourth(*xs)
+            lap[k] = lap_yz[k, x] + (xs[0] + xs[1])
         grad[1][k], grad[2][k] = grad_yz[k, 0, x], grad_yz[k, 1, x]
-        if k != 3:
-            lap[k] = lap_yz[k, x] + (xs[0] + xs[1])
-    size = size_of(strain_of(grad))
-    return center, grad, lap, size, 1.0 / center[3]
+    return center, grad, lap, sizes[x], 1.0 / center[3]
 
 
 def affine_update(terms, psi, rates, laps):
@@ -346,7 +347,10 @@
         )
 
 
-def inner_products(ops, t, flow, near, far, grad_yz, sums, high, wide, fields, hats):
+def inner_products(
+    ops, t, flow, near, far, grad_yz, lap_yz,
+    sums, high, wide, grad_x, lap_velocity, sizes, fields, hats,
+):
     even = is_even()
     valid = (ops.lane >= 3) & (ops.lane < LANES - 3)
     band = band_of(jnp.maximum(ops.lane - 2, 0))
@@ -362,14 +366,19 @@
         grad = [[None] * 3 for _ in range(3)]
         for k in range(3):
             center = wide[k, x + 3]
-            grad[0][k] = fourth(*(wide[k, x + 3 + step] for step in (1, -1, 2, -2)))
+            xs = [wide[k, x + 3 + step] for step in (1, -1, 2, -2)]
+            grad[0][k] = fourth(*xs)
             if 0 <= x < CX:
+                grad_x[k, x] = grad[0][k]
+                lap_velocity[k, x] = lap_yz[k, x] + (xs[0] + xs[1])
                 grad[1][k], grad[2][k] = grad_yz[k, 0, x], grad_yz[k, 1, x]
             else:
                 grad[1][k] = 0.5 * (ops.y_up(center) - ops.y_down(center))
                 grad[2][k] = fourth(*(turn(center, -step) for step in (1, -1, 2, -2)))
         strain = strain_of(grad)
         size = size_of(strain)
+        if 0 <= x < CX:
+            sizes[x] = size
         velocity = [wide[k, x + 3] for k in range(3)]
         for number, values in enumerate(filter_fields(velocity, strain, size)):
             fields[number, x + 1] = values
@@ -460,20 +469,28 @@
     return rates, laps
 
 
-def inner_kernel(flow, near, far, grad_yz, sums, high, wide, fields, hats):
-    inner_products(Ops(), 0, flow, near, far, grad_yz, sums, high, wide, fields, hats)
+def inner_kernel(
+    flow, near, far, grad_yz, lap_yz,
+    sums, high, wide, grad_x, lap_velocity, sizes,
+    fields, hats,
+):
+    inner_products(
+        Ops(), 0, flow, near, far, grad_yz, lap_yz,
+        sums, high, wide, grad_x, lap_velocity, sizes, fields, hats,
+    )
 
 
 def first_kernel(
-    rho, temp, psi, near, far, velocity, grad_yz, lap_yz, psi_rate, psi_lap,
+    rho, temp, psi, near, far, velocity, grad_x, lap_velocity, sizes,
+    grad_yz, lap_yz, psi_rate, psi_lap,
     first, second, message, columns,
     wide, psi_wide, work,
 ):
     ops = Ops()
     even = is_even()
     for k in range(3):
-        for i in range(1, CX + 5):
-            wide[k, i] = velocity[k, i]
+        for x in range(CX):
+            wide[k, x + 3] = velocity[k, x + 3]
     widen_scalars(0, rho, temp, near, far, even, wide)
     for k in range(5):
         widen(
@@ -484,7 +501,7 @@
             2, even, psi_wide,
         )
     for x in range(CX):
-        terms = state_terms(wide, grad_yz, lap_yz, x)
+        terms = state_terms(wide, grad_x, grad_yz, lap_velocity, lap_yz, sizes, x)
         rates, laps = psi_terms(psi_wide, psi_rate, psi_lap, terms[0][0], x)
         new, slope, sensitivity = affine_update(
             terms, [psi[k, x] for k in range(5)], rates, laps
@@ -518,15 +535,20 @@
 def later_kernel(
     flow, rho, temp, near, far, near_scalars, far_scalars,
     grad_yz, lap_yz, low, halo, first, second,
-    wide, message, columns,
+    wide, grad_x, lap_velocity, sizes, message, columns,
     high, fields, hats, work, bands, spread, sums,
 ):
     ops = Ops()
-    inner_products(ops, 1, flow, near, far, grad_yz, sums, high, wide, fields, hats)
+    inner_products(
+        ops, 1, flow, near, far, grad_yz, lap_yz,
+        sums, high, wide, grad_x, lap_velocity, sizes, fields, hats,
+    )
     widen_scalars(1, rho, temp, near_scalars, far_scalars, is_even(), wide)
     edge_products(ops, 1, low, high, halo, sums, bands, spread)
     for x in range(CX):
-        _, _, lap, size, inv_rho = state_terms(wide, grad_yz, lap_yz, x)
+        _, _, lap, size, inv_rho = state_terms(
+            wide, grad_x, grad_yz, lap_velocity, lap_yz, sizes, x
+        )
         size_rho = size * inv_rho
         for part, source in enumerate((first, second)):
             total = lap[0] * source[0, x] + lap[1] * source[1, x] + lap[2] * source[2, x]
@@ -561,7 +583,8 @@
 
 def base_kernel(
     add_other, span_cells,
-    wide, grad_yz, lap_yz, psi, coef_first, columns, other, later, later_other,
+    wide, grad_x, lap_velocity, sizes, grad_yz, lap_yz, psi, coef_first,
+    columns, other, later, later_other,
     base, drift, spread, coef_grad, near,
     psi_halos, psi_wide, coef_planes, psi_rate, psi_lap,
 ):
@@ -602,7 +625,7 @@
             psi_rate[k, x] = wide[1, x + 3] * by_y + wide[2, x + 3] * by_z
             psi_lap[k, x] = lap + both
     for x in range(CX):
-        terms = state_terms(wide, grad_yz, lap_yz, x)
+        terms = state_terms(wide, grad_x, grad_yz, lap_velocity, lap_yz, sizes, x)
         center = terms[0]
         rates, laps = psi_terms(psi_wide, psi_rate, psi_lap, center[0], x)
         new, slope, _ = affine_update(terms, [psi[k, x] for k in range(5)], rates, laps)
@@ -774,18 +797,24 @@
         1_000_000,
     )
     halo = span_edges(message, 0)
-    inner, high, velocity = call(
+    inner, high, velocity, grad_x, lap_velocity, sizes = call(
         inner_kernel,
         "inner",
-        (flow, near, far, grad_0),
-        [shape_of((2, CX)), shape_of((3,)), shape_of((3, CX + 6))],
+        (flow, near, far, grad_0, lap_0),
+        [
+            shape_of((2, CX)), shape_of((3,)), shape_of((3, CX + 6)),
+            shape_of((3, CX)), shape_of((3, CX)), shape_of((CX,)),
+        ],
         20_000_000,
         scratch((21, CX + 2), (21, CX)),
     )
     first, second, strips, sensitivity = call(
         first_kernel,
         "first",
-        (rho, temp, psi, near_scalars, far_scalars, velocity, grad_0, lap_0, psi_rate, psi_lap),
+        (
+            rho, temp, psi, near_scalars, far_scalars, velocity, grad_x, lap_velocity, sizes,
+            grad_0, lap_0, psi_rate, psi_lap,
+        ),
         [field, field, shape_of((2,)), shape_of(())],
         10_000_000,
         scratch((5, CX + 6), (5, CX + 6), (CX,)),
@@ -800,14 +829,17 @@
     )
     other = span_edges(message, 2)
     columns = span_sums(columns)
-    wide, message, later = call(
+    wide, grad_x, lap_velocity, sizes, message, later = call(
         later_kernel,
         "later",
         (
             flow, rho, temp, near, far, near_scalars, far_scalars,
             grad_1, lap_1, low, halo, first, second,
         ),
-        [planes, shape_of((1,), BF16), shape_of(())],
+        [
+            planes, shape_of((3, CX)), shape_of((3, CX)), shape_of((CX,)),
+            shape_of((1,), BF16), shape_of(()),
+        ],
         20_000_000,
         scratch((3,), (21, CX + 2), (21, CX), (2, CX), (2, 3), (21,), (2, CX)),
     )
@@ -825,7 +857,10 @@
     base, drift, spread, coef_grad, near = call(
         functools.partial(base_kernel, add_other, LANES * lax.axis_size("gz")),
         "base",
-        (wide, grad_1, lap_1, psi, coef_first, columns, other, later, later_other),
+        (
+            wide, grad_x, lap_velocity, sizes, grad_1, lap_1, psi, coef_first,
+            columns, other, later, later_other,
+        ),
         [
             field, shape_of((CX,)), shape_of((2, 2)),
             jax.ShapeDtypeStruct((2, CX, ROWS), F32), edges,

time: 29.1 us -> 28.8 us (0.990)
  no operation moved by 1% of the time
where the time goes in v11:
time: 28.8 us; the launch traced here: 28.7 us
  starting transfers between devices  14.8 us (51%)
  Pallas kernels  9.84 us (34%)
  waiting for transfers between devices  3.36 us (12%)
  between operations  0.72 us (2%)
    pallas_call x14, Pallas kernels, call(): pl.pallas_call(kernel, in_specs=in_specs or whole(len(inputs)), out_specs...  9.84 us
    ppermute x2, starting transfers between devices, local(): far = lax.ppermute(far, 'gx', across)  8.1 us
    ppermute x4, starting transfers between devices, span_edges(): before = lax.ppermute(message, 'gz', forward)  5.88 us
    ppermute x2, waiting for transfers between devices, local(): far = lax.ppermute(far, 'gx', across)  2.41 us
    ppermute x1, waiting for transfers between devices, local(): far_scalars = lax.ppermute(far_scalars, 'gx', across)  0.69 us
  transfers between devices with their start and end apart: 10, of which 3 were waited for; matrix products, arithmetic and copies ran while one was open for 0% of the time, Pallas kernels for 24%

profile of v11, /device:TPU:0, one launch (start us, length us, event | category | flops | bytes accessed | tf_op | source)
XLA Modules:
  0.0 28.7 jit_solution(9387981034408092221)
XLA Ops:
  0.6 1.2 %message.1 = (bf16[18,32,128]{2,1,0:T(8,128)(2,1)S(1)}, bf16[18,32,128]{2,1,0:T(8,128)(2,1)S(1)}, bf16[2,3,4,32,128]{4,3,2,1,0:T(8,128)(2,1)S(1)}, bf16[2,4,32,1...) custom-call(bf16[2,3,4,32,128]{4,3,2,1,0:T(8,128)(2,1)} %flow_far.1, ...), custom_call_target="tpu_custom_call" | custom-call | flops 1000000 | bytes 1605632 | tf_op jit(solution)/shard_map/message/pallas_call | solution.py:716
  1.9 5.5 %collective-permute-start.1 = (bf16[18,32,128]{2,1,0:T(8,128)(2,1)S(1)}, bf16[18,32,128]{2,1,0:T(8,128)(2,1)S(1)}, u32[]{:S(2)}, u32[]{:S(2)}) collective-permute-start(bf16[18,32,128]{2,1,0:T(8,128)(2,1)S(1)} %get-tuple-element.59), channel_id=1, source_target_pairs={{0,30},{2,4},{4,2},{6,8},{8,6},{10,12},{12,10},{14,16},{16,14},{18... | collective-permute-start | bytes 442376 | tf_op jit(solution)/shard_map/ppermute | solution.py:759
  7.3 0.3 pack.1
  7.6 0.5 %collective-permute-start.2 = (bf16[18,32,128]{2,1,0:T(8,128)(2,1)S(1)}, bf16[18,32,128]{2,1,0:T(8,128)(2,1)S(1)}, u32[]{:S(2)}, u32[]{:S(2)}) collective-permute-start(bf16[18,32,128]{2,1,0:T(8,128)(2,1)S(1)} %get-tuple-element.60), channel_id=1, source_target_pairs={{0,2},{2,0},{4,6},{6,4},{8,10},{10,8},{12,14},{14,12},{16,18},{18,... | collective-permute-start | bytes 442376 | tf_op jit(solution)/shard_map/ppermute | solution.py:774
  8.1 0.3 collective-permute-start.3
  8.4 1.7 %collective-permute-start.4 = (bf16[5,32,128]{2,1,0:T(8,128)(2,1)S(1)}, bf16[5,32,128]{2,1,0:T(8,128)(2,1)S(1)}, u32[]{:S(2)}, u32[]{:S(2)}) collective-permute-start(bf16[5,32,128]{2,1,0:T(8,128)(2,1)S(1)} %get-tuple-element.62), channel_id=1, source_target_pairs={{0,1},{1,0},{2,3},{3,2},{4,5},{5,4},{6,7},{7,6},{8,9},{9,8},{10,11... | collective-permute-start | bytes 122888 | tf_op jit(solution)/shard_map/ppermute | solution.py:687
  10.1 0.0 collective-permute-done.1.far
  10.2 0.2 bands.1
  10.4 2.0 %collective-permute-start.5 = (bf16[3,32,128]{2,1,0:T(8,128)(2,1)S(1)}, bf16[3,32,128]{2,1,0:T(8,128)(2,1)S(1)}, u32[]{:S(2)}, u32[]{:S(2)}) collective-permute-start(bf16[3,32,128]{2,1,0:T(8,128)(2,1)S(1)} %get-tuple-element.73), channel_id=1, source_target_pairs={{0,1},{1,0},{2,3},{3,2},{4,5},{5,4},{6,7},{7,6},{8,9},{9,8},{10,11... | collective-permute-start | bytes 73736 | tf_op jit(solution)/shard_map/ppermute | solution.py:687
  12.4 0.3 %rows.1 = (f32[5,4,32,128]{3,2,1,0:T(8,128)S(1)}, f32[5,4,32,128]{3,2,1,0:T(8,128)S(1)}, f32[5,4,32,128]{3,2,1,0:T(8,128)S(1)}, f32[5,4,32,128]{3,2,1,0:T(8,128)...) custom-call(bf16[2,3,4,32,128]{4,3,2,1,0:T(8,128)(2,1)S(1)} %get-tuple-element.54.flow, ...), custom_call_target="tpu_custom_call" | custom-call | flops 3000000 | bytes 2621440 | tf_op jit(solution)/shard_map/rows/pallas_call | solution.py:716
  12.7 0.9 %own.1 = (f32[5,2,4,32,128]{4,3,2,1,0:T(8,128)S(1)}, f32[5,2,4,32,128]{4,3,2,1,0:T(8,128)S(1)}, f32[5,4,32,128]{3,2,1,0:T(8,128)S(1)}, f32[5,4,32,128]{3,2,1,0:T...) custom-call(bf16[2,3,4,32,128]{4,3,2,1,0:T(8,128)(2,1)S(1)} %get-tuple-element.54.flow, ...), custom_call_target="tpu_custom_call" | custom-call | flops 5000000 | bytes 5283840 | tf_op jit(solution)/shard_map/own/pallas_call | solution.py:716
  13.7 1.0 %inner.1 = (f32[2,4,32,128]{3,2,1,0:T(8,128)S(1)}, f32[3,32,128]{2,1,0:T(8,128)S(1)}, f32[3,10,32,128]{3,2,1,0:T(8,128)S(1)}, f32[3,4,32,128]{3,2,1,0:T(8,128)S(...) custom-call(bf16[2,3,4,32,128]{4,3,2,1,0:T(8,128)(2,1)S(1)} %get-tuple-element.54.flow, ...), custom_call_target="tpu_custom_call" | custom-call | flops 20000000 | bytes 2605056 | tf_op jit(solution)/shard_map/inner/pallas_call | solution.py:716
  14.7 0.7 %collective-permute-done.3.far.far_scalars = bf16[18,32,128]{2,1,0:T(8,128)(2,1)S(1)} collective-permute-done((bf16[18,32,128]{2,1,0:T(8,128)(2,1)S(1)}, bf16[18,32,128]{2,1,0:T(8,128)(2,1)S(1)}, u32[]{:S(2)}, u32[]{:S(2)}) %collective-permute-start.3) | collective-permute-done | bytes 147488 | tf_op jit(solution)/shard_map/ppermute | solution.py:772
  15.4 0.7 %first.1 = (f32[5,4,32,128]{3,2,1,0:T(8,128)S(1)}, f32[5,4,32,128]{3,2,1,0:T(8,128)S(1)}, f32[2,32,128]{2,1,0:T(8,128)S(1)}, f32[32,128]{1,0:T(8,128)S(1)}) custom-call(bf16[2,4,32,128]{3,2,1,0:T(8,128)(2,1)S(1)} %get-tuple-element.55.rho, bf16[2,4,32,128]{3,2,1,0:T(8,128)(2,1)S(1)} %get-tuple-element.56.temp, f32[5,4,32,128]{3,2,1,0:T(8,128)S(1)} %get-tuple-element.57.psi, ...), custom_call_target="tpu_custom_call" | custom-call | flops 10000000 | bytes 4046848 | tf_op jit(solution)/shard_map/first/pallas_call | solution.py:716
  16.1 0.9 %edge.1 = (bf16[2,32,128]{2,1,0:T(8,128)(2,1)S(1)}, f32[32,128]{1,0:T(8,128)S(1)}) custom-call(f32[6,32,128]{2,1,0:T(8,128)S(1)} %get-tuple-element.72.low, f32[3,32,128]{2,1,0:T(8,128)S(1)} %get-tuple-element.90.high, bf16[3,32,128]{2,1,0:T(8,128)(2,1)S(1)} %collective-permute-done.5.halo, f32[2,4,32,128]{3,2,1,0:T(8,128)S(1)} %get-tuple-element.91.inner, ...), custom_call_target="tpu_custom_call" | custom-call | flops 20000000 | bytes 385024 | tf_op jit(solution)/shard_map/edge/pallas_call | solution.py:716
  17.0 1.6 %collective-permute-start.6 = (bf16[2,32,128]{2,1,0:T(8,128)(2,1)S(1)}, bf16[2,32,128]{2,1,0:T(8,128)(2,1)S(1)}, u32[]{:S(2)}, u32[]{:S(2)}) collective-permute-start(bf16[2,32,128]{2,1,0:T(8,128)(2,1)S(1)} %get-tuple-element.95), channel_id=1, source_target_pairs={{0,1},{1,0},{2,3},{3,2},{4,5},{5,4},{6,7},{7,6},{8,9},{9,8},{10,11... | collective-permute-start | bytes 49160 | tf_op jit(solution)/shard_map/ppermute | solution.py:687
  18.6 1.8 %later.1 = (f32[5,10,32,128]{3,2,1,0:T(8,128)S(1)}, f32[3,4,32,128]{3,2,1,0:T(8,128)S(1)}, f32[3,4,32,128]{3,2,1,0:T(8,128)S(1)}, f32[4,32,128]{2,1,0:T(8,128)S(...) custom-call(bf16[2,3,4,32,128]{4,3,2,1,0:T(8,128)(2,1)S(1)} %get-tuple-element.54.flow, ...), custom_call_target="tpu_custom_call" | custom-call | flops 20000000 | bytes 3981312 | tf_op jit(solution)/shard_map/later/pallas_call | solution.py:716
  20.4 0.6 %collective-permute-start.7 = (bf16[1,32,128]{2,1,0:T(8,128)(2,1)S(1)}, bf16[1,32,128]{2,1,0:T(8,128)(2,1)S(1)}, u32[]{:S(2)}, u32[]{:S(2)}) collective-permute-start(bf16[1,32,128]{2,1,0:T(8,128)(2,1)S(1)} %get-tuple-element.99), channel_id=1, source_target_pairs={{0,1},{1,0},{2,3},{3,2},{4,5},{5,4},{6,7},{7,6},{8,9},{9,8},{10,11... | collective-permute-start | bytes 24584 | tf_op jit(solution)/shard_map/ppermute | solution.py:687
  20.9 0.3 middle.1
  21.2 2.6 %collective-permute-start.9 = (bf16[5,2,32,128]{3,2,1,0:T(8,128)(2,1)S(1)}, bf16[5,2,32,128]{3,2,1,0:T(8,128)(2,1)S(1)}, u32[]{:S(2)}, u32[]{:S(2)}) collective-permute-start(bf16[5,2,32,128]{3,2,1,0:T(8,128)(2,1)S(1)} %get-tuple-element.104), channel_id=1, source_target_pairs={{0,30},{2,4},{4,2},{6,8},{8,6},{10,12},{12,10},{14,16},{16,14},{18... | collective-permute-start | bytes 245768 | tf_op jit(solution)/shard_map/ppermute | solution.py:856
  23.8 0.2 collective-permute-done.7.later_other
  24.1 1.4 %base.1 = (f32[5,4,32,128]{3,2,1,0:T(8,128)S(1)}, f32[4,32,128]{2,1,0:T(8,128)S(1)}, f32[2,2,32,128]{3,2,1,0:T(8,128)S(1)}, f32[2,4,32]{2,1,0:T(4,128)}, bf16[5,2,32,128]{3,2,1,0:T(8,128)(2,1)S(1)}) custom-call(f32[5,10,32,128]{3,2,1,0:T(8,128)S(1)} %get-tuple-element.84.wide, f32[3,4,32,128]{3,2,1,0:T(8,128)S(1)} %get-tuple-element.85.grad_x, ...), custom_call_target="tpu_custom_call" | custom-call | flops 15000000 | bytes 3253248 | tf_op jit(solution)/shard_map/base/pallas_call | solution.py:716
  25.5 2.4 %collective-permute-done.9.far = bf16[5,2,32,128]{3,2,1,0:T(8,128)(2,1)S(1)} collective-permute-done((bf16[5,2,32,128]{3,2,1,0:T(8,128)(2,1)S(1)}, bf16[5,2,32,128]{3,2,1,0:T(8,128)(2,1)S(1)}, u32[]{:S(2)}, u32[]{:S(2)}) %collective-permute-start.9) | collective-permute-done | bytes 81952 | tf_op jit(solution)/shard_map/ppermute | solution.py:856
  27.9 0.8 %last.1 = f32[5,4,32,128]{3,2,1,0:T(8,128)} custom-call(f32[5,4,32,128]{3,2,1,0:T(8,128)S(1)} %get-tuple-element.100.base, f32[4,32,128]{2,1,0:T(8,128)S(1)} %get-tuple-element.101.drift, f32[2,2,32,128]{3,2,1,0:T(8,128)S(1)} %get-tuple-element.102.spread, bf16[5,2,32,128]{3,2,1,0:T(8,128)(2,1)S(1)} %collective-permute-done.8.near_psi, ...), custom_call_target="tpu_custom_call" | custom-call | flops 1000000 | bytes 1032192 | tf_op jit(solution)/shard_map/last/pallas_call | solution.py:716
  (10 shorter events, 0.1 us)
Async XLA Ops:
  1.9 8.3 %collective-permute-start.1 = (bf16[18,32,128]{2,1,0:T(8,128)(2,1)S(1)}, bf16[18,32,128]{2,1,0:T(8,128)(2,1)S(1)}, u32[]{:S(2)}, u32[]{:S(2)}) collective-permute-start(bf16[18,32,128]{2,1,0:T(8,128)(2,1)S(1)} %get-tuple-element.59), channel_id=1, source_target_pairs={{0,30},{2,4},{4,2},{6,8},{8,6},{10,12},{12,10},{14,16},{16,14},{18... | collective-permute-start | bytes 442376 | tf_op jit(solution)/shard_map/ppermute | solution.py:759
  7.6 2.6 %collective-permute-start = (bf16[18,32,128]{2,1,0:T(8,128)(2,1)S(1)}, bf16[18,32,128]{2,1,0:T(8,128)(2,1)S(1)}, u32[]{:S(2)}, u32[]{:S(2)}) collective-permute-start(bf16[18,32,128]{2,1,0:T(8,128)(2,1)S(1)} %get-tuple-element.58), channel_id=1, source_target_pairs={{0,2},{2,0},{4,6},{6,4},{8,10},{10,8},{12,14},{14,12},{16,18},{18,... | collective-permute-start | bytes 442376 | tf_op jit(solution)/shard_map/ppermute | solution.py:773
  7.6 7.1 %collective-permute-start.2 = (bf16[18,32,128]{2,1,0:T(8,128)(2,1)S(1)}, bf16[18,32,128]{2,1,0:T(8,128)(2,1)S(1)}, u32[]{:S(2)}, u32[]{:S(2)}) collective-permute-start(bf16[18,32,128]{2,1,0:T(8,128)(2,1)S(1)} %get-tuple-element.60), channel_id=1, source_target_pairs={{0,2},{2,0},{4,6},{6,4},{8,10},{10,8},{12,14},{14,12},{16,18},{18,... | collective-permute-start | bytes 442376 | tf_op jit(solution)/shard_map/ppermute | solution.py:774
  8.1 7.3 %collective-permute-start.3 = (bf16[18,32,128]{2,1,0:T(8,128)(2,1)S(1)}, bf16[18,32,128]{2,1,0:T(8,128)(2,1)S(1)}, u32[]{:S(2)}, u32[]{:S(2)}) collective-permute-start(bf16[18,32,128]{2,1,0:T(8,128)(2,1)S(1)} %get-tuple-element.61), channel_id=1, source_target_pairs={{0,30},{2,4},{4,2},{6,8},{8,6},{10,12},{12,10},{14,16},{16,14},{18... | collective-permute-start | bytes 442376 | tf_op jit(solution)/shard_map/ppermute | solution.py:772
  8.4 4.3 %collective-permute-start.4 = (bf16[5,32,128]{2,1,0:T(8,128)(2,1)S(1)}, bf16[5,32,128]{2,1,0:T(8,128)(2,1)S(1)}, u32[]{:S(2)}, u32[]{:S(2)}) collective-permute-start(bf16[5,32,128]{2,1,0:T(8,128)(2,1)S(1)} %get-tuple-element.62), channel_id=1, source_target_pairs={{0,1},{1,0},{2,3},{3,2},{4,5},{5,4},{6,7},{7,6},{8,9},{9,8},{10,11... | collective-permute-start | bytes 122888 | tf_op jit(solution)/shard_map/ppermute | solution.py:687
  10.4 5.7 %collective-permute-start.5 = (bf16[3,32,128]{2,1,0:T(8,128)(2,1)S(1)}, bf16[3,32,128]{2,1,0:T(8,128)(2,1)S(1)}, u32[]{:S(2)}, u32[]{:S(2)}) collective-permute-start(bf16[3,32,128]{2,1,0:T(8,128)(2,1)S(1)} %get-tuple-element.73), channel_id=1, source_target_pairs={{0,1},{1,0},{2,3},{3,2},{4,5},{5,4},{6,7},{7,6},{8,9},{9,8},{10,11... | collective-permute-start | bytes 73736 | tf_op jit(solution)/shard_map/ppermute | solution.py:687
  17.0 4.0 %collective-permute-start.6 = (bf16[2,32,128]{2,1,0:T(8,128)(2,1)S(1)}, bf16[2,32,128]{2,1,0:T(8,128)(2,1)S(1)}, u32[]{:S(2)}, u32[]{:S(2)}) collective-permute-start(bf16[2,32,128]{2,1,0:T(8,128)(2,1)S(1)} %get-tuple-element.95), channel_id=1, source_target_pairs={{0,1},{1,0},{2,3},{3,2},{4,5},{5,4},{6,7},{7,6},{8,9},{9,8},{10,11... | collective-permute-start | bytes 49160 | tf_op jit(solution)/shard_map/ppermute | solution.py:687
  20.4 3.7 %collective-permute-start.7 = (bf16[1,32,128]{2,1,0:T(8,128)(2,1)S(1)}, bf16[1,32,128]{2,1,0:T(8,128)(2,1)S(1)}, u32[]{:S(2)}, u32[]{:S(2)}) collective-permute-start(bf16[1,32,128]{2,1,0:T(8,128)(2,1)S(1)} %get-tuple-element.99), channel_id=1, source_target_pairs={{0,1},{1,0},{2,3},{3,2},{4,5},{5,4},{6,7},{7,6},{8,9},{9,8},{10,11... | collective-permute-start | bytes 24584 | tf_op jit(solution)/shard_map/ppermute | solution.py:687
  21.2 6.6 %collective-permute-start.9 = (bf16[5,2,32,128]{3,2,1,0:T(8,128)(2,1)S(1)}, bf16[5,2,32,128]{3,2,1,0:T(8,128)(2,1)S(1)}, u32[]{:S(2)}, u32[]{:S(2)}) collective-permute-start(bf16[5,2,32,128]{3,2,1,0:T(8,128)(2,1)S(1)} %get-tuple-element.104), channel_id=1, source_target_pairs={{0,30},{2,4},{4,2},{6,8},{8,6},{10,12},{12,10},{14,16},{16,14},{18... | collective-permute-start | bytes 245768 | tf_op jit(solution)/shard_map/ppermute | solution.py:856
  25.5 2.4 %collective-permute-start.8 = (bf16[5,2,32,128]{3,2,1,0:T(8,128)(2,1)S(1)}, bf16[5,2,32,128]{3,2,1,0:T(8,128)(2,1)S(1)}, u32[]{:S(2)}, u32[]{:S(2)}) collective-permute-start(bf16[5,2,32,128]{3,2,1,0:T(8,128)(2,1)S(1)} %get-tuple-element.103), channel_id=1, source_target_pairs={{0,2},{2,0},{4,6},{6,4},{8,10},{10,8},{12,14},{14,12},{16,18},{18,... | collective-permute-start | bytes 245768 | tf_op jit(solution)/shard_map/ppermute | solution.py:871

commit v12 on v11

--- a/solution.py
+++ b/solution.py
@@ -287,7 +287,7 @@
             psi_lap[k, x] = psi_lap_y[k, x] + both
 
 
-def token_kernel(far, out):
+def token_kernel(far, _, out):
     out[...] = far[0].astype(F32)
 
 
@@ -481,7 +481,7 @@
 
 
 def first_kernel(
-    rho, temp, psi, near, far, velocity, grad_x, lap_velocity, sizes,
+    _, rho, temp, psi, near, far, velocity, grad_x, lap_velocity, sizes,
     grad_yz, lap_yz, psi_rate, psi_lap,
     first, second, message, columns,
     wide, psi_wide, work,
@@ -788,7 +788,7 @@
         5_000_000,
         scratch((2, 5, CX), (5, CX)),
     )
-    (token,) = call(token_kernel, "token", (far,), [shape_of(())], 100_000)
+    (token,) = call(token_kernel, "token", (far, rows[5]), [shape_of(())], 100_000)
     message, low = call(
         bands_kernel,
         "bands",
@@ -808,11 +808,13 @@
         20_000_000,
         scratch((21, CX + 2), (21, CX)),
     )
+    (token,) = call(token_kernel, "later_token", (far_scalars, sizes), [shape_of(())], 100_000)
     first, second, strips, sensitivity = call(
         first_kernel,
         "first",
         (
-            rho, temp, psi, near_scalars, far_scalars, velocity, grad_x, lap_velocity, sizes,
+            token, rho, temp, psi, near_scalars, far_scalars,
+            velocity, grad_x, lap_velocity, sizes,
             grad_0, lap_0, psi_rate, psi_lap,
         ),
         [field, field, shape_of((2,)), shape_of(())],

time: 28.8 us -> 28.4 us (0.986)
  starting transfers between devices: 14.8 us -> 14.5 us
    ppermute x1, starting transfers between devices: 0.5 us -> 0.01 us  [local(): near_scalars = lax.ppermute(near_scalars, 'gx', inside)]
    ppermute x1, starting transfers between devices: 0.26 us -> 0.68 us  [local(): far_scalars = lax.ppermute(far_scalars, 'gx', across)]
    pallas_call x14 -> x15, Pallas kernels: 9.84 us -> 9.86 us  [call(): pl.pallas_call(kernel, in_specs=in_specs or whole(len(inputs)), out_specs...]
  transfers between devices with their start and end apart: 10 -> 10, of which waited for: 3 -> 3; matrix products, arithmetic and copies ran while one was open for 0% -> 0% of each run, Pallas kernels for 24% -> 25%
where the time goes in v12:
time: 28.4 us; the launch traced here: 28.3 us
  starting transfers between devices  14.5 us (51%)
  Pallas kernels  9.86 us (35%)
  waiting for transfers between devices  3.16 us (11%)
  between operations  0.73 us (3%)
    pallas_call x15, Pallas kernels, call(): pl.pallas_call(kernel, in_specs=in_specs or whole(len(inputs)), out_specs...  9.86 us
    ppermute x2, starting transfers between devices, local(): far = lax.ppermute(far, 'gx', across)  8.19 us
    ppermute x4, starting transfers between devices, span_edges(): before = lax.ppermute(message, 'gz', forward)  5.63 us
    ppermute x2, waiting for transfers between devices, local(): far = lax.ppermute(far, 'gx', across)  2.37 us
    ppermute x1, starting transfers between devices, local(): far_scalars = lax.ppermute(far_scalars, 'gx', across)  0.68 us
    ppermute x1, waiting for transfers between devices, local(): far_scalars = lax.ppermute(far_scalars, 'gx', across)  0.62 us
  transfers between devices with their start and end apart: 10, of which 3 were waited for; matrix products, arithmetic and copies ran while one was open for 0% of the time, Pallas kernels for 25%

profile of v12, /device:TPU:0, one launch (start us, length us, event | category | flops | bytes accessed | tf_op | source)
XLA Modules:
  0.0 28.3 jit_solution(9992746912813621942)
XLA Ops:
  0.6 1.2 %message.1 = (bf16[18,32,128]{2,1,0:T(8,128)(2,1)S(1)}, bf16[18,32,128]{2,1,0:T(8,128)(2,1)S(1)}, bf16[2,3,4,32,128]{4,3,2,1,0:T(8,128)(2,1)S(1)}, bf16[2,4,32,1...) custom-call(bf16[2,3,4,32,128]{4,3,2,1,0:T(8,128)(2,1)} %flow_far.1, ...), custom_call_target="tpu_custom_call" | custom-call | flops 1000000 | bytes 1605632 | tf_op jit(solution)/shard_map/message/pallas_call | solution.py:716
  1.9 5.5 %collective-permute-start.1 = (bf16[18,32,128]{2,1,0:T(8,128)(2,1)S(1)}, bf16[18,32,128]{2,1,0:T(8,128)(2,1)S(1)}, u32[]{:S(2)}, u32[]{:S(2)}) collective-permute-start(bf16[18,32,128]{2,1,0:T(8,128)(2,1)S(1)} %get-tuple-element.59), channel_id=1, source_target_pairs={{0,30},{2,4},{4,2},{6,8},{8,6},{10,12},{12,10},{14,16},{16,14},{18... | collective-permute-start | bytes 442376 | tf_op jit(solution)/shard_map/ppermute | solution.py:759
  7.3 0.3 pack.1
  7.6 0.0 collective-permute-start
  7.6 0.7 %collective-permute-start.3 = (bf16[18,32,128]{2,1,0:T(8,128)(2,1)S(1)}, bf16[18,32,128]{2,1,0:T(8,128)(2,1)S(1)}, u32[]{:S(2)}, u32[]{:S(2)}) collective-permute-start(bf16[18,32,128]{2,1,0:T(8,128)(2,1)S(1)} %get-tuple-element.61), channel_id=1, source_target_pairs={{0,30},{2,4},{4,2},{6,8},{8,6},{10,12},{12,10},{14,16},{16,14},{18... | collective-permute-start | bytes 442376 | tf_op jit(solution)/shard_map/ppermute | solution.py:772
  8.3 0.0 collective-permute-start.2
  8.3 1.5 %collective-permute-start.4 = (bf16[5,32,128]{2,1,0:T(8,128)(2,1)S(1)}, bf16[5,32,128]{2,1,0:T(8,128)(2,1)S(1)}, u32[]{:S(2)}, u32[]{:S(2)}) collective-permute-start(bf16[5,32,128]{2,1,0:T(8,128)(2,1)S(1)} %get-tuple-element.62), channel_id=1, source_target_pairs={{0,1},{1,0},{2,3},{3,2},{4,5},{5,4},{6,7},{7,6},{8,9},{9,8},{10,11... | collective-permute-start | bytes 122888 | tf_op jit(solution)/shard_map/ppermute | solution.py:687
  9.8 0.3 %rows.1 = (f32[5,4,32,128]{3,2,1,0:T(8,128)S(1)}, f32[5,4,32,128]{3,2,1,0:T(8,128)S(1)}, f32[5,4,32,128]{3,2,1,0:T(8,128)S(1)}, f32[5,4,32,128]{3,2,1,0:T(8,128)...) custom-call(bf16[2,3,4,32,128]{4,3,2,1,0:T(8,128)(2,1)S(1)} %get-tuple-element.54.flow, ...), custom_call_target="tpu_custom_call" | custom-call | flops 3000000 | bytes 2621440 | tf_op jit(solution)/shard_map/rows/pallas_call | solution.py:716
  10.2 0.2 bands.1
  10.4 2.0 %collective-permute-start.5 = (bf16[3,32,128]{2,1,0:T(8,128)(2,1)S(1)}, bf16[3,32,128]{2,1,0:T(8,128)(2,1)S(1)}, u32[]{:S(2)}, u32[]{:S(2)}) collective-permute-start(bf16[3,32,128]{2,1,0:T(8,128)(2,1)S(1)} %get-tuple-element.73), channel_id=1, source_target_pairs={{0,1},{1,0},{2,3},{3,2},{4,5},{5,4},{6,7},{7,6},{8,9},{9,8},{10,11... | collective-permute-start | bytes 73736 | tf_op jit(solution)/shard_map/ppermute | solution.py:687
  12.4 0.9 %own.1 = (f32[5,2,4,32,128]{4,3,2,1,0:T(8,128)S(1)}, f32[5,2,4,32,128]{4,3,2,1,0:T(8,128)S(1)}, f32[5,4,32,128]{3,2,1,0:T(8,128)S(1)}, f32[5,4,32,128]{3,2,1,0:T...) custom-call(bf16[2,3,4,32,128]{4,3,2,1,0:T(8,128)(2,1)S(1)} %get-tuple-element.54.flow, ...), custom_call_target="tpu_custom_call" | custom-call | flops 5000000 | bytes 5283840 | tf_op jit(solution)/shard_map/own/pallas_call | solution.py:716
  13.3 1.0 %inner.1 = (f32[2,4,32,128]{3,2,1,0:T(8,128)S(1)}, f32[3,32,128]{2,1,0:T(8,128)S(1)}, f32[3,10,32,128]{3,2,1,0:T(8,128)S(1)}, f32[3,4,32,128]{3,2,1,0:T(8,128)S(...) custom-call(bf16[2,3,4,32,128]{4,3,2,1,0:T(8,128)(2,1)S(1)} %get-tuple-element.54.flow, ...), custom_call_target="tpu_custom_call" | custom-call | flops 20000000 | bytes 2605056 | tf_op jit(solution)/shard_map/inner/pallas_call | solution.py:716
  14.3 0.6 %collective-permute-done.3.far.far_scalars = bf16[18,32,128]{2,1,0:T(8,128)(2,1)S(1)} collective-permute-done((bf16[18,32,128]{2,1,0:T(8,128)(2,1)S(1)}, bf16[18,32,128]{2,1,0:T(8,128)(2,1)S(1)}, u32[]{:S(2)}, u32[]{:S(2)}) %collective-permute-start.3) | collective-permute-done | bytes 147488 | tf_op jit(solution)/shard_map/ppermute | solution.py:772
  15.0 0.7 %first.1 = (f32[5,4,32,128]{3,2,1,0:T(8,128)S(1)}, f32[5,4,32,128]{3,2,1,0:T(8,128)S(1)}, f32[2,32,128]{2,1,0:T(8,128)S(1)}, f32[32,128]{1,0:T(8,128)S(1)}) custom-call(f32[32,128]{1,0:T(8,128)S(1)} %later_token.1._, bf16[2,4,32,128]{3,2,1,0:T(8,128)(2,1)S(1)} %get-tuple-element.55.rho, bf16[2,4,32,128]{3,2,1,0:T(8,128)(2,1)S(1)} %get-tuple-element.56.temp, ...), custom_call_target="tpu_custom_call" | custom-call | flops 10000000 | bytes 4063232 | tf_op jit(solution)/shard_map/first/pallas_call | solution.py:716
  15.7 0.9 %edge.1 = (bf16[2,32,128]{2,1,0:T(8,128)(2,1)S(1)}, f32[32,128]{1,0:T(8,128)S(1)}) custom-call(f32[6,32,128]{2,1,0:T(8,128)S(1)} %get-tuple-element.72.low, f32[3,32,128]{2,1,0:T(8,128)S(1)} %get-tuple-element.90.high, bf16[3,32,128]{2,1,0:T(8,128)(2,1)S(1)} %collective-permute-done.5.halo, f32[2,4,32,128]{3,2,1,0:T(8,128)S(1)} %get-tuple-element.91.inner, ...), custom_call_target="tpu_custom_call" | custom-call | flops 20000000 | bytes 385024 | tf_op jit(solution)/shard_map/edge/pallas_call | solution.py:716
  16.6 1.6 %collective-permute-start.6 = (bf16[2,32,128]{2,1,0:T(8,128)(2,1)S(1)}, bf16[2,32,128]{2,1,0:T(8,128)(2,1)S(1)}, u32[]{:S(2)}, u32[]{:S(2)}) collective-permute-start(bf16[2,32,128]{2,1,0:T(8,128)(2,1)S(1)} %get-tuple-element.95), channel_id=1, source_target_pairs={{0,1},{1,0},{2,3},{3,2},{4,5},{5,4},{6,7},{7,6},{8,9},{9,8},{10,11... | collective-permute-start | bytes 49160 | tf_op jit(solution)/shard_map/ppermute | solution.py:687
  18.1 1.8 %later.1 = (f32[5,10,32,128]{3,2,1,0:T(8,128)S(1)}, f32[3,4,32,128]{3,2,1,0:T(8,128)S(1)}, f32[3,4,32,128]{3,2,1,0:T(8,128)S(1)}, f32[4,32,128]{2,1,0:T(8,128)S(...) custom-call(bf16[2,3,4,32,128]{4,3,2,1,0:T(8,128)(2,1)S(1)} %get-tuple-element.54.flow, ...), custom_call_target="tpu_custom_call" | custom-call | flops 20000000 | bytes 3981312 | tf_op jit(solution)/shard_map/later/pallas_call | solution.py:716
  20.0 0.6 %collective-permute-start.7 = (bf16[1,32,128]{2,1,0:T(8,128)(2,1)S(1)}, bf16[1,32,128]{2,1,0:T(8,128)(2,1)S(1)}, u32[]{:S(2)}, u32[]{:S(2)}) collective-permute-start(bf16[1,32,128]{2,1,0:T(8,128)(2,1)S(1)} %get-tuple-element.99), channel_id=1, source_target_pairs={{0,1},{1,0},{2,3},{3,2},{4,5},{5,4},{6,7},{7,6},{8,9},{9,8},{10,11... | collective-permute-start | bytes 24584 | tf_op jit(solution)/shard_map/ppermute | solution.py:687
  20.5 0.3 middle.1
  20.8 2.7 %collective-permute-start.9 = (bf16[5,2,32,128]{3,2,1,0:T(8,128)(2,1)S(1)}, bf16[5,2,32,128]{3,2,1,0:T(8,128)(2,1)S(1)}, u32[]{:S(2)}, u32[]{:S(2)}) collective-permute-start(bf16[5,2,32,128]{3,2,1,0:T(8,128)(2,1)S(1)} %get-tuple-element.104), channel_id=1, source_target_pairs={{0,30},{2,4},{4,2},{6,8},{8,6},{10,12},{12,10},{14,16},{16,14},{18... | collective-permute-start | bytes 245768 | tf_op jit(solution)/shard_map/ppermute | solution.py:858
  23.5 0.1 collective-permute-done.7.later_other
  23.7 1.4 %base.1 = (f32[5,4,32,128]{3,2,1,0:T(8,128)S(1)}, f32[4,32,128]{2,1,0:T(8,128)S(1)}, f32[2,2,32,128]{3,2,1,0:T(8,128)S(1)}, f32[2,4,32]{2,1,0:T(4,128)}, bf16[5,2,32,128]{3,2,1,0:T(8,128)(2,1)S(1)}) custom-call(f32[5,10,32,128]{3,2,1,0:T(8,128)S(1)} %get-tuple-element.84.wide, f32[3,4,32,128]{3,2,1,0:T(8,128)S(1)} %get-tuple-element.85.grad_x, ...), custom_call_target="tpu_custom_call" | custom-call | flops 15000000 | bytes 3253248 | tf_op jit(solution)/shard_map/base/pallas_call | solution.py:716
  25.1 2.4 %collective-permute-done.9.far = bf16[5,2,32,128]{3,2,1,0:T(8,128)(2,1)S(1)} collective-permute-done((bf16[5,2,32,128]{3,2,1,0:T(8,128)(2,1)S(1)}, bf16[5,2,32,128]{3,2,1,0:T(8,128)(2,1)S(1)}, u32[]{:S(2)}, u32[]{:S(2)}) %collective-permute-start.9) | collective-permute-done | bytes 81952 | tf_op jit(solution)/shard_map/ppermute | solution.py:858
  27.5 0.8 %last.1 = f32[5,4,32,128]{3,2,1,0:T(8,128)} custom-call(f32[5,4,32,128]{3,2,1,0:T(8,128)S(1)} %get-tuple-element.100.base, f32[4,32,128]{2,1,0:T(8,128)S(1)} %get-tuple-element.101.drift, f32[2,2,32,128]{3,2,1,0:T(8,128)S(1)} %get-tuple-element.102.spread, bf16[5,2,32,128]{3,2,1,0:T(8,128)(2,1)S(1)} %collective-permute-done.8.near_psi, ...), custom_call_target="tpu_custom_call" | custom-call | flops 1000000 | bytes 1032192 | tf_op jit(solution)/shard_map/last/pallas_call | solution.py:716
  (11 shorter events, 0.0 us)
Async XLA Ops:
  1.9 8.3 %collective-permute-start.1 = (bf16[18,32,128]{2,1,0:T(8,128)(2,1)S(1)}, bf16[18,32,128]{2,1,0:T(8,128)(2,1)S(1)}, u32[]{:S(2)}, u32[]{:S(2)}) collective-permute-start(bf16[18,32,128]{2,1,0:T(8,128)(2,1)S(1)} %get-tuple-element.59), channel_id=1, source_target_pairs={{0,30},{2,4},{4,2},{6,8},{8,6},{10,12},{12,10},{14,16},{16,14},{18... | collective-permute-start | bytes 442376 | tf_op jit(solution)/shard_map/ppermute | solution.py:759
  7.6 2.6 %collective-permute-start = (bf16[18,32,128]{2,1,0:T(8,128)(2,1)S(1)}, bf16[18,32,128]{2,1,0:T(8,128)(2,1)S(1)}, u32[]{:S(2)}, u32[]{:S(2)}) collective-permute-start(bf16[18,32,128]{2,1,0:T(8,128)(2,1)S(1)} %get-tuple-element.58), channel_id=1, source_target_pairs={{0,2},{2,0},{4,6},{6,4},{8,10},{10,8},{12,14},{14,12},{16,18},{18,... | collective-permute-start | bytes 442376 | tf_op jit(solution)/shard_map/ppermute | solution.py:773
  7.6 7.3 %collective-permute-start.3 = (bf16[18,32,128]{2,1,0:T(8,128)(2,1)S(1)}, bf16[18,32,128]{2,1,0:T(8,128)(2,1)S(1)}, u32[]{:S(2)}, u32[]{:S(2)}) collective-permute-start(bf16[18,32,128]{2,1,0:T(8,128)(2,1)S(1)} %get-tuple-element.61), channel_id=1, source_target_pairs={{0,30},{2,4},{4,2},{6,8},{8,6},{10,12},{12,10},{14,16},{16,14},{18... | collective-permute-start | bytes 442376 | tf_op jit(solution)/shard_map/ppermute | solution.py:772
  8.3 6.7 %collective-permute-start.2 = (bf16[18,32,128]{2,1,0:T(8,128)(2,1)S(1)}, bf16[18,32,128]{2,1,0:T(8,128)(2,1)S(1)}, u32[]{:S(2)}, u32[]{:S(2)}) collective-permute-start(bf16[18,32,128]{2,1,0:T(8,128)(2,1)S(1)} %get-tuple-element.60), channel_id=1, source_target_pairs={{0,2},{2,0},{4,6},{6,4},{8,10},{10,8},{12,14},{14,12},{16,18},{18,... | collective-permute-start | bytes 442376 | tf_op jit(solution)/shard_map/ppermute | solution.py:774
  8.3 4.1 %collective-permute-start.4 = (bf16[5,32,128]{2,1,0:T(8,128)(2,1)S(1)}, bf16[5,32,128]{2,1,0:T(8,128)(2,1)S(1)}, u32[]{:S(2)}, u32[]{:S(2)}) collective-permute-start(bf16[5,32,128]{2,1,0:T(8,128)(2,1)S(1)} %get-tuple-element.62), channel_id=1, source_target_pairs={{0,1},{1,0},{2,3},{3,2},{4,5},{5,4},{6,7},{7,6},{8,9},{9,8},{10,11... | collective-permute-start | bytes 122888 | tf_op jit(solution)/shard_map/ppermute | solution.py:687
  10.4 5.3 %collective-permute-start.5 = (bf16[3,32,128]{2,1,0:T(8,128)(2,1)S(1)}, bf16[3,32,128]{2,1,0:T(8,128)(2,1)S(1)}, u32[]{:S(2)}, u32[]{:S(2)}) collective-permute-start(bf16[3,32,128]{2,1,0:T(8,128)(2,1)S(1)} %get-tuple-element.73), channel_id=1, source_target_pairs={{0,1},{1,0},{2,3},{3,2},{4,5},{5,4},{6,7},{7,6},{8,9},{9,8},{10,11... | collective-permute-start | bytes 73736 | tf_op jit(solution)/shard_map/ppermute | solution.py:687
  16.6 4.0 %collective-permute-start.6 = (bf16[2,32,128]{2,1,0:T(8,128)(2,1)S(1)}, bf16[2,32,128]{2,1,0:T(8,128)(2,1)S(1)}, u32[]{:S(2)}, u32[]{:S(2)}) collective-permute-start(bf16[2,32,128]{2,1,0:T(8,128)(2,1)S(1)} %get-tuple-element.95), channel_id=1, source_target_pairs={{0,1},{1,0},{2,3},{3,2},{4,5},{5,4},{6,7},{7,6},{8,9},{9,8},{10,11... | collective-permute-start | bytes 49160 | tf_op jit(solution)/shard_map/ppermute | solution.py:687
  20.0 3.7 %collective-permute-start.7 = (bf16[1,32,128]{2,1,0:T(8,128)(2,1)S(1)}, bf16[1,32,128]{2,1,0:T(8,128)(2,1)S(1)}, u32[]{:S(2)}, u32[]{:S(2)}) collective-permute-start(bf16[1,32,128]{2,1,0:T(8,128)(2,1)S(1)} %get-tuple-element.99), channel_id=1, source_target_pairs={{0,1},{1,0},{2,3},{3,2},{4,5},{5,4},{6,7},{7,6},{8,9},{9,8},{10,11... | collective-permute-start | bytes 24584 | tf_op jit(solution)/shard_map/ppermute | solution.py:687
  20.8 6.6 %collective-permute-start.9 = (bf16[5,2,32,128]{3,2,1,0:T(8,128)(2,1)S(1)}, bf16[5,2,32,128]{3,2,1,0:T(8,128)(2,1)S(1)}, u32[]{:S(2)}, u32[]{:S(2)}) collective-permute-start(bf16[5,2,32,128]{3,2,1,0:T(8,128)(2,1)S(1)} %get-tuple-element.104), channel_id=1, source_target_pairs={{0,30},{2,4},{4,2},{6,8},{8,6},{10,12},{12,10},{14,16},{16,14},{18... | collective-permute-start | bytes 245768 | tf_op jit(solution)/shard_map/ppermute | solution.py:858
  25.1 2.4 %collective-permute-start.8 = (bf16[5,2,32,128]{3,2,1,0:T(8,128)(2,1)S(1)}, bf16[5,2,32,128]{3,2,1,0:T(8,128)(2,1)S(1)}, u32[]{:S(2)}, u32[]{:S(2)}) collective-permute-start(bf16[5,2,32,128]{3,2,1,0:T(8,128)(2,1)S(1)} %get-tuple-element.103), channel_id=1, source_target_pairs={{0,2},{2,0},{4,6},{6,4},{8,10},{10,8},{12,14},{14,12},{16,18},{18,... | collective-permute-start | bytes 245768 | tf_op jit(solution)/shard_map/ppermute | solution.py:873

commit v13 on v12

--- a/solution.py
+++ b/solution.py
@@ -28,8 +28,9 @@
 BAND_BLOCKS = 3
 VELOCITY = 0
 SCALARS = 18
-PSI = 8
-SCALAR_PLANES = 18
+MESSAGE = 22
+PSI = 4
+SCALAR_PLANES = 14
 
 
 def lane_ids():
@@ -177,10 +178,9 @@
 
 
 def fill_scalars(out, side, rho, temp, psi):
-    for t in range(2):
-        for i in range(2):
-            out[2 * t + i] = rho[t, 2 * side + i]
-            out[4 + 2 * t + i] = temp[t, 2 * side + i]
+    for i in range(2):
+        out[i] = rho[0, 2 * side + i]
+        out[2 + i] = temp[0, 2 * side + i]
     for k in range(5):
         for i in range(2):
             out[PSI + k * 2 + i] = psi[k, 2 * side + i].astype(BF16)
@@ -193,12 +193,21 @@
         message[first + number] = both.astype(BF16)
 
 
+def fill_later(out, side, rho, temp):
+    for i in range(2):
+        out[SCALARS + i] = rho[1, 2 * side + i]
+        out[SCALARS + 2 + i] = temp[1, 2 * side + i]
+
+
 def message_kernel(
     flow_far, rho_far, temp_far, psi_far, far, far_scalars, flow, rho, temp, psi, sems
 ):
     side = 1 - is_even().astype(jnp.int32)
     pieces = (
-        (flow_far.at[:, :, pl.ds(side, 3)], far.reshape((2, 3, 3, ROWS, LANES))),
+        (
+            flow_far.at[:, :, pl.ds(side, 3)],
+            far.at[pl.ds(VELOCITY, 18)].reshape((2, 3, 3, ROWS, LANES)),
+        ),
         (psi_far, psi),
         (rho_far, rho),
         (temp_far, temp),
@@ -213,6 +222,7 @@
     for copy in copies[1:4]:
         copy.wait()
     fill_scalars(far_scalars, side, rho, temp, psi)
+    fill_later(far, side, rho, temp)
     copies[0].wait()
     copies[4].wait()
 
@@ -225,6 +235,7 @@
             for i in range(3):
                 near[VELOCITY + t * 9 + k * 3 + i] = flow[t, k, side + i]
     fill_scalars(near_scalars, side, rho, temp, psi)
+    fill_later(near, side, rho, temp)
     items = []
     for t in range(2):
         for source in (rho, temp):
@@ -335,9 +346,9 @@
         wide[k, 3 + x] = source(x).astype(F32)
 
 
-def widen_scalars(t, rho, temp, near, far, even, wide):
+def widen_scalars(t, first, rho, temp, near, far, even, wide):
     for k, source in ((3, rho), (4, temp)):
-        number = (k - 3) * 4 + 2 * t
+        number = first + (k - 3) * 2
         widen(
             k,
             lambda x: source[t, x],
@@ -491,7 +502,7 @@
     for k in range(3):
         for x in range(CX):
             wide[k, x + 3] = velocity[k, x + 3]
-    widen_scalars(0, rho, temp, near, far, even, wide)
+    widen_scalars(0, 0, rho, temp, near, far, even, wide)
     for k in range(5):
         widen(
             k,
@@ -533,8 +544,7 @@
 
 
 def later_kernel(
-    flow, rho, temp, near, far, near_scalars, far_scalars,
-    grad_yz, lap_yz, low, halo, first, second,
+    flow, rho, temp, near, far, grad_yz, lap_yz, low, halo, first, second,
     wide, grad_x, lap_velocity, sizes, message, columns,
     high, fields, hats, work, bands, spread, sums,
 ):
@@ -543,7 +553,7 @@
         ops, 1, flow, near, far, grad_yz, lap_yz,
         sums, high, wide, grad_x, lap_velocity, sizes, fields, hats,
     )
-    widen_scalars(1, rho, temp, near_scalars, far_scalars, is_even(), wide)
+    widen_scalars(1, SCALARS, rho, temp, near, far, is_even(), wide)
     edge_products(ops, 1, low, high, halo, sums, bands, spread)
     for x in range(CX):
         _, _, lap, size, inv_rho = state_terms(
@@ -648,8 +658,9 @@
             out[k, i] = far[k, i].astype(F32)
 
 
-def last_kernel(base, drift, spread, near_psi, far_psi, out):
+def last_kernel(base, drift, spread, near_psi, far_psi, out_far, out, sems):
     even = is_even()
+    copies = []
     for k in range(5):
         ones = [near_psi[k, i].astype(F32) for i in range(2)]
         twos = [far_psi[k, i].astype(F32) for i in range(2)]
@@ -665,6 +676,10 @@
         out[k, 1] = base[k, 1] + drift[1] * ((1.0 / 12.0) * near)
         out[k, CX - 2] = base[k, CX - 2] - drift[CX - 2] * ((1.0 / 12.0) * after)
         out[k, CX - 1] = base[k, CX - 1] + high
+        copies.append(pltpu.make_async_copy(out.at[k], out_far.at[k], sems.at[k]))
+        copies[k].start()
+    for copy in copies:
+        copy.wait()
 
 
 def ring(axis):
@@ -706,7 +721,7 @@
     return [pltpu.VMEM(d + (ROWS, LANES), F32) for d in dims]
 
 
-def call(kernel, name, inputs, outputs, operations, buffers=(), in_specs=None):
+def call(kernel, name, inputs, outputs, operations, buffers=(), in_specs=None, out_specs=None):
     inputs = list(inputs)
     if in_specs:
         inputs[:4] = [
@@ -716,7 +731,7 @@
     return pl.pallas_call(
         kernel,
         in_specs=in_specs or whole(len(inputs)),
-        out_specs=whole(len(outputs)),
+        out_specs=out_specs or whole(len(outputs)),
         out_shape=list(outputs),
         scratch_shapes=list(buffers),
         compiler_params=pltpu.CompilerParams(vmem_limit_bytes=8 * 2**20),
@@ -745,7 +760,7 @@
         "message",
         inputs,
         [
-            shape_of((SCALARS,), BF16),
+            shape_of((MESSAGE,), BF16),
             shape_of((SCALAR_PLANES,), BF16),
             shape_of((2, 3, CX), BF16),
             shape_of((2, CX), BF16),
@@ -762,7 +777,7 @@
         "pack",
         (flow, rho, temp, psi),
         [
-            shape_of((SCALARS,), BF16),
+            shape_of((MESSAGE,), BF16),
             shape_of((SCALAR_PLANES,), BF16),
             shape_of((STRIP_BLOCKS + BAND_BLOCKS,), BF16),
             shape_of((6,)),
@@ -835,8 +850,7 @@
         later_kernel,
         "later",
         (
-            flow, rho, temp, near, far, near_scalars, far_scalars,
-            grad_1, lap_1, low, halo, first, second,
+            flow, rho, temp, near, far, grad_1, lap_1, low, halo, first, second,
         ),
         [
             planes, shape_of((3, CX)), shape_of((3, CX)), shape_of((CX,)),
@@ -872,7 +886,15 @@
     )
     near = lax.ppermute(near, "gx", inside)
     (far,) = call(widen_kernel, "widen", (far,), [shape_of((5, 2))], 100_000)
-    (out,) = call(last_kernel, "last", (base, drift, spread, near, far), [field], 1_000_000)
+    (out,) = call(
+        last_kernel,
+        "last",
+        (base, drift, spread, near, far),
+        [field],
+        1_000_000,
+        scratch((5, CX)) + [pltpu.SemaphoreType.DMA((5,))],
+        out_specs=stay[:1],
+    )
     return out, coef_grad
 
 

time: 28.4 us -> 28.2 us (level)
  waiting for transfers between devices: 3.16 us -> 2.24 us
  starting transfers between devices: 14.5 us -> 15.2 us
    ppermute x2, starting transfers between devices: 8.19 us -> 8.81 us  [local(): far = lax.ppermute(far, 'gx', across)]
    ppermute x1, waiting for transfers between devices: 0.62 us -> 0.01 us  [local(): far_scalars = lax.ppermute(far_scalars, 'gx', across)]
  transfers between devices with their start and end apart: 10 -> 10, of which waited for: 3 -> 2; matrix products, arithmetic and copies ran while one was open for 0% -> 0% of each run, Pallas kernels for 25% -> 25%
where the time goes in v13:
time: 28.2 us; the launch traced here: 28 us
  starting transfers between devices  15.2 us (54%)
  Pallas kernels  9.84 us (35%)
  waiting for transfers between devices  2.24 us (8%)
  between operations  0.73 us (3%)
    pallas_call x15, Pallas kernels, call(): pl.pallas_call(kernel, in_specs=in_specs or whole(len(inputs)), out_specs...  9.84 us
    ppermute x2, starting transfers between devices, local(): far = lax.ppermute(far, 'gx', across)  8.81 us
    ppermute x4, starting transfers between devices, span_edges(): before = lax.ppermute(message, 'gz', forward)  5.67 us
    ppermute x2, waiting for transfers between devices, local(): far = lax.ppermute(far, 'gx', across)  2.22 us
    ppermute x1, starting transfers between devices, local(): far_scalars = lax.ppermute(far_scalars, 'gx', across)  0.68 us
  transfers between devices with their start and end apart: 10, of which 2 were waited for; matrix products, arithmetic and copies ran while one was open for 0% of the time, Pallas kernels for 25%

profile of v13, /device:TPU:0, one launch (start us, length us, event | category | flops | bytes accessed | tf_op | source)
XLA Modules:
  0.0 28.0 jit_solution(11994725337874999217)
XLA Ops:
  0.6 1.2 %message.1 = (bf16[22,32,128]{2,1,0:T(8,128)(2,1)S(1)}, bf16[14,32,128]{2,1,0:T(8,128)(2,1)S(1)}, bf16[2,3,4,32,128]{4,3,2,1,0:T(8,128)(2,1)S(1)}, bf16[2,4,32,1...) custom-call(bf16[2,3,4,32,128]{4,3,2,1,0:T(8,128)(2,1)} %flow_far.1, ...), custom_call_target="tpu_custom_call" | custom-call | flops 1000000 | bytes 1605632 | tf_op jit(solution)/shard_map/message/pallas_call | solution.py:731
  1.9 5.5 %collective-permute-start.1 = (bf16[22,32,128]{2,1,0:T(8,128)(2,1)S(1)}, bf16[22,32,128]{2,1,0:T(8,128)(2,1)S(1)}, u32[]{:S(2)}, u32[]{:S(2)}) collective-permute-start(bf16[22,32,128]{2,1,0:T(8,128)(2,1)S(1)} %get-tuple-element.59), channel_id=1, source_target_pairs={{0,30},{2,4},{4,2},{6,8},{8,6},{10,12},{12,10},{14,16},{16,14},{18... | collective-permute-start | bytes 540680 | tf_op jit(solution)/shard_map/ppermute | solution.py:774
  7.3 0.3 pack.1
  7.6 0.0 collective-permute-start
  7.6 0.7 %collective-permute-start.4 = (bf16[14,32,128]{2,1,0:T(8,128)(2,1)S(1)}, bf16[14,32,128]{2,1,0:T(8,128)(2,1)S(1)}, u32[]{:S(2)}, u32[]{:S(2)}) collective-permute-start(bf16[14,32,128]{2,1,0:T(8,128)(2,1)S(1)} %get-tuple-element.72), channel_id=1, source_target_pairs={{0,30},{2,4},{4,2},{6,8},{8,6},{10,12},{12,10},{14,16},{16,14},{18... | collective-permute-start | bytes 344072 | tf_op jit(solution)/shard_map/ppermute | solution.py:787
  8.3 0.0 collective-permute-start.5
  8.3 1.5 %collective-permute-start.2 = (bf16[5,32,128]{2,1,0:T(8,128)(2,1)S(1)}, bf16[5,32,128]{2,1,0:T(8,128)(2,1)S(1)}, u32[]{:S(2)}, u32[]{:S(2)}) collective-permute-start(bf16[5,32,128]{2,1,0:T(8,128)(2,1)S(1)} %get-tuple-element.60), channel_id=1, source_target_pairs={{0,1},{1,0},{2,3},{3,2},{4,5},{5,4},{6,7},{7,6},{8,9},{9,8},{10,11... | collective-permute-start | bytes 122888 | tf_op jit(solution)/shard_map/ppermute | solution.py:702
  9.8 0.3 %rows.1 = (f32[5,4,32,128]{3,2,1,0:T(8,128)S(1)}, f32[5,4,32,128]{3,2,1,0:T(8,128)S(1)}, f32[5,4,32,128]{3,2,1,0:T(8,128)S(1)}, f32[5,4,32,128]{3,2,1,0:T(8,128)...) custom-call(bf16[2,3,4,32,128]{4,3,2,1,0:T(8,128)(2,1)S(1)} %get-tuple-element.54.flow, ...), custom_call_target="tpu_custom_call" | custom-call | flops 3000000 | bytes 2621440 | tf_op jit(solution)/shard_map/rows/pallas_call | solution.py:731
  10.2 0.3 %collective-permute-done.1.far = bf16[22,32,128]{2,1,0:T(8,128)(2,1)S(1)} collective-permute-done((bf16[22,32,128]{2,1,0:T(8,128)(2,1)S(1)}, bf16[22,32,128]{2,1,0:T(8,128)(2,1)S(1)}, u32[]{:S(2)}, u32[]{:S(2)}) %collective-permute-start.1) | collective-permute-done | bytes 180256 | tf_op jit(solution)/shard_map/ppermute | solution.py:774
  10.5 0.0 collective-permute-done.near
  10.5 0.2 bands.1
  10.7 2.0 %collective-permute-start.3 = (bf16[3,32,128]{2,1,0:T(8,128)(2,1)S(1)}, bf16[3,32,128]{2,1,0:T(8,128)(2,1)S(1)}, u32[]{:S(2)}, u32[]{:S(2)}) collective-permute-start(bf16[3,32,128]{2,1,0:T(8,128)(2,1)S(1)} %get-tuple-element.71), channel_id=1, source_target_pairs={{0,1},{1,0},{2,3},{3,2},{4,5},{5,4},{6,7},{7,6},{8,9},{9,8},{10,11... | collective-permute-start | bytes 73736 | tf_op jit(solution)/shard_map/ppermute | solution.py:702
  12.7 0.9 %own.1 = (f32[5,2,4,32,128]{4,3,2,1,0:T(8,128)S(1)}, f32[5,2,4,32,128]{4,3,2,1,0:T(8,128)S(1)}, f32[5,4,32,128]{3,2,1,0:T(8,128)S(1)}, f32[5,4,32,128]{3,2,1,0:T...) custom-call(bf16[2,3,4,32,128]{4,3,2,1,0:T(8,128)(2,1)S(1)} %get-tuple-element.54.flow, ...), custom_call_target="tpu_custom_call" | custom-call | flops 5000000 | bytes 5283840 | tf_op jit(solution)/shard_map/own/pallas_call | solution.py:731
  13.7 1.0 %inner.1 = (f32[2,4,32,128]{3,2,1,0:T(8,128)S(1)}, f32[3,32,128]{2,1,0:T(8,128)S(1)}, f32[3,10,32,128]{3,2,1,0:T(8,128)S(1)}, f32[3,4,32,128]{3,2,1,0:T(8,128)S(...) custom-call(bf16[2,3,4,32,128]{4,3,2,1,0:T(8,128)(2,1)S(1)} %get-tuple-element.54.flow, ...), custom_call_target="tpu_custom_call" | custom-call | flops 20000000 | bytes 2670592 | tf_op jit(solution)/shard_map/inner/pallas_call | solution.py:731
  14.7 0.7 %first.1 = (f32[5,4,32,128]{3,2,1,0:T(8,128)S(1)}, f32[5,4,32,128]{3,2,1,0:T(8,128)S(1)}, f32[2,32,128]{2,1,0:T(8,128)S(1)}, f32[32,128]{1,0:T(8,128)S(1)}) custom-call(f32[32,128]{1,0:T(8,128)S(1)} %later_token.1._, bf16[2,4,32,128]{3,2,1,0:T(8,128)(2,1)S(1)} %get-tuple-element.55.rho, bf16[2,4,32,128]{3,2,1,0:T(8,128)(2,1)S(1)} %get-tuple-element.56.temp, ...), custom_call_target="tpu_custom_call" | custom-call | flops 10000000 | bytes 3997696 | tf_op jit(solution)/shard_map/first/pallas_call | solution.py:731
  15.4 0.9 %edge.1 = (bf16[2,32,128]{2,1,0:T(8,128)(2,1)S(1)}, f32[32,128]{1,0:T(8,128)S(1)}) custom-call(f32[6,32,128]{2,1,0:T(8,128)S(1)} %get-tuple-element.70.low, f32[3,32,128]{2,1,0:T(8,128)S(1)} %get-tuple-element.90.high, bf16[3,32,128]{2,1,0:T(8,128)(2,1)S(1)} %collective-permute-done.3.halo, f32[2,4,32,128]{3,2,1,0:T(8,128)S(1)} %get-tuple-element.91.inner, ...), custom_call_target="tpu_custom_call" | custom-call | flops 20000000 | bytes 385024 | tf_op jit(solution)/shard_map/edge/pallas_call | solution.py:731
  16.3 1.5 %collective-permute-start.6 = (bf16[2,32,128]{2,1,0:T(8,128)(2,1)S(1)}, bf16[2,32,128]{2,1,0:T(8,128)(2,1)S(1)}, u32[]{:S(2)}, u32[]{:S(2)}) collective-permute-start(bf16[2,32,128]{2,1,0:T(8,128)(2,1)S(1)} %get-tuple-element.95), channel_id=1, source_target_pairs={{0,1},{1,0},{2,3},{3,2},{4,5},{5,4},{6,7},{7,6},{8,9},{9,8},{10,11... | collective-permute-start | bytes 49160 | tf_op jit(solution)/shard_map/ppermute | solution.py:702
  17.8 1.8 %later.1 = (f32[5,10,32,128]{3,2,1,0:T(8,128)S(1)}, f32[3,4,32,128]{3,2,1,0:T(8,128)S(1)}, f32[3,4,32,128]{3,2,1,0:T(8,128)S(1)}, f32[4,32,128]{2,1,0:T(8,128)S(...) custom-call(bf16[2,3,4,32,128]{4,3,2,1,0:T(8,128)(2,1)S(1)} %get-tuple-element.54.flow, ...), custom_call_target="tpu_custom_call" | custom-call | flops 20000000 | bytes 3751936 | tf_op jit(solution)/shard_map/later/pallas_call | solution.py:731
  19.6 0.7 %collective-permute-start.7 = (bf16[1,32,128]{2,1,0:T(8,128)(2,1)S(1)}, bf16[1,32,128]{2,1,0:T(8,128)(2,1)S(1)}, u32[]{:S(2)}, u32[]{:S(2)}) collective-permute-start(bf16[1,32,128]{2,1,0:T(8,128)(2,1)S(1)} %get-tuple-element.99), channel_id=1, source_target_pairs={{0,1},{1,0},{2,3},{3,2},{4,5},{5,4},{6,7},{7,6},{8,9},{9,8},{10,11... | collective-permute-start | bytes 24584 | tf_op jit(solution)/shard_map/ppermute | solution.py:702
  20.3 0.3 middle.1
  20.6 3.3 %collective-permute-start.9 = (bf16[5,2,32,128]{3,2,1,0:T(8,128)(2,1)S(1)}, bf16[5,2,32,128]{3,2,1,0:T(8,128)(2,1)S(1)}, u32[]{:S(2)}, u32[]{:S(2)}) collective-permute-start(bf16[5,2,32,128]{3,2,1,0:T(8,128)(2,1)S(1)} %get-tuple-element.104), channel_id=1, source_target_pairs={{0,30},{2,4},{4,2},{6,8},{8,6},{10,12},{12,10},{14,16},{16,14},{18... | collective-permute-start | bytes 245768 | tf_op jit(solution)/shard_map/ppermute | solution.py:872
  23.9 1.4 %base.1 = (f32[5,4,32,128]{3,2,1,0:T(8,128)S(1)}, f32[4,32,128]{2,1,0:T(8,128)S(1)}, f32[2,2,32,128]{3,2,1,0:T(8,128)S(1)}, f32[2,4,32]{2,1,0:T(4,128)}, bf16[5,2,32,128]{3,2,1,0:T(8,128)(2,1)S(1)}) custom-call(f32[5,10,32,128]{3,2,1,0:T(8,128)S(1)} %get-tuple-element.84.wide, f32[3,4,32,128]{3,2,1,0:T(8,128)S(1)} %get-tuple-element.85.grad_x, ...), custom_call_target="tpu_custom_call" | custom-call | flops 15000000 | bytes 3253248 | tf_op jit(solution)/shard_map/base/pallas_call | solution.py:731
  25.3 1.9 %collective-permute-done.9.far = bf16[5,2,32,128]{3,2,1,0:T(8,128)(2,1)S(1)} collective-permute-done((bf16[5,2,32,128]{3,2,1,0:T(8,128)(2,1)S(1)}, bf16[5,2,32,128]{3,2,1,0:T(8,128)(2,1)S(1)}, u32[]{:S(2)}, u32[]{:S(2)}) %collective-permute-start.9) | collective-permute-done | bytes 81952 | tf_op jit(solution)/shard_map/ppermute | solution.py:872
  27.2 0.8 %last.1 = f32[5,4,32,128]{3,2,1,0:T(8,128)} custom-call(f32[5,4,32,128]{3,2,1,0:T(8,128)S(1)} %get-tuple-element.100.base, f32[4,32,128]{2,1,0:T(8,128)S(1)} %get-tuple-element.101.drift, f32[2,2,32,128]{3,2,1,0:T(8,128)S(1)} %get-tuple-element.102.spread, bf16[5,2,32,128]{3,2,1,0:T(8,128)(2,1)S(1)} %collective-permute-done.8.near_psi, ...), custom_call_target="tpu_custom_call" | custom-call | flops 1000000 | bytes 1032192 | tf_op jit(solution)/shard_map/last/pallas_call | solution.py:731
  (11 shorter events, 0.0 us)
Async XLA Ops:
  1.9 8.7 %collective-permute-start.1 = (bf16[22,32,128]{2,1,0:T(8,128)(2,1)S(1)}, bf16[22,32,128]{2,1,0:T(8,128)(2,1)S(1)}, u32[]{:S(2)}, u32[]{:S(2)}) collective-permute-start(bf16[22,32,128]{2,1,0:T(8,128)(2,1)S(1)} %get-tuple-element.59), channel_id=1, source_target_pairs={{0,30},{2,4},{4,2},{6,8},{8,6},{10,12},{12,10},{14,16},{16,14},{18... | collective-permute-start | bytes 540680 | tf_op jit(solution)/shard_map/ppermute | solution.py:774
  7.6 2.9 %collective-permute-start = (bf16[22,32,128]{2,1,0:T(8,128)(2,1)S(1)}, bf16[22,32,128]{2,1,0:T(8,128)(2,1)S(1)}, u32[]{:S(2)}, u32[]{:S(2)}) collective-permute-start(bf16[22,32,128]{2,1,0:T(8,128)(2,1)S(1)} %get-tuple-element.58), channel_id=1, source_target_pairs={{0,2},{2,0},{4,6},{6,4},{8,10},{10,8},{12,14},{14,12},{16,18},{18,... | collective-permute-start | bytes 540680 | tf_op jit(solution)/shard_map/ppermute | solution.py:788
  7.6 7.1 %collective-permute-start.4 = (bf16[14,32,128]{2,1,0:T(8,128)(2,1)S(1)}, bf16[14,32,128]{2,1,0:T(8,128)(2,1)S(1)}, u32[]{:S(2)}, u32[]{:S(2)}) collective-permute-start(bf16[14,32,128]{2,1,0:T(8,128)(2,1)S(1)} %get-tuple-element.72), channel_id=1, source_target_pairs={{0,30},{2,4},{4,2},{6,8},{8,6},{10,12},{12,10},{14,16},{16,14},{18... | collective-permute-start | bytes 344072 | tf_op jit(solution)/shard_map/ppermute | solution.py:787
  8.3 6.4 %collective-permute-start.5 = (bf16[14,32,128]{2,1,0:T(8,128)(2,1)S(1)}, bf16[14,32,128]{2,1,0:T(8,128)(2,1)S(1)}, u32[]{:S(2)}, u32[]{:S(2)}) collective-permute-start(bf16[14,32,128]{2,1,0:T(8,128)(2,1)S(1)} %get-tuple-element.76), channel_id=1, source_target_pairs={{0,2},{2,0},{4,6},{6,4},{8,10},{10,8},{12,14},{14,12},{16,18},{18,... | collective-permute-start | bytes 344072 | tf_op jit(solution)/shard_map/ppermute | solution.py:789
  8.3 4.4 %collective-permute-start.2 = (bf16[5,32,128]{2,1,0:T(8,128)(2,1)S(1)}, bf16[5,32,128]{2,1,0:T(8,128)(2,1)S(1)}, u32[]{:S(2)}, u32[]{:S(2)}) collective-permute-start(bf16[5,32,128]{2,1,0:T(8,128)(2,1)S(1)} %get-tuple-element.60), channel_id=1, source_target_pairs={{0,1},{1,0},{2,3},{3,2},{4,5},{5,4},{6,7},{7,6},{8,9},{9,8},{10,11... | collective-permute-start | bytes 122888 | tf_op jit(solution)/shard_map/ppermute | solution.py:702
  10.7 4.7 %collective-permute-start.3 = (bf16[3,32,128]{2,1,0:T(8,128)(2,1)S(1)}, bf16[3,32,128]{2,1,0:T(8,128)(2,1)S(1)}, u32[]{:S(2)}, u32[]{:S(2)}) collective-permute-start(bf16[3,32,128]{2,1,0:T(8,128)(2,1)S(1)} %get-tuple-element.71), channel_id=1, source_target_pairs={{0,1},{1,0},{2,3},{3,2},{4,5},{5,4},{6,7},{7,6},{8,9},{9,8},{10,11... | collective-permute-start | bytes 73736 | tf_op jit(solution)/shard_map/ppermute | solution.py:702
  16.3 4.0 %collective-permute-start.6 = (bf16[2,32,128]{2,1,0:T(8,128)(2,1)S(1)}, bf16[2,32,128]{2,1,0:T(8,128)(2,1)S(1)}, u32[]{:S(2)}, u32[]{:S(2)}) collective-permute-start(bf16[2,32,128]{2,1,0:T(8,128)(2,1)S(1)} %get-tuple-element.95), channel_id=1, source_target_pairs={{0,1},{1,0},{2,3},{3,2},{4,5},{5,4},{6,7},{7,6},{8,9},{9,8},{10,11... | collective-permute-start | bytes 49160 | tf_op jit(solution)/shard_map/ppermute | solution.py:702
  19.6 4.3 %collective-permute-start.7 = (bf16[1,32,128]{2,1,0:T(8,128)(2,1)S(1)}, bf16[1,32,128]{2,1,0:T(8,128)(2,1)S(1)}, u32[]{:S(2)}, u32[]{:S(2)}) collective-permute-start(bf16[1,32,128]{2,1,0:T(8,128)(2,1)S(1)} %get-tuple-element.99), channel_id=1, source_target_pairs={{0,1},{1,0},{2,3},{3,2},{4,5},{5,4},{6,7},{7,6},{8,9},{9,8},{10,11... | collective-permute-start | bytes 24584 | tf_op jit(solution)/shard_map/ppermute | solution.py:702
  20.6 6.6 %collective-permute-start.9 = (bf16[5,2,32,128]{3,2,1,0:T(8,128)(2,1)S(1)}, bf16[5,2,32,128]{3,2,1,0:T(8,128)(2,1)S(1)}, u32[]{:S(2)}, u32[]{:S(2)}) collective-permute-start(bf16[5,2,32,128]{3,2,1,0:T(8,128)(2,1)S(1)} %get-tuple-element.104), channel_id=1, source_target_pairs={{0,30},{2,4},{4,2},{6,8},{8,6},{10,12},{12,10},{14,16},{16,14},{18... | collective-permute-start | bytes 245768 | tf_op jit(solution)/shard_map/ppermute | solution.py:872
  25.3 1.9 %collective-permute-start.8 = (bf16[5,2,32,128]{3,2,1,0:T(8,128)(2,1)S(1)}, bf16[5,2,32,128]{3,2,1,0:T(8,128)(2,1)S(1)}, u32[]{:S(2)}, u32[]{:S(2)}) collective-permute-start(bf16[5,2,32,128]{3,2,1,0:T(8,128)(2,1)S(1)} %get-tuple-element.103), channel_id=1, source_target_pairs={{0,2},{2,0},{4,6},{6,4},{8,10},{10,8},{12,14},{14,12},{16,18},{18,... | collective-permute-start | bytes 245768 | tf_op jit(solution)/shard_map/ppermute | solution.py:887

commit v14 on v13

--- a/solution.py
+++ b/solution.py
@@ -492,7 +492,7 @@
 
 
 def first_kernel(
-    _, rho, temp, psi, near, far, velocity, grad_x, lap_velocity, sizes,
+    _, products, rho, temp, psi, near, far, velocity, grad_x, lap_velocity, sizes,
     grad_yz, lap_yz, psi_rate, psi_lap,
     first, second, message, columns,
     wide, psi_wide, work,
@@ -521,26 +521,23 @@
             first[k, x] = new[k]
             second[k, x] = slope[k]
         work[x] = sensitivity
-    columns[...] = add_columns(ops, jnp.zeros((ROWS, LANES), F32), 16, lambda x: work[x])
+    total = add_columns(ops, products[...], 16, lambda x: work[x])
+    columns[...] = total
     items = [[part[k, x] for x in range(CX)] for part in (first, second) for k in range(5)]
-    for number in range(2):
-        message[number] = pack_strips(ops, items[8 * number : 8 * number + 8])
-
-
-def edge_kernel(
-    low, high, halo, inner, strips, sensitivity, message, columns, bands, spread, sums
-):
+    message[0] = pack_strips(ops, items[:8]).astype(BF16)
+    message[1] = add_parts(ops, pack_strips(ops, items[8:]), total).astype(BF16)
+
+
+def edge_kernel(low, high, halo, inner, columns, bands, spread, sums):
     ops = Ops()
     for part in range(2):
         for x in range(CX):
             sums[part, x] = inner[part, x]
     edge_products(ops, 0, low, high, halo, sums, bands, spread)
-    total = sensitivity[...]
+    total = jnp.zeros((ROWS, LANES), F32)
     for part in range(2):
         total = add_columns(ops, total, 4 * part, lambda x: sums[part, x], 1.0 / 256.0)
     columns[...] = total
-    message[0] = strips[0].astype(BF16)
-    message[1] = add_parts(ops, strips[1], total).astype(BF16)
 
 
 def later_kernel(
@@ -823,26 +820,25 @@
         20_000_000,
         scratch((21, CX + 2), (21, CX)),
     )
-    (token,) = call(token_kernel, "later_token", (far_scalars, sizes), [shape_of(())], 100_000)
-    first, second, strips, sensitivity = call(
+    (products,) = call(
+        edge_kernel,
+        "edge",
+        (low, high, halo, inner),
+        [shape_of(())],
+        20_000_000,
+        scratch((2, 3), (21,), (2, CX)),
+    )
+    (token,) = call(token_kernel, "later_token", (far_scalars, products), [shape_of(())], 100_000)
+    first, second, message, columns = call(
         first_kernel,
         "first",
         (
-            token, rho, temp, psi, near_scalars, far_scalars,
-            velocity, grad_x, lap_velocity, sizes,
-            grad_0, lap_0, psi_rate, psi_lap,
+            token, products, rho, temp, psi, near_scalars, far_scalars,
+            velocity, grad_x, lap_velocity, sizes, grad_0, lap_0, psi_rate, psi_lap,
         ),
-        [field, field, shape_of((2,)), shape_of(())],
+        [field, field, shape_of((2,), BF16), shape_of(())],
         10_000_000,
         scratch((5, CX + 6), (5, CX + 6), (CX,)),
-    )
-    message, columns = call(
-        edge_kernel,
-        "edge",
-        (low, high, halo, inner, strips, sensitivity),
-        [shape_of((2,), BF16), shape_of(())],
-        20_000_000,
-        scratch((2, 3), (21,), (2, CX)),
     )
     other = span_edges(message, 2)
     columns = span_sums(columns)

time: 28.2 us -> 28 us (level)
  no operation moved by 1% of the time
where the time goes in v14:
time: 28 us; the launch traced here: 27.9 us
  starting transfers between devices  15.2 us (54%)
  Pallas kernels  9.7 us (35%)
  waiting for transfers between devices  2.27 us (8%)
  between operations  0.74 us (3%)
    pallas_call x15, Pallas kernels, call(): pl.pallas_call(kernel, in_specs=in_specs or whole(len(inputs)), out_specs...  9.7 us
    ppermute x2, starting transfers between devices, local(): far = lax.ppermute(far, 'gx', across)  8.78 us
    ppermute x4, starting transfers between devices, span_edges(): before = lax.ppermute(message, 'gz', forward)  5.67 us
    ppermute x2, waiting for transfers between devices, local(): far = lax.ppermute(far, 'gx', across)  2.25 us
    ppermute x1, starting transfers between devices, local(): far_scalars = lax.ppermute(far_scalars, 'gx', across)  0.68 us
  transfers between devices with their start and end apart: 10, of which 2 were waited for; matrix products, arithmetic and copies ran while one was open for 0% of the time, Pallas kernels for 25%

profile of v14, /device:TPU:0, one launch (start us, length us, event | category | flops | bytes accessed | tf_op | source)
XLA Modules:
  0.0 27.9 jit_solution(800185041057846814)
XLA Ops:
  0.6 1.2 %message.1 = (bf16[22,32,128]{2,1,0:T(8,128)(2,1)S(1)}, bf16[14,32,128]{2,1,0:T(8,128)(2,1)S(1)}, bf16[2,3,4,32,128]{4,3,2,1,0:T(8,128)(2,1)S(1)}, bf16[2,4,32,1...) custom-call(bf16[2,3,4,32,128]{4,3,2,1,0:T(8,128)(2,1)} %flow_far.1, ...), custom_call_target="tpu_custom_call" | custom-call | flops 1000000 | bytes 1605632 | tf_op jit(solution)/shard_map/message/pallas_call | solution.py:728
  1.9 5.5 %collective-permute-start.1 = (bf16[22,32,128]{2,1,0:T(8,128)(2,1)S(1)}, bf16[22,32,128]{2,1,0:T(8,128)(2,1)S(1)}, u32[]{:S(2)}, u32[]{:S(2)}) collective-permute-start(bf16[22,32,128]{2,1,0:T(8,128)(2,1)S(1)} %get-tuple-element.57), channel_id=1, source_target_pairs={{0,30},{2,4},{4,2},{6,8},{8,6},{10,12},{12,10},{14,16},{16,14},{18... | collective-permute-start | bytes 540680 | tf_op jit(solution)/shard_map/ppermute | solution.py:771
  7.3 0.3 pack.1
  7.6 0.0 collective-permute-start
  7.6 0.7 %collective-permute-start.4 = (bf16[14,32,128]{2,1,0:T(8,128)(2,1)S(1)}, bf16[14,32,128]{2,1,0:T(8,128)(2,1)S(1)}, u32[]{:S(2)}, u32[]{:S(2)}) collective-permute-start(bf16[14,32,128]{2,1,0:T(8,128)(2,1)S(1)} %get-tuple-element.70), channel_id=1, source_target_pairs={{0,30},{2,4},{4,2},{6,8},{8,6},{10,12},{12,10},{14,16},{16,14},{18... | collective-permute-start | bytes 344072 | tf_op jit(solution)/shard_map/ppermute | solution.py:784
  8.3 0.0 collective-permute-start.5
  8.3 1.5 %collective-permute-start.2 = (bf16[5,32,128]{2,1,0:T(8,128)(2,1)S(1)}, bf16[5,32,128]{2,1,0:T(8,128)(2,1)S(1)}, u32[]{:S(2)}, u32[]{:S(2)}) collective-permute-start(bf16[5,32,128]{2,1,0:T(8,128)(2,1)S(1)} %get-tuple-element.58), channel_id=1, source_target_pairs={{0,1},{1,0},{2,3},{3,2},{4,5},{5,4},{6,7},{7,6},{8,9},{9,8},{10,11... | collective-permute-start | bytes 122888 | tf_op jit(solution)/shard_map/ppermute | solution.py:699
  9.8 0.3 %rows.1 = (f32[5,4,32,128]{3,2,1,0:T(8,128)S(1)}, f32[5,4,32,128]{3,2,1,0:T(8,128)S(1)}, f32[5,4,32,128]{3,2,1,0:T(8,128)S(1)}, f32[5,4,32,128]{3,2,1,0:T(8,128)...) custom-call(bf16[2,3,4,32,128]{4,3,2,1,0:T(8,128)(2,1)S(1)} %get-tuple-element.52.flow, ...), custom_call_target="tpu_custom_call" | custom-call | flops 3000000 | bytes 2621440 | tf_op jit(solution)/shard_map/rows/pallas_call | solution.py:728
  10.2 0.3 %collective-permute-done.1.far = bf16[22,32,128]{2,1,0:T(8,128)(2,1)S(1)} collective-permute-done((bf16[22,32,128]{2,1,0:T(8,128)(2,1)S(1)}, bf16[22,32,128]{2,1,0:T(8,128)(2,1)S(1)}, u32[]{:S(2)}, u32[]{:S(2)}) %collective-permute-start.1) | collective-permute-done | bytes 180256 | tf_op jit(solution)/shard_map/ppermute | solution.py:771
  10.5 0.0 collective-permute-done.near
  10.5 0.2 bands.1
  10.7 2.0 %collective-permute-start.3 = (bf16[3,32,128]{2,1,0:T(8,128)(2,1)S(1)}, bf16[3,32,128]{2,1,0:T(8,128)(2,1)S(1)}, u32[]{:S(2)}, u32[]{:S(2)}) collective-permute-start(bf16[3,32,128]{2,1,0:T(8,128)(2,1)S(1)} %get-tuple-element.69), channel_id=1, source_target_pairs={{0,1},{1,0},{2,3},{3,2},{4,5},{5,4},{6,7},{7,6},{8,9},{9,8},{10,11... | collective-permute-start | bytes 73736 | tf_op jit(solution)/shard_map/ppermute | solution.py:699
  12.7 0.9 %own.1 = (f32[5,2,4,32,128]{4,3,2,1,0:T(8,128)S(1)}, f32[5,2,4,32,128]{4,3,2,1,0:T(8,128)S(1)}, f32[5,4,32,128]{3,2,1,0:T(8,128)S(1)}, f32[5,4,32,128]{3,2,1,0:T...) custom-call(bf16[2,3,4,32,128]{4,3,2,1,0:T(8,128)(2,1)S(1)} %get-tuple-element.52.flow, ...), custom_call_target="tpu_custom_call" | custom-call | flops 5000000 | bytes 5283840 | tf_op jit(solution)/shard_map/own/pallas_call | solution.py:728
  13.7 1.0 %inner.1 = (f32[2,4,32,128]{3,2,1,0:T(8,128)S(1)}, f32[3,32,128]{2,1,0:T(8,128)S(1)}, f32[3,10,32,128]{3,2,1,0:T(8,128)S(1)}, f32[3,4,32,128]{3,2,1,0:T(8,128)S(...) custom-call(bf16[2,3,4,32,128]{4,3,2,1,0:T(8,128)(2,1)S(1)} %get-tuple-element.52.flow, ...), custom_call_target="tpu_custom_call" | custom-call | flops 20000000 | bytes 2670592 | tf_op jit(solution)/shard_map/inner/pallas_call | solution.py:728
  14.7 0.8 %edge.1._.products = f32[32,128]{1,0:T(8,128)S(1)} custom-call(f32[6,32,128]{2,1,0:T(8,128)S(1)} %get-tuple-element.68.low, f32[3,32,128]{2,1,0:T(8,128)S(1)} %get-tuple-element.73.high, bf16[3,32,128]{2,1,0:T(8,128)(2,1)S(1)} %collective-permute-done.3.halo, f32[2,4,32,128]{3,2,1,0:T(8,128)S(1)} %get-tuple-element.74.inner), custom_call_target="tpu_custom_call" | custom-call | flops 20000000 | bytes 319488 | tf_op jit(solution)/shard_map/edge/pallas_call | solution.py:728
  15.5 0.6 %first.1 = (f32[5,4,32,128]{3,2,1,0:T(8,128)S(1)}, f32[5,4,32,128]{3,2,1,0:T(8,128)S(1)}, bf16[2,32,128]{2,1,0:T(8,128)(2,1)S(1)}, f32[32,128]{1,0:T(8,128)S(1)}) custom-call(f32[32,128]{1,0:T(8,128)S(1)} %later_token.1._, f32[32,128]{1,0:T(8,128)S(1)} %edge.1._.products, bf16[2,4,32,128]{3,2,1,0:T(8,128)(2,1)S(1)} %get-tuple-element.53.rho, ...), custom_call_target="tpu_custom_call" | custom-call | flops 10000000 | bytes 3997696 | tf_op jit(solution)/shard_map/first/pallas_call | solution.py:728
  16.2 1.9 %collective-permute-start.6 = (bf16[2,32,128]{2,1,0:T(8,128)(2,1)S(1)}, bf16[2,32,128]{2,1,0:T(8,128)(2,1)S(1)}, u32[]{:S(2)}, u32[]{:S(2)}) collective-permute-start(bf16[2,32,128]{2,1,0:T(8,128)(2,1)S(1)} %get-tuple-element.91), channel_id=1, source_target_pairs={{0,1},{1,0},{2,3},{3,2},{4,5},{5,4},{6,7},{7,6},{8,9},{9,8},{10,11... | collective-permute-start | bytes 49160 | tf_op jit(solution)/shard_map/ppermute | solution.py:699
  18.1 1.8 %later.1 = (f32[5,10,32,128]{3,2,1,0:T(8,128)S(1)}, f32[3,4,32,128]{3,2,1,0:T(8,128)S(1)}, f32[3,4,32,128]{3,2,1,0:T(8,128)S(1)}, f32[4,32,128]{2,1,0:T(8,128)S(...) custom-call(bf16[2,3,4,32,128]{4,3,2,1,0:T(8,128)(2,1)S(1)} %get-tuple-element.52.flow, ...), custom_call_target="tpu_custom_call" | custom-call | flops 20000000 | bytes 3751936 | tf_op jit(solution)/shard_map/later/pallas_call | solution.py:728
  19.9 0.2 collective-permute-start.7
  20.1 0.3 middle.1
  20.4 3.3 %collective-permute-start.9 = (bf16[5,2,32,128]{3,2,1,0:T(8,128)(2,1)S(1)}, bf16[5,2,32,128]{3,2,1,0:T(8,128)(2,1)S(1)}, u32[]{:S(2)}, u32[]{:S(2)}) collective-permute-start(bf16[5,2,32,128]{3,2,1,0:T(8,128)(2,1)S(1)} %get-tuple-element.100), channel_id=1, source_target_pairs={{0,30},{2,4},{4,2},{6,8},{8,6},{10,12},{12,10},{14,16},{16,14},{18... | collective-permute-start | bytes 245768 | tf_op jit(solution)/shard_map/ppermute | solution.py:868
  23.7 1.4 %base.1 = (f32[5,4,32,128]{3,2,1,0:T(8,128)S(1)}, f32[4,32,128]{2,1,0:T(8,128)S(1)}, f32[2,2,32,128]{3,2,1,0:T(8,128)S(1)}, f32[2,4,32]{2,1,0:T(4,128)}, bf16[5,2,32,128]{3,2,1,0:T(8,128)(2,1)S(1)}) custom-call(f32[5,10,32,128]{3,2,1,0:T(8,128)S(1)} %get-tuple-element.84.wide, f32[3,4,32,128]{3,2,1,0:T(8,128)S(1)} %get-tuple-element.85.grad_x, ...), custom_call_target="tpu_custom_call" | custom-call | flops 15000000 | bytes 3253248 | tf_op jit(solution)/shard_map/base/pallas_call | solution.py:728
  25.1 1.9 %collective-permute-done.9.far = bf16[5,2,32,128]{3,2,1,0:T(8,128)(2,1)S(1)} collective-permute-done((bf16[5,2,32,128]{3,2,1,0:T(8,128)(2,1)S(1)}, bf16[5,2,32,128]{3,2,1,0:T(8,128)(2,1)S(1)}, u32[]{:S(2)}, u32[]{:S(2)}) %collective-permute-start.9) | collective-permute-done | bytes 81952 | tf_op jit(solution)/shard_map/ppermute | solution.py:868
  27.1 0.8 %last.1 = f32[5,4,32,128]{3,2,1,0:T(8,128)} custom-call(f32[5,4,32,128]{3,2,1,0:T(8,128)S(1)} %get-tuple-element.96.base, f32[4,32,128]{2,1,0:T(8,128)S(1)} %get-tuple-element.97.drift, f32[2,2,32,128]{3,2,1,0:T(8,128)S(1)} %get-tuple-element.98.spread, bf16[5,2,32,128]{3,2,1,0:T(8,128)(2,1)S(1)} %collective-permute-done.8.near_psi, ...), custom_call_target="tpu_custom_call" | custom-call | flops 1000000 | bytes 1032192 | tf_op jit(solution)/shard_map/last/pallas_call | solution.py:728
  (11 shorter events, 0.0 us)
Async XLA Ops:
  1.9 8.7 %collective-permute-start.1 = (bf16[22,32,128]{2,1,0:T(8,128)(2,1)S(1)}, bf16[22,32,128]{2,1,0:T(8,128)(2,1)S(1)}, u32[]{:S(2)}, u32[]{:S(2)}) collective-permute-start(bf16[22,32,128]{2,1,0:T(8,128)(2,1)S(1)} %get-tuple-element.57), channel_id=1, source_target_pairs={{0,30},{2,4},{4,2},{6,8},{8,6},{10,12},{12,10},{14,16},{16,14},{18... | collective-permute-start | bytes 540680 | tf_op jit(solution)/shard_map/ppermute | solution.py:771
  7.6 2.9 %collective-permute-start = (bf16[22,32,128]{2,1,0:T(8,128)(2,1)S(1)}, bf16[22,32,128]{2,1,0:T(8,128)(2,1)S(1)}, u32[]{:S(2)}, u32[]{:S(2)}) collective-permute-start(bf16[22,32,128]{2,1,0:T(8,128)(2,1)S(1)} %get-tuple-element.56), channel_id=1, source_target_pairs={{0,2},{2,0},{4,6},{6,4},{8,10},{10,8},{12,14},{14,12},{16,18},{18,... | collective-permute-start | bytes 540680 | tf_op jit(solution)/shard_map/ppermute | solution.py:785
  7.6 7.9 %collective-permute-start.4 = (bf16[14,32,128]{2,1,0:T(8,128)(2,1)S(1)}, bf16[14,32,128]{2,1,0:T(8,128)(2,1)S(1)}, u32[]{:S(2)}, u32[]{:S(2)}) collective-permute-start(bf16[14,32,128]{2,1,0:T(8,128)(2,1)S(1)} %get-tuple-element.70), channel_id=1, source_target_pairs={{0,30},{2,4},{4,2},{6,8},{8,6},{10,12},{12,10},{14,16},{16,14},{18... | collective-permute-start | bytes 344072 | tf_op jit(solution)/shard_map/ppermute | solution.py:784
  8.3 7.2 %collective-permute-start.5 = (bf16[14,32,128]{2,1,0:T(8,128)(2,1)S(1)}, bf16[14,32,128]{2,1,0:T(8,128)(2,1)S(1)}, u32[]{:S(2)}, u32[]{:S(2)}) collective-permute-start(bf16[14,32,128]{2,1,0:T(8,128)(2,1)S(1)} %get-tuple-element.75), channel_id=1, source_target_pairs={{0,2},{2,0},{4,6},{6,4},{8,10},{10,8},{12,14},{14,12},{16,18},{18,... | collective-permute-start | bytes 344072 | tf_op jit(solution)/shard_map/ppermute | solution.py:786
  8.3 4.4 %collective-permute-start.2 = (bf16[5,32,128]{2,1,0:T(8,128)(2,1)S(1)}, bf16[5,32,128]{2,1,0:T(8,128)(2,1)S(1)}, u32[]{:S(2)}, u32[]{:S(2)}) collective-permute-start(bf16[5,32,128]{2,1,0:T(8,128)(2,1)S(1)} %get-tuple-element.58), channel_id=1, source_target_pairs={{0,1},{1,0},{2,3},{3,2},{4,5},{5,4},{6,7},{7,6},{8,9},{9,8},{10,11... | collective-permute-start | bytes 122888 | tf_op jit(solution)/shard_map/ppermute | solution.py:699
  10.7 4.0 %collective-permute-start.3 = (bf16[3,32,128]{2,1,0:T(8,128)(2,1)S(1)}, bf16[3,32,128]{2,1,0:T(8,128)(2,1)S(1)}, u32[]{:S(2)}, u32[]{:S(2)}) collective-permute-start(bf16[3,32,128]{2,1,0:T(8,128)(2,1)S(1)} %get-tuple-element.69), channel_id=1, source_target_pairs={{0,1},{1,0},{2,3},{3,2},{4,5},{5,4},{6,7},{7,6},{8,9},{9,8},{10,11... | collective-permute-start | bytes 73736 | tf_op jit(solution)/shard_map/ppermute | solution.py:699
  16.2 4.0 %collective-permute-start.6 = (bf16[2,32,128]{2,1,0:T(8,128)(2,1)S(1)}, bf16[2,32,128]{2,1,0:T(8,128)(2,1)S(1)}, u32[]{:S(2)}, u32[]{:S(2)}) collective-permute-start(bf16[2,32,128]{2,1,0:T(8,128)(2,1)S(1)} %get-tuple-element.91), channel_id=1, source_target_pairs={{0,1},{1,0},{2,3},{3,2},{4,5},{5,4},{6,7},{7,6},{8,9},{9,8},{10,11... | collective-permute-start | bytes 49160 | tf_op jit(solution)/shard_map/ppermute | solution.py:699
  19.9 3.8 %collective-permute-start.7 = (bf16[1,32,128]{2,1,0:T(8,128)(2,1)S(1)}, bf16[1,32,128]{2,1,0:T(8,128)(2,1)S(1)}, u32[]{:S(2)}, u32[]{:S(2)}) collective-permute-start(bf16[1,32,128]{2,1,0:T(8,128)(2,1)S(1)} %get-tuple-element.95), channel_id=1, source_target_pairs={{0,1},{1,0},{2,3},{3,2},{4,5},{5,4},{6,7},{7,6},{8,9},{9,8},{10,11... | collective-permute-start | bytes 24584 | tf_op jit(solution)/shard_map/ppermute | solution.py:699
  20.4 6.6 %collective-permute-start.9 = (bf16[5,2,32,128]{3,2,1,0:T(8,128)(2,1)S(1)}, bf16[5,2,32,128]{3,2,1,0:T(8,128)(2,1)S(1)}, u32[]{:S(2)}, u32[]{:S(2)}) collective-permute-start(bf16[5,2,32,128]{3,2,1,0:T(8,128)(2,1)S(1)} %get-tuple-element.100), channel_id=1, source_target_pairs={{0,30},{2,4},{4,2},{6,8},{8,6},{10,12},{12,10},{14,16},{16,14},{18... | collective-permute-start | bytes 245768 | tf_op jit(solution)/shard_map/ppermute | solution.py:868
  25.1 1.9 %collective-permute-start.8 = (bf16[5,2,32,128]{3,2,1,0:T(8,128)(2,1)S(1)}, bf16[5,2,32,128]{3,2,1,0:T(8,128)(2,1)S(1)}, u32[]{:S(2)}, u32[]{:S(2)}) collective-permute-start(bf16[5,2,32,128]{3,2,1,0:T(8,128)(2,1)S(1)} %get-tuple-element.99), channel_id=1, source_target_pairs={{0,2},{2,0},{4,6},{6,4},{8,10},{10,8},{12,14},{14,12},{16,18},{18,... | collective-permute-start | bytes 245768 | tf_op jit(solution)/shard_map/ppermute | solution.py:883

commit v15 on v14

--- a/solution.py
+++ b/solution.py
@@ -28,9 +28,8 @@
 BAND_BLOCKS = 3
 VELOCITY = 0
 SCALARS = 18
-MESSAGE = 22
-PSI = 4
-SCALAR_PLANES = 14
+PSI = 8
+SCALAR_PLANES = 18
 
 
 def lane_ids():
@@ -178,9 +177,10 @@
 
 
 def fill_scalars(out, side, rho, temp, psi):
-    for i in range(2):
-        out[i] = rho[0, 2 * side + i]
-        out[2 + i] = temp[0, 2 * side + i]
+    for t in range(2):
+        for i in range(2):
+            out[2 * t + i] = rho[t, 2 * side + i]
+            out[4 + 2 * t + i] = temp[t, 2 * side + i]
     for k in range(5):
         for i in range(2):
             out[PSI + k * 2 + i] = psi[k, 2 * side + i].astype(BF16)
@@ -193,21 +193,12 @@
         message[first + number] = both.astype(BF16)
 
 
-def fill_later(out, side, rho, temp):
-    for i in range(2):
-        out[SCALARS + i] = rho[1, 2 * side + i]
-        out[SCALARS + 2 + i] = temp[1, 2 * side + i]
-
-
 def message_kernel(
     flow_far, rho_far, temp_far, psi_far, far, far_scalars, flow, rho, temp, psi, sems
 ):
     side = 1 - is_even().astype(jnp.int32)
     pieces = (
-        (
-            flow_far.at[:, :, pl.ds(side, 3)],
-            far.at[pl.ds(VELOCITY, 18)].reshape((2, 3, 3, ROWS, LANES)),
-        ),
+        (flow_far.at[:, :, pl.ds(side, 3)], far.reshape((2, 3, 3, ROWS, LANES))),
         (psi_far, psi),
         (rho_far, rho),
         (temp_far, temp),
@@ -222,7 +213,6 @@
     for copy in copies[1:4]:
         copy.wait()
     fill_scalars(far_scalars, side, rho, temp, psi)
-    fill_later(far, side, rho, temp)
     copies[0].wait()
     copies[4].wait()
 
@@ -235,7 +225,6 @@
             for i in range(3):
                 near[VELOCITY + t * 9 + k * 3 + i] = flow[t, k, side + i]
     fill_scalars(near_scalars, side, rho, temp, psi)
-    fill_later(near, side, rho, temp)
     items = []
     for t in range(2):
         for source in (rho, temp):
@@ -346,9 +335,9 @@
         wide[k, 3 + x] = source(x).astype(F32)
 
 
-def widen_scalars(t, first, rho, temp, near, far, even, wide):
+def widen_scalars(t, rho, temp, near, far, even, wide):
     for k, source in ((3, rho), (4, temp)):
-        number = first + (k - 3) * 2
+        number = (k - 3) * 4 + 2 * t
         widen(
             k,
             lambda x: source[t, x],
@@ -502,7 +491,7 @@
     for k in range(3):
         for x in range(CX):
             wide[k, x + 3] = velocity[k, x + 3]
-    widen_scalars(0, 0, rho, temp, near, far, even, wide)
+    widen_scalars(0, rho, temp, near, far, even, wide)
     for k in range(5):
         widen(
             k,
@@ -541,7 +530,8 @@
 
 
 def later_kernel(
-    flow, rho, temp, near, far, grad_yz, lap_yz, low, halo, first, second,
+    flow, rho, temp, near, far, near_scalars, far_scalars,
+    grad_yz, lap_yz, low, halo, first, second,
     wide, grad_x, lap_velocity, sizes, message, columns,
     high, fields, hats, work, bands, spread, sums,
 ):
@@ -550,7 +540,7 @@
         ops, 1, flow, near, far, grad_yz, lap_yz,
         sums, high, wide, grad_x, lap_velocity, sizes, fields, hats,
     )
-    widen_scalars(1, SCALARS, rho, temp, near, far, is_even(), wide)
+    widen_scalars(1, rho, temp, near_scalars, far_scalars, is_even(), wide)
     edge_products(ops, 1, low, high, halo, sums, bands, spread)
     for x in range(CX):
         _, _, lap, size, inv_rho = state_terms(
@@ -757,7 +747,7 @@
         "message",
         inputs,
         [
-            shape_of((MESSAGE,), BF16),
+            shape_of((SCALARS,), BF16),
             shape_of((SCALAR_PLANES,), BF16),
             shape_of((2, 3, CX), BF16),
             shape_of((2, CX), BF16),
@@ -774,7 +764,7 @@
         "pack",
         (flow, rho, temp, psi),
         [
-            shape_of((MESSAGE,), BF16),
+            shape_of((SCALARS,), BF16),
             shape_of((SCALAR_PLANES,), BF16),
             shape_of((STRIP_BLOCKS + BAND_BLOCKS,), BF16),
             shape_of((6,)),
@@ -846,7 +836,8 @@
         later_kernel,
         "later",
         (
-            flow, rho, temp, near, far, grad_1, lap_1, low, halo, first, second,
+            flow, rho, temp, near, far, near_scalars, far_scalars,
+            grad_1, lap_1, low, halo, first, second,
         ),
         [
             planes, shape_of((3, CX)), shape_of((3, CX)), shape_of((CX,)),

time: 28 us -> 27.7 us (0.989)
  waiting for transfers between devices: 2.27 us -> 1.93 us
    ppermute x2, waiting for transfers between devices: 2.25 us -> 1.91 us  [local(): far = lax.ppermute(far, 'gx', across)]
  transfers between devices with their start and end apart: 10 -> 10, of which waited for: 2 -> 1; matrix products, arithmetic and copies ran while one was open for 0% -> 0% of each run, Pallas kernels for 25% -> 26%
where the time goes in v15:
time: 27.7 us; the launch traced here: 27.5 us
  starting transfers between devices  15.1 us (55%)
  Pallas kernels  9.71 us (35%)
  waiting for transfers between devices  1.93 us (7%)
  between operations  0.76 us (3%)
    pallas_call x15, Pallas kernels, call(): pl.pallas_call(kernel, in_specs=in_specs or whole(len(inputs)), out_specs...  9.71 us
    ppermute x2, starting transfers between devices, local(): far = lax.ppermute(far, 'gx', across)  8.78 us
    ppermute x4, starting transfers between devices, span_edges(): before = lax.ppermute(message, 'gz', forward)  5.63 us
    ppermute x2, waiting for transfers between devices, local(): far = lax.ppermute(far, 'gx', across)  1.91 us
    ppermute x1, starting transfers between devices, local(): far_scalars = lax.ppermute(far_scalars, 'gx', across)  0.68 us
  transfers between devices with their start and end apart: 10, of which 1 were waited for; matrix products, arithmetic and copies ran while one was open for 0% of the time, Pallas kernels for 26%

profile of v15, /device:TPU:0, one launch (start us, length us, event | category | flops | bytes accessed | tf_op | source)
XLA Modules:
  0.0 27.5 jit_solution(10998296133162864224)
XLA Ops:
  0.6 1.2 %message.1 = (bf16[18,32,128]{2,1,0:T(8,128)(2,1)S(1)}, bf16[18,32,128]{2,1,0:T(8,128)(2,1)S(1)}, bf16[2,3,4,32,128]{4,3,2,1,0:T(8,128)(2,1)S(1)}, bf16[2,4,32,1...) custom-call(bf16[2,3,4,32,128]{4,3,2,1,0:T(8,128)(2,1)} %flow_far.1, ...), custom_call_target="tpu_custom_call" | custom-call | flops 1000000 | bytes 1605632 | tf_op jit(solution)/shard_map/message/pallas_call | solution.py:718
  1.9 5.5 %collective-permute-start.1 = (bf16[18,32,128]{2,1,0:T(8,128)(2,1)S(1)}, bf16[18,32,128]{2,1,0:T(8,128)(2,1)S(1)}, u32[]{:S(2)}, u32[]{:S(2)}) collective-permute-start(bf16[18,32,128]{2,1,0:T(8,128)(2,1)S(1)} %get-tuple-element.57), channel_id=1, source_target_pairs={{0,30},{2,4},{4,2},{6,8},{8,6},{10,12},{12,10},{14,16},{16,14},{18... | collective-permute-start | bytes 442376 | tf_op jit(solution)/shard_map/ppermute | solution.py:761
  7.3 0.3 pack.1
  7.6 0.0 collective-permute-start
  7.6 0.7 %collective-permute-start.3 = (bf16[18,32,128]{2,1,0:T(8,128)(2,1)S(1)}, bf16[18,32,128]{2,1,0:T(8,128)(2,1)S(1)}, u32[]{:S(2)}, u32[]{:S(2)}) collective-permute-start(bf16[18,32,128]{2,1,0:T(8,128)(2,1)S(1)} %get-tuple-element.59), channel_id=1, source_target_pairs={{0,30},{2,4},{4,2},{6,8},{8,6},{10,12},{12,10},{14,16},{16,14},{18... | collective-permute-start | bytes 442376 | tf_op jit(solution)/shard_map/ppermute | solution.py:774
  8.3 1.5 %collective-permute-start.4 = (bf16[5,32,128]{2,1,0:T(8,128)(2,1)S(1)}, bf16[5,32,128]{2,1,0:T(8,128)(2,1)S(1)}, u32[]{:S(2)}, u32[]{:S(2)}) collective-permute-start(bf16[5,32,128]{2,1,0:T(8,128)(2,1)S(1)} %get-tuple-element.60), channel_id=1, source_target_pairs={{0,1},{1,0},{2,3},{3,2},{4,5},{5,4},{6,7},{7,6},{8,9},{9,8},{10,11... | collective-permute-start | bytes 122888 | tf_op jit(solution)/shard_map/ppermute | solution.py:689
  9.8 0.3 %rows.1 = (f32[5,4,32,128]{3,2,1,0:T(8,128)S(1)}, f32[5,4,32,128]{3,2,1,0:T(8,128)S(1)}, f32[5,4,32,128]{3,2,1,0:T(8,128)S(1)}, f32[5,4,32,128]{3,2,1,0:T(8,128)...) custom-call(bf16[2,3,4,32,128]{4,3,2,1,0:T(8,128)(2,1)S(1)} %get-tuple-element.52.flow, ...), custom_call_target="tpu_custom_call" | custom-call | flops 3000000 | bytes 2621440 | tf_op jit(solution)/shard_map/rows/pallas_call | solution.py:718
  10.2 0.0 collective-permute-done.1.far
  10.2 0.2 bands.1
  10.4 2.0 %collective-permute-start.5 = (bf16[3,32,128]{2,1,0:T(8,128)(2,1)S(1)}, bf16[3,32,128]{2,1,0:T(8,128)(2,1)S(1)}, u32[]{:S(2)}, u32[]{:S(2)}) collective-permute-start(bf16[3,32,128]{2,1,0:T(8,128)(2,1)S(1)} %get-tuple-element.71), channel_id=1, source_target_pairs={{0,1},{1,0},{2,3},{3,2},{4,5},{5,4},{6,7},{7,6},{8,9},{9,8},{10,11... | collective-permute-start | bytes 73736 | tf_op jit(solution)/shard_map/ppermute | solution.py:689
  12.4 0.9 %own.1 = (f32[5,2,4,32,128]{4,3,2,1,0:T(8,128)S(1)}, f32[5,2,4,32,128]{4,3,2,1,0:T(8,128)S(1)}, f32[5,4,32,128]{3,2,1,0:T(8,128)S(1)}, f32[5,4,32,128]{3,2,1,0:T...) custom-call(bf16[2,3,4,32,128]{4,3,2,1,0:T(8,128)(2,1)S(1)} %get-tuple-element.52.flow, ...), custom_call_target="tpu_custom_call" | custom-call | flops 5000000 | bytes 5283840 | tf_op jit(solution)/shard_map/own/pallas_call | solution.py:718
  13.3 1.0 %inner.1 = (f32[2,4,32,128]{3,2,1,0:T(8,128)S(1)}, f32[3,32,128]{2,1,0:T(8,128)S(1)}, f32[3,10,32,128]{3,2,1,0:T(8,128)S(1)}, f32[3,4,32,128]{3,2,1,0:T(8,128)S(...) custom-call(bf16[2,3,4,32,128]{4,3,2,1,0:T(8,128)(2,1)S(1)} %get-tuple-element.52.flow, ...), custom_call_target="tpu_custom_call" | custom-call | flops 20000000 | bytes 2605056 | tf_op jit(solution)/shard_map/inner/pallas_call | solution.py:718
  14.3 0.8 %edge.1._.products = f32[32,128]{1,0:T(8,128)S(1)} custom-call(f32[6,32,128]{2,1,0:T(8,128)S(1)} %get-tuple-element.70.low, f32[3,32,128]{2,1,0:T(8,128)S(1)} %get-tuple-element.74.high, bf16[3,32,128]{2,1,0:T(8,128)(2,1)S(1)} %collective-permute-done.5.halo, f32[2,4,32,128]{3,2,1,0:T(8,128)S(1)} %get-tuple-element.75.inner), custom_call_target="tpu_custom_call" | custom-call | flops 20000000 | bytes 319488 | tf_op jit(solution)/shard_map/edge/pallas_call | solution.py:718
  15.1 0.0 collective-permute-done.3.far.far_scalars
  15.2 0.6 %first.1 = (f32[5,4,32,128]{3,2,1,0:T(8,128)S(1)}, f32[5,4,32,128]{3,2,1,0:T(8,128)S(1)}, bf16[2,32,128]{2,1,0:T(8,128)(2,1)S(1)}, f32[32,128]{1,0:T(8,128)S(1)}) custom-call(f32[32,128]{1,0:T(8,128)S(1)} %later_token.1._, f32[32,128]{1,0:T(8,128)S(1)} %edge.1._.products, bf16[2,4,32,128]{3,2,1,0:T(8,128)(2,1)S(1)} %get-tuple-element.53.rho, ...), custom_call_target="tpu_custom_call" | custom-call | flops 10000000 | bytes 4063232 | tf_op jit(solution)/shard_map/first/pallas_call | solution.py:718
  15.8 1.9 %collective-permute-start.6 = (bf16[2,32,128]{2,1,0:T(8,128)(2,1)S(1)}, bf16[2,32,128]{2,1,0:T(8,128)(2,1)S(1)}, u32[]{:S(2)}, u32[]{:S(2)}) collective-permute-start(bf16[2,32,128]{2,1,0:T(8,128)(2,1)S(1)} %get-tuple-element.91), channel_id=1, source_target_pairs={{0,1},{1,0},{2,3},{3,2},{4,5},{5,4},{6,7},{7,6},{8,9},{9,8},{10,11... | collective-permute-start | bytes 49160 | tf_op jit(solution)/shard_map/ppermute | solution.py:689
  17.8 1.8 %later.1 = (f32[5,10,32,128]{3,2,1,0:T(8,128)S(1)}, f32[3,4,32,128]{3,2,1,0:T(8,128)S(1)}, f32[3,4,32,128]{3,2,1,0:T(8,128)S(1)}, f32[4,32,128]{2,1,0:T(8,128)S(...) custom-call(bf16[2,3,4,32,128]{4,3,2,1,0:T(8,128)(2,1)S(1)} %get-tuple-element.52.flow, ...), custom_call_target="tpu_custom_call" | custom-call | flops 20000000 | bytes 3981312 | tf_op jit(solution)/shard_map/later/pallas_call | solution.py:718
  19.6 0.2 collective-permute-start.7
  19.8 0.0 collective-permute-done.6.other
  19.8 0.3 %middle.1 = (f32[5,4,32,128]{3,2,1,0:T(8,128)S(1)}, bf16[5,2,32,128]{3,2,1,0:T(8,128)(2,1)S(1)}, f32[4,32,128]{2,1,0:T(8,128)S(1)}) custom-call(f32[5,4,32,128]{3,2,1,0:T(8,128)S(1)} %get-tuple-element.89.first, f32[5,4,32,128]{3,2,1,0:T(8,128)S(1)} %get-tuple-element.83.second, f32[32,128]{1,0:T(8,128)S(1)} %get-tuple-element.90.columns, ...), custom_call_target="tpu_custom_call" | custom-call | flops 1000000 | bytes 1163264 | tf_op jit(solution)/shard_map/middle/pallas_call | solution.py:718
  20.1 3.3 %collective-permute-start.9 = (bf16[5,2,32,128]{3,2,1,0:T(8,128)(2,1)S(1)}, bf16[5,2,32,128]{3,2,1,0:T(8,128)(2,1)S(1)}, u32[]{:S(2)}, u32[]{:S(2)}) collective-permute-start(bf16[5,2,32,128]{3,2,1,0:T(8,128)(2,1)S(1)} %get-tuple-element.100), channel_id=1, source_target_pairs={{0,30},{2,4},{4,2},{6,8},{8,6},{10,12},{12,10},{14,16},{16,14},{18... | collective-permute-start | bytes 245768 | tf_op jit(solution)/shard_map/ppermute | solution.py:859
  23.4 1.4 %base.1 = (f32[5,4,32,128]{3,2,1,0:T(8,128)S(1)}, f32[4,32,128]{2,1,0:T(8,128)S(1)}, f32[2,2,32,128]{3,2,1,0:T(8,128)S(1)}, f32[2,4,32]{2,1,0:T(4,128)}, bf16[5,2,32,128]{3,2,1,0:T(8,128)(2,1)S(1)}) custom-call(f32[5,10,32,128]{3,2,1,0:T(8,128)S(1)} %get-tuple-element.84.wide, f32[3,4,32,128]{3,2,1,0:T(8,128)S(1)} %get-tuple-element.85.grad_x, ...), custom_call_target="tpu_custom_call" | custom-call | flops 15000000 | bytes 3253248 | tf_op jit(solution)/shard_map/base/pallas_call | solution.py:718
  24.8 1.9 %collective-permute-done.9.far = bf16[5,2,32,128]{3,2,1,0:T(8,128)(2,1)S(1)} collective-permute-done((bf16[5,2,32,128]{3,2,1,0:T(8,128)(2,1)S(1)}, bf16[5,2,32,128]{3,2,1,0:T(8,128)(2,1)S(1)}, u32[]{:S(2)}, u32[]{:S(2)}) %collective-permute-start.9) | collective-permute-done | bytes 81952 | tf_op jit(solution)/shard_map/ppermute | solution.py:859
  26.7 0.8 %last.1 = f32[5,4,32,128]{3,2,1,0:T(8,128)} custom-call(f32[5,4,32,128]{3,2,1,0:T(8,128)S(1)} %get-tuple-element.96.base, f32[4,32,128]{2,1,0:T(8,128)S(1)} %get-tuple-element.97.drift, f32[2,2,32,128]{3,2,1,0:T(8,128)S(1)} %get-tuple-element.98.spread, bf16[5,2,32,128]{3,2,1,0:T(8,128)(2,1)S(1)} %collective-permute-done.8.near_psi, ...), custom_call_target="tpu_custom_call" | custom-call | flops 1000000 | bytes 1032192 | tf_op jit(solution)/shard_map/last/pallas_call | solution.py:718
  (11 shorter events, 0.0 us)
Async XLA Ops:
  1.9 8.3 %collective-permute-start.1 = (bf16[18,32,128]{2,1,0:T(8,128)(2,1)S(1)}, bf16[18,32,128]{2,1,0:T(8,128)(2,1)S(1)}, u32[]{:S(2)}, u32[]{:S(2)}) collective-permute-start(bf16[18,32,128]{2,1,0:T(8,128)(2,1)S(1)} %get-tuple-element.57), channel_id=1, source_target_pairs={{0,30},{2,4},{4,2},{6,8},{8,6},{10,12},{12,10},{14,16},{16,14},{18... | collective-permute-start | bytes 442376 | tf_op jit(solution)/shard_map/ppermute | solution.py:761
  7.6 2.6 %collective-permute-start = (bf16[18,32,128]{2,1,0:T(8,128)(2,1)S(1)}, bf16[18,32,128]{2,1,0:T(8,128)(2,1)S(1)}, u32[]{:S(2)}, u32[]{:S(2)}) collective-permute-start(bf16[18,32,128]{2,1,0:T(8,128)(2,1)S(1)} %get-tuple-element.56), channel_id=1, source_target_pairs={{0,2},{2,0},{4,6},{6,4},{8,10},{10,8},{12,14},{14,12},{16,18},{18,... | collective-permute-start | bytes 442376 | tf_op jit(solution)/shard_map/ppermute | solution.py:775
  7.6 7.5 %collective-permute-start.3 = (bf16[18,32,128]{2,1,0:T(8,128)(2,1)S(1)}, bf16[18,32,128]{2,1,0:T(8,128)(2,1)S(1)}, u32[]{:S(2)}, u32[]{:S(2)}) collective-permute-start(bf16[18,32,128]{2,1,0:T(8,128)(2,1)S(1)} %get-tuple-element.59), channel_id=1, source_target_pairs={{0,30},{2,4},{4,2},{6,8},{8,6},{10,12},{12,10},{14,16},{16,14},{18... | collective-permute-start | bytes 442376 | tf_op jit(solution)/shard_map/ppermute | solution.py:774
  8.3 6.9 %collective-permute-start.2 = (bf16[18,32,128]{2,1,0:T(8,128)(2,1)S(1)}, bf16[18,32,128]{2,1,0:T(8,128)(2,1)S(1)}, u32[]{:S(2)}, u32[]{:S(2)}) collective-permute-start(bf16[18,32,128]{2,1,0:T(8,128)(2,1)S(1)} %get-tuple-element.58), channel_id=1, source_target_pairs={{0,2},{2,0},{4,6},{6,4},{8,10},{10,8},{12,14},{14,12},{16,18},{18,... | collective-permute-start | bytes 442376 | tf_op jit(solution)/shard_map/ppermute | solution.py:776
  8.3 4.1 %collective-permute-start.4 = (bf16[5,32,128]{2,1,0:T(8,128)(2,1)S(1)}, bf16[5,32,128]{2,1,0:T(8,128)(2,1)S(1)}, u32[]{:S(2)}, u32[]{:S(2)}) collective-permute-start(bf16[5,32,128]{2,1,0:T(8,128)(2,1)S(1)} %get-tuple-element.60), channel_id=1, source_target_pairs={{0,1},{1,0},{2,3},{3,2},{4,5},{5,4},{6,7},{7,6},{8,9},{9,8},{10,11... | collective-permute-start | bytes 122888 | tf_op jit(solution)/shard_map/ppermute | solution.py:689
  10.4 3.9 %collective-permute-start.5 = (bf16[3,32,128]{2,1,0:T(8,128)(2,1)S(1)}, bf16[3,32,128]{2,1,0:T(8,128)(2,1)S(1)}, u32[]{:S(2)}, u32[]{:S(2)}) collective-permute-start(bf16[3,32,128]{2,1,0:T(8,128)(2,1)S(1)} %get-tuple-element.71), channel_id=1, source_target_pairs={{0,1},{1,0},{2,3},{3,2},{4,5},{5,4},{6,7},{7,6},{8,9},{9,8},{10,11... | collective-permute-start | bytes 73736 | tf_op jit(solution)/shard_map/ppermute | solution.py:689
  15.8 4.0 %collective-permute-start.6 = (bf16[2,32,128]{2,1,0:T(8,128)(2,1)S(1)}, bf16[2,32,128]{2,1,0:T(8,128)(2,1)S(1)}, u32[]{:S(2)}, u32[]{:S(2)}) collective-permute-start(bf16[2,32,128]{2,1,0:T(8,128)(2,1)S(1)} %get-tuple-element.91), channel_id=1, source_target_pairs={{0,1},{1,0},{2,3},{3,2},{4,5},{5,4},{6,7},{7,6},{8,9},{9,8},{10,11... | collective-permute-start | bytes 49160 | tf_op jit(solution)/shard_map/ppermute | solution.py:689
  19.6 3.8 %collective-permute-start.7 = (bf16[1,32,128]{2,1,0:T(8,128)(2,1)S(1)}, bf16[1,32,128]{2,1,0:T(8,128)(2,1)S(1)}, u32[]{:S(2)}, u32[]{:S(2)}) collective-permute-start(bf16[1,32,128]{2,1,0:T(8,128)(2,1)S(1)} %get-tuple-element.95), channel_id=1, source_target_pairs={{0,1},{1,0},{2,3},{3,2},{4,5},{5,4},{6,7},{7,6},{8,9},{9,8},{10,11... | collective-permute-start | bytes 24584 | tf_op jit(solution)/shard_map/ppermute | solution.py:689
  20.1 6.6 %collective-permute-start.9 = (bf16[5,2,32,128]{3,2,1,0:T(8,128)(2,1)S(1)}, bf16[5,2,32,128]{3,2,1,0:T(8,128)(2,1)S(1)}, u32[]{:S(2)}, u32[]{:S(2)}) collective-permute-start(bf16[5,2,32,128]{3,2,1,0:T(8,128)(2,1)S(1)} %get-tuple-element.100), channel_id=1, source_target_pairs={{0,30},{2,4},{4,2},{6,8},{8,6},{10,12},{12,10},{14,16},{16,14},{18... | collective-permute-start | bytes 245768 | tf_op jit(solution)/shard_map/ppermute | solution.py:859
  24.8 1.9 %collective-permute-start.8 = (bf16[5,2,32,128]{3,2,1,0:T(8,128)(2,1)S(1)}, bf16[5,2,32,128]{3,2,1,0:T(8,128)(2,1)S(1)}, u32[]{:S(2)}, u32[]{:S(2)}) collective-permute-start(bf16[5,2,32,128]{3,2,1,0:T(8,128)(2,1)S(1)} %get-tuple-element.99), channel_id=1, source_target_pairs={{0,2},{2,0},{4,6},{6,4},{8,10},{10,8},{12,14},{14,12},{16,18},{18,... | collective-permute-start | bytes 245768 | tf_op jit(solution)/shard_map/ppermute | solution.py:874

commit v16 on v15

--- a/solution.py
+++ b/solution.py
@@ -156,7 +156,7 @@
         else:
             lap_psi = laps[k]
             if k < 3:
-                for other in range(5):
+                for other in range(5 if k == 0 else 0):
                     rate = rate + psi[other] * grad[k][other]
                 rate = rate + NU_MOL * (inv_rho * lap_psi)
                 eddy = size_rho * lap_psi
@@ -283,7 +283,10 @@
         along_z = flow[0, 2, x].astype(F32)
         for k in range(5):
             by_z, both = z_terms(ops, psi[k, x], psi_halos[k, x])
-            psi_rate[k, x] = rate_y[k, x] + along_z * by_z
+            rate = rate_y[k, x] + along_z * by_z
+            for other in range(5 if k in (1, 2) else 0):
+                rate = rate + psi[other, x] * grad_0[other, k - 1, x]
+            psi_rate[k, x] = rate
             psi_lap[k, x] = psi_lap_y[k, x] + both
 
 
@@ -619,7 +622,10 @@
         for k in range(5):
             by_y, lap = y_terms(ops, psi[k, x])
             by_z, both = z_terms(ops, psi[k, x], psi_halos[k, x])
-            psi_rate[k, x] = wide[1, x + 3] * by_y + wide[2, x + 3] * by_z
+            rate = wide[1, x + 3] * by_y + wide[2, x + 3] * by_z
+            for other in range(5 if k in (1, 2) else 0):
+                rate = rate + psi[other, x] * grad_yz[other, k - 1, x]
+            psi_rate[k, x] = rate
             psi_lap[k, x] = lap + both
     for x in range(CX):
         terms = state_terms(wide, grad_x, grad_yz, lap_velocity, lap_yz, sizes, x)

time: 27.7 us -> 27.6 us (level)
  Pallas kernels: 9.71 us -> 9.3 us
  waiting for transfers between devices: 1.93 us -> 2.27 us
    pallas_call x15, Pallas kernels: 9.71 us -> 9.3 us  [call(): pl.pallas_call(kernel, in_specs=in_specs or whole(len(inputs)), out_specs...]
    ppermute x2, waiting for transfers between devices: 1.91 us -> 2.25 us  [local(): far = lax.ppermute(far, 'gx', across)]
  transfers between devices with their start and end apart: 10 -> 10, of which waited for: 1 -> 1; matrix products, arithmetic and copies ran while one was open for 0% -> 0% of each run, Pallas kernels for 26% -> 25%
where the time goes in v16:
time: 27.6 us; the launch traced here: 27.4 us
  starting transfers between devices  15.1 us (55%)
  Pallas kernels  9.3 us (34%)
  waiting for transfers between devices  2.27 us (8%)
  between operations  0.76 us (3%)
    pallas_call x15, Pallas kernels, call(): pl.pallas_call(kernel, in_specs=in_specs or whole(len(inputs)), out_specs...  9.3 us
    ppermute x2, starting transfers between devices, local(): far = lax.ppermute(far, 'gx', across)  8.78 us
    ppermute x4, starting transfers between devices, span_edges(): before = lax.ppermute(message, 'gz', forward)  5.63 us
    ppermute x2, waiting for transfers between devices, local(): far = lax.ppermute(far, 'gx', across)  2.25 us
    ppermute x1, starting transfers between devices, local(): far_scalars = lax.ppermute(far_scalars, 'gx', across)  0.68 us
  transfers between devices with their start and end apart: 10, of which 1 were waited for; matrix products, arithmetic and copies ran while one was open for 0% of the time, Pallas kernels for 25%

profile of v16, /device:TPU:0, one launch (start us, length us, event | category | flops | bytes accessed | tf_op | source)
XLA Modules:
  0.0 27.4 jit_solution(17452499785902938698)
XLA Ops:
  0.6 1.2 %message.1 = (bf16[18,32,128]{2,1,0:T(8,128)(2,1)S(1)}, bf16[18,32,128]{2,1,0:T(8,128)(2,1)S(1)}, bf16[2,3,4,32,128]{4,3,2,1,0:T(8,128)(2,1)S(1)}, bf16[2,4,32,1...) custom-call(bf16[2,3,4,32,128]{4,3,2,1,0:T(8,128)(2,1)} %flow_far.1, ...), custom_call_target="tpu_custom_call" | custom-call | flops 1000000 | bytes 1605632 | tf_op jit(solution)/shard_map/message/pallas_call | solution.py:724
  1.9 5.5 %collective-permute-start.1 = (bf16[18,32,128]{2,1,0:T(8,128)(2,1)S(1)}, bf16[18,32,128]{2,1,0:T(8,128)(2,1)S(1)}, u32[]{:S(2)}, u32[]{:S(2)}) collective-permute-start(bf16[18,32,128]{2,1,0:T(8,128)(2,1)S(1)} %get-tuple-element.57), channel_id=1, source_target_pairs={{0,30},{2,4},{4,2},{6,8},{8,6},{10,12},{12,10},{14,16},{16,14},{18... | collective-permute-start | bytes 442376 | tf_op jit(solution)/shard_map/ppermute | solution.py:767
  7.3 0.3 pack.1
  7.6 0.0 collective-permute-start
  7.6 0.7 %collective-permute-start.3 = (bf16[18,32,128]{2,1,0:T(8,128)(2,1)S(1)}, bf16[18,32,128]{2,1,0:T(8,128)(2,1)S(1)}, u32[]{:S(2)}, u32[]{:S(2)}) collective-permute-start(bf16[18,32,128]{2,1,0:T(8,128)(2,1)S(1)} %get-tuple-element.59), channel_id=1, source_target_pairs={{0,30},{2,4},{4,2},{6,8},{8,6},{10,12},{12,10},{14,16},{16,14},{18... | collective-permute-start | bytes 442376 | tf_op jit(solution)/shard_map/ppermute | solution.py:780
  8.3 1.5 %collective-permute-start.4 = (bf16[5,32,128]{2,1,0:T(8,128)(2,1)S(1)}, bf16[5,32,128]{2,1,0:T(8,128)(2,1)S(1)}, u32[]{:S(2)}, u32[]{:S(2)}) collective-permute-start(bf16[5,32,128]{2,1,0:T(8,128)(2,1)S(1)} %get-tuple-element.60), channel_id=1, source_target_pairs={{0,1},{1,0},{2,3},{3,2},{4,5},{5,4},{6,7},{7,6},{8,9},{9,8},{10,11... | collective-permute-start | bytes 122888 | tf_op jit(solution)/shard_map/ppermute | solution.py:695
  9.8 0.3 %rows.1 = (f32[5,4,32,128]{3,2,1,0:T(8,128)S(1)}, f32[5,4,32,128]{3,2,1,0:T(8,128)S(1)}, f32[5,4,32,128]{3,2,1,0:T(8,128)S(1)}, f32[5,4,32,128]{3,2,1,0:T(8,128)...) custom-call(bf16[2,3,4,32,128]{4,3,2,1,0:T(8,128)(2,1)S(1)} %get-tuple-element.52.flow, ...), custom_call_target="tpu_custom_call" | custom-call | flops 3000000 | bytes 2621440 | tf_op jit(solution)/shard_map/rows/pallas_call | solution.py:724
  10.2 0.0 collective-permute-done.1.far
  10.2 0.2 bands.1
  10.4 2.0 %collective-permute-start.5 = (bf16[3,32,128]{2,1,0:T(8,128)(2,1)S(1)}, bf16[3,32,128]{2,1,0:T(8,128)(2,1)S(1)}, u32[]{:S(2)}, u32[]{:S(2)}) collective-permute-start(bf16[3,32,128]{2,1,0:T(8,128)(2,1)S(1)} %get-tuple-element.71), channel_id=1, source_target_pairs={{0,1},{1,0},{2,3},{3,2},{4,5},{5,4},{6,7},{7,6},{8,9},{9,8},{10,11... | collective-permute-start | bytes 73736 | tf_op jit(solution)/shard_map/ppermute | solution.py:695
  12.4 0.9 %own.1 = (f32[5,2,4,32,128]{4,3,2,1,0:T(8,128)S(1)}, f32[5,2,4,32,128]{4,3,2,1,0:T(8,128)S(1)}, f32[5,4,32,128]{3,2,1,0:T(8,128)S(1)}, f32[5,4,32,128]{3,2,1,0:T...) custom-call(bf16[2,3,4,32,128]{4,3,2,1,0:T(8,128)(2,1)S(1)} %get-tuple-element.52.flow, ...), custom_call_target="tpu_custom_call" | custom-call | flops 5000000 | bytes 5283840 | tf_op jit(solution)/shard_map/own/pallas_call | solution.py:724
  13.3 1.0 %inner.1 = (f32[2,4,32,128]{3,2,1,0:T(8,128)S(1)}, f32[3,32,128]{2,1,0:T(8,128)S(1)}, f32[3,10,32,128]{3,2,1,0:T(8,128)S(1)}, f32[3,4,32,128]{3,2,1,0:T(8,128)S(...) custom-call(bf16[2,3,4,32,128]{4,3,2,1,0:T(8,128)(2,1)S(1)} %get-tuple-element.52.flow, ...), custom_call_target="tpu_custom_call" | custom-call | flops 20000000 | bytes 2605056 | tf_op jit(solution)/shard_map/inner/pallas_call | solution.py:724
  14.3 0.0 collective-permute-done.5.halo
  14.4 0.8 %edge.1._.products = f32[32,128]{1,0:T(8,128)S(1)} custom-call(f32[6,32,128]{2,1,0:T(8,128)S(1)} %get-tuple-element.70.low, f32[3,32,128]{2,1,0:T(8,128)S(1)} %get-tuple-element.74.high, bf16[3,32,128]{2,1,0:T(8,128)(2,1)S(1)} %collective-permute-done.5.halo, f32[2,4,32,128]{3,2,1,0:T(8,128)S(1)} %get-tuple-element.75.inner), custom_call_target="tpu_custom_call" | custom-call | flops 20000000 | bytes 319488 | tf_op jit(solution)/shard_map/edge/pallas_call | solution.py:724
  15.2 0.0 collective-permute-done.2.near.near_scalars
  15.2 0.6 %first.1 = (f32[5,4,32,128]{3,2,1,0:T(8,128)S(1)}, f32[5,4,32,128]{3,2,1,0:T(8,128)S(1)}, bf16[2,32,128]{2,1,0:T(8,128)(2,1)S(1)}, f32[32,128]{1,0:T(8,128)S(1)}) custom-call(f32[32,128]{1,0:T(8,128)S(1)} %later_token.1._, f32[32,128]{1,0:T(8,128)S(1)} %edge.1._.products, bf16[2,4,32,128]{3,2,1,0:T(8,128)(2,1)S(1)} %get-tuple-element.53.rho, ...), custom_call_target="tpu_custom_call" | custom-call | flops 10000000 | bytes 4063232 | tf_op jit(solution)/shard_map/first/pallas_call | solution.py:724
  15.7 1.9 %collective-permute-start.6 = (bf16[2,32,128]{2,1,0:T(8,128)(2,1)S(1)}, bf16[2,32,128]{2,1,0:T(8,128)(2,1)S(1)}, u32[]{:S(2)}, u32[]{:S(2)}) collective-permute-start(bf16[2,32,128]{2,1,0:T(8,128)(2,1)S(1)} %get-tuple-element.91), channel_id=1, source_target_pairs={{0,1},{1,0},{2,3},{3,2},{4,5},{5,4},{6,7},{7,6},{8,9},{9,8},{10,11... | collective-permute-start | bytes 49160 | tf_op jit(solution)/shard_map/ppermute | solution.py:695
  17.7 1.8 %later.1 = (f32[5,10,32,128]{3,2,1,0:T(8,128)S(1)}, f32[3,4,32,128]{3,2,1,0:T(8,128)S(1)}, f32[3,4,32,128]{3,2,1,0:T(8,128)S(1)}, f32[4,32,128]{2,1,0:T(8,128)S(...) custom-call(bf16[2,3,4,32,128]{4,3,2,1,0:T(8,128)(2,1)S(1)} %get-tuple-element.52.flow, ...), custom_call_target="tpu_custom_call" | custom-call | flops 20000000 | bytes 3981312 | tf_op jit(solution)/shard_map/later/pallas_call | solution.py:724
  19.5 0.2 collective-permute-start.7
  19.7 0.3 %middle.1 = (f32[5,4,32,128]{3,2,1,0:T(8,128)S(1)}, bf16[5,2,32,128]{3,2,1,0:T(8,128)(2,1)S(1)}, f32[4,32,128]{2,1,0:T(8,128)S(1)}) custom-call(f32[5,4,32,128]{3,2,1,0:T(8,128)S(1)} %get-tuple-element.89.first, f32[5,4,32,128]{3,2,1,0:T(8,128)S(1)} %get-tuple-element.83.second, f32[32,128]{1,0:T(8,128)S(1)} %get-tuple-element.90.columns, ...), custom_call_target="tpu_custom_call" | custom-call | flops 1000000 | bytes 1163264 | tf_op jit(solution)/shard_map/middle/pallas_call | solution.py:724
  20.0 3.3 %collective-permute-start.9 = (bf16[5,2,32,128]{3,2,1,0:T(8,128)(2,1)S(1)}, bf16[5,2,32,128]{3,2,1,0:T(8,128)(2,1)S(1)}, u32[]{:S(2)}, u32[]{:S(2)}) collective-permute-start(bf16[5,2,32,128]{3,2,1,0:T(8,128)(2,1)S(1)} %get-tuple-element.100), channel_id=1, source_target_pairs={{0,30},{2,4},{4,2},{6,8},{8,6},{10,12},{12,10},{14,16},{16,14},{18... | collective-permute-start | bytes 245768 | tf_op jit(solution)/shard_map/ppermute | solution.py:865
  23.3 1.1 %base.1 = (f32[5,4,32,128]{3,2,1,0:T(8,128)S(1)}, f32[4,32,128]{2,1,0:T(8,128)S(1)}, f32[2,2,32,128]{3,2,1,0:T(8,128)S(1)}, f32[2,4,32]{2,1,0:T(4,128)}, bf16[5,2,32,128]{3,2,1,0:T(8,128)(2,1)S(1)}) custom-call(f32[5,10,32,128]{3,2,1,0:T(8,128)S(1)} %get-tuple-element.84.wide, f32[3,4,32,128]{3,2,1,0:T(8,128)S(1)} %get-tuple-element.85.grad_x, ...), custom_call_target="tpu_custom_call" | custom-call | flops 15000000 | bytes 3253248 | tf_op jit(solution)/shard_map/base/pallas_call | solution.py:724
  24.4 2.2 %collective-permute-done.9.far = bf16[5,2,32,128]{3,2,1,0:T(8,128)(2,1)S(1)} collective-permute-done((bf16[5,2,32,128]{3,2,1,0:T(8,128)(2,1)S(1)}, bf16[5,2,32,128]{3,2,1,0:T(8,128)(2,1)S(1)}, u32[]{:S(2)}, u32[]{:S(2)}) %collective-permute-start.9) | collective-permute-done | bytes 81952 | tf_op jit(solution)/shard_map/ppermute | solution.py:865
  26.7 0.8 %last.1 = f32[5,4,32,128]{3,2,1,0:T(8,128)} custom-call(f32[5,4,32,128]{3,2,1,0:T(8,128)S(1)} %get-tuple-element.96.base, f32[4,32,128]{2,1,0:T(8,128)S(1)} %get-tuple-element.97.drift, f32[2,2,32,128]{3,2,1,0:T(8,128)S(1)} %get-tuple-element.98.spread, bf16[5,2,32,128]{3,2,1,0:T(8,128)(2,1)S(1)} %collective-permute-done.8.near_psi, ...), custom_call_target="tpu_custom_call" | custom-call | flops 1000000 | bytes 1032192 | tf_op jit(solution)/shard_map/last/pallas_call | solution.py:724
  (11 shorter events, 0.0 us)
Async XLA Ops:
  1.9 8.3 %collective-permute-start.1 = (bf16[18,32,128]{2,1,0:T(8,128)(2,1)S(1)}, bf16[18,32,128]{2,1,0:T(8,128)(2,1)S(1)}, u32[]{:S(2)}, u32[]{:S(2)}) collective-permute-start(bf16[18,32,128]{2,1,0:T(8,128)(2,1)S(1)} %get-tuple-element.57), channel_id=1, source_target_pairs={{0,30},{2,4},{4,2},{6,8},{8,6},{10,12},{12,10},{14,16},{16,14},{18... | collective-permute-start | bytes 442376 | tf_op jit(solution)/shard_map/ppermute | solution.py:767
  7.6 2.6 %collective-permute-start = (bf16[18,32,128]{2,1,0:T(8,128)(2,1)S(1)}, bf16[18,32,128]{2,1,0:T(8,128)(2,1)S(1)}, u32[]{:S(2)}, u32[]{:S(2)}) collective-permute-start(bf16[18,32,128]{2,1,0:T(8,128)(2,1)S(1)} %get-tuple-element.56), channel_id=1, source_target_pairs={{0,2},{2,0},{4,6},{6,4},{8,10},{10,8},{12,14},{14,12},{16,18},{18,... | collective-permute-start | bytes 442376 | tf_op jit(solution)/shard_map/ppermute | solution.py:781
  7.6 7.5 %collective-permute-start.3 = (bf16[18,32,128]{2,1,0:T(8,128)(2,1)S(1)}, bf16[18,32,128]{2,1,0:T(8,128)(2,1)S(1)}, u32[]{:S(2)}, u32[]{:S(2)}) collective-permute-start(bf16[18,32,128]{2,1,0:T(8,128)(2,1)S(1)} %get-tuple-element.59), channel_id=1, source_target_pairs={{0,30},{2,4},{4,2},{6,8},{8,6},{10,12},{12,10},{14,16},{16,14},{18... | collective-permute-start | bytes 442376 | tf_op jit(solution)/shard_map/ppermute | solution.py:780
  8.3 6.9 %collective-permute-start.2 = (bf16[18,32,128]{2,1,0:T(8,128)(2,1)S(1)}, bf16[18,32,128]{2,1,0:T(8,128)(2,1)S(1)}, u32[]{:S(2)}, u32[]{:S(2)}) collective-permute-start(bf16[18,32,128]{2,1,0:T(8,128)(2,1)S(1)} %get-tuple-element.58), channel_id=1, source_target_pairs={{0,2},{2,0},{4,6},{6,4},{8,10},{10,8},{12,14},{14,12},{16,18},{18,... | collective-permute-start | bytes 442376 | tf_op jit(solution)/shard_map/ppermute | solution.py:782
  8.3 4.1 %collective-permute-start.4 = (bf16[5,32,128]{2,1,0:T(8,128)(2,1)S(1)}, bf16[5,32,128]{2,1,0:T(8,128)(2,1)S(1)}, u32[]{:S(2)}, u32[]{:S(2)}) collective-permute-start(bf16[5,32,128]{2,1,0:T(8,128)(2,1)S(1)} %get-tuple-element.60), channel_id=1, source_target_pairs={{0,1},{1,0},{2,3},{3,2},{4,5},{5,4},{6,7},{7,6},{8,9},{9,8},{10,11... | collective-permute-start | bytes 122888 | tf_op jit(solution)/shard_map/ppermute | solution.py:695
  10.4 3.9 %collective-permute-start.5 = (bf16[3,32,128]{2,1,0:T(8,128)(2,1)S(1)}, bf16[3,32,128]{2,1,0:T(8,128)(2,1)S(1)}, u32[]{:S(2)}, u32[]{:S(2)}) collective-permute-start(bf16[3,32,128]{2,1,0:T(8,128)(2,1)S(1)} %get-tuple-element.71), channel_id=1, source_target_pairs={{0,1},{1,0},{2,3},{3,2},{4,5},{5,4},{6,7},{7,6},{8,9},{9,8},{10,11... | collective-permute-start | bytes 73736 | tf_op jit(solution)/shard_map/ppermute | solution.py:695
  15.7 4.0 %collective-permute-start.6 = (bf16[2,32,128]{2,1,0:T(8,128)(2,1)S(1)}, bf16[2,32,128]{2,1,0:T(8,128)(2,1)S(1)}, u32[]{:S(2)}, u32[]{:S(2)}) collective-permute-start(bf16[2,32,128]{2,1,0:T(8,128)(2,1)S(1)} %get-tuple-element.91), channel_id=1, source_target_pairs={{0,1},{1,0},{2,3},{3,2},{4,5},{5,4},{6,7},{7,6},{8,9},{9,8},{10,11... | collective-permute-start | bytes 49160 | tf_op jit(solution)/shard_map/ppermute | solution.py:695
  19.5 3.8 %collective-permute-start.7 = (bf16[1,32,128]{2,1,0:T(8,128)(2,1)S(1)}, bf16[1,32,128]{2,1,0:T(8,128)(2,1)S(1)}, u32[]{:S(2)}, u32[]{:S(2)}) collective-permute-start(bf16[1,32,128]{2,1,0:T(8,128)(2,1)S(1)} %get-tuple-element.95), channel_id=1, source_target_pairs={{0,1},{1,0},{2,3},{3,2},{4,5},{5,4},{6,7},{7,6},{8,9},{9,8},{10,11... | collective-permute-start | bytes 24584 | tf_op jit(solution)/shard_map/ppermute | solution.py:695
  20.0 6.6 %collective-permute-start.9 = (bf16[5,2,32,128]{3,2,1,0:T(8,128)(2,1)S(1)}, bf16[5,2,32,128]{3,2,1,0:T(8,128)(2,1)S(1)}, u32[]{:S(2)}, u32[]{:S(2)}) collective-permute-start(bf16[5,2,32,128]{3,2,1,0:T(8,128)(2,1)S(1)} %get-tuple-element.100), channel_id=1, source_target_pairs={{0,30},{2,4},{4,2},{6,8},{8,6},{10,12},{12,10},{14,16},{16,14},{18... | collective-permute-start | bytes 245768 | tf_op jit(solution)/shard_map/ppermute | solution.py:865
  24.4 2.3 %collective-permute-start.8 = (bf16[5,2,32,128]{3,2,1,0:T(8,128)(2,1)S(1)}, bf16[5,2,32,128]{3,2,1,0:T(8,128)(2,1)S(1)}, u32[]{:S(2)}, u32[]{:S(2)}) collective-permute-start(bf16[5,2,32,128]{3,2,1,0:T(8,128)(2,1)S(1)} %get-tuple-element.99), channel_id=1, source_target_pairs={{0,2},{2,0},{4,6},{6,4},{8,10},{10,8},{12,14},{14,12},{16,18},{18,... | collective-permute-start | bytes 245768 | tf_op jit(solution)/shard_map/ppermute | solution.py:880

commit v17 on v15

--- a/solution.py
+++ b/solution.py
@@ -135,7 +135,8 @@
         else:
             xs = [wide[k, x + 3 + step] for step in (1, -1, 2, -2)]
             grad[0][k] = fourth(*xs)
-            lap[k] = lap_yz[k, x] + (xs[0] + xs[1])
+            if k != 3:
+                lap[k] = lap_yz[k, x] + (xs[0] + xs[1])
         grad[1][k], grad[2][k] = grad_yz[k, 0, x], grad_yz[k, 1, x]
     return center, grad, lap, sizes[x], 1.0 / center[3]
 
@@ -249,7 +250,9 @@
         for k in range(5):
             for x in range(CX):
                 values = flow[t, k, x] if k < 3 else (rho if k == 3 else temp)[t, x]
-                grad_y[k, x], lap_y[k, x] = y_terms(ops, values.astype(F32))
+                grad_y[k, x], lap = y_terms(ops, values.astype(F32))
+                if k != 3:
+                    lap_y[k, x] = lap
     for x in range(CX):
         along_y = flow[0, 1, x].astype(F32)
         for k in range(5):
@@ -278,7 +281,8 @@
                 values = flow[t, k, x] if k < 3 else (rho if k == 3 else temp)[t, x]
                 by_z, both = z_terms(ops, values.astype(F32), halos[t, k, x])
                 grad_yz[k, 0, x], grad_yz[k, 1, x] = grad_y[k, x], by_z
-                lap_yz[k, x] = lap_y[k, x] + both
+                if k != 3:
+                    lap_yz[k, x] = lap_y[k, x] + both
     for x in range(CX):
         along_z = flow[0, 2, x].astype(F32)
         for k in range(5):

time: 27.7 us -> 27.7 us (level)
  no operation moved by 1% of the time
where the time goes in v17:
time: 27.7 us; the launch traced here: 27.5 us
  starting transfers between devices  15.1 us (55%)
  Pallas kernels  9.7 us (35%)
  waiting for transfers between devices  1.93 us (7%)
  between operations  0.76 us (3%)
    pallas_call x15, Pallas kernels, call(): pl.pallas_call(kernel, in_specs=in_specs or whole(len(inputs)), out_specs...  9.7 us
    ppermute x2, starting transfers between devices, local(): far = lax.ppermute(far, 'gx', across)  8.78 us
    ppermute x4, starting transfers between devices, span_edges(): before = lax.ppermute(message, 'gz', forward)  5.64 us
    ppermute x2, waiting for transfers between devices, local(): far = lax.ppermute(far, 'gx', across)  1.91 us
    ppermute x1, starting transfers between devices, local(): far_scalars = lax.ppermute(far_scalars, 'gx', across)  0.68 us
  transfers between devices with their start and end apart: 10, of which 1 were waited for; matrix products, arithmetic and copies ran while one was open for 0% of the time, Pallas kernels for 26%

profile of v17, /device:TPU:0, one launch (start us, length us, event | category | flops | bytes accessed | tf_op | source)
XLA Modules:
  0.0 27.5 jit_solution(6499393885474960460)
XLA Ops:
  0.6 1.2 %message.1 = (bf16[18,32,128]{2,1,0:T(8,128)(2,1)S(1)}, bf16[18,32,128]{2,1,0:T(8,128)(2,1)S(1)}, bf16[2,3,4,32,128]{4,3,2,1,0:T(8,128)(2,1)S(1)}, bf16[2,4,32,1...) custom-call(bf16[2,3,4,32,128]{4,3,2,1,0:T(8,128)(2,1)} %flow_far.1, ...), custom_call_target="tpu_custom_call" | custom-call | flops 1000000 | bytes 1605632 | tf_op jit(solution)/shard_map/message/pallas_call | solution.py:722
  1.9 5.5 %collective-permute-start.1 = (bf16[18,32,128]{2,1,0:T(8,128)(2,1)S(1)}, bf16[18,32,128]{2,1,0:T(8,128)(2,1)S(1)}, u32[]{:S(2)}, u32[]{:S(2)}) collective-permute-start(bf16[18,32,128]{2,1,0:T(8,128)(2,1)S(1)} %get-tuple-element.57), channel_id=1, source_target_pairs={{0,30},{2,4},{4,2},{6,8},{8,6},{10,12},{12,10},{14,16},{16,14},{18... | collective-permute-start | bytes 442376 | tf_op jit(solution)/shard_map/ppermute | solution.py:765
  7.3 0.3 pack.1
  7.6 0.0 collective-permute-start
  7.6 0.7 %collective-permute-start.3 = (bf16[18,32,128]{2,1,0:T(8,128)(2,1)S(1)}, bf16[18,32,128]{2,1,0:T(8,128)(2,1)S(1)}, u32[]{:S(2)}, u32[]{:S(2)}) collective-permute-start(bf16[18,32,128]{2,1,0:T(8,128)(2,1)S(1)} %get-tuple-element.59), channel_id=1, source_target_pairs={{0,30},{2,4},{4,2},{6,8},{8,6},{10,12},{12,10},{14,16},{16,14},{18... | collective-permute-start | bytes 442376 | tf_op jit(solution)/shard_map/ppermute | solution.py:778
  8.3 1.5 %collective-permute-start.4 = (bf16[5,32,128]{2,1,0:T(8,128)(2,1)S(1)}, bf16[5,32,128]{2,1,0:T(8,128)(2,1)S(1)}, u32[]{:S(2)}, u32[]{:S(2)}) collective-permute-start(bf16[5,32,128]{2,1,0:T(8,128)(2,1)S(1)} %get-tuple-element.60), channel_id=1, source_target_pairs={{0,1},{1,0},{2,3},{3,2},{4,5},{5,4},{6,7},{7,6},{8,9},{9,8},{10,11... | collective-permute-start | bytes 122888 | tf_op jit(solution)/shard_map/ppermute | solution.py:693
  9.8 0.3 %rows.1 = (f32[5,4,32,128]{3,2,1,0:T(8,128)S(1)}, f32[5,4,32,128]{3,2,1,0:T(8,128)S(1)}, f32[5,4,32,128]{3,2,1,0:T(8,128)S(1)}, f32[5,4,32,128]{3,2,1,0:T(8,128)...) custom-call(bf16[2,3,4,32,128]{4,3,2,1,0:T(8,128)(2,1)S(1)} %get-tuple-element.52.flow, ...), custom_call_target="tpu_custom_call" | custom-call | flops 3000000 | bytes 2621440 | tf_op jit(solution)/shard_map/rows/pallas_call | solution.py:722
  10.2 0.0 collective-permute-done.near
  10.2 0.2 bands.1
  10.4 2.0 %collective-permute-start.5 = (bf16[3,32,128]{2,1,0:T(8,128)(2,1)S(1)}, bf16[3,32,128]{2,1,0:T(8,128)(2,1)S(1)}, u32[]{:S(2)}, u32[]{:S(2)}) collective-permute-start(bf16[3,32,128]{2,1,0:T(8,128)(2,1)S(1)} %get-tuple-element.71), channel_id=1, source_target_pairs={{0,1},{1,0},{2,3},{3,2},{4,5},{5,4},{6,7},{7,6},{8,9},{9,8},{10,11... | collective-permute-start | bytes 73736 | tf_op jit(solution)/shard_map/ppermute | solution.py:693
  12.4 0.9 %own.1 = (f32[5,2,4,32,128]{4,3,2,1,0:T(8,128)S(1)}, f32[5,2,4,32,128]{4,3,2,1,0:T(8,128)S(1)}, f32[5,4,32,128]{3,2,1,0:T(8,128)S(1)}, f32[5,4,32,128]{3,2,1,0:T...) custom-call(bf16[2,3,4,32,128]{4,3,2,1,0:T(8,128)(2,1)S(1)} %get-tuple-element.52.flow, ...), custom_call_target="tpu_custom_call" | custom-call | flops 5000000 | bytes 5283840 | tf_op jit(solution)/shard_map/own/pallas_call | solution.py:722
  13.3 1.0 %inner.1 = (f32[2,4,32,128]{3,2,1,0:T(8,128)S(1)}, f32[3,32,128]{2,1,0:T(8,128)S(1)}, f32[3,10,32,128]{3,2,1,0:T(8,128)S(1)}, f32[3,4,32,128]{3,2,1,0:T(8,128)S(...) custom-call(bf16[2,3,4,32,128]{4,3,2,1,0:T(8,128)(2,1)S(1)} %get-tuple-element.52.flow, ...), custom_call_target="tpu_custom_call" | custom-call | flops 20000000 | bytes 2605056 | tf_op jit(solution)/shard_map/inner/pallas_call | solution.py:722
  14.3 0.0 collective-permute-done.5.halo
  14.3 0.8 %edge.1._.products = f32[32,128]{1,0:T(8,128)S(1)} custom-call(f32[6,32,128]{2,1,0:T(8,128)S(1)} %get-tuple-element.70.low, f32[3,32,128]{2,1,0:T(8,128)S(1)} %get-tuple-element.74.high, bf16[3,32,128]{2,1,0:T(8,128)(2,1)S(1)} %collective-permute-done.5.halo, f32[2,4,32,128]{3,2,1,0:T(8,128)S(1)} %get-tuple-element.75.inner), custom_call_target="tpu_custom_call" | custom-call | flops 20000000 | bytes 319488 | tf_op jit(solution)/shard_map/edge/pallas_call | solution.py:722
  15.2 0.0 collective-permute-done.2.near.near_scalars
  15.2 0.6 %first.1 = (f32[5,4,32,128]{3,2,1,0:T(8,128)S(1)}, f32[5,4,32,128]{3,2,1,0:T(8,128)S(1)}, bf16[2,32,128]{2,1,0:T(8,128)(2,1)S(1)}, f32[32,128]{1,0:T(8,128)S(1)}) custom-call(f32[32,128]{1,0:T(8,128)S(1)} %later_token.1._, f32[32,128]{1,0:T(8,128)S(1)} %edge.1._.products, bf16[2,4,32,128]{3,2,1,0:T(8,128)(2,1)S(1)} %get-tuple-element.53.rho, ...), custom_call_target="tpu_custom_call" | custom-call | flops 10000000 | bytes 4063232 | tf_op jit(solution)/shard_map/first/pallas_call | solution.py:722
  15.8 1.9 %collective-permute-start.6 = (bf16[2,32,128]{2,1,0:T(8,128)(2,1)S(1)}, bf16[2,32,128]{2,1,0:T(8,128)(2,1)S(1)}, u32[]{:S(2)}, u32[]{:S(2)}) collective-permute-start(bf16[2,32,128]{2,1,0:T(8,128)(2,1)S(1)} %get-tuple-element.91), channel_id=1, source_target_pairs={{0,1},{1,0},{2,3},{3,2},{4,5},{5,4},{6,7},{7,6},{8,9},{9,8},{10,11... | collective-permute-start | bytes 49160 | tf_op jit(solution)/shard_map/ppermute | solution.py:693
  17.8 1.8 %later.1 = (f32[5,10,32,128]{3,2,1,0:T(8,128)S(1)}, f32[3,4,32,128]{3,2,1,0:T(8,128)S(1)}, f32[3,4,32,128]{3,2,1,0:T(8,128)S(1)}, f32[4,32,128]{2,1,0:T(8,128)S(...) custom-call(bf16[2,3,4,32,128]{4,3,2,1,0:T(8,128)(2,1)S(1)} %get-tuple-element.52.flow, ...), custom_call_target="tpu_custom_call" | custom-call | flops 20000000 | bytes 3981312 | tf_op jit(solution)/shard_map/later/pallas_call | solution.py:722
  19.6 0.2 collective-permute-start.7
  19.8 0.3 %middle.1 = (f32[5,4,32,128]{3,2,1,0:T(8,128)S(1)}, bf16[5,2,32,128]{3,2,1,0:T(8,128)(2,1)S(1)}, f32[4,32,128]{2,1,0:T(8,128)S(1)}) custom-call(f32[5,4,32,128]{3,2,1,0:T(8,128)S(1)} %get-tuple-element.89.first, f32[5,4,32,128]{3,2,1,0:T(8,128)S(1)} %get-tuple-element.83.second, f32[32,128]{1,0:T(8,128)S(1)} %get-tuple-element.90.columns, ...), custom_call_target="tpu_custom_call" | custom-call | flops 1000000 | bytes 1163264 | tf_op jit(solution)/shard_map/middle/pallas_call | solution.py:722
  20.1 3.3 %collective-permute-start.9 = (bf16[5,2,32,128]{3,2,1,0:T(8,128)(2,1)S(1)}, bf16[5,2,32,128]{3,2,1,0:T(8,128)(2,1)S(1)}, u32[]{:S(2)}, u32[]{:S(2)}) collective-permute-start(bf16[5,2,32,128]{3,2,1,0:T(8,128)(2,1)S(1)} %get-tuple-element.100), channel_id=1, source_target_pairs={{0,30},{2,4},{4,2},{6,8},{8,6},{10,12},{12,10},{14,16},{16,14},{18... | collective-permute-start | bytes 245768 | tf_op jit(solution)/shard_map/ppermute | solution.py:863
  23.4 1.4 %base.1 = (f32[5,4,32,128]{3,2,1,0:T(8,128)S(1)}, f32[4,32,128]{2,1,0:T(8,128)S(1)}, f32[2,2,32,128]{3,2,1,0:T(8,128)S(1)}, f32[2,4,32]{2,1,0:T(4,128)}, bf16[5,2,32,128]{3,2,1,0:T(8,128)(2,1)S(1)}) custom-call(f32[5,10,32,128]{3,2,1,0:T(8,128)S(1)} %get-tuple-element.84.wide, f32[3,4,32,128]{3,2,1,0:T(8,128)S(1)} %get-tuple-element.85.grad_x, ...), custom_call_target="tpu_custom_call" | custom-call | flops 15000000 | bytes 3253248 | tf_op jit(solution)/shard_map/base/pallas_call | solution.py:722
  24.8 1.9 %collective-permute-done.9.far = bf16[5,2,32,128]{3,2,1,0:T(8,128)(2,1)S(1)} collective-permute-done((bf16[5,2,32,128]{3,2,1,0:T(8,128)(2,1)S(1)}, bf16[5,2,32,128]{3,2,1,0:T(8,128)(2,1)S(1)}, u32[]{:S(2)}, u32[]{:S(2)}) %collective-permute-start.9) | collective-permute-done | bytes 81952 | tf_op jit(solution)/shard_map/ppermute | solution.py:863
  26.7 0.8 %last.1 = f32[5,4,32,128]{3,2,1,0:T(8,128)} custom-call(f32[5,4,32,128]{3,2,1,0:T(8,128)S(1)} %get-tuple-element.96.base, f32[4,32,128]{2,1,0:T(8,128)S(1)} %get-tuple-element.97.drift, f32[2,2,32,128]{3,2,1,0:T(8,128)S(1)} %get-tuple-element.98.spread, bf16[5,2,32,128]{3,2,1,0:T(8,128)(2,1)S(1)} %collective-permute-done.8.near_psi, ...), custom_call_target="tpu_custom_call" | custom-call | flops 1000000 | bytes 1032192 | tf_op jit(solution)/shard_map/last/pallas_call | solution.py:722
  (11 shorter events, 0.0 us)
Async XLA Ops:
  1.9 8.3 %collective-permute-start.1 = (bf16[18,32,128]{2,1,0:T(8,128)(2,1)S(1)}, bf16[18,32,128]{2,1,0:T(8,128)(2,1)S(1)}, u32[]{:S(2)}, u32[]{:S(2)}) collective-permute-start(bf16[18,32,128]{2,1,0:T(8,128)(2,1)S(1)} %get-tuple-element.57), channel_id=1, source_target_pairs={{0,30},{2,4},{4,2},{6,8},{8,6},{10,12},{12,10},{14,16},{16,14},{18... | collective-permute-start | bytes 442376 | tf_op jit(solution)/shard_map/ppermute | solution.py:765
  7.6 2.6 %collective-permute-start = (bf16[18,32,128]{2,1,0:T(8,128)(2,1)S(1)}, bf16[18,32,128]{2,1,0:T(8,128)(2,1)S(1)}, u32[]{:S(2)}, u32[]{:S(2)}) collective-permute-start(bf16[18,32,128]{2,1,0:T(8,128)(2,1)S(1)} %get-tuple-element.56), channel_id=1, source_target_pairs={{0,2},{2,0},{4,6},{6,4},{8,10},{10,8},{12,14},{14,12},{16,18},{18,... | collective-permute-start | bytes 442376 | tf_op jit(solution)/shard_map/ppermute | solution.py:779
  7.6 7.5 %collective-permute-start.3 = (bf16[18,32,128]{2,1,0:T(8,128)(2,1)S(1)}, bf16[18,32,128]{2,1,0:T(8,128)(2,1)S(1)}, u32[]{:S(2)}, u32[]{:S(2)}) collective-permute-start(bf16[18,32,128]{2,1,0:T(8,128)(2,1)S(1)} %get-tuple-element.59), channel_id=1, source_target_pairs={{0,30},{2,4},{4,2},{6,8},{8,6},{10,12},{12,10},{14,16},{16,14},{18... | collective-permute-start | bytes 442376 | tf_op jit(solution)/shard_map/ppermute | solution.py:778
  8.3 6.9 %collective-permute-start.2 = (bf16[18,32,128]{2,1,0:T(8,128)(2,1)S(1)}, bf16[18,32,128]{2,1,0:T(8,128)(2,1)S(1)}, u32[]{:S(2)}, u32[]{:S(2)}) collective-permute-start(bf16[18,32,128]{2,1,0:T(8,128)(2,1)S(1)} %get-tuple-element.58), channel_id=1, source_target_pairs={{0,2},{2,0},{4,6},{6,4},{8,10},{10,8},{12,14},{14,12},{16,18},{18,... | collective-permute-start | bytes 442376 | tf_op jit(solution)/shard_map/ppermute | solution.py:780
  8.3 4.1 %collective-permute-start.4 = (bf16[5,32,128]{2,1,0:T(8,128)(2,1)S(1)}, bf16[5,32,128]{2,1,0:T(8,128)(2,1)S(1)}, u32[]{:S(2)}, u32[]{:S(2)}) collective-permute-start(bf16[5,32,128]{2,1,0:T(8,128)(2,1)S(1)} %get-tuple-element.60), channel_id=1, source_target_pairs={{0,1},{1,0},{2,3},{3,2},{4,5},{5,4},{6,7},{7,6},{8,9},{9,8},{10,11... | collective-permute-start | bytes 122888 | tf_op jit(solution)/shard_map/ppermute | solution.py:693
  10.4 3.9 %collective-permute-start.5 = (bf16[3,32,128]{2,1,0:T(8,128)(2,1)S(1)}, bf16[3,32,128]{2,1,0:T(8,128)(2,1)S(1)}, u32[]{:S(2)}, u32[]{:S(2)}) collective-permute-start(bf16[3,32,128]{2,1,0:T(8,128)(2,1)S(1)} %get-tuple-element.71), channel_id=1, source_target_pairs={{0,1},{1,0},{2,3},{3,2},{4,5},{5,4},{6,7},{7,6},{8,9},{9,8},{10,11... | collective-permute-start | bytes 73736 | tf_op jit(solution)/shard_map/ppermute | solution.py:693
  15.8 4.0 %collective-permute-start.6 = (bf16[2,32,128]{2,1,0:T(8,128)(2,1)S(1)}, bf16[2,32,128]{2,1,0:T(8,128)(2,1)S(1)}, u32[]{:S(2)}, u32[]{:S(2)}) collective-permute-start(bf16[2,32,128]{2,1,0:T(8,128)(2,1)S(1)} %get-tuple-element.91), channel_id=1, source_target_pairs={{0,1},{1,0},{2,3},{3,2},{4,5},{5,4},{6,7},{7,6},{8,9},{9,8},{10,11... | collective-permute-start | bytes 49160 | tf_op jit(solution)/shard_map/ppermute | solution.py:693
  19.6 3.8 %collective-permute-start.7 = (bf16[1,32,128]{2,1,0:T(8,128)(2,1)S(1)}, bf16[1,32,128]{2,1,0:T(8,128)(2,1)S(1)}, u32[]{:S(2)}, u32[]{:S(2)}) collective-permute-start(bf16[1,32,128]{2,1,0:T(8,128)(2,1)S(1)} %get-tuple-element.95), channel_id=1, source_target_pairs={{0,1},{1,0},{2,3},{3,2},{4,5},{5,4},{6,7},{7,6},{8,9},{9,8},{10,11... | collective-permute-start | bytes 24584 | tf_op jit(solution)/shard_map/ppermute | solution.py:693
  20.1 6.6 %collective-permute-start.9 = (bf16[5,2,32,128]{3,2,1,0:T(8,128)(2,1)S(1)}, bf16[5,2,32,128]{3,2,1,0:T(8,128)(2,1)S(1)}, u32[]{:S(2)}, u32[]{:S(2)}) collective-permute-start(bf16[5,2,32,128]{3,2,1,0:T(8,128)(2,1)S(1)} %get-tuple-element.100), channel_id=1, source_target_pairs={{0,30},{2,4},{4,2},{6,8},{8,6},{10,12},{12,10},{14,16},{16,14},{18... | collective-permute-start | bytes 245768 | tf_op jit(solution)/shard_map/ppermute | solution.py:863
  24.8 1.9 %collective-permute-start.8 = (bf16[5,2,32,128]{3,2,1,0:T(8,128)(2,1)S(1)}, bf16[5,2,32,128]{3,2,1,0:T(8,128)(2,1)S(1)}, u32[]{:S(2)}, u32[]{:S(2)}) collective-permute-start(bf16[5,2,32,128]{3,2,1,0:T(8,128)(2,1)S(1)} %get-tuple-element.99), channel_id=1, source_target_pairs={{0,2},{2,0},{4,6},{6,4},{8,10},{10,8},{12,14},{14,12},{16,18},{18,... | collective-permute-start | bytes 245768 | tf_op jit(solution)/shard_map/ppermute | solution.py:878
